TPU v7x, 32 devices: a whole 2x2x4 slice. The times are simulated.
32 devices in a mesh: seq: 8 (over z, y), tensor: 4 (over x, core).
Axes of the slice: x: 2, y: 2, z: 4, core: 2. Of those that a mesh axis runs over, the one named last changes fastest.
Arguments:
- tokens: bfloat16 [4096, 2048], P('seq'), may hold values from -6 to 6
- norm_gain: float32 [2048], replicated, may hold values from 0.1 to 1.9
- w_qk: bfloat16 [2048, 2048], P(None, 'tensor'), may hold values from -0.125 to 0.125
- w_value: bfloat16 [2048, 2048], P(None, 'tensor'), may hold values from -0.125 to 0.125
- w_out: bfloat16 [2048, 2048], P('tensor'), may hold values from -0.125 to 0.125
- w_up: bfloat16 [2048, 8192], P(None, 'tensor'), may hold values from -0.125 to 0.125
- w_down: bfloat16 [8192, 2048], P('tensor'), may hold values from -0.0625 to 0.0625
- centroids: float32 [16, 256, 128], P('tensor', 'seq'), may hold values from -6 to 6
- clusters: int32 [16, 4096], P('tensor', 'seq'), may hold values from 0 to 255, as said below
- slots: int32 [16, 4096], P('tensor', 'seq'), may hold values from 0 to 3, as said below
Outputs:
- layer_out: bfloat16 [4096, 2048], P(('seq', 'tensor'))
- new_centroids: float32 [16, 256, 128], P('tensor', 'seq')
Inputs may be any that keep to these rules, and one draw needn't show every extreme that they name: `clusters`: within each head and each aligned block of 512 tokens (the tokens of one index of seq) no two tokens have the same cluster and the same slot, so a cluster holds at most 4 tokens of a block; in every such block some cluster holds exactly 4 tokens. `slots`: slots pair with clusters as stated for clusters.
All inputs are finite; a program needn't handle non-finite values.
Results may differ from a plain program's by a relative error of at most 0.01.
Values may be sent and summed in bfloat16 or wider, within the bound.
No kernel may reach another device: no remote copies, remote signals or barrier semaphores. Data moves between devices by JAX's collectives and lax.ppermute only.
A program may use at most 128 MiB of HBM per device.

v0:
```python
import functools

import jax
import jax.numpy as jnp
from jax import lax
from jax.experimental import pallas as pl
from jax.experimental.pallas import tpu as pltpu
from jax.sharding import PartitionSpec as P


CLUSTERS = 256
CAP = 4

SCORE_SCALE = 2.0
EMA_DECAY = 0.9
NORM_EPS = 1e-06
BOTH = ("seq", "tensor")
EXTRA = 16
VMEM_LIMIT = 60 * 1024 * 1024


def rounded(term_value):
    return lax.optimization_barrier(term_value.astype(jnp.bfloat16)).astype(jnp.float32)


def owner_pairs(step, seq_count, tensor_count):
    pairs = []
    for s in range(seq_count):
        for t in range(tensor_count):
            z, y, c = s // 2, s % 2, t % 2
            dest_s = 2 * (z ^ step) + c
            dest_t = (t - c) + (y ^ (z & 1))
            pairs.append((s * tensor_count + t, dest_s * tensor_count + dest_t))
    return pairs


def turned(pairs):
    return [(b, a) for a, b in pairs]


def any_spec():
    return pl.BlockSpec(memory_space=pl.ANY)


def vmem_spec():
    return pl.BlockSpec(memory_space=pltpu.VMEM)


def params():
    return pltpu.CompilerParams(vmem_limit_bytes=VMEM_LIMIT)


def cost(flops, moved, transcendentals=0):
    return pl.CostEstimate(
        flops=flops, bytes_accessed=moved, transcendentals=transcendentals
    )


def shape(dims, kind=jnp.bfloat16):
    return jax.ShapeDtypeStruct(dims, kind)


def project_body(tokens, gain, w_qk, w_value, clusters, *rest, heads, width):
    outs, normed = rest[:heads], rest[heads]
    qk_buf, val_buf, sems = rest[heads + 1 :]
    z = lax.axis_index("seq") >> 1
    pairs = heads // 2
    span = 2 * width

    def copies(p):
        block = p ^ (z >> 1)
        cols = pl.ds(pl.multiple_of(block * span, span), span)
        return (
            pltpu.make_async_copy(w_qk.at[:, cols], qk_buf.at[p], sems.at[2 * p]),
            pltpu.make_async_copy(w_value.at[:, cols], val_buf.at[p], sems.at[2 * p + 1]),
        )

    for p in range(pairs):
        for copy in copies(p):
            copy.start()
    wide = tokens[...].astype(jnp.float32)
    mean = jnp.mean(wide * wide, axis=-1, keepdims=True)
    normed[...] = (wide * lax.rsqrt(mean + NORM_EPS) * gain[...]).astype(jnp.bfloat16)
    rows = tokens.shape[0]
    odd = (z & 1) == 1
    row_at = lax.broadcasted_iota(jnp.int32, (EXTRA, span), 0)
    for p in range(pairs):
        key_copy, val_copy = copies(p)
        key_copy.wait()
        key_proj = jnp.dot(normed[...], qk_buf[p], preferred_element_type=jnp.float32)
        units = []
        for q in range(2):
            k = key_proj[:, q * width : (q + 1) * width]
            total = jnp.sum(k * k, axis=-1, keepdims=True)
            units.append((k * lax.rsqrt(total + NORM_EPS)).astype(jnp.bfloat16))
        val_copy.wait()
        val_proj = jnp.dot(normed[...], val_buf[p], preferred_element_type=jnp.float32)
        values = [
            val_proj[:, q * width : (q + 1) * width].astype(jnp.bfloat16) for q in range(2)
        ]
        for q in range(2):
            out = outs[2 * p + q]
            out[:rows, :width] = jnp.where(odd, units[1 - q], units[q])
            out[:rows, width:] = jnp.where(odd, values[1 - q], values[q])
            id_row = clusters[pl.ds((2 * p + q) ^ z, 1), :].astype(jnp.float32)
            tail = jnp.zeros((EXTRA, span), jnp.float32)
            for part in range(rows // span):
                piece = id_row[:, part * span : (part + 1) * span]
                tail = jnp.where(row_at == part, piece, tail)
            out[rows:, :] = tail.astype(jnp.bfloat16)


def project(tokens, gain, w_qk, w_value, clusters, heads, width):
    rows, depth = tokens.shape
    pairs = heads // 2
    return pl.pallas_call(
        functools.partial(project_body, heads=heads, width=width),
        out_shape=(shape((rows + EXTRA, 2 * width)),) * heads + (shape((rows, depth)),),
        in_specs=[vmem_spec(), vmem_spec(), any_spec(), any_spec(), vmem_spec()],
        out_specs=(vmem_spec(),) * (heads + 1),
        scratch_shapes=[
            pltpu.VMEM((pairs, depth, 2 * width), jnp.bfloat16),
            pltpu.VMEM((pairs, depth, 2 * width), jnp.bfloat16),
            pltpu.SemaphoreType.DMA((2 * pairs,)),
        ],
        compiler_params=params(),
        cost_estimate=cost(
            4 * rows * depth * heads * width,
            4 * (depth * heads * width + rows * depth + rows * heads * width),
        ),
        name="project",
    )(tokens, gain.reshape(1, depth), w_qk, w_value, clusters)


def up_body(normed, w_up, hidden):
    grown = jnp.dot(normed[...], w_up[...], preferred_element_type=jnp.float32)
    hidden[...] = jnp.maximum(grown, 0.0).astype(jnp.bfloat16)


def up(normed, w_up, blocks=2):
    rows, depth = normed.shape
    units = w_up.shape[1]
    block = units // blocks
    return pl.pallas_call(
        up_body,
        grid=(blocks,),
        out_shape=shape((rows, units)),
        in_specs=[
            pl.BlockSpec((rows, depth), lambda i: (0, 0)),
            pl.BlockSpec((depth, block), lambda i: (0, i)),
        ],
        out_specs=pl.BlockSpec((rows, block), lambda i: (0, i)),
        compiler_params=params(),
        cost_estimate=cost(2 * rows * depth * units, 2 * depth * units + 4 * rows * depth),
        name="grow",
    )(normed, w_up)


def down_body(hidden, w_down, mine, away, *, share):
    core = lax.axis_index("tensor") % 2
    part = jnp.dot(hidden[...], w_down[...], preferred_element_type=jnp.float32)
    even = core == 0
    for x in range(2):
        low = part[(2 * x) * share : (2 * x + 1) * share]
        high = part[(2 * x + 1) * share : (2 * x + 2) * share]
        mine[x] = jnp.where(even, low, high)
        away[x] = jnp.where(even, high, low).astype(jnp.bfloat16)


def down(hidden, w_down, share, blocks=2):
    rows, units = hidden.shape
    depth = w_down.shape[1]
    block = depth // blocks
    out = pl.BlockSpec((2, share, block), lambda i: (0, 0, i))
    return pl.pallas_call(
        functools.partial(down_body, share=share),
        grid=(blocks,),
        out_shape=(shape((2, share, depth), jnp.float32), shape((2, share, depth))),
        in_specs=[
            pl.BlockSpec((rows, units), lambda i: (0, 0)),
            pl.BlockSpec((units, block), lambda i: (0, i)),
        ],
        out_specs=(out, out),
        compiler_params=params(),
        cost_estimate=cost(2 * rows * depth * units, 2 * depth * units + 6 * rows * depth),
        name="shrink",
    )(hidden, w_down)


def pick_body(mine, got, sent):
    away = 1 - lax.axis_index("tensor") // 2
    sent[...] = (mine[away] + got[away].astype(jnp.float32)).astype(jnp.bfloat16)


def pick(mine, got):
    return pl.pallas_call(
        pick_body,
        out_shape=shape(mine.shape[1:]),
        in_specs=[vmem_spec(), vmem_spec()],
        out_specs=vmem_spec(),
        compiler_params=params(),
        cost_estimate=cost(mine.size, mine.size * 4),
        name="pick",
    )(mine, got)


def block_of(b, heads):
    z = lax.axis_index("seq") >> 1
    core = lax.axis_index("tensor") % 2
    pair = z ^ (b % heads)
    return 2 * pair + (core ^ (pair & 1) ^ (b // heads))


def attend_body(*refs, heads, width, owned, steps, first):
    if first:
        own, other = refs[:heads], refs[heads : 2 * heads]
        outs = refs[2 * heads : 2 * heads + len(steps)]
        kv, id_rows = refs[2 * heads + len(steps) : 2 * heads + len(steps) + 2]
        query, id_cols, acc, den = refs[2 * heads + len(steps) + 2 :]
        rows = kv.shape[1]
        for b, source in enumerate(list(own) + list(other)):
            kv[b] = source[:rows, :]
            tile = source[rows:, :].astype(jnp.float32)
            id_row = jnp.concatenate(
                [tile[r : r + 1, :] for r in range(rows // (2 * width))], axis=1
            )
            id_rows[b] = jnp.broadcast_to(id_row, (8, rows))
    else:
        kv, id_rows = refs[:2]
        outs = refs[2 : 2 + len(steps)]
        query, id_cols, acc, den = refs[2 + len(steps) :]
        rows = kv.shape[1]

    count = 2 * heads
    cluster_col = lax.broadcasted_iota(jnp.int32, (owned, rows), 0)
    wanted = jnp.concatenate(
        [cluster_col + owned * block_of(k, heads) for k in steps], axis=0
    ).astype(jnp.float32)
    sums = jnp.zeros((len(steps) * owned, width), jnp.float32)
    for b in range(count):
        one_hot = jnp.where(wanted == id_rows[b, :1, :], 1.0, 0.0).astype(jnp.bfloat16)
        sums = sums + jnp.dot(one_hot, kv[b, :, :width], preferred_element_type=jnp.float32)

    def pair(b, masked):
        score = lax.dot_general(
            query[...],
            kv[b, :, :width],
            (((1,), (1,)), ((), ())),
            preferred_element_type=jnp.float32,
        )
        weight = jnp.exp(score)
        same = jnp.concatenate([id_cols[...]] * (rows // width), axis=1) == id_rows[b, :1, :]
        if masked:
            row_at = lax.broadcasted_iota(jnp.int32, weight.shape, 0)
            col_at = lax.broadcasted_iota(jnp.int32, weight.shape, 1)
            same = jnp.logical_and(same, col_at <= row_at)
        weight = jnp.where(same, weight, 0.0)
        share = weight[:, :width]
        for part in range(1, rows // width):
            share = share + weight[:, part * width : (part + 1) * width]
        mixed = jnp.dot(
            weight.astype(jnp.bfloat16), kv[b, :, width:], preferred_element_type=jnp.float32
        )
        if masked:
            den[...] = share
            acc[...] = mixed
        else:
            den[...] += share
            acc[...] += mixed

    for at, k in enumerate(steps):
        query[...] = kv[k, :, :width] * jnp.bfloat16(SCORE_SCALE)
        for part in range(rows // width):
            here = pl.ds(part * width, width)
            id_cols[here, :] = jnp.transpose(
                jnp.broadcast_to(id_rows[k, :1, part * width : (part + 1) * width], (width, width))
            )
        pair(k, True)
        block = block_of(k, heads)

        def per_key(b, carry):
            @pl.when(block_of(b, heads) < block)
            def _():
                pair(b, False)

            return carry

        lax.fori_loop(0, count, per_key, 0)
        out = outs[at]
        whole = jnp.sum(den[...], axis=-1, keepdims=True)
        out[:rows, :] = (acc[...] / whole).astype(jnp.bfloat16)
        out[rows:, :] = sums[at * owned : (at + 1) * owned].astype(jnp.bfloat16)


def attend(inputs, heads, rows, width, owned, steps, first):
    result = shape((rows + owned, width))
    out_shape = (result,) * len(steps)
    if first:
        out_shape += (
            shape((2 * heads, rows, 2 * width)),
            shape((2 * heads, 8, rows), jnp.float32),
        )
    units = (heads * heads + heads // 2) * len(steps) // heads
    return pl.pallas_call(
        functools.partial(
            attend_body, heads=heads, width=width, owned=owned, steps=steps, first=first
        ),
        out_shape=out_shape,
        in_specs=[vmem_spec()] * len(inputs),
        out_specs=(vmem_spec(),) * len(out_shape),
        scratch_shapes=[
            pltpu.VMEM((rows, width), jnp.bfloat16),
            pltpu.VMEM((rows, width), jnp.float32),
            pltpu.VMEM((rows, width), jnp.float32),
            pltpu.VMEM((rows, width), jnp.float32),
        ],
        compiler_params=params(),
        cost_estimate=cost(
            units * rows * rows * width * 8,
            2 * heads * rows * width * 4,
            units * rows * rows,
        ),
        name="attend",
    )(*inputs)


def cut_body(*refs, heads, share):
    back, centroids = refs[:heads], refs[heads]
    kept, away, updated = refs[heads + 1], refs[heads + 2 : -1], refs[-1]
    z = lax.axis_index("seq") >> 1
    at = lax.axis_index("tensor")
    owned = centroids.shape[1]
    for k in range(heads):
        for turn in range(len(away) + 1):
            here = pl.ds(pl.multiple_of((at ^ turn) * share, share), share)
            (kept if turn == 0 else away[turn - 1])[k] = back[k][here, :]
        rows = back[k].shape[0] - owned
        sums = back[k][rows:, :].astype(jnp.float32)
        head = z ^ k
        updated[head] = EMA_DECAY * centroids[head] + (1.0 - EMA_DECAY) * sums


def cut(back, centroids, share, tensor_count):
    heads, width = len(back), back[0].shape[1]
    piece = shape((heads, share, width))
    return pl.pallas_call(
        functools.partial(cut_body, heads=heads, share=share),
        out_shape=(piece,) * tensor_count + (shape(centroids.shape, jnp.float32),),
        in_specs=[vmem_spec()] * (heads + 1),
        out_specs=(vmem_spec(),) * (tensor_count + 1),
        compiler_params=params(),
        cost_estimate=cost(centroids.size, 2 * heads * tensor_count * share * width * 2),
        name="cut",
    )(*back, centroids)


def mix_body(*refs, heads, width, groups):
    pieces, weights = refs[:groups], refs[groups : 2 * groups]
    tokens, mine, got, came, out, left, buf, sems = refs[2 * groups :]
    copies = [
        pltpu.make_async_copy(weights[g], buf.at[g], sems.at[g]) for g in range(groups)
    ]
    for copy in copies:
        copy.start()
    z = lax.axis_index("seq") >> 1
    at = lax.axis_index("tensor")
    share = out.shape[0]
    for g in range(groups):
        for k in range(heads):
            cols = pl.ds(pl.multiple_of((z ^ k) * width, width), width)
            left[g, :, cols] = pieces[g][k]
    x = at // 2
    total = mine[x] + got[x].astype(jnp.float32) + came[...].astype(jnp.float32)
    for g in range(groups):
        copies[g].wait()
        total = total + jnp.dot(left[g], buf[g], preferred_element_type=jnp.float32)
    here = pl.ds(pl.multiple_of(at * share, share), share)
    out[...] = (tokens[here, :].astype(jnp.float32) + total).astype(jnp.bfloat16)


def mix(pieces, weights, tokens, mine, got, came):
    groups = len(pieces)
    heads, share, width = pieces[0].shape
    depth = tokens.shape[1]
    return pl.pallas_call(
        functools.partial(mix_body, heads=heads, width=width, groups=groups),
        out_shape=shape((share, depth)),
        in_specs=[vmem_spec()] * groups + [any_spec()] * groups + [vmem_spec()] * 4,
        out_specs=vmem_spec(),
        scratch_shapes=[
            pltpu.VMEM((groups, share, heads * width), jnp.bfloat16),
            pltpu.VMEM((groups, heads * width, depth), jnp.bfloat16),
            pltpu.SemaphoreType.DMA((groups,)),
        ],
        compiler_params=params(),
        cost_estimate=cost(
            2 * groups * share * heads * width * depth,
            2 * groups * heads * width * depth + 8 * share * depth,
        ),
        name="mix",
    )(*pieces, *weights, tokens, mine, got, came)


def by_heads(
    tokens, norm_gain, w_qk, w_value, w_out, w_up, w_down, centroids, clusters, slots
):
    tok_rows, _ = tokens.shape
    seq_count = lax.axis_size("seq")
    tensor_count = lax.axis_size("tensor")
    heads = clusters.shape[0]
    owned = centroids.shape[1]
    width = w_qk.shape[1] // heads
    share = tok_rows // tensor_count
    swaps = [None] + [[(t, t ^ d) for t in range(tensor_count)] for d in range(1, tensor_count)]

    w_x = lax.ppermute(w_out, "tensor", swaps[2])
    w_core = lax.ppermute(w_out, "tensor", swaps[1])

    *messages, normed = project(tokens, norm_gain, w_qk, w_value, clusters, heads, width)
    steps = [owner_pairs(k, seq_count, tensor_count) for k in range(heads)]
    own, other = [None] * heads, [None] * heads
    for k in reversed(range(heads)):
        own[k] = lax.ppermute(messages[k], BOTH, steps[k])
    hidden = up(normed, w_up)
    for k in range(heads):
        other[k] = lax.ppermute(own[k], "tensor", swaps[1])
    mine, sent = down(hidden, w_down, share)
    got = lax.ppermute(sent, "tensor", swaps[1])
    picked = pick(mine, got)
    came = lax.ppermute(picked, "tensor", swaps[2])
    w_both = lax.ppermute(w_x, "tensor", swaps[1])

    back = [None] * heads
    far = tuple(reversed(range(heads // 2, heads)))
    near = tuple(reversed(range(heads // 2)))
    *results, kv, id_rows = attend(
        own + other, heads, tok_rows, width, owned, far, True
    )
    for k, result in zip(far, results):
        back[k] = lax.ppermute(result, BOTH, turned(steps[k]))
    results = attend([kv, id_rows], heads, tok_rows, width, owned, near, False)
    for k, result in zip(near, results):
        back[k] = lax.ppermute(result, BOTH, turned(steps[k]))

    kept, *away, new_centroids = cut(back, centroids, share, tensor_count)
    arrived = [lax.ppermute(away[d - 1], "tensor", swaps[d]) for d in range(1, tensor_count)]
    mixed_rows = mix(
        [kept] + arrived, [w_out, w_core, w_x, w_both], tokens, mine, got, came
    )
    return (mixed_rows, new_centroids)


def by_clusters(tokens, norm_gain, w_qk, w_value, w_out, w_up, w_down, centroids, clusters, slots):
    tok_rows = tokens.shape[0]
    seq_count = lax.axis_size("seq")
    tensor_count = lax.axis_size("tensor")
    heads_here = clusters.shape[0]
    owned_count = centroids.shape[1]
    head_width = w_qk.shape[1] // heads_here
    share_rows = tok_rows // tensor_count
    row_first = lax.axis_index("tensor") * share_rows
    tokens_wide = tokens.astype(jnp.float32)
    normed = (
        tokens_wide
        * lax.rsqrt(jnp.mean(tokens_wide * tokens_wide, axis=-1, keepdims=True) + NORM_EPS)
        * norm_gain
    ).astype(jnp.bfloat16)
    key_proj = jnp.dot(normed, w_qk, preferred_element_type=jnp.float32).reshape(
        tok_rows, heads_here, head_width
    )
    key_unit = (
        key_proj * lax.rsqrt(jnp.sum(key_proj * key_proj, axis=-1, keepdims=True) + NORM_EPS)
    ).astype(jnp.bfloat16)
    val_proj = (
        jnp.dot(normed, w_value, preferred_element_type=jnp.float32)
        .astype(jnp.bfloat16)
        .reshape(tok_rows, heads_here, head_width)
    )
    positions = lax.axis_index("seq") * tok_rows + jnp.arange(tok_rows, dtype=jnp.int32)
    pos_high = (positions // 256).astype(jnp.float32).astype(jnp.bfloat16)
    pos_low = (positions % 256).astype(jnp.float32).astype(jnp.bfloat16)
    flat_slot = clusters.T * CAP + slots.T
    head_grid = jnp.broadcast_to(jnp.arange(heads_here, dtype=jnp.int32)[None, :], flat_slot.shape)
    slot_total = CLUSTERS * CAP
    layout = (heads_here, seq_count, owned_count, CAP)
    key_buf = (
        jnp.zeros((heads_here, slot_total, head_width), jnp.bfloat16)
        .at[head_grid, flat_slot]
        .set(key_unit)
        .reshape(layout + (head_width,))
    )
    val_buf = (
        jnp.zeros((heads_here, slot_total, head_width), jnp.bfloat16)
        .at[head_grid, flat_slot]
        .set(val_proj)
        .reshape(layout + (head_width,))
    )
    high_buf = (
        jnp.full((heads_here, slot_total), 256.0, jnp.bfloat16)
        .at[head_grid, flat_slot]
        .set(jnp.broadcast_to(pos_high[:, None], flat_slot.shape))
        .reshape(layout)
    )
    low_buf = (
        jnp.zeros((heads_here, slot_total), jnp.bfloat16)
        .at[head_grid, flat_slot]
        .set(jnp.broadcast_to(pos_low[:, None], flat_slot.shape))
        .reshape(layout)
    )
    key_in = lax.all_to_all(key_buf, "seq", split_axis=1, concat_axis=1, tiled=True)
    val_in = lax.all_to_all(val_buf, "seq", split_axis=1, concat_axis=1, tiled=True)
    high_in = lax.all_to_all(high_buf, "seq", split_axis=1, concat_axis=1, tiled=True)
    low_in = lax.all_to_all(low_buf, "seq", split_axis=1, concat_axis=1, tiled=True)
    scores = (
        jnp.einsum("hskad,htkbd->hksatb", key_in, key_in, preferred_element_type=jnp.float32)
        * SCORE_SCALE
    )
    key_place = high_in.astype(jnp.float32) * 256.0 + low_in.astype(jnp.float32)
    ordered = jnp.transpose(key_place, (0, 2, 1, 3))
    causal = ordered[:, :, None, None, :, :] <= ordered[:, :, :, :, None, None]
    exponent = jnp.where(causal, jnp.exp(scores), 0.0)
    weights = (exponent / jnp.sum(exponent, axis=(4, 5), keepdims=True)).astype(jnp.bfloat16)
    mixed_out = jnp.einsum(
        "hksatb,htkbd->hskad", weights, val_in, preferred_element_type=jnp.float32
    ).astype(jnp.bfloat16)
    returned_back = lax.all_to_all(mixed_out, "seq", split_axis=1, concat_axis=1, tiled=True)
    one_hot = (clusters[:, :, None] == jnp.arange(CLUSTERS, dtype=jnp.int32)[None, None, :]).astype(
        jnp.bfloat16
    )
    local_sums = jnp.einsum("htk,thd->hkd", one_hot, key_unit, preferred_element_type=jnp.float32)
    totals = lax.psum_scatter(
        local_sums.astype(jnp.bfloat16), "seq", scatter_dimension=1, tiled=True
    ).astype(jnp.float32)
    new_centroids = EMA_DECAY * centroids + (1.0 - EMA_DECAY) * totals
    returned = returned_back.reshape(heads_here, slot_total, head_width)
    attended = returned[head_grid, flat_slot].reshape(tok_rows, heads_here * head_width)
    attn_part = jnp.dot(attended, w_out, preferred_element_type=jnp.float32)
    hidden = jax.nn.relu(jnp.dot(normed, w_up, preferred_element_type=jnp.float32)).astype(
        jnp.bfloat16
    )
    ffn_part = jnp.dot(hidden, w_down, preferred_element_type=jnp.float32)
    summed = lax.psum_scatter(
        rounded(attn_part + ffn_part).astype(jnp.bfloat16),
        "tensor",
        scatter_dimension=0,
        tiled=True,
    ).astype(jnp.float32)
    own_rows = lax.dynamic_slice_in_dim(tokens_wide, row_first, share_rows, 0)
    mixed_rows = (own_rows + summed).astype(jnp.bfloat16)
    return (mixed_rows, new_centroids)


def solution(mesh):
    in_specs = (
        P("seq", None),
        P(),
        P(None, "tensor"),
        P(None, "tensor"),
        P("tensor", None),
        P(None, "tensor"),
        P("tensor", None),
        P("tensor", "seq", None),
        P("tensor", "seq"),
        P("tensor", "seq"),
    )
    out_specs = (P(("seq", "tensor"), None), P("tensor", "seq", None))
    sizes = dict(mesh.shape)

    def local(*args):
        heads = args[8].shape[0]
        fits = (
            sizes["tensor"] == 4
            and sizes["seq"] == 2 * heads
            and heads & (heads - 1) == 0
            and heads > 1
        )
        if not fits:
            return by_clusters(*args)
        return by_heads(*args)

    return jax.shard_map(
        local, mesh=mesh, in_specs=in_specs, out_specs=out_specs, check_vma=False
    )
```

profile of v0, /device:TPU:0, one launch (start us, length us, event | category | flops | bytes accessed | tf_op | source)
XLA Modules:
  0.0 137.0 jit_solution(13846730934468006481)
XLA Ops:
  0.6 3.0 %collective-permute-start.16 = (bf16[512,2048]{1,0:T(8,128)(2,1)}, bf16[512,2048]{1,0:T(8,128)(2,1)S(1)}, u32[]{:S(2)}, u32[]{:S(2)}) collective-permute-start(bf16[512,2048]{1,0:T(8,128)(2,1)} %refs_4_.3), channel_id=1, source_target_pairs={{0,2},{1,3},{2,0},{3,1},{4,6},{5,7},{6,4},{7,5},{8,10},{9,11},{10,... | collective-permute-start | bytes 6291464 | tf_op jit(solution)/shard_map/ppermute | solution.py:416
  3.7 9.6 %project.1 = (bf16[528,256]{1,0:T(8,128)(2,1)}, bf16[528,256]{1,0:T(8,128)(2,1)}, bf16[528,256]{1,0:T(8,128)(2,1)}, bf16[528,256]{1,0:T(8,128)(2,1)}, bf16[512,2048]{1,0:T(8,128)(2,1)}) custom-call(bf16[512,2048]{1,0:T(8,128)(2,1)} %refs_8_.1, f32[1,2048]{1,0:T(1,128)} %bitcast.1, bf16[2048,512]{1,0:T(8,128)(2,1)} %w_qk.1, bf16[2048,512]{1,0:T(8,128)(2,1)} %w_value.1, ...), custom_call_target="tpu_custom_call" | custom-call | flops 2147483648 | bytes 9437184 | tf_op jit(solution)/shard_map/project/pallas_call | solution.py:116
  13.2 1.6 %collective-permute-start = (bf16[528,256]{1,0:T(8,128)(2,1)}, bf16[528,256]{1,0:T(8,128)(2,1)S(1)}, u32[]{:S(2)}, u32[]{:S(2)}) collective-permute-start(bf16[528,256]{1,0:T(8,128)(2,1)} %get-tuple-element.20), channel_id=1, source_target_pairs={{0,0},{1,4},{2,2},{3,6},{4,1},{5,5},{6,3},{7,7},{8,9},{9,13},{10,1... | collective-permute-start | bytes 811016 | tf_op jit(solution)/shard_map/ppermute | solution.py:423
  14.9 2.4 %collective-permute-start.1 = (bf16[528,256]{1,0:T(8,128)(2,1)}, bf16[528,256]{1,0:T(8,128)(2,1)S(1)}, u32[]{:S(2)}, u32[]{:S(2)}) collective-permute-start(bf16[528,256]{1,0:T(8,128)(2,1)} %get-tuple-element.21), channel_id=1, source_target_pairs={{0,8},{1,12},{2,10},{3,14},{4,9},{5,13},{6,11},{7,15},{8,1},{9,5},... | collective-permute-start | bytes 811016 | tf_op jit(solution)/shard_map/ppermute | solution.py:423
  17.3 2.6 %collective-permute-start.2 = (bf16[528,256]{1,0:T(8,128)(2,1)}, bf16[528,256]{1,0:T(8,128)(2,1)S(1)}, u32[]{:S(2)}, u32[]{:S(2)}) collective-permute-start(bf16[528,256]{1,0:T(8,128)(2,1)} %get-tuple-element.22), channel_id=1, source_target_pairs={{0,16},{1,20},{2,18},{3,22},{4,17},{5,21},{6,19},{7,23},{8,25},{9,... | collective-permute-start | bytes 811016 | tf_op jit(solution)/shard_map/ppermute | solution.py:423
  19.9 29.6 %collective-permute-done.16.refs_6_ = bf16[512,2048]{1,0:T(8,128)(2,1)S(1)} collective-permute-done((bf16[512,2048]{1,0:T(8,128)(2,1)}, bf16[512,2048]{1,0:T(8,128)(2,1)S(1)}, u32[]{:S(2)}, u32[]{:S(2)}) %collective-permute-start.16) | collective-permute-done | bytes 2097184 | tf_op jit(solution)/shard_map/ppermute | solution.py:416
  49.5 9.3 %grow.1.hidden = bf16[512,2048]{1,0:T(8,128)(2,1)} custom-call(bf16[512,2048]{1,0:T(8,128)(2,1)} %get-tuple-element.34.normed, bf16[2048,2048]{1,0:T(8,128)(2,1)} %w_up.1), custom_call_target="tpu_custom_call" | custom-call | flops 4294967296 | bytes 12582912 | tf_op jit(solution)/shard_map/grow/pallas_call | solution.py:144
  58.8 3.9 %collective-permute-start.3 = (bf16[528,256]{1,0:T(8,128)(2,1)}, bf16[528,256]{1,0:T(8,128)(2,1)}, u32[]{:S(2)}, u32[]{:S(2)}) collective-permute-start(bf16[528,256]{1,0:T(8,128)(2,1)} %get-tuple-element.23), channel_id=1, source_target_pairs={{0,24},{1,28},{2,26},{3,30},{4,25},{5,29},{6,27},{7,31},{8,17},{9,... | collective-permute-start | bytes 811016 | tf_op jit(solution)/shard_map/ppermute | solution.py:423
  62.7 8.8 %shrink.1 = (f32[2,128,2048]{2,1,0:T(8,128)}, bf16[2,128,2048]{2,1,0:T(8,128)(2,1)}) custom-call(bf16[512,2048]{1,0:T(8,128)(2,1)} %grow.1.hidden, bf16[2048,2048]{1,0:T(8,128)(2,1)} %w_down.1), custom_call_target="tpu_custom_call" | custom-call | flops 4294967296 | bytes 14680064 | tf_op jit(solution)/shard_map/shrink/pallas_call | solution.py:175
  71.5 1.1 collective-permute-start.18
  73.2 2.3 %collective-permute-done.4.refs_4_ = bf16[528,256]{1,0:T(8,128)(2,1)S(1)} collective-permute-done((bf16[528,256]{1,0:T(8,128)(2,1)S(1)}, bf16[528,256]{1,0:T(8,128)(2,1)S(1)}, u32[]{:S(2)}, u32[]{:S(2)}) %collective-permute-start.4) | collective-permute-done | bytes 270368 | tf_op jit(solution)/shard_map/ppermute | solution.py:426
  77.8 10.3 %attend.2 = (bf16[544,128]{1,0:T(8,128)(2,1)}, bf16[544,128]{1,0:T(8,128)(2,1)}, bf16[8,512,256]{2,1,0:T(8,128)(2,1)}, f32[8,8,512]{2,1,0:T(8,128)}) custom-call(bf16[528,256]{1,0:T(8,128)(2,1)} %copy-done.10, bf16[528,256]{1,0:T(8,128)(2,1)} %copy-done.11, bf16[528,256]{1,0:T(8,128)(2,1)} %copy-done.12, bf16[528,256]{1,0:T(8,128)(2,1)} %collective-permute-done.3.refs_3_, ...), custom_call_target="tpu_custom_call" | custom-call | flops 2415919104 | bytes 2097152 | tf_op jit(solution)/shard_map/attend/pallas_call | solution.py:304
  88.1 5.5 %attend.3 = (bf16[544,128]{1,0:T(8,128)(2,1)}, bf16[544,128]{1,0:T(8,128)(2,1)}) custom-call(bf16[8,512,256]{2,1,0:T(8,128)(2,1)} %get-tuple-element.24.refs_0_, f32[8,8,512]{2,1,0:T(8,128)} %get-tuple-element.25.refs_1_), custom_call_target="tpu_custom_call" | custom-call | flops 2415919104 | bytes 2097152 | tf_op jit(solution)/shard_map/attend/pallas_call | solution.py:304
  93.6 1.7 %collective-permute-start.8 = (bf16[544,128]{1,0:T(8,128)(2,1)}, bf16[544,128]{1,0:T(8,128)(2,1)S(1)}, u32[]{:S(2)}, u32[]{:S(2)}) collective-permute-start(bf16[544,128]{1,0:T(8,128)(2,1)} %get-tuple-element.26), channel_id=1, source_target_pairs={{0,0},{4,1},{2,2},{6,3},{1,4},{5,5},{3,6},{7,7},{9,8},{13,9},{11,1... | collective-permute-start | bytes 417800 | tf_op jit(solution)/shard_map/ppermute | solution.py:443
  95.3 3.4 %collective-permute-start.9 = (bf16[544,128]{1,0:T(8,128)(2,1)}, bf16[544,128]{1,0:T(8,128)(2,1)S(1)}, u32[]{:S(2)}, u32[]{:S(2)}) collective-permute-start(bf16[544,128]{1,0:T(8,128)(2,1)} %get-tuple-element.27), channel_id=1, source_target_pairs={{8,0},{12,1},{10,2},{14,3},{9,4},{13,5},{11,6},{15,7},{1,8},{5,9},... | collective-permute-start | bytes 417800 | tf_op jit(solution)/shard_map/ppermute | solution.py:443
  98.7 1.0 copy-done
  99.6 2.7 %pick.1 = bf16[128,2048]{1,0:T(8,128)(2,1)} custom-call(f32[2,128,2048]{2,1,0:T(8,128)} %get-tuple-element.35.mine.refs_9_, bf16[2,128,2048]{2,1,0:T(8,128)(2,1)} %copy-done), custom_call_target="tpu_custom_call" | custom-call | flops 524288 | bytes 2097152 | tf_op jit(solution)/shard_map/pick/pallas_call | solution.py:196
  102.4 1.5 %collective-permute-start.19 = (bf16[128,2048]{1,0:T(8,128)(2,1)}, bf16[128,2048]{1,0:T(8,128)(2,1)S(1)}, u32[]{:S(2)}, u32[]{:S(2)}) collective-permute-start(bf16[128,2048]{1,0:T(8,128)(2,1)} %pick.1), channel_id=1, source_target_pairs={{0,2},{1,3},{2,0},{3,1},{4,6},{5,7},{6,4},{7,5},{8,10},{9,11},{10,... | collective-permute-start | bytes 1572872 | tf_op jit(solution)/shard_map/ppermute | solution.py:430
  104.0 2.6 %collective-permute-start.11 = (bf16[544,128]{1,0:T(8,128)(2,1)S(1)}, bf16[544,128]{1,0:T(8,128)(2,1)S(1)}, u32[]{:S(2)}, u32[]{:S(2)}) collective-permute-start(bf16[544,128]{1,0:T(8,128)(2,1)S(1)} %copy-done.16), channel_id=1, source_target_pairs={{24,0},{28,1},{26,2},{30,3},{25,4},{29,5},{27,6},{31,7},{17,8},{21... | collective-permute-start | bytes 417800 | tf_op jit(solution)/shard_map/ppermute | solution.py:440
  106.5 10.2 %collective-permute-done.10.refs_2_ = bf16[544,128]{1,0:T(8,128)(2,1)S(1)} collective-permute-done((bf16[544,128]{1,0:T(8,128)(2,1)S(1)}, bf16[544,128]{1,0:T(8,128)(2,1)S(1)}, u32[]{:S(2)}, u32[]{:S(2)}) %collective-permute-start.10) | collective-permute-done | bytes 139296 | tf_op jit(solution)/shard_map/ppermute | solution.py:440
  118.0 1.9 %cut.1 = (bf16[4,128,128]{2,1,0:T(8,128)(2,1)}, bf16[4,128,128]{2,1,0:T(8,128)(2,1)}, bf16[4,128,128]{2,1,0:T(8,128)(2,1)}, bf16[4,128,128]{2,1,0:T(8,128)(2,1)}, f32[4,32,128]{2,1,0:T(8,128)}) custom-call(bf16[544,128]{1,0:T(8,128)(2,1)} %copy-done.3, bf16[544,128]{1,0:T(8,128)(2,1)} %copy-done.4, bf16[544,128]{1,0:T(8,128)(2,1)} %copy-done.5, ...), custom_call_target="tpu_custom_call" | custom-call | flops 16384 | bytes 1048576 | tf_op jit(solution)/shard_map/cut/pallas_call | solution.py:346
  121.9 4.8 %collective-permute-done.13.refs_2_ = bf16[4,128,128]{2,1,0:T(8,128)(2,1)S(1)} collective-permute-done((bf16[4,128,128]{2,1,0:T(8,128)(2,1)}, bf16[4,128,128]{2,1,0:T(8,128)(2,1)S(1)}, u32[]{:S(2)}, u32[]{:S(2)}) %collective-permute-start.13) | collective-permute-done | bytes 131104 | tf_op jit(solution)/shard_map/ppermute | solution.py:446
  126.7 1.7 %collective-permute-done.14.refs_3_ = bf16[4,128,128]{2,1,0:T(8,128)(2,1)S(1)} collective-permute-done((bf16[4,128,128]{2,1,0:T(8,128)(2,1)}, bf16[4,128,128]{2,1,0:T(8,128)(2,1)S(1)}, u32[]{:S(2)}, u32[]{:S(2)}) %collective-permute-start.14) | collective-permute-done | bytes 131104 | tf_op jit(solution)/shard_map/ppermute | solution.py:446
  129.2 7.6 %mix.1 = bf16[128,2048]{1,0:T(8,128)(2,1)} custom-call(bf16[4,128,128]{2,1,0:T(8,128)(2,1)} %get-tuple-element.30.refs_0_, bf16[4,128,128]{2,1,0:T(8,128)(2,1)} %copy-done.7, bf16[4,128,128]{2,1,0:T(8,128)(2,1)} %copy-done.8, bf16[4,128,128]{2,1,0:T(8,128)(2,1)} %copy-done.9, bf16[512,2048]{1,0:T(8,128)(2,1)} %refs_4_.3, ...), custom_call_target="tpu_custom_call" | custom-call | flops 1073741824 | bytes 10485760 | tf_op jit(solution)/shard_map/mix/pallas_call | solution.py:385
  (60 shorter events, 6.9 us)
Async XLA Ops:
  0.6 48.9 %collective-permute-start.16 = (bf16[512,2048]{1,0:T(8,128)(2,1)}, bf16[512,2048]{1,0:T(8,128)(2,1)S(1)}, u32[]{:S(2)}, u32[]{:S(2)}) collective-permute-start(bf16[512,2048]{1,0:T(8,128)(2,1)} %refs_4_.3), channel_id=1, source_target_pairs={{0,2},{1,3},{2,0},{3,1},{4,6},{5,7},{6,4},{7,5},{8,10},{9,11},{10,... | collective-permute-start | bytes 6291464 | tf_op jit(solution)/shard_map/ppermute | solution.py:416
  3.7 124.7 %collective-permute-start.15 = (bf16[512,2048]{1,0:T(8,128)(2,1)}, bf16[512,2048]{1,0:T(8,128)(2,1)}, u32[]{:S(2)}, u32[]{:S(2)}) collective-permute-start(bf16[512,2048]{1,0:T(8,128)(2,1)} %refs_4_.3), channel_id=1, source_target_pairs={{0,1},{1,0},{2,3},{3,2},{4,5},{5,4},{6,7},{7,6},{8,9},{9,8},{10,11... | collective-permute-start | bytes 6291464 | tf_op jit(solution)/shard_map/ppermute | solution.py:417
  13.2 45.6 %collective-permute-start = (bf16[528,256]{1,0:T(8,128)(2,1)}, bf16[528,256]{1,0:T(8,128)(2,1)S(1)}, u32[]{:S(2)}, u32[]{:S(2)}) collective-permute-start(bf16[528,256]{1,0:T(8,128)(2,1)} %get-tuple-element.20), channel_id=1, source_target_pairs={{0,0},{1,4},{2,2},{3,6},{4,1},{5,5},{6,3},{7,7},{8,9},{9,13},{10,1... | collective-permute-start | bytes 811016 | tf_op jit(solution)/shard_map/ppermute | solution.py:423
  14.9 56.7 %collective-permute-start.1 = (bf16[528,256]{1,0:T(8,128)(2,1)}, bf16[528,256]{1,0:T(8,128)(2,1)S(1)}, u32[]{:S(2)}, u32[]{:S(2)}) collective-permute-start(bf16[528,256]{1,0:T(8,128)(2,1)} %get-tuple-element.21), channel_id=1, source_target_pairs={{0,8},{1,12},{2,10},{3,14},{4,9},{5,13},{6,11},{7,15},{8,1},{9,5},... | collective-permute-start | bytes 811016 | tf_op jit(solution)/shard_map/ppermute | solution.py:423
  17.3 55.4 %collective-permute-start.2 = (bf16[528,256]{1,0:T(8,128)(2,1)}, bf16[528,256]{1,0:T(8,128)(2,1)S(1)}, u32[]{:S(2)}, u32[]{:S(2)}) collective-permute-start(bf16[528,256]{1,0:T(8,128)(2,1)} %get-tuple-element.22), channel_id=1, source_target_pairs={{0,16},{1,20},{2,18},{3,22},{4,17},{5,21},{6,19},{7,23},{8,25},{9,... | collective-permute-start | bytes 811016 | tf_op jit(solution)/shard_map/ppermute | solution.py:423
  49.5 78.9 %collective-permute-start.17 = (bf16[512,2048]{1,0:T(8,128)(2,1)S(1)}, bf16[512,2048]{1,0:T(8,128)(2,1)}, u32[]{:S(2)}, u32[]{:S(2)}) collective-permute-start(bf16[512,2048]{1,0:T(8,128)(2,1)S(1)} %collective-permute-done.16.refs_6_), channel_id=1, source_target_pairs={{0,1},{1,0},{2,3},{3,2},{4,5},{5,4},{6,7},{7,6},{8,9},{9,8},{10,11... | collective-permute-start | bytes 6291464 | tf_op jit(solution)/shard_map/ppermute | solution.py:431
  58.8 13.9 %copy-start.10 = (bf16[528,256]{1,0:T(8,128)(2,1)}, bf16[528,256]{1,0:T(8,128)(2,1)S(1)}, u32[]{:S(2)}) copy-start(bf16[528,256]{1,0:T(8,128)(2,1)S(1)} %collective-permute-done.refs_0_) | copy-start | bytes 811012
  58.8 13.9 %collective-permute-start.3 = (bf16[528,256]{1,0:T(8,128)(2,1)}, bf16[528,256]{1,0:T(8,128)(2,1)}, u32[]{:S(2)}, u32[]{:S(2)}) collective-permute-start(bf16[528,256]{1,0:T(8,128)(2,1)} %get-tuple-element.23), channel_id=1, source_target_pairs={{0,24},{1,28},{2,26},{3,30},{4,25},{5,29},{6,27},{7,31},{8,17},{9,... | collective-permute-start | bytes 811016 | tf_op jit(solution)/shard_map/ppermute | solution.py:423
  71.5 27.1 %collective-permute-start.18 = (bf16[2,128,2048]{2,1,0:T(8,128)(2,1)}, bf16[2,128,2048]{2,1,0:T(8,128)(2,1)S(1)}, u32[]{:S(2)}, u32[]{:S(2)}) collective-permute-start(bf16[2,128,2048]{2,1,0:T(8,128)(2,1)} %get-tuple-element.36), channel_id=1, source_target_pairs={{0,1},{1,0},{2,3},{3,2},{4,5},{5,4},{6,7},{7,6},{8,9},{9,8},{10,11... | collective-permute-start | bytes 3145736 | tf_op jit(solution)/shard_map/ppermute | solution.py:428
  72.7 2.9 %collective-permute-start.4 = (bf16[528,256]{1,0:T(8,128)(2,1)S(1)}, bf16[528,256]{1,0:T(8,128)(2,1)S(1)}, u32[]{:S(2)}, u32[]{:S(2)}) collective-permute-start(bf16[528,256]{1,0:T(8,128)(2,1)S(1)} %collective-permute-done.refs_0_), channel_id=1, source_target_pairs={{0,1},{1,0},{2,3},{3,2},{4,5},{5,4},{6,7},{7,6},{8,9},{9,8},{10,11... | collective-permute-start | bytes 811016 | tf_op jit(solution)/shard_map/ppermute | solution.py:426
  72.8 3.2 %collective-permute-start.5 = (bf16[528,256]{1,0:T(8,128)(2,1)S(1)}, bf16[528,256]{1,0:T(8,128)(2,1)S(1)}, u32[]{:S(2)}, u32[]{:S(2)}) collective-permute-start(bf16[528,256]{1,0:T(8,128)(2,1)S(1)} %collective-permute-done.1.refs_1_), channel_id=1, source_target_pairs={{0,1},{1,0},{2,3},{3,2},{4,5},{5,4},{6,7},{7,6},{8,9},{9,8},{10,11... | collective-permute-start | bytes 811016 | tf_op jit(solution)/shard_map/ppermute | solution.py:426
  75.5 1.5 %collective-permute-start.6 = (bf16[528,256]{1,0:T(8,128)(2,1)S(1)}, bf16[528,256]{1,0:T(8,128)(2,1)S(1)}, u32[]{:S(2)}, u32[]{:S(2)}) collective-permute-start(bf16[528,256]{1,0:T(8,128)(2,1)S(1)} %collective-permute-done.2.refs_2_), channel_id=1, source_target_pairs={{0,1},{1,0},{2,3},{3,2},{4,5},{5,4},{6,7},{7,6},{8,9},{9,8},{10,11... | collective-permute-start | bytes 811016 | tf_op jit(solution)/shard_map/ppermute | solution.py:426
  75.9 1.9 %collective-permute-start.7 = (bf16[528,256]{1,0:T(8,128)(2,1)}, bf16[528,256]{1,0:T(8,128)(2,1)}, u32[]{:S(2)}, u32[]{:S(2)}) collective-permute-start(bf16[528,256]{1,0:T(8,128)(2,1)} %collective-permute-done.3.refs_3_), channel_id=1, source_target_pairs={{0,1},{1,0},{2,3},{3,2},{4,5},{5,4},{6,7},{7,6},{8,9},{9,8},{10,11... | collective-permute-start | bytes 811016 | tf_op jit(solution)/shard_map/ppermute | solution.py:426
  93.6 10.4 %copy-start.16 = (bf16[544,128]{1,0:T(8,128)(2,1)S(1)}, bf16[544,128]{1,0:T(8,128)(2,1)}, u32[]{:S(2)}) copy-start(bf16[544,128]{1,0:T(8,128)(2,1)} %get-tuple-element.29) | copy-start | bytes 417796
  93.6 10.3 %collective-permute-start.8 = (bf16[544,128]{1,0:T(8,128)(2,1)}, bf16[544,128]{1,0:T(8,128)(2,1)S(1)}, u32[]{:S(2)}, u32[]{:S(2)}) collective-permute-start(bf16[544,128]{1,0:T(8,128)(2,1)} %get-tuple-element.26), channel_id=1, source_target_pairs={{0,0},{4,1},{2,2},{6,3},{1,4},{5,5},{3,6},{7,7},{9,8},{13,9},{11,1... | collective-permute-start | bytes 417800 | tf_op jit(solution)/shard_map/ppermute | solution.py:443
  95.3 8.7 %collective-permute-start.9 = (bf16[544,128]{1,0:T(8,128)(2,1)}, bf16[544,128]{1,0:T(8,128)(2,1)S(1)}, u32[]{:S(2)}, u32[]{:S(2)}) collective-permute-start(bf16[544,128]{1,0:T(8,128)(2,1)} %get-tuple-element.27), channel_id=1, source_target_pairs={{8,0},{12,1},{10,2},{14,3},{9,4},{13,5},{11,6},{15,7},{1,8},{5,9},... | collective-permute-start | bytes 417800 | tf_op jit(solution)/shard_map/ppermute | solution.py:443
  102.4 26.0 %collective-permute-start.19 = (bf16[128,2048]{1,0:T(8,128)(2,1)}, bf16[128,2048]{1,0:T(8,128)(2,1)S(1)}, u32[]{:S(2)}, u32[]{:S(2)}) collective-permute-start(bf16[128,2048]{1,0:T(8,128)(2,1)} %pick.1), channel_id=1, source_target_pairs={{0,2},{1,3},{2,0},{3,1},{4,6},{5,7},{6,4},{7,5},{8,10},{9,11},{10,... | collective-permute-start | bytes 1572872 | tf_op jit(solution)/shard_map/ppermute | solution.py:430
  103.9 12.9 %copy-start.3 = (bf16[544,128]{1,0:T(8,128)(2,1)}, bf16[544,128]{1,0:T(8,128)(2,1)S(1)}, u32[]{:S(2)}) copy-start(bf16[544,128]{1,0:T(8,128)(2,1)S(1)} %collective-permute-done.8.refs_0_) | copy-start | bytes 417796
  103.9 12.9 %collective-permute-start.10 = (bf16[544,128]{1,0:T(8,128)(2,1)S(1)}, bf16[544,128]{1,0:T(8,128)(2,1)S(1)}, u32[]{:S(2)}, u32[]{:S(2)}) collective-permute-start(bf16[544,128]{1,0:T(8,128)(2,1)S(1)} %copy-done.17), channel_id=1, source_target_pairs={{16,0},{20,1},{18,2},{22,3},{17,4},{21,5},{19,6},{23,7},{25,8},{29... | collective-permute-start | bytes 417800 | tf_op jit(solution)/shard_map/ppermute | solution.py:440
  104.0 12.8 %copy-start.4 = (bf16[544,128]{1,0:T(8,128)(2,1)}, bf16[544,128]{1,0:T(8,128)(2,1)S(1)}, u32[]{:S(2)}) copy-start(bf16[544,128]{1,0:T(8,128)(2,1)S(1)} %collective-permute-done.9.refs_1_) | copy-start | bytes 417796
  104.0 12.8 %collective-permute-start.11 = (bf16[544,128]{1,0:T(8,128)(2,1)S(1)}, bf16[544,128]{1,0:T(8,128)(2,1)S(1)}, u32[]{:S(2)}, u32[]{:S(2)}) collective-permute-start(bf16[544,128]{1,0:T(8,128)(2,1)S(1)} %copy-done.16), channel_id=1, source_target_pairs={{24,0},{28,1},{26,2},{30,3},{25,4},{29,5},{27,6},{31,7},{17,8},{21... | collective-permute-start | bytes 417800 | tf_op jit(solution)/shard_map/ppermute | solution.py:440
  120.0 1.6 %collective-permute-start.12 = (bf16[4,128,128]{2,1,0:T(8,128)(2,1)}, bf16[4,128,128]{2,1,0:T(8,128)(2,1)S(1)}, u32[]{:S(2)}, u32[]{:S(2)}) collective-permute-start(bf16[4,128,128]{2,1,0:T(8,128)(2,1)} %get-tuple-element.31), channel_id=1, source_target_pairs={{0,1},{1,0},{2,3},{3,2},{4,5},{5,4},{6,7},{7,6},{8,9},{9,8},{10,11... | collective-permute-start | bytes 393224 | tf_op jit(solution)/shard_map/ppermute | solution.py:446
  120.1 6.6 %collective-permute-start.13 = (bf16[4,128,128]{2,1,0:T(8,128)(2,1)}, bf16[4,128,128]{2,1,0:T(8,128)(2,1)S(1)}, u32[]{:S(2)}, u32[]{:S(2)}) collective-permute-start(bf16[4,128,128]{2,1,0:T(8,128)(2,1)} %get-tuple-element.32), channel_id=1, source_target_pairs={{0,2},{1,3},{2,0},{3,1},{4,6},{5,7},{6,4},{7,5},{8,10},{9,11},{10,... | collective-permute-start | bytes 393224 | tf_op jit(solution)/shard_map/ppermute | solution.py:446
  121.6 6.8 %collective-permute-start.14 = (bf16[4,128,128]{2,1,0:T(8,128)(2,1)}, bf16[4,128,128]{2,1,0:T(8,128)(2,1)S(1)}, u32[]{:S(2)}, u32[]{:S(2)}) collective-permute-start(bf16[4,128,128]{2,1,0:T(8,128)(2,1)} %get-tuple-element.33), channel_id=1, source_target_pairs={{0,3},{1,2},{2,1},{3,0},{4,7},{5,6},{6,5},{7,4},{8,11},{9,10},{10,... | collective-permute-start | bytes 393224 | tf_op jit(solution)/shard_map/ppermute | solution.py:446
  (14 other events, 46.9 us)
where the time goes:
time: 137 us
  Pallas kernels  55.7 us (41%)
  waiting for transfers between devices  51.1 us (37%)
  starting transfers between devices  26.1 us (19%)
  local copies, waits for them, and re-layouts  3.12 us (2%)
    ppermute x1, waiting for transfers between devices, by_heads(): w_x = lax.ppermute(w_out, 'tensor', swaps[2])  29.6 us
    pallas_call x2, Pallas kernels, attend(): pl.pallas_call(functools.partial(attend_body, heads=heads, width=width, o...  15.7 us
    ppermute x4, starting transfers between devices, by_heads(): own[k] = lax.ppermute(messages[k], BOTH, steps[k])  10.5 us
    ppermute x4, waiting for transfers between devices, by_heads(): back[k] = lax.ppermute(result, BOTH, turned(steps[k]))  10.2 us
    pallas_call x1, Pallas kernels, project(): pl.pallas_call(functools.partial(project_body, heads=heads, width=width),...  9.57 us
    pallas_call x1, Pallas kernels, up(): pl.pallas_call(up_body, grid=(blocks,), out_shape=shape((rows, units)), i...  9.3 us
    pallas_call x1, Pallas kernels, down(): pl.pallas_call(functools.partial(down_body, share=share), grid=(blocks,),...  8.79 us
    ppermute x4, starting transfers between devices, by_heads(): back[k] = lax.ppermute(result, BOTH, turned(steps[k]))  7.68 us
  transfers between devices with their start and end apart: 20, of which 8 were waited for; matrix products, arithmetic and copies ran while one was open for 0% of the time, Pallas kernels for 35%

commit v1 on v0

--- a/solution.py
+++ b/solution.py
@@ -16,7 +16,7 @@
 NORM_EPS = 1e-06
 BOTH = ("seq", "tensor")
 EXTRA = 16
-VMEM_LIMIT = 60 * 1024 * 1024
+MIB = 1024 * 1024
 
 
 def rounded(term_value):
@@ -46,8 +46,12 @@
     return pl.BlockSpec(memory_space=pltpu.VMEM)
 
 
-def params():
-    return pltpu.CompilerParams(vmem_limit_bytes=VMEM_LIMIT)
+def held(value):
+    return pltpu.with_memory_space_constraint(value, pltpu.HBM)
+
+
+def params(mib):
+    return pltpu.CompilerParams(vmem_limit_bytes=mib * MIB)
 
 
 def cost(flops, moved, transcendentals=0):
@@ -60,9 +64,23 @@
     return jax.ShapeDtypeStruct(dims, kind)
 
 
-def project_body(tokens, gain, w_qk, w_value, clusters, *rest, heads, width):
+def project_body(
+    tokens_at, gain_at, w_qk, w_value, clusters_at, *rest, heads, width, parts
+):
     outs, normed = rest[:heads], rest[heads]
-    qk_buf, val_buf, sems = rest[heads + 1 :]
+    tokens, gain, clusters, qk_buf, val_buf, sems, token_sems, small_sems = rest[heads + 1 :]
+    step = tokens.shape[0] // parts
+    small = (
+        pltpu.make_async_copy(gain_at, gain, small_sems.at[0]),
+        pltpu.make_async_copy(clusters_at, clusters, small_sems.at[1]),
+    )
+    slabs = [pl.ds(r * step, step) for r in range(parts)]
+    slab_copies = [
+        pltpu.make_async_copy(tokens_at.at[here, :], tokens.at[here, :], token_sems.at[r])
+        for r, here in enumerate(slabs)
+    ]
+    for copy in (small[0], *slab_copies, small[1]):
+        copy.start()
     z = lax.axis_index("seq") >> 1
     pairs = heads // 2
     span = 2 * width
@@ -78,9 +96,13 @@
     for p in range(pairs):
         for copy in copies(p):
             copy.start()
-    wide = tokens[...].astype(jnp.float32)
-    mean = jnp.mean(wide * wide, axis=-1, keepdims=True)
-    normed[...] = (wide * lax.rsqrt(mean + NORM_EPS) * gain[...]).astype(jnp.bfloat16)
+    small[0].wait()
+    for copy, here in zip(slab_copies, slabs):
+        copy.wait()
+        wide = tokens[here, :].astype(jnp.float32)
+        mean = jnp.mean(wide * wide, axis=-1, keepdims=True)
+        normed[here, :] = (wide * lax.rsqrt(mean + NORM_EPS) * gain[...]).astype(jnp.bfloat16)
+    small[1].wait()
     rows = tokens.shape[0]
     odd = (z & 1) == 1
     row_at = lax.broadcasted_iota(jnp.int32, (EXTRA, span), 0)
@@ -110,26 +132,31 @@
             out[rows:, :] = tail.astype(jnp.bfloat16)
 
 
-def project(tokens, gain, w_qk, w_value, clusters, heads, width):
+def project(tokens, gain, w_qk, w_value, clusters, heads, width, parts=4):
     rows, depth = tokens.shape
     pairs = heads // 2
     return pl.pallas_call(
-        functools.partial(project_body, heads=heads, width=width),
+        functools.partial(project_body, heads=heads, width=width, parts=parts),
         out_shape=(shape((rows + EXTRA, 2 * width)),) * heads + (shape((rows, depth)),),
-        in_specs=[vmem_spec(), vmem_spec(), any_spec(), any_spec(), vmem_spec()],
+        in_specs=[any_spec()] * 5,
         out_specs=(vmem_spec(),) * (heads + 1),
         scratch_shapes=[
+            pltpu.VMEM((rows, depth), jnp.bfloat16),
+            pltpu.VMEM((1, depth), jnp.float32),
+            pltpu.VMEM(clusters.shape, jnp.int32),
             pltpu.VMEM((pairs, depth, 2 * width), jnp.bfloat16),
             pltpu.VMEM((pairs, depth, 2 * width), jnp.bfloat16),
             pltpu.SemaphoreType.DMA((2 * pairs,)),
+            pltpu.SemaphoreType.DMA((parts,)),
+            pltpu.SemaphoreType.DMA((2,)),
         ],
-        compiler_params=params(),
+        compiler_params=params(20),
         cost_estimate=cost(
             4 * rows * depth * heads * width,
             4 * (depth * heads * width + rows * depth + rows * heads * width),
         ),
         name="project",
-    )(tokens, gain.reshape(1, depth), w_qk, w_value, clusters)
+    )(*[held(a) for a in (tokens, gain.reshape(1, depth), w_qk, w_value, clusters)])
 
 
 def up_body(normed, w_up, hidden):
@@ -150,58 +177,48 @@
             pl.BlockSpec((depth, block), lambda i: (0, i)),
         ],
         out_specs=pl.BlockSpec((rows, block), lambda i: (0, i)),
-        compiler_params=params(),
+        compiler_params=params(24),
         cost_estimate=cost(2 * rows * depth * units, 2 * depth * units + 4 * rows * depth),
         name="grow",
     )(normed, w_up)
 
 
-def down_body(hidden, w_down, mine, away, *, share):
-    core = lax.axis_index("tensor") % 2
-    part = jnp.dot(hidden[...], w_down[...], preferred_element_type=jnp.float32)
-    even = core == 0
-    for x in range(2):
-        low = part[(2 * x) * share : (2 * x + 1) * share]
-        high = part[(2 * x + 1) * share : (2 * x + 2) * share]
-        mine[x] = jnp.where(even, low, high)
-        away[x] = jnp.where(even, high, low).astype(jnp.bfloat16)
+def down_body(hidden, w_down, mine, far, away, held, *, share):
+    at = lax.axis_index("tensor")
+    held[...] = jnp.dot(hidden[...], w_down[...], preferred_element_type=jnp.float32)
+
+    def quarter(turn):
+        return held[pl.ds(pl.multiple_of((at ^ turn) * share, share), share), :]
+
+    mine[...] = quarter(0)
+    far[...] = quarter(2)
+    away[0] = quarter(1).astype(jnp.bfloat16)
+    away[1] = quarter(3).astype(jnp.bfloat16)
 
 
 def down(hidden, w_down, share, blocks=2):
     rows, units = hidden.shape
     depth = w_down.shape[1]
     block = depth // blocks
-    out = pl.BlockSpec((2, share, block), lambda i: (0, 0, i))
+    one = pl.BlockSpec((share, block), lambda i: (0, i))
     return pl.pallas_call(
         functools.partial(down_body, share=share),
         grid=(blocks,),
-        out_shape=(shape((2, share, depth), jnp.float32), shape((2, share, depth))),
+        out_shape=(
+            shape((share, depth), jnp.float32),
+            shape((share, depth), jnp.float32),
+            shape((2, share, depth)),
+        ),
         in_specs=[
             pl.BlockSpec((rows, units), lambda i: (0, 0)),
             pl.BlockSpec((units, block), lambda i: (0, i)),
         ],
-        out_specs=(out, out),
-        compiler_params=params(),
+        out_specs=(one, one, pl.BlockSpec((2, share, block), lambda i: (0, 0, i))),
+        scratch_shapes=[pltpu.VMEM((rows, block), jnp.float32)],
+        compiler_params=params(26),
         cost_estimate=cost(2 * rows * depth * units, 2 * depth * units + 6 * rows * depth),
         name="shrink",
     )(hidden, w_down)
-
-
-def pick_body(mine, got, sent):
-    away = 1 - lax.axis_index("tensor") // 2
-    sent[...] = (mine[away] + got[away].astype(jnp.float32)).astype(jnp.bfloat16)
-
-
-def pick(mine, got):
-    return pl.pallas_call(
-        pick_body,
-        out_shape=shape(mine.shape[1:]),
-        in_specs=[vmem_spec(), vmem_spec()],
-        out_specs=vmem_spec(),
-        compiler_params=params(),
-        cost_estimate=cost(mine.size, mine.size * 4),
-        name="pick",
-    )(mine, got)
 
 
 def block_of(b, heads):
@@ -214,10 +231,13 @@
 def attend_body(*refs, heads, width, owned, steps, first):
     if first:
         own, other = refs[:heads], refs[heads : 2 * heads]
-        outs = refs[2 * heads : 2 * heads + len(steps)]
-        kv, id_rows = refs[2 * heads + len(steps) : 2 * heads + len(steps) + 2]
-        query, id_cols, acc, den = refs[2 * heads + len(steps) + 2 :]
+        far, got = refs[2 * heads : 2 * heads + 2]
+        refs = refs[2 * heads + 2 :]
+        outs = refs[: len(steps)]
+        kv, id_rows, picked = refs[len(steps) : len(steps) + 3]
+        query, id_cols, acc, den = refs[len(steps) + 3 :]
         rows = kv.shape[1]
+        picked[...] = (far[...] + got[1].astype(jnp.float32)).astype(jnp.bfloat16)
         for b, source in enumerate(list(own) + list(other)):
             kv[b] = source[:rows, :]
             tile = source[rows:, :].astype(jnp.float32)
@@ -299,6 +319,7 @@
         out_shape += (
             shape((2 * heads, rows, 2 * width)),
             shape((2 * heads, 8, rows), jnp.float32),
+            shape(inputs[-2].shape),
         )
     units = (heads * heads + heads // 2) * len(steps) // heads
     return pl.pallas_call(
@@ -314,7 +335,7 @@
             pltpu.VMEM((rows, width), jnp.float32),
             pltpu.VMEM((rows, width), jnp.float32),
         ],
-        compiler_params=params(),
+        compiler_params=params(20),
         cost_estimate=cost(
             units * rows * rows * width * 8,
             2 * heads * rows * width * 4,
@@ -324,81 +345,121 @@
     )(*inputs)
 
 
-def cut_body(*refs, heads, share):
-    back, centroids = refs[:heads], refs[heads]
-    kept, away, updated = refs[heads + 1], refs[heads + 2 : -1], refs[-1]
-    z = lax.axis_index("seq") >> 1
+def cut_body(*refs, count, share):
+    back, kept, away, sums = refs[:count], refs[count], refs[count + 1 : -1], refs[-1]
     at = lax.axis_index("tensor")
-    owned = centroids.shape[1]
-    for k in range(heads):
+    for k in range(count):
         for turn in range(len(away) + 1):
             here = pl.ds(pl.multiple_of((at ^ turn) * share, share), share)
             (kept if turn == 0 else away[turn - 1])[k] = back[k][here, :]
-        rows = back[k].shape[0] - owned
-        sums = back[k][rows:, :].astype(jnp.float32)
-        head = z ^ k
-        updated[head] = EMA_DECAY * centroids[head] + (1.0 - EMA_DECAY) * sums
-
-
-def cut(back, centroids, share, tensor_count):
-    heads, width = len(back), back[0].shape[1]
-    piece = shape((heads, share, width))
+        rows = back[k].shape[0] - sums.shape[1]
+        sums[k] = back[k][rows:, :].astype(jnp.float32)
+
+
+def cut(back, owned, share, tensor_count):
+    count, width = len(back), back[0].shape[1]
+    piece = shape((count, share, width))
     return pl.pallas_call(
-        functools.partial(cut_body, heads=heads, share=share),
-        out_shape=(piece,) * tensor_count + (shape(centroids.shape, jnp.float32),),
-        in_specs=[vmem_spec()] * (heads + 1),
+        functools.partial(cut_body, count=count, share=share),
+        out_shape=(piece,) * tensor_count + (shape((count, owned, width), jnp.float32),),
+        in_specs=[vmem_spec()] * count,
         out_specs=(vmem_spec(),) * (tensor_count + 1),
-        compiler_params=params(),
-        cost_estimate=cost(centroids.size, 2 * heads * tensor_count * share * width * 2),
+        compiler_params=params(8),
+        cost_estimate=cost(0, 4 * count * tensor_count * share * width),
         name="cut",
-    )(*back, centroids)
-
-
-def mix_body(*refs, heads, width, groups):
+    )(*back)
+
+
+def head_rows(weights, buf, sems, steps, width):
+    z = lax.axis_index("seq") >> 1
+    copies = []
+    for g, w in enumerate(weights):
+        for i, k in enumerate(steps):
+            here = pl.ds(pl.multiple_of((z ^ k) * width, width), width)
+            to = pl.ds((g * len(steps) + i) * width, width)
+            copies.append(
+                pltpu.make_async_copy(
+                    w.at[here, :], buf.at[to, :], sems.at[g * len(steps) + i]
+                )
+            )
+    return copies
+
+
+def side_by_side(pieces, count):
+    return jnp.concatenate([p[k] for p in pieces for k in range(count)], axis=1)
+
+
+def mix_first_body(*refs, groups, width, steps, later):
     pieces, weights = refs[:groups], refs[groups : 2 * groups]
-    tokens, mine, got, came, out, left, buf, sems = refs[2 * groups :]
-    copies = [
-        pltpu.make_async_copy(weights[g], buf.at[g], sems.at[g]) for g in range(groups)
-    ]
-    for copy in copies:
+    tokens, mine, got, total, kept, buf, sems, later_sems = refs[2 * groups :]
+    now = head_rows(weights, buf, sems, steps, width)
+    then = head_rows(weights, kept, later_sems, later, width)
+    for copy in now + then:
         copy.start()
+    share = total.shape[0]
+    at = lax.axis_index("tensor")
+    here = pl.ds(pl.multiple_of(at * share, share), share)
+    left = side_by_side(pieces, len(steps))
+    known = tokens[here, :].astype(jnp.float32) + mine[...] + got[0].astype(jnp.float32)
+    for copy in now:
+        copy.wait()
+    total[...] = known + jnp.dot(left, buf[...], preferred_element_type=jnp.float32)
+    for copy in then:
+        copy.wait()
+
+
+def mix_first(pieces, weights, tokens, mine, got, steps, later):
+    groups = len(pieces)
+    count, share, width = pieces[0].shape
+    depth = tokens.shape[1]
+    held = (groups * count * width, depth)
+    return pl.pallas_call(
+        functools.partial(
+            mix_first_body, groups=groups, width=width, steps=steps, later=later
+        ),
+        out_shape=(shape((share, depth), jnp.float32), shape(held)),
+        in_specs=[vmem_spec()] * groups + [any_spec()] * groups + [vmem_spec()] * 3,
+        out_specs=(vmem_spec(), vmem_spec()),
+        scratch_shapes=[
+            pltpu.VMEM(held, jnp.bfloat16),
+            pltpu.SemaphoreType.DMA((groups * count,)),
+            pltpu.SemaphoreType.DMA((groups * count,)),
+        ],
+        compiler_params=params(24),
+        cost_estimate=cost(
+            2 * groups * share * count * width * depth,
+            4 * groups * count * width * depth + 8 * share * depth,
+        ),
+        name="mix_first",
+    )(*pieces, *weights, tokens, mine, got)
+
+
+def mix_last_body(*refs, groups, steps, later):
+    pieces = refs[:groups]
+    total, held, came, first_sums, last_sums, centroids, out, updated = refs[groups:]
     z = lax.axis_index("seq") >> 1
-    at = lax.axis_index("tensor")
-    share = out.shape[0]
-    for g in range(groups):
-        for k in range(heads):
-            cols = pl.ds(pl.multiple_of((z ^ k) * width, width), width)
-            left[g, :, cols] = pieces[g][k]
-    x = at // 2
-    total = mine[x] + got[x].astype(jnp.float32) + came[...].astype(jnp.float32)
-    for g in range(groups):
-        copies[g].wait()
-        total = total + jnp.dot(left[g], buf[g], preferred_element_type=jnp.float32)
-    here = pl.ds(pl.multiple_of(at * share, share), share)
-    out[...] = (tokens[here, :].astype(jnp.float32) + total).astype(jnp.bfloat16)
-
-
-def mix(pieces, weights, tokens, mine, got, came):
+    left = side_by_side(pieces, len(later))
+    known = total[...] + came[...].astype(jnp.float32)
+    summed = known + jnp.dot(left, held[...], preferred_element_type=jnp.float32)
+    out[...] = summed.astype(jnp.bfloat16)
+    for sums, turns in ((first_sums, steps), (last_sums, later)):
+        for i, k in enumerate(turns):
+            head = z ^ k
+            updated[head] = EMA_DECAY * centroids[head] + (1.0 - EMA_DECAY) * sums[i]
+
+
+def mix_last(pieces, total, held, came, first_sums, last_sums, centroids, steps, later):
     groups = len(pieces)
-    heads, share, width = pieces[0].shape
-    depth = tokens.shape[1]
+    share, depth = total.shape
     return pl.pallas_call(
-        functools.partial(mix_body, heads=heads, width=width, groups=groups),
-        out_shape=shape((share, depth)),
-        in_specs=[vmem_spec()] * groups + [any_spec()] * groups + [vmem_spec()] * 4,
-        out_specs=vmem_spec(),
-        scratch_shapes=[
-            pltpu.VMEM((groups, share, heads * width), jnp.bfloat16),
-            pltpu.VMEM((groups, heads * width, depth), jnp.bfloat16),
-            pltpu.SemaphoreType.DMA((groups,)),
-        ],
-        compiler_params=params(),
-        cost_estimate=cost(
-            2 * groups * share * heads * width * depth,
-            2 * groups * heads * width * depth + 8 * share * depth,
-        ),
-        name="mix",
-    )(*pieces, *weights, tokens, mine, got, came)
+        functools.partial(mix_last_body, groups=groups, steps=steps, later=later),
+        out_shape=(shape((share, depth)), shape(centroids.shape, jnp.float32)),
+        in_specs=[vmem_spec()] * (groups + 6),
+        out_specs=(vmem_spec(), vmem_spec()),
+        compiler_params=params(16),
+        cost_estimate=cost(2 * held.size * share, 2 * held.size + 8 * share * depth),
+        name="mix_last",
+    )(*pieces, total, held, came, first_sums, last_sums, centroids)
 
 
 def by_heads(
@@ -421,31 +482,36 @@
     own, other = [None] * heads, [None] * heads
     for k in reversed(range(heads)):
         own[k] = lax.ppermute(messages[k], BOTH, steps[k])
-    hidden = up(normed, w_up)
+    hidden = up(normed, held(w_up))
     for k in range(heads):
         other[k] = lax.ppermute(own[k], "tensor", swaps[1])
-    mine, sent = down(hidden, w_down, share)
+    mine, far, sent = down(hidden, held(w_down), share)
     got = lax.ppermute(sent, "tensor", swaps[1])
-    picked = pick(mine, got)
+
+    early, late = (heads - 1, 0), (heads - 2, 1)
+    back, pieces, sums = [None] * heads, {}, {}
+    *results, kv, id_rows, picked = attend(
+        own + other + [far, got], heads, tok_rows, width, owned, early, True
+    )
+    for k, result in zip(early, results):
+        back[k] = lax.ppermute(result, BOTH, turned(steps[k]))
+    results = attend([kv, id_rows], heads, tok_rows, width, owned, late, False)
+    for k, result in zip(late, results):
+        back[k] = lax.ppermute(result, BOTH, turned(steps[k]))
+    w_both = lax.ppermute(w_x, "tensor", swaps[1])
     came = lax.ppermute(picked, "tensor", swaps[2])
-    w_both = lax.ppermute(w_x, "tensor", swaps[1])
-
-    back = [None] * heads
-    far = tuple(reversed(range(heads // 2, heads)))
-    near = tuple(reversed(range(heads // 2)))
-    *results, kv, id_rows = attend(
-        own + other, heads, tok_rows, width, owned, far, True
-    )
-    for k, result in zip(far, results):
-        back[k] = lax.ppermute(result, BOTH, turned(steps[k]))
-    results = attend([kv, id_rows], heads, tok_rows, width, owned, near, False)
-    for k, result in zip(near, results):
-        back[k] = lax.ppermute(result, BOTH, turned(steps[k]))
-
-    kept, *away, new_centroids = cut(back, centroids, share, tensor_count)
-    arrived = [lax.ppermute(away[d - 1], "tensor", swaps[d]) for d in range(1, tensor_count)]
-    mixed_rows = mix(
-        [kept] + arrived, [w_out, w_core, w_x, w_both], tokens, mine, got, came
+
+    for name, turns in (("early", early), ("late", late)):
+        kept, *away, sums[name] = cut([back[k] for k in turns], owned, share, tensor_count)
+        pieces[name] = [kept] + [
+            lax.ppermute(away[d - 1], "tensor", swaps[d])
+            for d in range(1, tensor_count)
+        ]
+    total, late_rows = mix_first(
+        pieces["early"], [held(w_out), w_core, w_x, w_both], tokens, mine, got, early, late
+    )
+    mixed_rows, new_centroids = mix_last(
+        pieces["late"], total, late_rows, came, sums["early"], sums["late"], centroids, early, late
     )
     return (mixed_rows, new_centroids)
 
@@ -572,7 +638,7 @@
             sizes["tensor"] == 4
             and sizes["seq"] == 2 * heads
             and heads & (heads - 1) == 0
-            and heads > 1
+            and heads == 4
         )
         if not fits:
             return by_clusters(*args)

time: 137 us -> 126 us (0.920); the launches traced: 137 us -> 124 us
  Pallas kernels: 55.7 us -> 36.7 us
  starting transfers between devices: 26.1 us -> 31.7 us
  waiting for transfers between devices: 51.1 us -> 54.9 us
  local copies, waits for them, and re-layouts: 3.12 us -> 0.01 us
    ppermute x4, waiting for transfers between devices: 0.01 us -> 17.3 us  [by_heads(): own[k] = lax.ppermute(messages[k], BOTH, steps[k])]
    pallas_call x4 -> x5, Pallas kernels: 21.8 us -> 11.6 us  [the longest x1 7.93 us: project(): pl.pallas_call(functools.partial(project_body, heads=heads, width=width,...]
    ppermute x4, waiting for transfers between devices: 10.2 us -> 3.38 us  [by_heads(): back[k] = lax.ppermute(result, BOTH, turned(steps[k]))]
    pallas_call x2, Pallas kernels: 15.7 us -> 10.7 us  [attend(): pl.pallas_call(functools.partial(attend_body, heads=heads, width=width, o...]
    ppermute x3 -> x6, starting transfers between devices: 0.94 us -> 5.01 us  [by_heads(): lax.ppermute(away[d - 1], 'tensor', swaps[d])]
    ppermute x4, starting transfers between devices: 7.68 us -> 11.5 us  [by_heads(): back[k] = lax.ppermute(result, BOTH, turned(steps[k]))]
    unnamed x36 -> x4, local copies, waits for them, and re-layouts: 3.12 us -> 0.01 us
    ppermute x1, waiting for transfers between devices: 29.6 us -> 26.8 us  [by_heads(): w_x = lax.ppermute(w_out, 'tensor', swaps[2])]
  transfers between devices with their start and end apart: 20 -> 23, of which waited for: 8 -> 10; matrix products, arithmetic and copies ran while one was open for 0% -> 0% of each run, Pallas kernels for 35% -> 28%
where the time goes in v1:
time: 126 us; the launch traced here: 124 us
  waiting for transfers between devices  54.9 us (44%)
  Pallas kernels  36.7 us (29%)
  starting transfers between devices  31.7 us (25%)
    ppermute x1, waiting for transfers between devices, by_heads(): w_x = lax.ppermute(w_out, 'tensor', swaps[2])  26.8 us
    ppermute x4, waiting for transfers between devices, by_heads(): own[k] = lax.ppermute(messages[k], BOTH, steps[k])  17.3 us
    ppermute x4, starting transfers between devices, by_heads(): back[k] = lax.ppermute(result, BOTH, turned(steps[k]))  11.5 us
    pallas_call x2, Pallas kernels, attend(): pl.pallas_call(functools.partial(attend_body, heads=heads, width=width, o...  10.7 us
    ppermute x4, starting transfers between devices, by_heads(): own[k] = lax.ppermute(messages[k], BOTH, steps[k])  7.95 us
    pallas_call x1, Pallas kernels, project(): pl.pallas_call(functools.partial(project_body, heads=heads, width=width,...  7.93 us
    pallas_call x1, Pallas kernels, down(): pl.pallas_call(functools.partial(down_body, share=share), grid=(blocks,),...  7.38 us
    pallas_call x1, Pallas kernels, up(): pl.pallas_call(up_body, grid=(blocks,), out_shape=shape((rows, units)), i...  7 us
  transfers between devices with their start and end apart: 23, of which 10 were waited for; matrix products, arithmetic and copies ran while one was open for 0% of the time, Pallas kernels for 28%

profile of v1, /device:TPU:0, one launch (start us, length us, event | category | flops | bytes accessed | tf_op | source)
XLA Modules:
  0.0 124.1 jit_solution(2138044460220079984)
XLA Ops:
  0.6 3.0 %collective-permute-start.20 = (bf16[512,2048]{1,0:T(8,128)(2,1)}, bf16[512,2048]{1,0:T(8,128)(2,1)S(1)}, u32[]{:S(2)}, u32[]{:S(2)}) collective-permute-start(bf16[512,2048]{1,0:T(8,128)(2,1)} %refs_4_.1), channel_id=1, source_target_pairs={{0,2},{1,3},{2,0},{3,1},{4,6},{5,7},{6,4},{7,5},{8,10},{9,11},{10,... | collective-permute-start | bytes 6291464 | tf_op jit(solution)/shard_map/ppermute | solution.py:477
  3.7 7.9 %project.1 = (bf16[528,256]{1,0:T(8,128)(2,1)S(1)}, bf16[528,256]{1,0:T(8,128)(2,1)S(1)}, bf16[528,256]{1,0:T(8,128)(2,1)S(1)}, bf16[528,256]{1,0:T(8,128)(2,1)S(1)}, bf16[512,2048]{1,0:T(8,128)(2,1)S(1)}) custom-call(bf16[512,2048]{1,0:T(8,128)(2,1)} %refs_8_.1, f32[1,2048]{1,0:T(1,128)} %bitcast.1, bf16[2048,512]{1,0:T(8,128)(2,1)} %w_qk.1, ...), custom_call_target="tpu_custom_call" | custom-call | flops 2147483648 | bytes 9437184 | tf_op jit(solution)/shard_map/project/pallas_call | solution.py:138
  12.3 3.4 %collective-permute-start.1 = (bf16[528,256]{1,0:T(8,128)(2,1)S(1)}, bf16[528,256]{1,0:T(8,128)(2,1)S(1)}, u32[]{:S(2)}, u32[]{:S(2)}) collective-permute-start(bf16[528,256]{1,0:T(8,128)(2,1)S(1)} %get-tuple-element.30), channel_id=1, source_target_pairs={{0,8},{1,12},{2,10},{3,14},{4,9},{5,13},{6,11},{7,15},{8,1},{9,5},... | collective-permute-start | bytes 811016 | tf_op jit(solution)/shard_map/ppermute | solution.py:484
  15.7 7.0 %grow.1.hidden = bf16[512,2048]{1,0:T(8,128)(2,1)S(1)} custom-call(bf16[512,2048]{1,0:T(8,128)(2,1)S(1)} %get-tuple-element.33.normed, bf16[2048,2048]{1,0:T(8,128)(2,1)} %w_up.1), custom_call_target="tpu_custom_call" | custom-call | flops 4294967296 | bytes 12582912 | tf_op jit(solution)/shard_map/grow/pallas_call | solution.py:171
  22.7 26.8 %collective-permute-done.20.refs_6_ = bf16[512,2048]{1,0:T(8,128)(2,1)S(1)} collective-permute-done((bf16[512,2048]{1,0:T(8,128)(2,1)}, bf16[512,2048]{1,0:T(8,128)(2,1)S(1)}, u32[]{:S(2)}, u32[]{:S(2)}) %collective-permute-start.20) | collective-permute-done | bytes 2097184 | tf_op jit(solution)/shard_map/ppermute | solution.py:477
  49.5 7.4 %shrink.1 = (f32[128,2048]{1,0:T(8,128)S(1)}, f32[128,2048]{1,0:T(8,128)S(1)}, bf16[2,128,2048]{2,1,0:T(8,128)(2,1)S(1)}) custom-call(bf16[512,2048]{1,0:T(8,128)(2,1)S(1)} %grow.1.hidden, bf16[2048,2048]{1,0:T(8,128)(2,1)} %w_down.1), custom_call_target="tpu_custom_call" | custom-call | flops 4294967296 | bytes 14680064 | tf_op jit(solution)/shard_map/shrink/pallas_call | solution.py:204
  57.5 2.8 %collective-permute-start.2 = (bf16[528,256]{1,0:T(8,128)(2,1)S(1)}, bf16[528,256]{1,0:T(8,128)(2,1)S(1)}, u32[]{:S(2)}, u32[]{:S(2)}) collective-permute-start(bf16[528,256]{1,0:T(8,128)(2,1)S(1)} %get-tuple-element.31), channel_id=1, source_target_pairs={{0,16},{1,20},{2,18},{3,22},{4,17},{5,21},{6,19},{7,23},{8,25},{9,... | collective-permute-start | bytes 811016 | tf_op jit(solution)/shard_map/ppermute | solution.py:484
  61.4 17.3 %collective-permute-done.2.refs_2_ = bf16[528,256]{1,0:T(8,128)(2,1)S(1)} collective-permute-done((bf16[528,256]{1,0:T(8,128)(2,1)S(1)}, bf16[528,256]{1,0:T(8,128)(2,1)S(1)}, u32[]{:S(2)}, u32[]{:S(2)}) %collective-permute-start.2) | collective-permute-done | bytes 270368 | tf_op jit(solution)/shard_map/ppermute | solution.py:484
  78.7 1.3 %collective-permute-start.4 = (bf16[528,256]{1,0:T(8,128)(2,1)S(1)}, bf16[528,256]{1,0:T(8,128)(2,1)S(1)}, u32[]{:S(2)}, u32[]{:S(2)}) collective-permute-start(bf16[528,256]{1,0:T(8,128)(2,1)S(1)} %collective-permute-done.refs_0_), channel_id=1, source_target_pairs={{0,1},{1,0},{2,3},{3,2},{4,5},{5,4},{6,7},{7,6},{8,9},{9,8},{10,11... | collective-permute-start | bytes 811016 | tf_op jit(solution)/shard_map/ppermute | solution.py:487
  83.1 5.5 %attend.2 = (bf16[544,128]{1,0:T(8,128)(2,1)S(1)}, bf16[544,128]{1,0:T(8,128)(2,1)S(1)}, bf16[8,512,256]{2,1,0:T(8,128)(2,1)S(1)}, f32[8,8,512]{2,1,0:T(8,128)S(1)}, bf16[128,2048]{1,0:T(8,128)(2,1)S(1)}) custom-call(bf16[528,256]{1,0:T(8,128)(2,1)S(1)} %collective-permute-done.refs_0_, bf16[528,256]{1,0:T(8,128)(2,1)S(1)} %collective-permute-done.1.refs_1_, ...), custom_call_target="tpu_custom_call" | custom-call | flops 2415919104 | bytes 2097152 | tf_op jit(solution)/shard_map/attend/pallas_call | solution.py:325
  88.7 3.9 %collective-permute-start.14 = (bf16[544,128]{1,0:T(8,128)(2,1)S(1)}, bf16[544,128]{1,0:T(8,128)(2,1)S(1)}, u32[]{:S(2)}, u32[]{:S(2)}) collective-permute-start(bf16[544,128]{1,0:T(8,128)(2,1)S(1)} %get-tuple-element.44), channel_id=1, source_target_pairs={{24,0},{28,1},{26,2},{30,3},{25,4},{29,5},{27,6},{31,7},{17,8},{21... | collective-permute-start | bytes 417800 | tf_op jit(solution)/shard_map/ppermute | solution.py:497
  93.4 1.6 %collective-permute-start.22 = (bf16[128,2048]{1,0:T(8,128)(2,1)S(1)}, bf16[128,2048]{1,0:T(8,128)(2,1)S(1)}, u32[]{:S(2)}, u32[]{:S(2)}) collective-permute-start(bf16[128,2048]{1,0:T(8,128)(2,1)S(1)} %get-tuple-element.53), channel_id=1, source_target_pairs={{0,2},{1,3},{2,0},{3,1},{4,6},{5,7},{6,4},{7,5},{8,10},{9,11},{10,... | collective-permute-start | bytes 1572872 | tf_op jit(solution)/shard_map/ppermute | solution.py:502
  95.0 5.2 %attend.3 = (bf16[544,128]{1,0:T(8,128)(2,1)S(1)}, bf16[544,128]{1,0:T(8,128)(2,1)S(1)}) custom-call(bf16[8,512,256]{2,1,0:T(8,128)(2,1)S(1)} %get-tuple-element.36.refs_0_, f32[8,8,512]{2,1,0:T(8,128)S(1)} %get-tuple-element.37.refs_1_), custom_call_target="tpu_custom_call" | custom-call | flops 2415919104 | bytes 2097152 | tf_op jit(solution)/shard_map/attend/pallas_call | solution.py:325
  100.2 4.5 %collective-permute-start.9 = (bf16[544,128]{1,0:T(8,128)(2,1)S(1)}, bf16[544,128]{1,0:T(8,128)(2,1)S(1)}, u32[]{:S(2)}, u32[]{:S(2)}) collective-permute-start(bf16[544,128]{1,0:T(8,128)(2,1)S(1)} %get-tuple-element.38), channel_id=1, source_target_pairs={{16,0},{20,1},{18,2},{22,3},{17,4},{21,5},{19,6},{23,7},{25,8},{29... | collective-permute-start | bytes 417800 | tf_op jit(solution)/shard_map/ppermute | solution.py:500
  104.7 2.3 %collective-permute-start.10 = (bf16[544,128]{1,0:T(8,128)(2,1)S(1)}, bf16[544,128]{1,0:T(8,128)(2,1)S(1)}, u32[]{:S(2)}, u32[]{:S(2)}) collective-permute-start(bf16[544,128]{1,0:T(8,128)(2,1)S(1)} %get-tuple-element.39), channel_id=1, source_target_pairs={{8,0},{12,1},{10,2},{14,3},{9,4},{13,5},{11,6},{15,7},{1,8},{5,9},... | collective-permute-start | bytes 417800 | tf_op jit(solution)/shard_map/ppermute | solution.py:500
  107.0 1.5 %collective-permute-done.9.refs_0_ = bf16[544,128]{1,0:T(8,128)(2,1)S(1)} collective-permute-done((bf16[544,128]{1,0:T(8,128)(2,1)S(1)}, bf16[544,128]{1,0:T(8,128)(2,1)S(1)}, u32[]{:S(2)}, u32[]{:S(2)}) %collective-permute-start.9) | collective-permute-done | bytes 139296 | tf_op jit(solution)/shard_map/ppermute | solution.py:500
  108.4 1.4 %collective-permute-start.16 = (bf16[2,128,128]{2,1,0:T(8,128)(2,1)S(1)}, bf16[2,128,128]{2,1,0:T(8,128)(2,1)S(1)}, u32[]{:S(2)}, u32[]{:S(2)}) collective-permute-start(bf16[2,128,128]{2,1,0:T(8,128)(2,1)S(1)} %get-tuple-element.47), channel_id=1, source_target_pairs={{0,1},{1,0},{2,3},{3,2},{4,5},{5,4},{6,7},{7,6},{8,9},{9,8},{10,11... | collective-permute-start | bytes 196616 | tf_op jit(solution)/shard_map/ppermute | solution.py:507
  109.8 1.9 %collective-permute-done.10.refs_1_ = bf16[544,128]{1,0:T(8,128)(2,1)S(1)} collective-permute-done((bf16[544,128]{1,0:T(8,128)(2,1)S(1)}, bf16[544,128]{1,0:T(8,128)(2,1)S(1)}, u32[]{:S(2)}, u32[]{:S(2)}) %collective-permute-start.10) | collective-permute-done | bytes 139296 | tf_op jit(solution)/shard_map/ppermute | solution.py:500
  111.9 2.0 %collective-permute-start.18 = (bf16[2,128,128]{2,1,0:T(8,128)(2,1)S(1)}, bf16[2,128,128]{2,1,0:T(8,128)(2,1)S(1)}, u32[]{:S(2)}, u32[]{:S(2)}) collective-permute-start(bf16[2,128,128]{2,1,0:T(8,128)(2,1)S(1)} %get-tuple-element.49), channel_id=1, source_target_pairs={{0,3},{1,2},{2,1},{3,0},{4,7},{5,6},{6,5},{7,4},{8,11},{9,10},{10,... | collective-permute-start | bytes 196616 | tf_op jit(solution)/shard_map/ppermute | solution.py:507
  113.9 2.8 %collective-permute-done.17.refs_2_ = bf16[2,128,128]{2,1,0:T(8,128)(2,1)S(1)} collective-permute-done((bf16[2,128,128]{2,1,0:T(8,128)(2,1)S(1)}, bf16[2,128,128]{2,1,0:T(8,128)(2,1)S(1)}, u32[]{:S(2)}, u32[]{:S(2)}) %collective-permute-start.17) | collective-permute-done | bytes 65568 | tf_op jit(solution)/shard_map/ppermute | solution.py:507
  117.8 1.5 %collective-permute-start.13 = (bf16[2,128,128]{2,1,0:T(8,128)(2,1)S(1)}, bf16[2,128,128]{2,1,0:T(8,128)(2,1)S(1)}, u32[]{:S(2)}, u32[]{:S(2)}) collective-permute-start(bf16[2,128,128]{2,1,0:T(8,128)(2,1)S(1)} %get-tuple-element.43), channel_id=1, source_target_pairs={{0,3},{1,2},{2,1},{3,0},{4,7},{5,6},{6,5},{7,4},{8,11},{9,10},{10,... | collective-permute-start | bytes 196616 | tf_op jit(solution)/shard_map/ppermute | solution.py:507
  119.2 2.1 %mix_first.1 = (f32[128,2048]{1,0:T(8,128)S(1)}, bf16[1024,2048]{1,0:T(8,128)(2,1)S(1)}) custom-call(bf16[2,128,128]{2,1,0:T(8,128)(2,1)S(1)} %get-tuple-element.46.refs_0_, bf16[2,128,128]{2,1,0:T(8,128)(2,1)S(1)} %collective-permute-done.16.refs_1_, bf16[2,128,128]{2,1,0:T(8,128)(2,1)S(1)} %collective-permute-done.17.refs_2_, ...), custom_call_target="tpu_custom_call" | custom-call | flops 536870912 | bytes 10485760 | tf_op jit(solution)/shard_map/mix_first/pallas_call | solution.py:416
  121.4 1.2 collective-permute-done.12.refs_2_
  122.6 1.5 %mix_last.1 = (bf16[128,2048]{1,0:T(8,128)(2,1)}, f32[4,32,128]{2,1,0:T(8,128)}) custom-call(bf16[2,128,128]{2,1,0:T(8,128)(2,1)S(1)} %get-tuple-element.40.refs_0_, bf16[2,128,128]{2,1,0:T(8,128)(2,1)S(1)} %collective-permute-done.11.refs_1_, bf16[2,128,128]{2,1,0:T(8,128)(2,1)S(1)} %collective-permute-done.12.refs_2_, ...), custom_call_target="tpu_custom_call" | custom-call | flops 536870912 | bytes 6291456 | tf_op jit(solution)/shard_map/mix_last/pallas_call | solution.py:454
  (35 shorter events, 7.6 us)
Async XLA Ops:
  0.6 48.9 %collective-permute-start.20 = (bf16[512,2048]{1,0:T(8,128)(2,1)}, bf16[512,2048]{1,0:T(8,128)(2,1)S(1)}, u32[]{:S(2)}, u32[]{:S(2)}) collective-permute-start(bf16[512,2048]{1,0:T(8,128)(2,1)} %refs_4_.1), channel_id=1, source_target_pairs={{0,2},{1,3},{2,0},{3,1},{4,6},{5,7},{6,4},{7,5},{8,10},{9,11},{10,... | collective-permute-start | bytes 6291464 | tf_op jit(solution)/shard_map/ppermute | solution.py:477
  3.7 114.1 %collective-permute-start.19 = (bf16[512,2048]{1,0:T(8,128)(2,1)}, bf16[512,2048]{1,0:T(8,128)(2,1)S(1)}, u32[]{:S(2)}, u32[]{:S(2)}) collective-permute-start(bf16[512,2048]{1,0:T(8,128)(2,1)} %refs_4_.1), channel_id=1, source_target_pairs={{0,1},{1,0},{2,3},{3,2},{4,5},{5,4},{6,7},{7,6},{8,9},{9,8},{10,11... | collective-permute-start | bytes 6291464 | tf_op jit(solution)/shard_map/ppermute | solution.py:478
  11.6 45.9 %collective-permute-start = (bf16[528,256]{1,0:T(8,128)(2,1)S(1)}, bf16[528,256]{1,0:T(8,128)(2,1)S(1)}, u32[]{:S(2)}, u32[]{:S(2)}) collective-permute-start(bf16[528,256]{1,0:T(8,128)(2,1)S(1)} %get-tuple-element.29), channel_id=1, source_target_pairs={{0,0},{1,4},{2,2},{3,6},{4,1},{5,5},{6,3},{7,7},{8,9},{9,13},{10,1... | collective-permute-start | bytes 811016 | tf_op jit(solution)/shard_map/ppermute | solution.py:484
  12.3 48.0 %collective-permute-start.1 = (bf16[528,256]{1,0:T(8,128)(2,1)S(1)}, bf16[528,256]{1,0:T(8,128)(2,1)S(1)}, u32[]{:S(2)}, u32[]{:S(2)}) collective-permute-start(bf16[528,256]{1,0:T(8,128)(2,1)S(1)} %get-tuple-element.30), channel_id=1, source_target_pairs={{0,8},{1,12},{2,10},{3,14},{4,9},{5,13},{6,11},{7,15},{8,1},{9,5},... | collective-permute-start | bytes 811016 | tf_op jit(solution)/shard_map/ppermute | solution.py:484
  49.5 69.7 %collective-permute-start.21 = (bf16[512,2048]{1,0:T(8,128)(2,1)S(1)}, bf16[512,2048]{1,0:T(8,128)(2,1)S(1)}, u32[]{:S(2)}, u32[]{:S(2)}) collective-permute-start(bf16[512,2048]{1,0:T(8,128)(2,1)S(1)} %collective-permute-done.20.refs_6_), channel_id=1, source_target_pairs={{0,1},{1,0},{2,3},{3,2},{4,5},{5,4},{6,7},{7,6},{8,9},{9,8},{10,11... | collective-permute-start | bytes 6291464 | tf_op jit(solution)/shard_map/ppermute | solution.py:501
  56.9 26.2 %collective-permute-start.8 = (bf16[2,128,2048]{2,1,0:T(8,128)(2,1)S(1)}, bf16[2,128,2048]{2,1,0:T(8,128)(2,1)S(1)}, u32[]{:S(2)}, u32[]{:S(2)}) collective-permute-start(bf16[2,128,2048]{2,1,0:T(8,128)(2,1)S(1)} %get-tuple-element.35), channel_id=1, source_target_pairs={{0,1},{1,0},{2,3},{3,2},{4,5},{5,4},{6,7},{7,6},{8,9},{9,8},{10,11... | collective-permute-start | bytes 3145736 | tf_op jit(solution)/shard_map/ppermute | solution.py:489
  57.5 21.2 %collective-permute-start.2 = (bf16[528,256]{1,0:T(8,128)(2,1)S(1)}, bf16[528,256]{1,0:T(8,128)(2,1)S(1)}, u32[]{:S(2)}, u32[]{:S(2)}) collective-permute-start(bf16[528,256]{1,0:T(8,128)(2,1)S(1)} %get-tuple-element.31), channel_id=1, source_target_pairs={{0,16},{1,20},{2,18},{3,22},{4,17},{5,21},{6,19},{7,23},{8,25},{9,... | collective-permute-start | bytes 811016 | tf_op jit(solution)/shard_map/ppermute | solution.py:484
  60.3 19.7 %collective-permute-start.3 = (bf16[528,256]{1,0:T(8,128)(2,1)S(1)}, bf16[528,256]{1,0:T(8,128)(2,1)S(1)}, u32[]{:S(2)}, u32[]{:S(2)}) collective-permute-start(bf16[528,256]{1,0:T(8,128)(2,1)S(1)} %get-tuple-element.32), channel_id=1, source_target_pairs={{0,24},{1,28},{2,26},{3,30},{4,25},{5,29},{6,27},{7,31},{8,17},{9,... | collective-permute-start | bytes 811016 | tf_op jit(solution)/shard_map/ppermute | solution.py:484
  78.7 2.5 %collective-permute-start.4 = (bf16[528,256]{1,0:T(8,128)(2,1)S(1)}, bf16[528,256]{1,0:T(8,128)(2,1)S(1)}, u32[]{:S(2)}, u32[]{:S(2)}) collective-permute-start(bf16[528,256]{1,0:T(8,128)(2,1)S(1)} %collective-permute-done.refs_0_), channel_id=1, source_target_pairs={{0,1},{1,0},{2,3},{3,2},{4,5},{5,4},{6,7},{7,6},{8,9},{9,8},{10,11... | collective-permute-start | bytes 811016 | tf_op jit(solution)/shard_map/ppermute | solution.py:487
  80.0 1.6 %collective-permute-start.5 = (bf16[528,256]{1,0:T(8,128)(2,1)S(1)}, bf16[528,256]{1,0:T(8,128)(2,1)S(1)}, u32[]{:S(2)}, u32[]{:S(2)}) collective-permute-start(bf16[528,256]{1,0:T(8,128)(2,1)S(1)} %collective-permute-done.1.refs_1_), channel_id=1, source_target_pairs={{0,1},{1,0},{2,3},{3,2},{4,5},{5,4},{6,7},{7,6},{8,9},{9,8},{10,11... | collective-permute-start | bytes 811016 | tf_op jit(solution)/shard_map/ppermute | solution.py:487
  81.2 1.5 %collective-permute-start.6 = (bf16[528,256]{1,0:T(8,128)(2,1)S(1)}, bf16[528,256]{1,0:T(8,128)(2,1)S(1)}, u32[]{:S(2)}, u32[]{:S(2)}) collective-permute-start(bf16[528,256]{1,0:T(8,128)(2,1)S(1)} %collective-permute-done.2.refs_2_), channel_id=1, source_target_pairs={{0,1},{1,0},{2,3},{3,2},{4,5},{5,4},{6,7},{7,6},{8,9},{9,8},{10,11... | collective-permute-start | bytes 811016 | tf_op jit(solution)/shard_map/ppermute | solution.py:487
  81.6 1.5 %collective-permute-start.7 = (bf16[528,256]{1,0:T(8,128)(2,1)S(1)}, bf16[528,256]{1,0:T(8,128)(2,1)S(1)}, u32[]{:S(2)}, u32[]{:S(2)}) collective-permute-start(bf16[528,256]{1,0:T(8,128)(2,1)S(1)} %collective-permute-done.3.refs_3_), channel_id=1, source_target_pairs={{0,1},{1,0},{2,3},{3,2},{4,5},{5,4},{6,7},{7,6},{8,9},{9,8},{10,11... | collective-permute-start | bytes 811016 | tf_op jit(solution)/shard_map/ppermute | solution.py:487
  88.7 11.5 %collective-permute-start.14 = (bf16[544,128]{1,0:T(8,128)(2,1)S(1)}, bf16[544,128]{1,0:T(8,128)(2,1)S(1)}, u32[]{:S(2)}, u32[]{:S(2)}) collective-permute-start(bf16[544,128]{1,0:T(8,128)(2,1)S(1)} %get-tuple-element.44), channel_id=1, source_target_pairs={{24,0},{28,1},{26,2},{30,3},{25,4},{29,5},{27,6},{31,7},{17,8},{21... | collective-permute-start | bytes 417800 | tf_op jit(solution)/shard_map/ppermute | solution.py:497
  92.6 12.1 %collective-permute-start.15 = (bf16[544,128]{1,0:T(8,128)(2,1)S(1)}, bf16[544,128]{1,0:T(8,128)(2,1)S(1)}, u32[]{:S(2)}, u32[]{:S(2)}) collective-permute-start(bf16[544,128]{1,0:T(8,128)(2,1)S(1)} %get-tuple-element.45), channel_id=1, source_target_pairs={{0,0},{4,1},{2,2},{6,3},{1,4},{5,5},{3,6},{7,7},{9,8},{13,9},{11,1... | collective-permute-start | bytes 417800 | tf_op jit(solution)/shard_map/ppermute | solution.py:497
  93.4 29.2 %collective-permute-start.22 = (bf16[128,2048]{1,0:T(8,128)(2,1)S(1)}, bf16[128,2048]{1,0:T(8,128)(2,1)S(1)}, u32[]{:S(2)}, u32[]{:S(2)}) collective-permute-start(bf16[128,2048]{1,0:T(8,128)(2,1)S(1)} %get-tuple-element.53), channel_id=1, source_target_pairs={{0,2},{1,3},{2,0},{3,1},{4,6},{5,7},{6,4},{7,5},{8,10},{9,11},{10,... | collective-permute-start | bytes 1572872 | tf_op jit(solution)/shard_map/ppermute | solution.py:502
  95.0 24.2 %copy-start = (bf16[512,2048]{1,0:T(8,128)(2,1)S(1)}, bf16[512,2048]{1,0:T(8,128)(2,1)}, u32[]{:S(2)}) copy-start(bf16[512,2048]{1,0:T(8,128)(2,1)} %refs_8_.1) | copy-start | bytes 6291460
  100.2 8.2 %collective-permute-start.9 = (bf16[544,128]{1,0:T(8,128)(2,1)S(1)}, bf16[544,128]{1,0:T(8,128)(2,1)S(1)}, u32[]{:S(2)}, u32[]{:S(2)}) collective-permute-start(bf16[544,128]{1,0:T(8,128)(2,1)S(1)} %get-tuple-element.38), channel_id=1, source_target_pairs={{16,0},{20,1},{18,2},{22,3},{17,4},{21,5},{19,6},{23,7},{25,8},{29... | collective-permute-start | bytes 417800 | tf_op jit(solution)/shard_map/ppermute | solution.py:500
  104.7 7.1 %collective-permute-start.10 = (bf16[544,128]{1,0:T(8,128)(2,1)S(1)}, bf16[544,128]{1,0:T(8,128)(2,1)S(1)}, u32[]{:S(2)}, u32[]{:S(2)}) collective-permute-start(bf16[544,128]{1,0:T(8,128)(2,1)S(1)} %get-tuple-element.39), channel_id=1, source_target_pairs={{8,0},{12,1},{10,2},{14,3},{9,4},{13,5},{11,6},{15,7},{1,8},{5,9},... | collective-permute-start | bytes 417800 | tf_op jit(solution)/shard_map/ppermute | solution.py:500
  108.4 3.5 %collective-permute-start.16 = (bf16[2,128,128]{2,1,0:T(8,128)(2,1)S(1)}, bf16[2,128,128]{2,1,0:T(8,128)(2,1)S(1)}, u32[]{:S(2)}, u32[]{:S(2)}) collective-permute-start(bf16[2,128,128]{2,1,0:T(8,128)(2,1)S(1)} %get-tuple-element.47), channel_id=1, source_target_pairs={{0,1},{1,0},{2,3},{3,2},{4,5},{5,4},{6,7},{7,6},{8,9},{9,8},{10,11... | collective-permute-start | bytes 196616 | tf_op jit(solution)/shard_map/ppermute | solution.py:507
  111.7 5.0 %collective-permute-start.17 = (bf16[2,128,128]{2,1,0:T(8,128)(2,1)S(1)}, bf16[2,128,128]{2,1,0:T(8,128)(2,1)S(1)}, u32[]{:S(2)}, u32[]{:S(2)}) collective-permute-start(bf16[2,128,128]{2,1,0:T(8,128)(2,1)S(1)} %get-tuple-element.48), channel_id=1, source_target_pairs={{0,2},{1,3},{2,0},{3,1},{4,6},{5,7},{6,4},{7,5},{8,10},{9,11},{10,... | collective-permute-start | bytes 196616 | tf_op jit(solution)/shard_map/ppermute | solution.py:507
  111.9 5.9 %collective-permute-start.18 = (bf16[2,128,128]{2,1,0:T(8,128)(2,1)S(1)}, bf16[2,128,128]{2,1,0:T(8,128)(2,1)S(1)}, u32[]{:S(2)}, u32[]{:S(2)}) collective-permute-start(bf16[2,128,128]{2,1,0:T(8,128)(2,1)S(1)} %get-tuple-element.49), channel_id=1, source_target_pairs={{0,3},{1,2},{2,1},{3,0},{4,7},{5,6},{6,5},{7,4},{8,11},{9,10},{10,... | collective-permute-start | bytes 196616 | tf_op jit(solution)/shard_map/ppermute | solution.py:507
  116.7 4.7 %collective-permute-start.11 = (bf16[2,128,128]{2,1,0:T(8,128)(2,1)S(1)}, bf16[2,128,128]{2,1,0:T(8,128)(2,1)S(1)}, u32[]{:S(2)}, u32[]{:S(2)}) collective-permute-start(bf16[2,128,128]{2,1,0:T(8,128)(2,1)S(1)} %get-tuple-element.41), channel_id=1, source_target_pairs={{0,1},{1,0},{2,3},{3,2},{4,5},{5,4},{6,7},{7,6},{8,9},{9,8},{10,11... | collective-permute-start | bytes 196616 | tf_op jit(solution)/shard_map/ppermute | solution.py:507
  117.8 4.8 %collective-permute-start.12 = (bf16[2,128,128]{2,1,0:T(8,128)(2,1)S(1)}, bf16[2,128,128]{2,1,0:T(8,128)(2,1)S(1)}, u32[]{:S(2)}, u32[]{:S(2)}) collective-permute-start(bf16[2,128,128]{2,1,0:T(8,128)(2,1)S(1)} %get-tuple-element.42), channel_id=1, source_target_pairs={{0,2},{1,3},{2,0},{3,1},{4,6},{5,7},{6,4},{7,5},{8,10},{9,11},{10,... | collective-permute-start | bytes 196616 | tf_op jit(solution)/shard_map/ppermute | solution.py:507
  117.8 4.8 %collective-permute-start.13 = (bf16[2,128,128]{2,1,0:T(8,128)(2,1)S(1)}, bf16[2,128,128]{2,1,0:T(8,128)(2,1)S(1)}, u32[]{:S(2)}, u32[]{:S(2)}) collective-permute-start(bf16[2,128,128]{2,1,0:T(8,128)(2,1)S(1)} %get-tuple-element.43), channel_id=1, source_target_pairs={{0,3},{1,2},{2,1},{3,0},{4,7},{5,6},{6,5},{7,4},{8,11},{9,10},{10,... | collective-permute-start | bytes 196616 | tf_op jit(solution)/shard_map/ppermute | solution.py:507
  (1 other events, 3.3 us)

commit v2 on v1

--- a/solution.py
+++ b/solution.py
@@ -14,7 +14,8 @@
 SCORE_SCALE = 2.0
 EMA_DECAY = 0.9
 NORM_EPS = 1e-06
-BOTH = ("seq", "tensor")
+SEQ, TENSOR = "seq", "tensor"
+BOTH = (SEQ, TENSOR)
 EXTRA = 16
 MIB = 1024 * 1024
 
@@ -64,99 +65,121 @@
     return jax.ShapeDtypeStruct(dims, kind)
 
 
-def project_body(
-    tokens_at, gain_at, w_qk, w_value, clusters_at, *rest, heads, width, parts
+def unit_heads(normed, w_qk, w_value, outs, clusters, steps, width):
+    z = lax.axis_index(SEQ) >> 1
+    rows = normed.shape[0]
+    span = 2 * width
+    odd = (z & 1) == 1
+    row_at = lax.broadcasted_iota(jnp.int32, (EXTRA, span), 0)
+    key_proj = jnp.dot(normed[...], w_qk[...], preferred_element_type=jnp.float32)
+    units = []
+    for q in range(2):
+        k = key_proj[:, q * width : (q + 1) * width]
+        total = jnp.sum(k * k, axis=-1, keepdims=True)
+        units.append((k * lax.rsqrt(total + NORM_EPS)).astype(jnp.bfloat16))
+    val_proj = jnp.dot(normed[...], w_value[...], preferred_element_type=jnp.float32)
+    values = [val_proj[:, q * width : (q + 1) * width].astype(jnp.bfloat16) for q in range(2)]
+    for q, out in enumerate(outs):
+        out[:rows, :width] = jnp.where(odd, units[1 - q], units[q])
+        out[:rows, width:] = jnp.where(odd, values[1 - q], values[q])
+        id_row = clusters[pl.ds(steps[q] ^ z, 1), :].astype(jnp.float32)
+        tail = jnp.zeros((EXTRA, span), jnp.float32)
+        for part in range(rows // span):
+            piece = id_row[:, part * span : (part + 1) * span]
+            tail = jnp.where(row_at == part, piece, tail)
+        out[rows:, :] = tail.astype(jnp.bfloat16)
+
+
+def project_far_body(
+    tokens_at, gain_at, w_qk, w_value, clusters_at, w_out, *rest, heads, width, parts
 ):
-    outs, normed = rest[:heads], rest[heads]
-    tokens, gain, clusters, qk_buf, val_buf, sems, token_sems, small_sems = rest[heads + 1 :]
+    out_low, out_high, normed, clusters, qk_next, val_next, out_part = rest[:7]
+    tokens, gain, qk_buf, val_buf, sems, token_sems = rest[7:]
+    z = lax.axis_index(SEQ) >> 1
+    y = lax.axis_index(SEQ) & 1
     step = tokens.shape[0] // parts
-    small = (
-        pltpu.make_async_copy(gain_at, gain, small_sems.at[0]),
-        pltpu.make_async_copy(clusters_at, clusters, small_sems.at[1]),
-    )
+    span = 2 * width
     slabs = [pl.ds(r * step, step) for r in range(parts)]
     slab_copies = [
         pltpu.make_async_copy(tokens_at.at[here, :], tokens.at[here, :], token_sems.at[r])
         for r, here in enumerate(slabs)
     ]
-    for copy in (small[0], *slab_copies, small[1]):
+
+    def columns(block):
+        return pl.ds(pl.multiple_of(block * span, span), span)
+
+    first, second = columns(1 ^ (z >> 1)), columns(z >> 1)
+    half = out_part.shape[1]
+    out_cols = pl.ds(pl.multiple_of(y * half, half), half)
+    copies = [
+        pltpu.make_async_copy(gain_at, gain, sems.at[0]),
+        pltpu.make_async_copy(w_qk.at[:, first], qk_buf, sems.at[1]),
+        pltpu.make_async_copy(w_value.at[:, first], val_buf, sems.at[2]),
+        pltpu.make_async_copy(clusters_at, clusters, sems.at[3]),
+        pltpu.make_async_copy(w_out.at[:, out_cols], out_part, sems.at[4]),
+        pltpu.make_async_copy(w_qk.at[:, second], qk_next, sems.at[5]),
+        pltpu.make_async_copy(w_value.at[:, second], val_next, sems.at[6]),
+    ]
+    for copy in (copies[0], *slab_copies, *copies[1:]):
         copy.start()
-    z = lax.axis_index("seq") >> 1
-    pairs = heads // 2
-    span = 2 * width
-
-    def copies(p):
-        block = p ^ (z >> 1)
-        cols = pl.ds(pl.multiple_of(block * span, span), span)
-        return (
-            pltpu.make_async_copy(w_qk.at[:, cols], qk_buf.at[p], sems.at[2 * p]),
-            pltpu.make_async_copy(w_value.at[:, cols], val_buf.at[p], sems.at[2 * p + 1]),
-        )
-
-    for p in range(pairs):
-        for copy in copies(p):
-            copy.start()
-    small[0].wait()
+    copies[0].wait()
     for copy, here in zip(slab_copies, slabs):
         copy.wait()
         wide = tokens[here, :].astype(jnp.float32)
         mean = jnp.mean(wide * wide, axis=-1, keepdims=True)
         normed[here, :] = (wide * lax.rsqrt(mean + NORM_EPS) * gain[...]).astype(jnp.bfloat16)
-    small[1].wait()
-    rows = tokens.shape[0]
-    odd = (z & 1) == 1
-    row_at = lax.broadcasted_iota(jnp.int32, (EXTRA, span), 0)
-    for p in range(pairs):
-        key_copy, val_copy = copies(p)
-        key_copy.wait()
-        key_proj = jnp.dot(normed[...], qk_buf[p], preferred_element_type=jnp.float32)
-        units = []
-        for q in range(2):
-            k = key_proj[:, q * width : (q + 1) * width]
-            total = jnp.sum(k * k, axis=-1, keepdims=True)
-            units.append((k * lax.rsqrt(total + NORM_EPS)).astype(jnp.bfloat16))
-        val_copy.wait()
-        val_proj = jnp.dot(normed[...], val_buf[p], preferred_element_type=jnp.float32)
-        values = [
-            val_proj[:, q * width : (q + 1) * width].astype(jnp.bfloat16) for q in range(2)
-        ]
-        for q in range(2):
-            out = outs[2 * p + q]
-            out[:rows, :width] = jnp.where(odd, units[1 - q], units[q])
-            out[:rows, width:] = jnp.where(odd, values[1 - q], values[q])
-            id_row = clusters[pl.ds((2 * p + q) ^ z, 1), :].astype(jnp.float32)
-            tail = jnp.zeros((EXTRA, span), jnp.float32)
-            for part in range(rows // span):
-                piece = id_row[:, part * span : (part + 1) * span]
-                tail = jnp.where(row_at == part, piece, tail)
-            out[rows:, :] = tail.astype(jnp.bfloat16)
-
-
-def project(tokens, gain, w_qk, w_value, clusters, heads, width, parts=4):
+    for copy in copies[1:4]:
+        copy.wait()
+    unit_heads(normed, qk_buf, val_buf, (out_low, out_high), clusters, (2, 3), width)
+    for copy in copies[4:]:
+        copy.wait()
+
+
+def project_far(tokens, gain, w_qk, w_value, clusters, w_out, heads, width, parts=4):
     rows, depth = tokens.shape
-    pairs = heads // 2
-    return pl.pallas_call(
-        functools.partial(project_body, heads=heads, width=width, parts=parts),
-        out_shape=(shape((rows + EXTRA, 2 * width)),) * heads + (shape((rows, depth)),),
-        in_specs=[any_spec()] * 5,
-        out_specs=(vmem_spec(),) * (heads + 1),
+    message = shape((rows + EXTRA, 2 * width))
+    pair = (depth, 2 * width)
+    return pl.pallas_call(
+        functools.partial(project_far_body, heads=heads, width=width, parts=parts),
+        out_shape=(
+            message,
+            message,
+            shape((rows, depth)),
+            shape(clusters.shape, jnp.int32),
+            shape(pair),
+            shape(pair),
+            shape((w_out.shape[0], w_out.shape[1] // 2)),
+        ),
+        in_specs=[any_spec()] * 6,
+        out_specs=(vmem_spec(),) * 7,
         scratch_shapes=[
             pltpu.VMEM((rows, depth), jnp.bfloat16),
             pltpu.VMEM((1, depth), jnp.float32),
-            pltpu.VMEM(clusters.shape, jnp.int32),
-            pltpu.VMEM((pairs, depth, 2 * width), jnp.bfloat16),
-            pltpu.VMEM((pairs, depth, 2 * width), jnp.bfloat16),
-            pltpu.SemaphoreType.DMA((2 * pairs,)),
+            pltpu.VMEM(pair, jnp.bfloat16),
+            pltpu.VMEM(pair, jnp.bfloat16),
+            pltpu.SemaphoreType.DMA((7,)),
             pltpu.SemaphoreType.DMA((parts,)),
-            pltpu.SemaphoreType.DMA((2,)),
         ],
         compiler_params=params(20),
-        cost_estimate=cost(
-            4 * rows * depth * heads * width,
-            4 * (depth * heads * width + rows * depth + rows * heads * width),
-        ),
-        name="project",
-    )(*[held(a) for a in (tokens, gain.reshape(1, depth), w_qk, w_value, clusters)])
+        cost_estimate=cost(8 * rows * depth * width, 2 * rows * depth + 12 * depth * width),
+    )(*[held(a) for a in (tokens, gain.reshape(1, depth), w_qk, w_value, clusters, w_out)])
+
+
+def project_near_body(normed, w_qk, w_value, clusters, out_low, out_high, *, width):
+    unit_heads(normed, w_qk, w_value, (out_low, out_high), clusters, (0, 1), width)
+
+
+def project_near(normed, w_qk, w_value, clusters, width):
+    rows, depth = normed.shape
+    message = shape((rows + EXTRA, 2 * width))
+    return pl.pallas_call(
+        functools.partial(project_near_body, width=width),
+        out_shape=(message, message),
+        in_specs=[vmem_spec()] * 4,
+        out_specs=(vmem_spec(),) * 2,
+        compiler_params=params(14),
+        cost_estimate=cost(8 * rows * depth * width, 2 * rows * depth + 8 * depth * width),
+    )(normed, w_qk, w_value, clusters)
 
 
 def up_body(normed, w_up, hidden):
@@ -179,12 +202,11 @@
         out_specs=pl.BlockSpec((rows, block), lambda i: (0, i)),
         compiler_params=params(24),
         cost_estimate=cost(2 * rows * depth * units, 2 * depth * units + 4 * rows * depth),
-        name="grow",
     )(normed, w_up)
 
 
 def down_body(hidden, w_down, mine, far, away, held, *, share):
-    at = lax.axis_index("tensor")
+    at = lax.axis_index(TENSOR)
     held[...] = jnp.dot(hidden[...], w_down[...], preferred_element_type=jnp.float32)
 
     def quarter(turn):
@@ -217,13 +239,27 @@
         scratch_shapes=[pltpu.VMEM((rows, block), jnp.float32)],
         compiler_params=params(26),
         cost_estimate=cost(2 * rows * depth * units, 2 * depth * units + 6 * rows * depth),
-        name="shrink",
     )(hidden, w_down)
 
 
+def pick_body(far, got, sent):
+    sent[...] = (far[...] + got[1].astype(jnp.float32)).astype(jnp.bfloat16)
+
+
+def pick(far, got):
+    return pl.pallas_call(
+        pick_body,
+        out_shape=shape(far.shape),
+        in_specs=[vmem_spec(), vmem_spec()],
+        out_specs=vmem_spec(),
+        compiler_params=params(6),
+        cost_estimate=cost(far.size, far.size * 8),
+    )(far, got)
+
+
 def block_of(b, heads):
-    z = lax.axis_index("seq") >> 1
-    core = lax.axis_index("tensor") % 2
+    z = lax.axis_index(SEQ) >> 1
+    core = lax.axis_index(TENSOR) % 2
     pair = z ^ (b % heads)
     return 2 * pair + (core ^ (pair & 1) ^ (b // heads))
 
@@ -231,13 +267,11 @@
 def attend_body(*refs, heads, width, owned, steps, first):
     if first:
         own, other = refs[:heads], refs[heads : 2 * heads]
-        far, got = refs[2 * heads : 2 * heads + 2]
-        refs = refs[2 * heads + 2 :]
+        refs = refs[2 * heads :]
         outs = refs[: len(steps)]
-        kv, id_rows, picked = refs[len(steps) : len(steps) + 3]
-        query, id_cols, acc, den = refs[len(steps) + 3 :]
+        kv, id_rows = refs[len(steps) : len(steps) + 2]
+        query, id_cols, acc, den = refs[len(steps) + 2 :]
         rows = kv.shape[1]
-        picked[...] = (far[...] + got[1].astype(jnp.float32)).astype(jnp.bfloat16)
         for b, source in enumerate(list(own) + list(other)):
             kv[b] = source[:rows, :]
             tile = source[rows:, :].astype(jnp.float32)
@@ -319,7 +353,6 @@
         out_shape += (
             shape((2 * heads, rows, 2 * width)),
             shape((2 * heads, 8, rows), jnp.float32),
-            shape(inputs[-2].shape),
         )
     units = (heads * heads + heads // 2) * len(steps) // heads
     return pl.pallas_call(
@@ -341,13 +374,12 @@
             2 * heads * rows * width * 4,
             units * rows * rows,
         ),
-        name="attend",
     )(*inputs)
 
 
 def cut_body(*refs, count, share):
     back, kept, away, sums = refs[:count], refs[count], refs[count + 1 : -1], refs[-1]
-    at = lax.axis_index("tensor")
+    at = lax.axis_index(TENSOR)
     for k in range(count):
         for turn in range(len(away) + 1):
             here = pl.ds(pl.multiple_of((at ^ turn) * share, share), share)
@@ -366,22 +398,27 @@
         out_specs=(vmem_spec(),) * (tensor_count + 1),
         compiler_params=params(8),
         cost_estimate=cost(0, 4 * count * tensor_count * share * width),
-        name="cut",
     )(*back)
 
 
 def head_rows(weights, buf, sems, steps, width):
-    z = lax.axis_index("seq") >> 1
+    z = lax.axis_index(SEQ) >> 1
+    y = lax.axis_index(SEQ) & 1
     copies = []
-    for g, w in enumerate(weights):
+    for g, source in enumerate(weights):
         for i, k in enumerate(steps):
             here = pl.ds(pl.multiple_of((z ^ k) * width, width), width)
             to = pl.ds((g * len(steps) + i) * width, width)
-            copies.append(
-                pltpu.make_async_copy(
-                    w.at[here, :], buf.at[to, :], sems.at[g * len(steps) + i]
+            for turn, w in enumerate(source):
+                half = w.shape[1]
+                cols = pl.ds(0, half)
+                if len(source) == 2:
+                    cols = pl.ds(pl.multiple_of((y ^ turn) * half, half), half)
+                copies.append(
+                    pltpu.make_async_copy(
+                        w.at[here, :], buf.at[to, cols], sems.at[len(copies)]
+                    )
                 )
-            )
     return copies
 
 
@@ -390,14 +427,15 @@
 
 
 def mix_first_body(*refs, groups, width, steps, later):
-    pieces, weights = refs[:groups], refs[groups : 2 * groups]
-    tokens, mine, got, total, kept, buf, sems, later_sems = refs[2 * groups :]
+    pieces, flat = refs[:groups], refs[groups : groups + 6]
+    tokens, mine, got, total, kept, buf, sems, later_sems = refs[groups + 6 :]
+    weights = [flat[0:1], flat[1:2], flat[2:4], flat[4:6]]
     now = head_rows(weights, buf, sems, steps, width)
     then = head_rows(weights, kept, later_sems, later, width)
     for copy in now + then:
         copy.start()
     share = total.shape[0]
-    at = lax.axis_index("tensor")
+    at = lax.axis_index(TENSOR)
     here = pl.ds(pl.multiple_of(at * share, share), share)
     left = side_by_side(pieces, len(steps))
     known = tokens[here, :].astype(jnp.float32) + mine[...] + got[0].astype(jnp.float32)
@@ -418,26 +456,25 @@
             mix_first_body, groups=groups, width=width, steps=steps, later=later
         ),
         out_shape=(shape((share, depth), jnp.float32), shape(held)),
-        in_specs=[vmem_spec()] * groups + [any_spec()] * groups + [vmem_spec()] * 3,
+        in_specs=[vmem_spec()] * groups + [any_spec()] * 6 + [vmem_spec()] * 3,
         out_specs=(vmem_spec(), vmem_spec()),
         scratch_shapes=[
             pltpu.VMEM(held, jnp.bfloat16),
-            pltpu.SemaphoreType.DMA((groups * count,)),
-            pltpu.SemaphoreType.DMA((groups * count,)),
+            pltpu.SemaphoreType.DMA((6 * count,)),
+            pltpu.SemaphoreType.DMA((6 * count,)),
         ],
         compiler_params=params(24),
         cost_estimate=cost(
             2 * groups * share * count * width * depth,
             4 * groups * count * width * depth + 8 * share * depth,
         ),
-        name="mix_first",
     )(*pieces, *weights, tokens, mine, got)
 
 
 def mix_last_body(*refs, groups, steps, later):
     pieces = refs[:groups]
     total, held, came, first_sums, last_sums, centroids, out, updated = refs[groups:]
-    z = lax.axis_index("seq") >> 1
+    z = lax.axis_index(SEQ) >> 1
     left = side_by_side(pieces, len(later))
     known = total[...] + came[...].astype(jnp.float32)
     summed = known + jnp.dot(left, held[...], preferred_element_type=jnp.float32)
@@ -458,7 +495,6 @@
         out_specs=(vmem_spec(), vmem_spec()),
         compiler_params=params(16),
         cost_estimate=cost(2 * held.size * share, 2 * held.size + 8 * share * depth),
-        name="mix_last",
     )(*pieces, total, held, came, first_sums, last_sums, centroids)
 
 
@@ -466,65 +502,72 @@
     tokens, norm_gain, w_qk, w_value, w_out, w_up, w_down, centroids, clusters, slots
 ):
     tok_rows, _ = tokens.shape
-    seq_count = lax.axis_size("seq")
-    tensor_count = lax.axis_size("tensor")
+    seq_count = lax.axis_size(SEQ)
+    tensor_count = lax.axis_size(TENSOR)
     heads = clusters.shape[0]
     owned = centroids.shape[1]
     width = w_qk.shape[1] // heads
     share = tok_rows // tensor_count
     swaps = [None] + [[(t, t ^ d) for t in range(tensor_count)] for d in range(1, tensor_count)]
 
-    w_x = lax.ppermute(w_out, "tensor", swaps[2])
-    w_core = lax.ppermute(w_out, "tensor", swaps[1])
-
-    *messages, normed = project(tokens, norm_gain, w_qk, w_value, clusters, heads, width)
+    w_core = lax.ppermute(w_out, TENSOR, swaps[1])
     steps = [owner_pairs(k, seq_count, tensor_count) for k in range(heads)]
-    own, other = [None] * heads, [None] * heads
-    for k in reversed(range(heads)):
+    swap_y = [(s, s ^ 1) for s in range(seq_count)]
+    messages, own, other = [None] * heads, [None] * heads, [None] * heads
+    messages[2], messages[3], normed, ids, qk_next, val_next, out_part = project_far(
+        tokens, norm_gain, w_qk, w_value, clusters, w_out, heads, width
+    )
+    for k in (3, 2):
+        own[k] = lax.ppermute(messages[k], BOTH, steps[k])
+    far_here = lax.ppermute(out_part, TENSOR, swaps[2])
+    messages[0], messages[1] = project_near(normed, qk_next, val_next, ids, width)
+    for k in (1, 0):
         own[k] = lax.ppermute(messages[k], BOTH, steps[k])
     hidden = up(normed, held(w_up))
+    mine, far, sent = down(hidden, held(w_down), share)
+    got = lax.ppermute(sent, TENSOR, swaps[1])
     for k in range(heads):
-        other[k] = lax.ppermute(own[k], "tensor", swaps[1])
-    mine, far, sent = down(hidden, held(w_down), share)
-    got = lax.ppermute(sent, "tensor", swaps[1])
+        other[k] = lax.ppermute(own[k], TENSOR, swaps[1])
+    picked = pick(far, got)
+    came = lax.ppermute(picked, TENSOR, swaps[2])
+    far_there = lax.ppermute(far_here, SEQ, swap_y)
+    both_here = lax.ppermute(far_here, TENSOR, swaps[1])
+    both_there = lax.ppermute(far_there, TENSOR, swaps[1])
 
     early, late = (heads - 1, 0), (heads - 2, 1)
     back, pieces, sums = [None] * heads, {}, {}
-    *results, kv, id_rows, picked = attend(
-        own + other + [far, got], heads, tok_rows, width, owned, early, True
+    *results, kv, id_rows = attend(
+        own + other, heads, tok_rows, width, owned, early, True
     )
     for k, result in zip(early, results):
         back[k] = lax.ppermute(result, BOTH, turned(steps[k]))
     results = attend([kv, id_rows], heads, tok_rows, width, owned, late, False)
     for k, result in zip(late, results):
         back[k] = lax.ppermute(result, BOTH, turned(steps[k]))
-    w_both = lax.ppermute(w_x, "tensor", swaps[1])
-    came = lax.ppermute(picked, "tensor", swaps[2])
-
-    for name, turns in (("early", early), ("late", late)):
+
+    for name, turns in (("e", early), ("l", late)):
         kept, *away, sums[name] = cut([back[k] for k in turns], owned, share, tensor_count)
         pieces[name] = [kept] + [
-            lax.ppermute(away[d - 1], "tensor", swaps[d])
+            lax.ppermute(away[d - 1], TENSOR, swaps[d])
             for d in range(1, tensor_count)
         ]
-    total, late_rows = mix_first(
-        pieces["early"], [held(w_out), w_core, w_x, w_both], tokens, mine, got, early, late
-    )
+    weights = [held(w_out), w_core, far_here, far_there, both_here, both_there]
+    total, late_rows = mix_first(pieces["e"], weights, tokens, mine, got, early, late)
     mixed_rows, new_centroids = mix_last(
-        pieces["late"], total, late_rows, came, sums["early"], sums["late"], centroids, early, late
+        pieces["l"], total, late_rows, came, sums["e"], sums["l"], centroids, early, late
     )
     return (mixed_rows, new_centroids)
 
 
 def by_clusters(tokens, norm_gain, w_qk, w_value, w_out, w_up, w_down, centroids, clusters, slots):
     tok_rows = tokens.shape[0]
-    seq_count = lax.axis_size("seq")
-    tensor_count = lax.axis_size("tensor")
+    seq_count = lax.axis_size(SEQ)
+    tensor_count = lax.axis_size(TENSOR)
     heads_here = clusters.shape[0]
     owned_count = centroids.shape[1]
     head_width = w_qk.shape[1] // heads_here
     share_rows = tok_rows // tensor_count
-    row_first = lax.axis_index("tensor") * share_rows
+    row_first = lax.axis_index(TENSOR) * share_rows
     tokens_wide = tokens.astype(jnp.float32)
     normed = (
         tokens_wide
@@ -542,7 +585,7 @@
         .astype(jnp.bfloat16)
         .reshape(tok_rows, heads_here, head_width)
     )
-    positions = lax.axis_index("seq") * tok_rows + jnp.arange(tok_rows, dtype=jnp.int32)
+    positions = lax.axis_index(SEQ) * tok_rows + jnp.arange(tok_rows, dtype=jnp.int32)
     pos_high = (positions // 256).astype(jnp.float32).astype(jnp.bfloat16)
     pos_low = (positions % 256).astype(jnp.float32).astype(jnp.bfloat16)
     flat_slot = clusters.T * CAP + slots.T
@@ -573,10 +616,10 @@
         .set(jnp.broadcast_to(pos_low[:, None], flat_slot.shape))
         .reshape(layout)
     )
-    key_in = lax.all_to_all(key_buf, "seq", split_axis=1, concat_axis=1, tiled=True)
-    val_in = lax.all_to_all(val_buf, "seq", split_axis=1, concat_axis=1, tiled=True)
-    high_in = lax.all_to_all(high_buf, "seq", split_axis=1, concat_axis=1, tiled=True)
-    low_in = lax.all_to_all(low_buf, "seq", split_axis=1, concat_axis=1, tiled=True)
+    key_in = lax.all_to_all(key_buf, SEQ, split_axis=1, concat_axis=1, tiled=True)
+    val_in = lax.all_to_all(val_buf, SEQ, split_axis=1, concat_axis=1, tiled=True)
+    high_in = lax.all_to_all(high_buf, SEQ, split_axis=1, concat_axis=1, tiled=True)
+    low_in = lax.all_to_all(low_buf, SEQ, split_axis=1, concat_axis=1, tiled=True)
     scores = (
         jnp.einsum("hskad,htkbd->hksatb", key_in, key_in, preferred_element_type=jnp.float32)
         * SCORE_SCALE
@@ -589,13 +632,13 @@
     mixed_out = jnp.einsum(
         "hksatb,htkbd->hskad", weights, val_in, preferred_element_type=jnp.float32
     ).astype(jnp.bfloat16)
-    returned_back = lax.all_to_all(mixed_out, "seq", split_axis=1, concat_axis=1, tiled=True)
+    returned_back = lax.all_to_all(mixed_out, SEQ, split_axis=1, concat_axis=1, tiled=True)
     one_hot = (clusters[:, :, None] == jnp.arange(CLUSTERS, dtype=jnp.int32)[None, None, :]).astype(
         jnp.bfloat16
     )
     local_sums = jnp.einsum("htk,thd->hkd", one_hot, key_unit, preferred_element_type=jnp.float32)
     totals = lax.psum_scatter(
-        local_sums.astype(jnp.bfloat16), "seq", scatter_dimension=1, tiled=True
+        local_sums.astype(jnp.bfloat16), SEQ, scatter_dimension=1, tiled=True
     ).astype(jnp.float32)
     new_centroids = EMA_DECAY * centroids + (1.0 - EMA_DECAY) * totals
     returned = returned_back.reshape(heads_here, slot_total, head_width)
@@ -607,7 +650,7 @@
     ffn_part = jnp.dot(hidden, w_down, preferred_element_type=jnp.float32)
     summed = lax.psum_scatter(
         rounded(attn_part + ffn_part).astype(jnp.bfloat16),
-        "tensor",
+        TENSOR,
         scatter_dimension=0,
         tiled=True,
     ).astype(jnp.float32)
@@ -618,25 +661,25 @@
 
 def solution(mesh):
     in_specs = (
-        P("seq", None),
+        P(SEQ, None),
         P(),
-        P(None, "tensor"),
-        P(None, "tensor"),
-        P("tensor", None),
-        P(None, "tensor"),
-        P("tensor", None),
-        P("tensor", "seq", None),
-        P("tensor", "seq"),
-        P("tensor", "seq"),
-    )
-    out_specs = (P(("seq", "tensor"), None), P("tensor", "seq", None))
+        P(None, TENSOR),
+        P(None, TENSOR),
+        P(TENSOR, None),
+        P(None, TENSOR),
+        P(TENSOR, None),
+        P(TENSOR, SEQ, None),
+        P(TENSOR, SEQ),
+        P(TENSOR, SEQ),
+    )
+    out_specs = (P((SEQ, TENSOR), None), P(TENSOR, SEQ, None))
     sizes = dict(mesh.shape)
 
     def local(*args):
         heads = args[8].shape[0]
         fits = (
-            sizes["tensor"] == 4
-            and sizes["seq"] == 2 * heads
+            sizes[TENSOR] == 4
+            and sizes[SEQ] == 2 * heads
             and heads & (heads - 1) == 0
             and heads == 4
         )

time: 126 us -> 115 us (0.913); the launches traced: 124 us -> 114 us
  waiting for transfers between devices: 54.9 us -> 46.2 us
  Pallas kernels: 36.7 us -> 34.8 us
    ppermute x4, waiting for transfers between devices: 17.3 us -> 0.01 us  [by_heads(): own[k] = lax.ppermute(messages[k], BOTH, steps[k])]
    ppermute x4, waiting for transfers between devices: 3.38 us -> 12.9 us  [by_heads(): back[k] = lax.ppermute(result, BOTH, turned(steps[k]))]
    ppermute x4, starting transfers between devices: 7.95 us -> 10.3 us  [by_heads(): own[k] = lax.ppermute(messages[k], BOTH, steps[k])]
    pallas_call x1 -> x3, Pallas kernels: 7.93 us -> 6.07 us  [the longest x1 4.62 us: project_far(): pl.pallas_call(functools.partial(project_far_body, heads=heads, width=wid...]
    ppermute x15 -> x17, waiting for transfers between devices: 34.2 us -> 33.3 us  [the longest x1 15.1 us: by_heads(): far_here = lax.ppermute(out_part, TENSOR, swaps[2])]
    ppermute x15 -> x17, starting transfers between devices: 12.3 us -> 12 us  [the longest x6 4.44 us: by_heads(): lax.ppermute(away[d - 1], TENSOR, swaps[d])]
  transfers between devices with their start and end apart: 23 -> 25, of which waited for: 10 -> 11; matrix products, arithmetic and copies ran while one was open for 0% -> 0% of each run, Pallas kernels for 28% -> 25%
where the time goes in v2:
time: 115 us; the launch traced here: 114 us
  waiting for transfers between devices  46.2 us (40%)
  Pallas kernels  34.8 us (30%)
  starting transfers between devices  32.5 us (28%)
    ppermute x1, waiting for transfers between devices, by_heads(): far_here = lax.ppermute(out_part, TENSOR, swaps[2])  15.1 us
    ppermute x4, waiting for transfers between devices, by_heads(): back[k] = lax.ppermute(result, BOTH, turned(steps[k]))  12.9 us
    ppermute x6, waiting for transfers between devices, by_heads(): lax.ppermute(away[d - 1], TENSOR, swaps[d])  12.1 us
    pallas_call x2, Pallas kernels, attend(): pl.pallas_call(functools.partial(attend_body, heads=heads, width=width, o...  10.6 us
    ppermute x4, starting transfers between devices, by_heads(): own[k] = lax.ppermute(messages[k], BOTH, steps[k])  10.3 us
    ppermute x4, starting transfers between devices, by_heads(): back[k] = lax.ppermute(result, BOTH, turned(steps[k]))  10.3 us
    pallas_call x1, Pallas kernels, down(): pl.pallas_call(functools.partial(down_body, share=share), grid=(blocks,),...  7.38 us
    pallas_call x1, Pallas kernels, up(): pl.pallas_call(up_body, grid=(blocks,), out_shape=shape((rows, units)), i...  7 us
  transfers between devices with their start and end apart: 25, of which 11 were waited for; matrix products, arithmetic and copies ran while one was open for 0% of the time, Pallas kernels for 25%

profile of v2, /device:TPU:0, one launch (start us, length us, event | category | flops | bytes accessed | tf_op | source)
XLA Modules:
  0.0 114.4 jit_solution(13044644488257113273)
XLA Ops:
  0.6 4.6 %shard_map.104 = (bf16[528,256]{1,0:T(8,128)(2,1)S(1)}, bf16[528,256]{1,0:T(8,128)(2,1)S(1)}, bf16[512,2048]{1,0:T(8,128)(2,1)S(1)}, s32[4,512]{1,0:T(4,128)S(1)...) custom-call(bf16[512,2048]{1,0:T(8,128)(2,1)} %refs_10_.1, ...), custom_call_target="tpu_custom_call" | custom-call | flops 1073741824 | bytes 5242880 | tf_op jit(solution)/shard_map/pallas_call | solution.py:142
  5.3 3.0 %collective-permute-start.19 = (bf16[512,1024]{1,0:T(8,128)(2,1)S(1)}, bf16[512,1024]{1,0:T(8,128)(2,1)S(1)}, u32[]{:S(2)}, u32[]{:S(2)}) collective-permute-start(bf16[512,1024]{1,0:T(8,128)(2,1)S(1)} %get-tuple-element.54), channel_id=1, source_target_pairs={{0,2},{1,3},{2,0},{3,1},{4,6},{5,7},{6,4},{7,5},{8,10},{9,11},{10,... | collective-permute-start | bytes 3145736 | tf_op jit(solution)/shard_map/ppermute | solution.py:522
  10.4 3.4 %collective-permute-start.1 = (bf16[528,256]{1,0:T(8,128)(2,1)S(1)}, bf16[528,256]{1,0:T(8,128)(2,1)S(1)}, u32[]{:S(2)}, u32[]{:S(2)}) collective-permute-start(bf16[528,256]{1,0:T(8,128)(2,1)S(1)} %get-tuple-element.37), channel_id=1, source_target_pairs={{0,8},{1,12},{2,10},{3,14},{4,9},{5,13},{6,11},{7,15},{8,1},{9,5},... | collective-permute-start | bytes 811016 | tf_op jit(solution)/shard_map/ppermute | solution.py:525
  13.7 2.6 %collective-permute-start.2 = (bf16[528,256]{1,0:T(8,128)(2,1)S(1)}, bf16[528,256]{1,0:T(8,128)(2,1)S(1)}, u32[]{:S(2)}, u32[]{:S(2)}) collective-permute-start(bf16[528,256]{1,0:T(8,128)(2,1)S(1)} %get-tuple-element.38), channel_id=1, source_target_pairs={{0,16},{1,20},{2,18},{3,22},{4,17},{5,21},{6,19},{7,23},{8,25},{9,... | collective-permute-start | bytes 811016 | tf_op jit(solution)/shard_map/ppermute | solution.py:521
  16.3 15.1 %collective-permute-done.19.refs_6_ = bf16[512,1024]{1,0:T(8,128)(2,1)S(1)} collective-permute-done((bf16[512,1024]{1,0:T(8,128)(2,1)S(1)}, bf16[512,1024]{1,0:T(8,128)(2,1)S(1)}, u32[]{:S(2)}, u32[]{:S(2)}) %collective-permute-start.19) | collective-permute-done | bytes 1048608 | tf_op jit(solution)/shard_map/ppermute | solution.py:522
  31.5 1.8 %collective-permute-start.20 = (bf16[512,1024]{1,0:T(8,128)(2,1)S(1)}, bf16[512,1024]{1,0:T(8,128)(2,1)S(1)}, u32[]{:S(2)}, u32[]{:S(2)}) collective-permute-start(bf16[512,1024]{1,0:T(8,128)(2,1)S(1)} %collective-permute-done.19.refs_6_), channel_id=1, source_target_pairs={{0,4},{4,0},{8,12},{12,8},{16,20},{20,16},{24,28},{28,24},{1,5},{5... | collective-permute-start | bytes 3145736 | tf_op jit(solution)/shard_map/ppermute | solution.py:533
  33.2 7.0 %shard_map.110.hidden = bf16[512,2048]{1,0:T(8,128)(2,1)S(1)} custom-call(bf16[512,2048]{1,0:T(8,128)(2,1)S(1)} %get-tuple-element.32.normed, bf16[2048,2048]{1,0:T(8,128)(2,1)} %w_up.1), custom_call_target="tpu_custom_call" | custom-call | flops 4294967296 | bytes 12582912 | tf_op jit(solution)/shard_map/pallas_call | solution.py:194
  40.3 3.7 %collective-permute-start.3 = (bf16[528,256]{1,0:T(8,128)(2,1)S(1)}, bf16[528,256]{1,0:T(8,128)(2,1)S(1)}, u32[]{:S(2)}, u32[]{:S(2)}) collective-permute-start(bf16[528,256]{1,0:T(8,128)(2,1)S(1)} %get-tuple-element.39), channel_id=1, source_target_pairs={{0,24},{1,28},{2,26},{3,30},{4,25},{5,29},{6,27},{7,31},{8,17},{9,... | collective-permute-start | bytes 811016 | tf_op jit(solution)/shard_map/ppermute | solution.py:521
  44.4 7.4 %shard_map.111 = (f32[128,2048]{1,0:T(8,128)S(1)}, f32[128,2048]{1,0:T(8,128)S(1)}, bf16[2,128,2048]{2,1,0:T(8,128)(2,1)S(1)}) custom-call(bf16[512,2048]{1,0:T(8,128)(2,1)S(1)} %shard_map.110.hidden, bf16[2048,2048]{1,0:T(8,128)(2,1)} %w_down.1), custom_call_target="tpu_custom_call" | custom-call | flops 4294967296 | bytes 14680064 | tf_op jit(solution)/shard_map/pallas_call | solution.py:226
  52.5 2.4 %collective-permute-done.6.refs_6_ = bf16[528,256]{1,0:T(8,128)(2,1)S(1)} collective-permute-done((bf16[528,256]{1,0:T(8,128)(2,1)S(1)}, bf16[528,256]{1,0:T(8,128)(2,1)S(1)}, u32[]{:S(2)}, u32[]{:S(2)}) %collective-permute-start.6) | collective-permute-done | bytes 270368 | tf_op jit(solution)/shard_map/ppermute | solution.py:530
  55.1 3.6 %collective-permute-done.20.refs_7_ = bf16[512,1024]{1,0:T(8,128)(2,1)S(1)} collective-permute-done((bf16[512,1024]{1,0:T(8,128)(2,1)S(1)}, bf16[512,1024]{1,0:T(8,128)(2,1)S(1)}, u32[]{:S(2)}, u32[]{:S(2)}) %collective-permute-start.20) | collective-permute-done | bytes 1048608 | tf_op jit(solution)/shard_map/ppermute | solution.py:533
  58.7 5.4 %shard_map.106 = (bf16[544,128]{1,0:T(8,128)(2,1)S(1)}, bf16[544,128]{1,0:T(8,128)(2,1)S(1)}, bf16[8,512,256]{2,1,0:T(8,128)(2,1)S(1)}, f32[8,8,512]{2,1,0:T(8,128)S(1)}) custom-call(bf16[528,256]{1,0:T(8,128)(2,1)S(1)} %collective-permute-done.refs_0_, bf16[528,256]{1,0:T(8,128)(2,1)S(1)} %collective-permute-done.1.refs_1_, ...), custom_call_target="tpu_custom_call" | custom-call | flops 2415919104 | bytes 2097152 | tf_op jit(solution)/shard_map/pallas_call | solution.py:358
  64.1 5.2 %shard_map.107 = (bf16[544,128]{1,0:T(8,128)(2,1)S(1)}, bf16[544,128]{1,0:T(8,128)(2,1)S(1)}) custom-call(bf16[8,512,256]{2,1,0:T(8,128)(2,1)S(1)} %get-tuple-element.40.refs_0_, f32[8,8,512]{2,1,0:T(8,128)S(1)} %get-tuple-element.41.refs_1_), custom_call_target="tpu_custom_call" | custom-call | flops 2415919104 | bytes 2097152 | tf_op jit(solution)/shard_map/pallas_call | solution.py:358
  69.3 2.6 %collective-permute-start.8 = (bf16[544,128]{1,0:T(8,128)(2,1)S(1)}, bf16[544,128]{1,0:T(8,128)(2,1)S(1)}, u32[]{:S(2)}, u32[]{:S(2)}) collective-permute-start(bf16[544,128]{1,0:T(8,128)(2,1)S(1)} %get-tuple-element.42), channel_id=1, source_target_pairs={{16,0},{20,1},{18,2},{22,3},{17,4},{21,5},{19,6},{23,7},{25,8},{29... | collective-permute-start | bytes 417800 | tf_op jit(solution)/shard_map/ppermute | solution.py:546
  71.9 7.5 %collective-permute-done.8.refs_0_ = bf16[544,128]{1,0:T(8,128)(2,1)S(1)} collective-permute-done((bf16[544,128]{1,0:T(8,128)(2,1)S(1)}, bf16[544,128]{1,0:T(8,128)(2,1)S(1)}, u32[]{:S(2)}, u32[]{:S(2)}) %collective-permute-start.8) | collective-permute-done | bytes 139296 | tf_op jit(solution)/shard_map/ppermute | solution.py:546
  79.4 4.2 %collective-permute-start.13 = (bf16[544,128]{1,0:T(8,128)(2,1)S(1)}, bf16[544,128]{1,0:T(8,128)(2,1)S(1)}, u32[]{:S(2)}, u32[]{:S(2)}) collective-permute-start(bf16[544,128]{1,0:T(8,128)(2,1)S(1)} %get-tuple-element.48), channel_id=1, source_target_pairs={{24,0},{28,1},{26,2},{30,3},{25,4},{29,5},{27,6},{31,7},{17,8},{21... | collective-permute-start | bytes 417800 | tf_op jit(solution)/shard_map/ppermute | solution.py:543
  84.4 2.8 %collective-permute-done.13.refs_0_ = bf16[544,128]{1,0:T(8,128)(2,1)S(1)} collective-permute-done((bf16[544,128]{1,0:T(8,128)(2,1)S(1)}, bf16[544,128]{1,0:T(8,128)(2,1)S(1)}, u32[]{:S(2)}, u32[]{:S(2)}) %collective-permute-start.13) | collective-permute-done | bytes 139296 | tf_op jit(solution)/shard_map/ppermute | solution.py:543
  88.6 2.8 %collective-permute-start.9 = (bf16[544,128]{1,0:T(8,128)(2,1)S(1)}, bf16[544,128]{1,0:T(8,128)(2,1)S(1)}, u32[]{:S(2)}, u32[]{:S(2)}) collective-permute-start(bf16[544,128]{1,0:T(8,128)(2,1)S(1)} %get-tuple-element.43), channel_id=1, source_target_pairs={{8,0},{12,1},{10,2},{14,3},{9,4},{13,5},{11,6},{15,7},{1,8},{5,9},... | collective-permute-start | bytes 417800 | tf_op jit(solution)/shard_map/ppermute | solution.py:546
  91.4 2.7 %collective-permute-done.9.refs_1_ = bf16[544,128]{1,0:T(8,128)(2,1)S(1)} collective-permute-done((bf16[544,128]{1,0:T(8,128)(2,1)S(1)}, bf16[544,128]{1,0:T(8,128)(2,1)S(1)}, u32[]{:S(2)}, u32[]{:S(2)}) %collective-permute-start.9) | collective-permute-done | bytes 139296 | tf_op jit(solution)/shard_map/ppermute | solution.py:546
  95.3 1.5 %collective-permute-start.16 = (bf16[2,128,128]{2,1,0:T(8,128)(2,1)S(1)}, bf16[2,128,128]{2,1,0:T(8,128)(2,1)S(1)}, u32[]{:S(2)}, u32[]{:S(2)}) collective-permute-start(bf16[2,128,128]{2,1,0:T(8,128)(2,1)S(1)} %get-tuple-element.52), channel_id=1, source_target_pairs={{0,2},{1,3},{2,0},{3,1},{4,6},{5,7},{6,4},{7,5},{8,10},{9,11},{10,... | collective-permute-start | bytes 196616 | tf_op jit(solution)/shard_map/ppermute | solution.py:551
  96.8 6.0 %collective-permute-done.16.refs_2_ = bf16[2,128,128]{2,1,0:T(8,128)(2,1)S(1)} collective-permute-done((bf16[2,128,128]{2,1,0:T(8,128)(2,1)S(1)}, bf16[2,128,128]{2,1,0:T(8,128)(2,1)S(1)}, u32[]{:S(2)}, u32[]{:S(2)}) %collective-permute-start.16) | collective-permute-done | bytes 65568 | tf_op jit(solution)/shard_map/ppermute | solution.py:551
  103.5 3.6 %collective-permute-done.17.refs_3_ = bf16[2,128,128]{2,1,0:T(8,128)(2,1)S(1)} collective-permute-done((bf16[2,128,128]{2,1,0:T(8,128)(2,1)S(1)}, bf16[2,128,128]{2,1,0:T(8,128)(2,1)S(1)}, u32[]{:S(2)}, u32[]{:S(2)}) %collective-permute-start.17) | collective-permute-done | bytes 65568 | tf_op jit(solution)/shard_map/ppermute | solution.py:551
  109.0 2.2 %shard_map.112 = (f32[128,2048]{1,0:T(8,128)S(1)}, bf16[1024,2048]{1,0:T(8,128)(2,1)S(1)}) custom-call(bf16[2,128,128]{2,1,0:T(8,128)(2,1)S(1)} %get-tuple-element.50.refs_0_, bf16[2,128,128]{2,1,0:T(8,128)(2,1)S(1)} %collective-permute-done.15.refs_1_, bf16[2,128,128]{2,1,0:T(8,128)(2,1)S(1)} %collective-permute-done.16.refs_2_, ...), custom_call_target="tpu_custom_call" | custom-call | flops 536870912 | bytes 10485760 | tf_op jit(solution)/shard_map/pallas_call | solution.py:454
  112.8 1.5 %shard_map.114 = (bf16[128,2048]{1,0:T(8,128)(2,1)}, f32[4,32,128]{2,1,0:T(8,128)}) custom-call(bf16[2,128,128]{2,1,0:T(8,128)(2,1)S(1)} %get-tuple-element.44.refs_0_, bf16[2,128,128]{2,1,0:T(8,128)(2,1)S(1)} %collective-permute-done.10.refs_1_, bf16[2,128,128]{2,1,0:T(8,128)(2,1)S(1)} %collective-permute-done.11.refs_2_, ...), custom_call_target="tpu_custom_call" | custom-call | flops 536870912 | bytes 6291456 | tf_op jit(solution)/shard_map/pallas_call | solution.py:491
  (43 shorter events, 11.0 us)
Async XLA Ops:
  5.3 26.2 %collective-permute-start.19 = (bf16[512,1024]{1,0:T(8,128)(2,1)S(1)}, bf16[512,1024]{1,0:T(8,128)(2,1)S(1)}, u32[]{:S(2)}, u32[]{:S(2)}) collective-permute-start(bf16[512,1024]{1,0:T(8,128)(2,1)S(1)} %get-tuple-element.54), channel_id=1, source_target_pairs={{0,2},{1,3},{2,0},{3,1},{4,6},{5,7},{6,4},{7,5},{8,10},{9,11},{10,... | collective-permute-start | bytes 3145736 | tf_op jit(solution)/shard_map/ppermute | solution.py:522
  8.3 99.0 %collective-permute-start.18 = (bf16[512,2048]{1,0:T(8,128)(2,1)S(1)}, bf16[512,2048]{1,0:T(8,128)(2,1)S(1)}, u32[]{:S(2)}, u32[]{:S(2)}) collective-permute-start(bf16[512,2048]{1,0:T(8,128)(2,1)S(1)} %copy-done.2), channel_id=1, source_target_pairs={{0,1},{1,0},{2,3},{3,2},{4,5},{5,4},{6,7},{7,6},{8,9},{9,8},{10,11... | collective-permute-start | bytes 6291464 | tf_op jit(solution)/shard_map/ppermute | solution.py:513
  9.7 30.6 %collective-permute-start = (bf16[528,256]{1,0:T(8,128)(2,1)S(1)}, bf16[528,256]{1,0:T(8,128)(2,1)S(1)}, u32[]{:S(2)}, u32[]{:S(2)}) collective-permute-start(bf16[528,256]{1,0:T(8,128)(2,1)S(1)} %get-tuple-element.36), channel_id=1, source_target_pairs={{0,0},{1,4},{2,2},{3,6},{4,1},{5,5},{6,3},{7,7},{8,9},{9,13},{10,1... | collective-permute-start | bytes 811016 | tf_op jit(solution)/shard_map/ppermute | solution.py:525
  10.4 33.6 %collective-permute-start.1 = (bf16[528,256]{1,0:T(8,128)(2,1)S(1)}, bf16[528,256]{1,0:T(8,128)(2,1)S(1)}, u32[]{:S(2)}, u32[]{:S(2)}) collective-permute-start(bf16[528,256]{1,0:T(8,128)(2,1)S(1)} %get-tuple-element.37), channel_id=1, source_target_pairs={{0,8},{1,12},{2,10},{3,14},{4,9},{5,13},{6,11},{7,15},{8,1},{9,5},... | collective-permute-start | bytes 811016 | tf_op jit(solution)/shard_map/ppermute | solution.py:525
  13.7 30.2 %collective-permute-start.2 = (bf16[528,256]{1,0:T(8,128)(2,1)S(1)}, bf16[528,256]{1,0:T(8,128)(2,1)S(1)}, u32[]{:S(2)}, u32[]{:S(2)}) collective-permute-start(bf16[528,256]{1,0:T(8,128)(2,1)S(1)} %get-tuple-element.38), channel_id=1, source_target_pairs={{0,16},{1,20},{2,18},{3,22},{4,17},{5,21},{6,19},{7,23},{8,25},{9,... | collective-permute-start | bytes 811016 | tf_op jit(solution)/shard_map/ppermute | solution.py:521
  31.5 27.2 %collective-permute-start.20 = (bf16[512,1024]{1,0:T(8,128)(2,1)S(1)}, bf16[512,1024]{1,0:T(8,128)(2,1)S(1)}, u32[]{:S(2)}, u32[]{:S(2)}) collective-permute-start(bf16[512,1024]{1,0:T(8,128)(2,1)S(1)} %collective-permute-done.19.refs_6_), channel_id=1, source_target_pairs={{0,4},{4,0},{8,12},{12,8},{16,20},{20,16},{24,28},{28,24},{1,5},{5... | collective-permute-start | bytes 3145736 | tf_op jit(solution)/shard_map/ppermute | solution.py:533
  40.3 11.6 %collective-permute-start.3 = (bf16[528,256]{1,0:T(8,128)(2,1)S(1)}, bf16[528,256]{1,0:T(8,128)(2,1)S(1)}, u32[]{:S(2)}, u32[]{:S(2)}) collective-permute-start(bf16[528,256]{1,0:T(8,128)(2,1)S(1)} %get-tuple-element.39), channel_id=1, source_target_pairs={{0,24},{1,28},{2,26},{3,30},{4,25},{5,29},{6,27},{7,31},{8,17},{9,... | collective-permute-start | bytes 811016 | tf_op jit(solution)/shard_map/ppermute | solution.py:521
  43.9 8.1 %collective-permute-start.4 = (bf16[528,256]{1,0:T(8,128)(2,1)S(1)}, bf16[528,256]{1,0:T(8,128)(2,1)S(1)}, u32[]{:S(2)}, u32[]{:S(2)}) collective-permute-start(bf16[528,256]{1,0:T(8,128)(2,1)S(1)} %collective-permute-done.refs_0_), channel_id=1, source_target_pairs={{0,1},{1,0},{2,3},{3,2},{4,5},{5,4},{6,7},{7,6},{8,9},{9,8},{10,11... | collective-permute-start | bytes 811016 | tf_op jit(solution)/shard_map/ppermute | solution.py:530
  44.0 8.4 %collective-permute-start.5 = (bf16[528,256]{1,0:T(8,128)(2,1)S(1)}, bf16[528,256]{1,0:T(8,128)(2,1)S(1)}, u32[]{:S(2)}, u32[]{:S(2)}) collective-permute-start(bf16[528,256]{1,0:T(8,128)(2,1)S(1)} %collective-permute-done.1.refs_1_), channel_id=1, source_target_pairs={{0,1},{1,0},{2,3},{3,2},{4,5},{5,4},{6,7},{7,6},{8,9},{9,8},{10,11... | collective-permute-start | bytes 811016 | tf_op jit(solution)/shard_map/ppermute | solution.py:530
  51.8 31.8 %collective-permute-start.23 = (bf16[2,128,2048]{2,1,0:T(8,128)(2,1)S(1)}, bf16[2,128,2048]{2,1,0:T(8,128)(2,1)S(1)}, u32[]{:S(2)}, u32[]{:S(2)}) collective-permute-start(bf16[2,128,2048]{2,1,0:T(8,128)(2,1)S(1)} %get-tuple-element.56), channel_id=1, source_target_pairs={{0,1},{1,0},{2,3},{3,2},{4,5},{5,4},{6,7},{7,6},{8,9},{9,8},{10,11... | collective-permute-start | bytes 3145736 | tf_op jit(solution)/shard_map/ppermute | solution.py:528
  52.0 3.0 %collective-permute-start.6 = (bf16[528,256]{1,0:T(8,128)(2,1)S(1)}, bf16[528,256]{1,0:T(8,128)(2,1)S(1)}, u32[]{:S(2)}, u32[]{:S(2)}) collective-permute-start(bf16[528,256]{1,0:T(8,128)(2,1)S(1)} %collective-permute-done.2.refs_2_), channel_id=1, source_target_pairs={{0,1},{1,0},{2,3},{3,2},{4,5},{5,4},{6,7},{7,6},{8,9},{9,8},{10,11... | collective-permute-start | bytes 811016 | tf_op jit(solution)/shard_map/ppermute | solution.py:530
  52.4 6.3 %collective-permute-start.7 = (bf16[528,256]{1,0:T(8,128)(2,1)S(1)}, bf16[528,256]{1,0:T(8,128)(2,1)S(1)}, u32[]{:S(2)}, u32[]{:S(2)}) collective-permute-start(bf16[528,256]{1,0:T(8,128)(2,1)S(1)} %collective-permute-done.3.refs_3_), channel_id=1, source_target_pairs={{0,1},{1,0},{2,3},{3,2},{4,5},{5,4},{6,7},{7,6},{8,9},{9,8},{10,11... | collective-permute-start | bytes 811016 | tf_op jit(solution)/shard_map/ppermute | solution.py:530
  54.9 53.5 %collective-permute-start.21 = (bf16[512,1024]{1,0:T(8,128)(2,1)S(1)}, bf16[512,1024]{1,0:T(8,128)(2,1)S(1)}, u32[]{:S(2)}, u32[]{:S(2)}) collective-permute-start(bf16[512,1024]{1,0:T(8,128)(2,1)S(1)} %collective-permute-done.19.refs_6_), channel_id=1, source_target_pairs={{0,1},{1,0},{2,3},{3,2},{4,5},{5,4},{6,7},{7,6},{8,9},{9,8},{10,11... | collective-permute-start | bytes 3145736 | tf_op jit(solution)/shard_map/ppermute | solution.py:534
  58.7 50.3 %collective-permute-start.22 = (bf16[512,1024]{1,0:T(8,128)(2,1)S(1)}, bf16[512,1024]{1,0:T(8,128)(2,1)S(1)}, u32[]{:S(2)}, u32[]{:S(2)}) collective-permute-start(bf16[512,1024]{1,0:T(8,128)(2,1)S(1)} %collective-permute-done.20.refs_7_), channel_id=1, source_target_pairs={{0,1},{1,0},{2,3},{3,2},{4,5},{5,4},{6,7},{7,6},{8,9},{9,8},{10,11... | collective-permute-start | bytes 3145736 | tf_op jit(solution)/shard_map/ppermute | solution.py:535
  69.3 10.1 %collective-permute-start.8 = (bf16[544,128]{1,0:T(8,128)(2,1)S(1)}, bf16[544,128]{1,0:T(8,128)(2,1)S(1)}, u32[]{:S(2)}, u32[]{:S(2)}) collective-permute-start(bf16[544,128]{1,0:T(8,128)(2,1)S(1)} %get-tuple-element.42), channel_id=1, source_target_pairs={{16,0},{20,1},{18,2},{22,3},{17,4},{21,5},{19,6},{23,7},{25,8},{29... | collective-permute-start | bytes 417800 | tf_op jit(solution)/shard_map/ppermute | solution.py:546
  79.4 7.8 %collective-permute-start.13 = (bf16[544,128]{1,0:T(8,128)(2,1)S(1)}, bf16[544,128]{1,0:T(8,128)(2,1)S(1)}, u32[]{:S(2)}, u32[]{:S(2)}) collective-permute-start(bf16[544,128]{1,0:T(8,128)(2,1)S(1)} %get-tuple-element.48), channel_id=1, source_target_pairs={{24,0},{28,1},{26,2},{30,3},{25,4},{29,5},{27,6},{31,7},{17,8},{21... | collective-permute-start | bytes 417800 | tf_op jit(solution)/shard_map/ppermute | solution.py:543
  83.7 4.9 %collective-permute-start.14 = (bf16[544,128]{1,0:T(8,128)(2,1)S(1)}, bf16[544,128]{1,0:T(8,128)(2,1)S(1)}, u32[]{:S(2)}, u32[]{:S(2)}) collective-permute-start(bf16[544,128]{1,0:T(8,128)(2,1)S(1)} %get-tuple-element.49), channel_id=1, source_target_pairs={{0,0},{4,1},{2,2},{6,3},{1,4},{5,5},{3,6},{7,7},{9,8},{13,9},{11,1... | collective-permute-start | bytes 417800 | tf_op jit(solution)/shard_map/ppermute | solution.py:543
  87.2 25.7 %collective-permute-start.24 = (bf16[128,2048]{1,0:T(8,128)(2,1)S(1)}, bf16[128,2048]{1,0:T(8,128)(2,1)S(1)}, u32[]{:S(2)}, u32[]{:S(2)}) collective-permute-start(bf16[128,2048]{1,0:T(8,128)(2,1)S(1)} %shard_map.113), channel_id=1, source_target_pairs={{0,2},{1,3},{2,0},{3,1},{4,6},{5,7},{6,4},{7,5},{8,10},{9,11},{10,... | collective-permute-start | bytes 1572872 | tf_op jit(solution)/shard_map/ppermute | solution.py:532
  88.6 5.4 %collective-permute-start.9 = (bf16[544,128]{1,0:T(8,128)(2,1)S(1)}, bf16[544,128]{1,0:T(8,128)(2,1)S(1)}, u32[]{:S(2)}, u32[]{:S(2)}) collective-permute-start(bf16[544,128]{1,0:T(8,128)(2,1)S(1)} %get-tuple-element.43), channel_id=1, source_target_pairs={{8,0},{12,1},{10,2},{14,3},{9,4},{13,5},{11,6},{15,7},{1,8},{5,9},... | collective-permute-start | bytes 417800 | tf_op jit(solution)/shard_map/ppermute | solution.py:546
  95.3 7.5 %collective-permute-start.16 = (bf16[2,128,128]{2,1,0:T(8,128)(2,1)S(1)}, bf16[2,128,128]{2,1,0:T(8,128)(2,1)S(1)}, u32[]{:S(2)}, u32[]{:S(2)}) collective-permute-start(bf16[2,128,128]{2,1,0:T(8,128)(2,1)S(1)} %get-tuple-element.52), channel_id=1, source_target_pairs={{0,2},{1,3},{2,0},{3,1},{4,6},{5,7},{6,4},{7,5},{8,10},{9,11},{10,... | collective-permute-start | bytes 196616 | tf_op jit(solution)/shard_map/ppermute | solution.py:551
  102.8 4.3 %collective-permute-start.17 = (bf16[2,128,128]{2,1,0:T(8,128)(2,1)S(1)}, bf16[2,128,128]{2,1,0:T(8,128)(2,1)S(1)}, u32[]{:S(2)}, u32[]{:S(2)}) collective-permute-start(bf16[2,128,128]{2,1,0:T(8,128)(2,1)S(1)} %get-tuple-element.53), channel_id=1, source_target_pairs={{0,3},{1,2},{2,1},{3,0},{4,7},{5,6},{6,5},{7,4},{8,11},{9,10},{10,... | collective-permute-start | bytes 196616 | tf_op jit(solution)/shard_map/ppermute | solution.py:551
  107.2 4.1 %collective-permute-start.10 = (bf16[2,128,128]{2,1,0:T(8,128)(2,1)S(1)}, bf16[2,128,128]{2,1,0:T(8,128)(2,1)S(1)}, u32[]{:S(2)}, u32[]{:S(2)}) collective-permute-start(bf16[2,128,128]{2,1,0:T(8,128)(2,1)S(1)} %get-tuple-element.45), channel_id=1, source_target_pairs={{0,1},{1,0},{2,3},{3,2},{4,5},{5,4},{6,7},{7,6},{8,9},{9,8},{10,11... | collective-permute-start | bytes 196616 | tf_op jit(solution)/shard_map/ppermute | solution.py:551
  107.3 4.6 %collective-permute-start.11 = (bf16[2,128,128]{2,1,0:T(8,128)(2,1)S(1)}, bf16[2,128,128]{2,1,0:T(8,128)(2,1)S(1)}, u32[]{:S(2)}, u32[]{:S(2)}) collective-permute-start(bf16[2,128,128]{2,1,0:T(8,128)(2,1)S(1)} %get-tuple-element.46), channel_id=1, source_target_pairs={{0,2},{1,3},{2,0},{3,1},{4,6},{5,7},{6,4},{7,5},{8,10},{9,11},{10,... | collective-permute-start | bytes 196616 | tf_op jit(solution)/shard_map/ppermute | solution.py:551
  108.5 4.3 %collective-permute-start.12 = (bf16[2,128,128]{2,1,0:T(8,128)(2,1)S(1)}, bf16[2,128,128]{2,1,0:T(8,128)(2,1)S(1)}, u32[]{:S(2)}, u32[]{:S(2)}) collective-permute-start(bf16[2,128,128]{2,1,0:T(8,128)(2,1)S(1)} %get-tuple-element.47), channel_id=1, source_target_pairs={{0,3},{1,2},{2,1},{3,0},{4,7},{5,6},{6,5},{7,4},{8,11},{9,10},{10,... | collective-permute-start | bytes 196616 | tf_op jit(solution)/shard_map/ppermute | solution.py:551
  (4 other events, 52.5 us)

commit v3 on v2

--- a/solution.py
+++ b/solution.py
@@ -91,10 +91,10 @@
 
 
 def project_far_body(
-    tokens_at, gain_at, w_qk, w_value, clusters_at, w_out, *rest, heads, width, parts
+    tokens_at, gain_at, w_qk, w_value, clusters_at, w_out, *rest, width, stages, parts
 ):
-    out_low, out_high, normed, clusters, qk_next, val_next, out_part = rest[:7]
-    tokens, gain, qk_buf, val_buf, sems, token_sems = rest[7:]
+    out_low, out_high, normed, clusters, qk_next, val_next, out_early, out_late = rest[:8]
+    tokens, gain, qk_buf, val_buf, sems, token_sems, out_sems = rest[8:]
     z = lax.axis_index(SEQ) >> 1
     y = lax.axis_index(SEQ) & 1
     step = tokens.shape[0] // parts
@@ -109,18 +109,28 @@
         return pl.ds(pl.multiple_of(block * span, span), span)
 
     first, second = columns(1 ^ (z >> 1)), columns(z >> 1)
-    half = out_part.shape[1]
+    half = out_early.shape[1]
     out_cols = pl.ds(pl.multiple_of(y * half, half), half)
+    out_copies = []
+    for part, turns in ((out_early, stages[0]), (out_late, stages[1])):
+        for i, k in enumerate(turns):
+            here = pl.ds(pl.multiple_of((z ^ k) * width, width), width)
+            out_copies.append(
+                pltpu.make_async_copy(
+                    w_out.at[here, out_cols],
+                    part.at[pl.ds(i * width, width), :],
+                    out_sems.at[len(out_copies)],
+                )
+            )
     copies = [
         pltpu.make_async_copy(gain_at, gain, sems.at[0]),
         pltpu.make_async_copy(w_qk.at[:, first], qk_buf, sems.at[1]),
         pltpu.make_async_copy(w_value.at[:, first], val_buf, sems.at[2]),
         pltpu.make_async_copy(clusters_at, clusters, sems.at[3]),
-        pltpu.make_async_copy(w_out.at[:, out_cols], out_part, sems.at[4]),
-        pltpu.make_async_copy(w_qk.at[:, second], qk_next, sems.at[5]),
-        pltpu.make_async_copy(w_value.at[:, second], val_next, sems.at[6]),
+        pltpu.make_async_copy(w_qk.at[:, second], qk_next, sems.at[4]),
+        pltpu.make_async_copy(w_value.at[:, second], val_next, sems.at[5]),
     ]
-    for copy in (copies[0], *slab_copies, *copies[1:]):
+    for copy in (copies[0], *slab_copies, *copies[1:4], *out_copies, *copies[4:]):
         copy.start()
     copies[0].wait()
     for copy, here in zip(slab_copies, slabs):
@@ -131,16 +141,16 @@
     for copy in copies[1:4]:
         copy.wait()
     unit_heads(normed, qk_buf, val_buf, (out_low, out_high), clusters, (2, 3), width)
-    for copy in copies[4:]:
+    for copy in copies[4:] + out_copies:
         copy.wait()
 
 
-def project_far(tokens, gain, w_qk, w_value, clusters, w_out, heads, width, parts=4):
+def project_far(tokens, gain, w_qk, w_value, clusters, w_out, width, stages, parts=4):
     rows, depth = tokens.shape
     message = shape((rows + EXTRA, 2 * width))
     pair = (depth, 2 * width)
     return pl.pallas_call(
-        functools.partial(project_far_body, heads=heads, width=width, parts=parts),
+        functools.partial(project_far_body, width=width, stages=stages, parts=parts),
         out_shape=(
             message,
             message,
@@ -148,17 +158,19 @@
             shape(clusters.shape, jnp.int32),
             shape(pair),
             shape(pair),
-            shape((w_out.shape[0], w_out.shape[1] // 2)),
+            shape((2 * width, w_out.shape[1] // 2)),
+            shape((2 * width, w_out.shape[1] // 2)),
         ),
         in_specs=[any_spec()] * 6,
-        out_specs=(vmem_spec(),) * 7,
+        out_specs=(vmem_spec(),) * 8,
         scratch_shapes=[
             pltpu.VMEM((rows, depth), jnp.bfloat16),
             pltpu.VMEM((1, depth), jnp.float32),
             pltpu.VMEM(pair, jnp.bfloat16),
             pltpu.VMEM(pair, jnp.bfloat16),
-            pltpu.SemaphoreType.DMA((7,)),
+            pltpu.SemaphoreType.DMA((6,)),
             pltpu.SemaphoreType.DMA((parts,)),
+            pltpu.SemaphoreType.DMA((4,)),
         ],
         compiler_params=params(20),
         cost_estimate=cost(8 * rows * depth * width, 2 * rows * depth + 12 * depth * width),
@@ -403,22 +415,14 @@
 
 def head_rows(weights, buf, sems, steps, width):
     z = lax.axis_index(SEQ) >> 1
-    y = lax.axis_index(SEQ) & 1
     copies = []
-    for g, source in enumerate(weights):
+    for g, w in enumerate(weights):
         for i, k in enumerate(steps):
             here = pl.ds(pl.multiple_of((z ^ k) * width, width), width)
             to = pl.ds((g * len(steps) + i) * width, width)
-            for turn, w in enumerate(source):
-                half = w.shape[1]
-                cols = pl.ds(0, half)
-                if len(source) == 2:
-                    cols = pl.ds(pl.multiple_of((y ^ turn) * half, half), half)
-                copies.append(
-                    pltpu.make_async_copy(
-                        w.at[here, :], buf.at[to, cols], sems.at[len(copies)]
-                    )
-                )
+            copies.append(
+                pltpu.make_async_copy(w.at[here, :], buf.at[to, :], sems.at[len(copies)])
+            )
     return copies
 
 
@@ -426,10 +430,27 @@
     return jnp.concatenate([p[k] for p in pieces for k in range(count)], axis=1)
 
 
+def products(pieces, count, near_rows, far_halves, known, put):
+    y = lax.axis_index(SEQ) & 1
+    half = far_halves[0].shape[1]
+    near = side_by_side(pieces[:2], count)
+    same, cross = side_by_side(pieces[2:3], count), side_by_side(pieces[3:4], count)
+    for turn in range(2):
+        cols = pl.ds(pl.multiple_of((y ^ turn) * half, half), half)
+        total = known(cols)
+        for left, rows in (
+            (near, near_rows[:, cols]),
+            (same, far_halves[turn][...]),
+            (cross, far_halves[2 + turn][...]),
+        ):
+            total = total + jnp.dot(left, rows, preferred_element_type=jnp.float32)
+        put(cols, total)
+
+
 def mix_first_body(*refs, groups, width, steps, later):
-    pieces, flat = refs[:groups], refs[groups : groups + 6]
+    pieces, weights = refs[:groups], refs[groups : groups + 2]
+    far_halves = refs[groups + 2 : groups + 6]
     tokens, mine, got, total, kept, buf, sems, later_sems = refs[groups + 6 :]
-    weights = [flat[0:1], flat[1:2], flat[2:4], flat[4:6]]
     now = head_rows(weights, buf, sems, steps, width)
     then = head_rows(weights, kept, later_sems, later, width)
     for copy in now + then:
@@ -437,65 +458,77 @@
     share = total.shape[0]
     at = lax.axis_index(TENSOR)
     here = pl.ds(pl.multiple_of(at * share, share), share)
-    left = side_by_side(pieces, len(steps))
-    known = tokens[here, :].astype(jnp.float32) + mine[...] + got[0].astype(jnp.float32)
     for copy in now:
         copy.wait()
-    total[...] = known + jnp.dot(left, buf[...], preferred_element_type=jnp.float32)
+
+    def known(cols):
+        base = tokens[here, cols].astype(jnp.float32) + mine[:, cols]
+        return base + got[0, :, cols].astype(jnp.float32)
+
+    def put(cols, value):
+        total[:, cols] = value
+
+    products(pieces, len(steps), buf, far_halves, known, put)
     for copy in then:
         copy.wait()
 
 
-def mix_first(pieces, weights, tokens, mine, got, steps, later):
+def mix_first(pieces, weights, far_halves, tokens, mine, got, steps, later):
     groups = len(pieces)
     count, share, width = pieces[0].shape
     depth = tokens.shape[1]
-    held = (groups * count * width, depth)
+    rows = (2 * count * width, depth)
     return pl.pallas_call(
         functools.partial(
             mix_first_body, groups=groups, width=width, steps=steps, later=later
         ),
-        out_shape=(shape((share, depth), jnp.float32), shape(held)),
-        in_specs=[vmem_spec()] * groups + [any_spec()] * 6 + [vmem_spec()] * 3,
+        out_shape=(shape((share, depth), jnp.float32), shape(rows)),
+        in_specs=[vmem_spec()] * groups + [any_spec()] * 2 + [vmem_spec()] * 7,
         out_specs=(vmem_spec(), vmem_spec()),
         scratch_shapes=[
-            pltpu.VMEM(held, jnp.bfloat16),
-            pltpu.SemaphoreType.DMA((6 * count,)),
-            pltpu.SemaphoreType.DMA((6 * count,)),
+            pltpu.VMEM(rows, jnp.bfloat16),
+            pltpu.SemaphoreType.DMA((2 * count,)),
+            pltpu.SemaphoreType.DMA((2 * count,)),
         ],
-        compiler_params=params(24),
+        compiler_params=params(20),
         cost_estimate=cost(
             2 * groups * share * count * width * depth,
             4 * groups * count * width * depth + 8 * share * depth,
         ),
-    )(*pieces, *weights, tokens, mine, got)
+    )(*pieces, *weights, *far_halves, tokens, mine, got)
 
 
 def mix_last_body(*refs, groups, steps, later):
-    pieces = refs[:groups]
-    total, held, came, first_sums, last_sums, centroids, out, updated = refs[groups:]
+    pieces, far_halves = refs[:groups], refs[groups : groups + 4]
+    total, kept, came, first_sums, last_sums, centroids, out, updated = refs[groups + 4 :]
     z = lax.axis_index(SEQ) >> 1
-    left = side_by_side(pieces, len(later))
-    known = total[...] + came[...].astype(jnp.float32)
-    summed = known + jnp.dot(left, held[...], preferred_element_type=jnp.float32)
-    out[...] = summed.astype(jnp.bfloat16)
+
+    def known(cols):
+        return total[:, cols] + came[:, cols].astype(jnp.float32)
+
+    def put(cols, value):
+        out[:, cols] = value.astype(jnp.bfloat16)
+
+    products(pieces, len(later), kept, far_halves, known, put)
     for sums, turns in ((first_sums, steps), (last_sums, later)):
         for i, k in enumerate(turns):
             head = z ^ k
             updated[head] = EMA_DECAY * centroids[head] + (1.0 - EMA_DECAY) * sums[i]
 
 
-def mix_last(pieces, total, held, came, first_sums, last_sums, centroids, steps, later):
+def mix_last(
+    pieces, far_halves, total, kept, came, first_sums, last_sums, centroids, steps, later
+):
     groups = len(pieces)
     share, depth = total.shape
     return pl.pallas_call(
         functools.partial(mix_last_body, groups=groups, steps=steps, later=later),
         out_shape=(shape((share, depth)), shape(centroids.shape, jnp.float32)),
-        in_specs=[vmem_spec()] * (groups + 6),
+        in_specs=[vmem_spec()] * (groups + 10),
         out_specs=(vmem_spec(), vmem_spec()),
         compiler_params=params(16),
-        cost_estimate=cost(2 * held.size * share, 2 * held.size + 8 * share * depth),
-    )(*pieces, total, held, came, first_sums, last_sums, centroids)
+        cost_estimate=cost(4 * kept.size * share, 4 * kept.size + 8 * share * depth),
+    )(*pieces, *far_halves, total, kept, came, first_sums, last_sums, centroids)
 
 
 def by_heads(
@@ -514,12 +547,17 @@
     steps = [owner_pairs(k, seq_count, tensor_count) for k in range(heads)]
     swap_y = [(s, s ^ 1) for s in range(seq_count)]
     messages, own, other = [None] * heads, [None] * heads, [None] * heads
-    messages[2], messages[3], normed, ids, qk_next, val_next, out_part = project_far(
-        tokens, norm_gain, w_qk, w_value, clusters, w_out, heads, width
+    early, late = (heads - 1, 0), (heads - 2, 1)
+    messages[2], messages[3], normed, ids, qk_next, val_next, *out_parts = project_far(
+        tokens, norm_gain, w_qk, w_value, clusters, w_out, width, (early, late)
     )
     for k in (3, 2):
         own[k] = lax.ppermute(messages[k], BOTH, steps[k])
-    far_here = lax.ppermute(out_part, TENSOR, swaps[2])
+    halves = {}
+    for name, part in zip("el", out_parts):
+        here = lax.ppermute(part, TENSOR, swaps[2])
+        there = lax.ppermute(here, SEQ, swap_y)
+        halves[name] = [here, there] + [lax.ppermute(w, TENSOR, swaps[1]) for w in (here, there)]
     messages[0], messages[1] = project_near(normed, qk_next, val_next, ids, width)
     for k in (1, 0):
         own[k] = lax.ppermute(messages[k], BOTH, steps[k])
@@ -530,11 +568,6 @@
         other[k] = lax.ppermute(own[k], TENSOR, swaps[1])
     picked = pick(far, got)
     came = lax.ppermute(picked, TENSOR, swaps[2])
-    far_there = lax.ppermute(far_here, SEQ, swap_y)
-    both_here = lax.ppermute(far_here, TENSOR, swaps[1])
-    both_there = lax.ppermute(far_there, TENSOR, swaps[1])
-
-    early, late = (heads - 1, 0), (heads - 2, 1)
     back, pieces, sums = [None] * heads, {}, {}
     *results, kv, id_rows = attend(
         own + other, heads, tok_rows, width, owned, early, True
@@ -551,10 +584,12 @@
             lax.ppermute(away[d - 1], TENSOR, swaps[d])
             for d in range(1, tensor_count)
         ]
-    weights = [held(w_out), w_core, far_here, far_there, both_here, both_there]
-    total, late_rows = mix_first(pieces["e"], weights, tokens, mine, got, early, late)
+    total, late_rows = mix_first(
+        pieces["e"], [held(w_out), w_core], halves["e"], tokens, mine, got, early, late
+    )
     mixed_rows, new_centroids = mix_last(
-        pieces["l"], total, late_rows, came, sums["e"], sums["l"], centroids, early, late
+        pieces["l"], halves["l"], total, late_rows, came, sums["e"], sums["l"],
+        centroids, early, late,
     )
     return (mixed_rows, new_centroids)
 

time: 115 us -> 123 us (1.070)
  waiting for transfers between devices: 46.2 us -> 56.3 us
  starting transfers between devices: 32.5 us -> 30.7 us
    ppermute x4, waiting for transfers between devices: 0.01 us -> 8.69 us  [by_heads(): own[k] = lax.ppermute(messages[k], BOTH, steps[k])]
    ppermute x6, waiting for transfers between devices: 12.1 us -> 19.4 us  [by_heads(): lax.ppermute(away[d - 1], TENSOR, swaps[d])]
    ppermute x4, starting transfers between devices: 10.3 us -> 4.42 us  [by_heads(): own[k] = lax.ppermute(messages[k], BOTH, steps[k])]
    ppermute x4 -> x8, waiting for transfers between devices: 18.7 us -> 14.1 us  [the longest x2 14.1 us: by_heads(): there = lax.ppermute(here, SEQ, swap_y)]
    ppermute x1, starting transfers between devices: 0.01 us -> 4.41 us  [by_heads(): w_core = lax.ppermute(w_out, TENSOR, swaps[1])]
    ppermute x4, waiting for transfers between devices: 2.45 us -> 0.01 us  [by_heads(): other[k] = lax.ppermute(own[k], TENSOR, swaps[1])]
    ppermute x4, starting transfers between devices: 1.04 us -> 3.33 us  [by_heads(): other[k] = lax.ppermute(own[k], TENSOR, swaps[1])]
    ppermute x6, starting transfers between devices: 4.44 us -> 2.88 us  [by_heads(): lax.ppermute(away[d - 1], TENSOR, swaps[d])]
  transfers between devices with their start and end apart: 25 -> 29, of which waited for: 11 -> 12; matrix products, arithmetic and copies ran while one was open for 0% -> 0% of each run, Pallas kernels for 25% -> 22%
where the time goes in v3:
time: 123 us; the launch traced here: 122 us
  waiting for transfers between devices  56.3 us (46%)
  Pallas kernels  34.5 us (28%)
  starting transfers between devices  30.7 us (25%)
    ppermute x6, waiting for transfers between devices, by_heads(): lax.ppermute(away[d - 1], TENSOR, swaps[d])  19.4 us
    ppermute x2, waiting for transfers between devices, by_heads(): there = lax.ppermute(here, SEQ, swap_y)  14.1 us
    ppermute x4, waiting for transfers between devices, by_heads(): back[k] = lax.ppermute(result, BOTH, turned(steps[k]))  14 us
    pallas_call x2, Pallas kernels, attend(): pl.pallas_call(functools.partial(attend_body, heads=heads, width=width, o...  10.6 us
    ppermute x4, starting transfers between devices, by_heads(): back[k] = lax.ppermute(result, BOTH, turned(steps[k]))  8.99 us
    ppermute x4, waiting for transfers between devices, by_heads(): own[k] = lax.ppermute(messages[k], BOTH, steps[k])  8.69 us
    pallas_call x1, Pallas kernels, down(): pl.pallas_call(functools.partial(down_body, share=share), grid=(blocks,),...  7.38 us
    pallas_call x1, Pallas kernels, up(): pl.pallas_call(up_body, grid=(blocks,), out_shape=shape((rows, units)), i...  7 us
  transfers between devices with their start and end apart: 29, of which 12 were waited for; matrix products, arithmetic and copies ran while one was open for 0% of the time, Pallas kernels for 22%

profile of v3, /device:TPU:0, one launch (start us, length us, event | category | flops | bytes accessed | tf_op | source)
XLA Modules:
  0.0 122.3 jit_solution(8214396748118152662)
XLA Ops:
  0.6 4.4 %shard_map.104 = (bf16[528,256]{1,0:T(8,128)(2,1)S(1)}, bf16[528,256]{1,0:T(8,128)(2,1)S(1)}, bf16[512,2048]{1,0:T(8,128)(2,1)S(1)}, s32[4,512]{1,0:T(4,128)S(1)...) custom-call(bf16[512,2048]{1,0:T(8,128)(2,1)} %refs_10_.1, ...), custom_call_target="tpu_custom_call" | custom-call | flops 1073741824 | bytes 5242880 | tf_op jit(solution)/shard_map/pallas_call | solution.py:152
  5.1 1.4 %shard_map.105 = (bf16[528,256]{1,0:T(8,128)(2,1)S(1)}, bf16[528,256]{1,0:T(8,128)(2,1)S(1)}) custom-call(bf16[512,2048]{1,0:T(8,128)(2,1)S(1)} %get-tuple-element.33.normed, bf16[2048,256]{1,0:T(8,128)(2,1)S(1)} %get-tuple-element.34.w_qk, bf16[2048,256]{1,0:T(8,128)(2,1)S(1)} %get-tuple-element.35.w_value, s32[4,512]{1,0:T(4,128)S(1)} %get-tuple-element.36.clusters), custom_call_target="tpu_custom_call" | custom-call | flops 1073741824 | bytes 4194304 | tf_op jit(solution)/shard_map/pallas_call | solution.py:187
  7.2 4.4 %collective-permute-start.22 = (bf16[512,2048]{1,0:T(8,128)(2,1)S(1)}, bf16[512,2048]{1,0:T(8,128)(2,1)S(1)}, u32[]{:S(2)}, u32[]{:S(2)}) collective-permute-start(bf16[512,2048]{1,0:T(8,128)(2,1)S(1)} %copy-done.2), channel_id=1, source_target_pairs={{0,1},{1,0},{2,3},{3,2},{4,5},{5,4},{6,7},{7,6},{8,9},{9,8},{10,11... | collective-permute-start | bytes 6291464 | tf_op jit(solution)/shard_map/ppermute | solution.py:546
  12.6 2.6 %collective-permute-start.2 = (bf16[528,256]{1,0:T(8,128)(2,1)S(1)}, bf16[528,256]{1,0:T(8,128)(2,1)S(1)}, u32[]{:S(2)}, u32[]{:S(2)}) collective-permute-start(bf16[528,256]{1,0:T(8,128)(2,1)S(1)} %get-tuple-element.39), channel_id=1, source_target_pairs={{0,16},{1,20},{2,18},{3,22},{4,17},{5,21},{6,19},{7,23},{8,25},{9,... | collective-permute-start | bytes 811016 | tf_op jit(solution)/shard_map/ppermute | solution.py:555
  15.3 2.0 %collective-permute-start.4 = (bf16[528,256]{1,0:T(8,128)(2,1)S(1)}, bf16[528,256]{1,0:T(8,128)(2,1)S(1)}, u32[]{:S(2)}, u32[]{:S(2)}) collective-permute-start(bf16[528,256]{1,0:T(8,128)(2,1)S(1)} %collective-permute-done.refs_0_), channel_id=1, source_target_pairs={{0,1},{1,0},{2,3},{3,2},{4,5},{5,4},{6,7},{7,6},{8,9},{9,8},{10,11... | collective-permute-start | bytes 811016 | tf_op jit(solution)/shard_map/ppermute | solution.py:568
  17.3 7.0 %shard_map.110.hidden = bf16[512,2048]{1,0:T(8,128)(2,1)S(1)} custom-call(bf16[512,2048]{1,0:T(8,128)(2,1)S(1)} %get-tuple-element.33.normed, bf16[2048,2048]{1,0:T(8,128)(2,1)} %w_up.1), custom_call_target="tpu_custom_call" | custom-call | flops 4294967296 | bytes 12582912 | tf_op jit(solution)/shard_map/pallas_call | solution.py:206
  25.1 1.5 %collective-permute-start.23 = (bf16[256,1024]{1,0:T(8,128)(2,1)S(1)}, bf16[256,1024]{1,0:T(8,128)(2,1)S(1)}, u32[]{:S(2)}, u32[]{:S(2)}) collective-permute-start(bf16[256,1024]{1,0:T(8,128)(2,1)S(1)} %get-tuple-element.56), channel_id=1, source_target_pairs={{0,2},{1,3},{2,0},{3,1},{4,6},{5,7},{6,4},{7,5},{8,10},{9,11},{10,... | collective-permute-start | bytes 1572872 | tf_op jit(solution)/shard_map/ppermute | solution.py:558
  26.6 7.9 %collective-permute-done.2.refs_2_ = bf16[528,256]{1,0:T(8,128)(2,1)S(1)} collective-permute-done((bf16[528,256]{1,0:T(8,128)(2,1)S(1)}, bf16[528,256]{1,0:T(8,128)(2,1)S(1)}, u32[]{:S(2)}, u32[]{:S(2)}) %collective-permute-start.2) | collective-permute-done | bytes 270368 | tf_op jit(solution)/shard_map/ppermute | solution.py:555
  35.8 7.4 %shard_map.111 = (f32[128,2048]{1,0:T(8,128)S(1)}, f32[128,2048]{1,0:T(8,128)S(1)}, bf16[2,128,2048]{2,1,0:T(8,128)(2,1)S(1)}) custom-call(bf16[512,2048]{1,0:T(8,128)(2,1)S(1)} %shard_map.110.hidden, bf16[2048,2048]{1,0:T(8,128)(2,1)} %w_down.1), custom_call_target="tpu_custom_call" | custom-call | flops 4294967296 | bytes 14680064 | tf_op jit(solution)/shard_map/pallas_call | solution.py:238
  43.2 1.6 %collective-permute-start.13 = (bf16[256,1024]{1,0:T(8,128)(2,1)S(1)}, bf16[256,1024]{1,0:T(8,128)(2,1)S(1)}, u32[]{:S(2)}, u32[]{:S(2)}) collective-permute-start(bf16[256,1024]{1,0:T(8,128)(2,1)S(1)} %get-tuple-element.49), channel_id=1, source_target_pairs={{0,2},{1,3},{2,0},{3,1},{4,6},{5,7},{6,4},{7,5},{8,10},{9,11},{10,... | collective-permute-start | bytes 1572872 | tf_op jit(solution)/shard_map/ppermute | solution.py:558
  44.8 5.4 %shard_map.106 = (bf16[544,128]{1,0:T(8,128)(2,1)S(1)}, bf16[544,128]{1,0:T(8,128)(2,1)S(1)}, bf16[8,512,256]{2,1,0:T(8,128)(2,1)S(1)}, f32[8,8,512]{2,1,0:T(8,128)S(1)}) custom-call(bf16[528,256]{1,0:T(8,128)(2,1)S(1)} %collective-permute-done.refs_0_, bf16[528,256]{1,0:T(8,128)(2,1)S(1)} %collective-permute-done.1.refs_1_, ...), custom_call_target="tpu_custom_call" | custom-call | flops 2415919104 | bytes 2097152 | tf_op jit(solution)/shard_map/pallas_call | solution.py:370
  50.2 5.2 %shard_map.107 = (bf16[544,128]{1,0:T(8,128)(2,1)S(1)}, bf16[544,128]{1,0:T(8,128)(2,1)S(1)}) custom-call(bf16[8,512,256]{2,1,0:T(8,128)(2,1)S(1)} %get-tuple-element.41.refs_0_, f32[8,8,512]{2,1,0:T(8,128)S(1)} %get-tuple-element.42.refs_1_), custom_call_target="tpu_custom_call" | custom-call | flops 2415919104 | bytes 2097152 | tf_op jit(solution)/shard_map/pallas_call | solution.py:370
  55.4 7.5 %collective-permute-start.8 = (bf16[544,128]{1,0:T(8,128)(2,1)S(1)}, bf16[544,128]{1,0:T(8,128)(2,1)S(1)}, u32[]{:S(2)}, u32[]{:S(2)}) collective-permute-start(bf16[544,128]{1,0:T(8,128)(2,1)S(1)} %get-tuple-element.43), channel_id=1, source_target_pairs={{16,0},{20,1},{18,2},{22,3},{17,4},{21,5},{19,6},{23,7},{25,8},{29... | collective-permute-start | bytes 417800 | tf_op jit(solution)/shard_map/ppermute | solution.py:579
  62.9 7.4 %collective-permute-done.8.refs_0_ = bf16[544,128]{1,0:T(8,128)(2,1)S(1)} collective-permute-done((bf16[544,128]{1,0:T(8,128)(2,1)S(1)}, bf16[544,128]{1,0:T(8,128)(2,1)S(1)}, u32[]{:S(2)}, u32[]{:S(2)}) %collective-permute-start.8) | collective-permute-done | bytes 139296 | tf_op jit(solution)/shard_map/ppermute | solution.py:579
  72.7 5.8 %collective-permute-done.17.refs_0_ = bf16[544,128]{1,0:T(8,128)(2,1)S(1)} collective-permute-done((bf16[544,128]{1,0:T(8,128)(2,1)S(1)}, bf16[544,128]{1,0:T(8,128)(2,1)S(1)}, u32[]{:S(2)}, u32[]{:S(2)}) %collective-permute-start.17) | collective-permute-done | bytes 139296 | tf_op jit(solution)/shard_map/ppermute | solution.py:576
  78.5 2.3 %collective-permute-start.24 = (bf16[256,1024]{1,0:T(8,128)(2,1)S(1)}, bf16[256,1024]{1,0:T(8,128)(2,1)S(1)}, u32[]{:S(2)}, u32[]{:S(2)}) collective-permute-start(bf16[256,1024]{1,0:T(8,128)(2,1)S(1)} %collective-permute-done.23.refs_6_), channel_id=1, source_target_pairs={{0,4},{4,0},{8,12},{12,8},{16,20},{20,16},{24,28},{28,24},{1,5},{5... | collective-permute-start | bytes 1572872 | tf_op jit(solution)/shard_map/ppermute | solution.py:559
  82.1 3.3 %collective-permute-done.20.refs_2_ = bf16[2,128,128]{2,1,0:T(8,128)(2,1)S(1)} collective-permute-done((bf16[2,128,128]{2,1,0:T(8,128)(2,1)S(1)}, bf16[2,128,128]{2,1,0:T(8,128)(2,1)S(1)}, u32[]{:S(2)}, u32[]{:S(2)}) %collective-permute-start.20) | collective-permute-done | bytes 65568 | tf_op jit(solution)/shard_map/ppermute | solution.py:584
  85.4 8.2 %collective-permute-done.24.refs_7_ = bf16[256,1024]{1,0:T(8,128)(2,1)S(1)} collective-permute-done((bf16[256,1024]{1,0:T(8,128)(2,1)S(1)}, bf16[256,1024]{1,0:T(8,128)(2,1)S(1)}, u32[]{:S(2)}, u32[]{:S(2)}) %collective-permute-start.24) | collective-permute-done | bytes 524320 | tf_op jit(solution)/shard_map/ppermute | solution.py:559
  94.3 3.0 %collective-permute-done.21.refs_3_ = bf16[2,128,128]{2,1,0:T(8,128)(2,1)S(1)} collective-permute-done((bf16[2,128,128]{2,1,0:T(8,128)(2,1)S(1)}, bf16[2,128,128]{2,1,0:T(8,128)(2,1)S(1)}, u32[]{:S(2)}, u32[]{:S(2)}) %collective-permute-start.21) | collective-permute-done | bytes 65568 | tf_op jit(solution)/shard_map/ppermute | solution.py:584
  98.1 6.0 %collective-permute-done.14.refs_5_ = bf16[256,1024]{1,0:T(8,128)(2,1)S(1)} collective-permute-done((bf16[256,1024]{1,0:T(8,128)(2,1)S(1)}, bf16[256,1024]{1,0:T(8,128)(2,1)S(1)}, u32[]{:S(2)}, u32[]{:S(2)}) %collective-permute-start.14) | collective-permute-done | bytes 524320 | tf_op jit(solution)/shard_map/ppermute | solution.py:559
  104.6 1.5 %collective-permute-start.11 = (bf16[2,128,128]{2,1,0:T(8,128)(2,1)S(1)}, bf16[2,128,128]{2,1,0:T(8,128)(2,1)S(1)}, u32[]{:S(2)}, u32[]{:S(2)}) collective-permute-start(bf16[2,128,128]{2,1,0:T(8,128)(2,1)S(1)} %get-tuple-element.47), channel_id=1, source_target_pairs={{0,2},{1,3},{2,0},{3,1},{4,6},{5,7},{6,4},{7,5},{8,10},{9,11},{10,... | collective-permute-start | bytes 196616 | tf_op jit(solution)/shard_map/ppermute | solution.py:584
  106.2 2.0 %shard_map.112 = (f32[128,2048]{1,0:T(8,128)S(1)}, bf16[512,2048]{1,0:T(8,128)(2,1)S(1)}) custom-call(bf16[2,128,128]{2,1,0:T(8,128)(2,1)S(1)} %get-tuple-element.52.refs_0_, bf16[2,128,128]{2,1,0:T(8,128)(2,1)S(1)} %collective-permute-done.19.refs_1_, bf16[2,128,128]{2,1,0:T(8,128)(2,1)S(1)} %collective-permute-done.20.refs_2_, ...), custom_call_target="tpu_custom_call" | custom-call | flops 536870912 | bytes 10485760 | tf_op jit(solution)/shard_map/pallas_call | solution.py:481
  108.2 12.0 %collective-permute-done.11.refs_2_ = bf16[2,128,128]{2,1,0:T(8,128)(2,1)S(1)} collective-permute-done((bf16[2,128,128]{2,1,0:T(8,128)(2,1)S(1)}, bf16[2,128,128]{2,1,0:T(8,128)(2,1)S(1)}, u32[]{:S(2)}, u32[]{:S(2)}) %collective-permute-start.11) | collective-permute-done | bytes 65568 | tf_op jit(solution)/shard_map/ppermute | solution.py:584
  120.8 1.5 %shard_map.114 = (bf16[128,2048]{1,0:T(8,128)(2,1)}, f32[4,32,128]{2,1,0:T(8,128)}) custom-call(bf16[2,128,128]{2,1,0:T(8,128)(2,1)S(1)} %get-tuple-element.45.refs_0_, bf16[2,128,128]{2,1,0:T(8,128)(2,1)S(1)} %collective-permute-done.10.refs_1_, bf16[2,128,128]{2,1,0:T(8,128)(2,1)S(1)} %collective-permute-done.11.refs_2_, ...), custom_call_target="tpu_custom_call" | custom-call | flops 536870912 | bytes 6291456 | tf_op jit(solution)/shard_map/pallas_call | solution.py:524
  (51 shorter events, 10.4 us)
Async XLA Ops:
  6.5 8.8 %collective-permute-start = (bf16[528,256]{1,0:T(8,128)(2,1)S(1)}, bf16[528,256]{1,0:T(8,128)(2,1)S(1)}, u32[]{:S(2)}, u32[]{:S(2)}) collective-permute-start(bf16[528,256]{1,0:T(8,128)(2,1)S(1)} %get-tuple-element.37), channel_id=1, source_target_pairs={{0,0},{1,4},{2,2},{3,6},{4,1},{5,5},{6,3},{7,7},{8,9},{9,13},{10,1... | collective-permute-start | bytes 811016 | tf_op jit(solution)/shard_map/ppermute | solution.py:563
  7.2 98.9 %collective-permute-start.22 = (bf16[512,2048]{1,0:T(8,128)(2,1)S(1)}, bf16[512,2048]{1,0:T(8,128)(2,1)S(1)}, u32[]{:S(2)}, u32[]{:S(2)}) collective-permute-start(bf16[512,2048]{1,0:T(8,128)(2,1)S(1)} %copy-done.2), channel_id=1, source_target_pairs={{0,1},{1,0},{2,3},{3,2},{4,5},{5,4},{6,7},{7,6},{8,9},{9,8},{10,11... | collective-permute-start | bytes 6291464 | tf_op jit(solution)/shard_map/ppermute | solution.py:546
  11.6 13.5 %collective-permute-start.1 = (bf16[528,256]{1,0:T(8,128)(2,1)S(1)}, bf16[528,256]{1,0:T(8,128)(2,1)S(1)}, u32[]{:S(2)}, u32[]{:S(2)}) collective-permute-start(bf16[528,256]{1,0:T(8,128)(2,1)S(1)} %get-tuple-element.38), channel_id=1, source_target_pairs={{0,8},{1,12},{2,10},{3,14},{4,9},{5,13},{6,11},{7,15},{8,1},{9,5},... | collective-permute-start | bytes 811016 | tf_op jit(solution)/shard_map/ppermute | solution.py:563
  12.6 21.9 %collective-permute-start.2 = (bf16[528,256]{1,0:T(8,128)(2,1)S(1)}, bf16[528,256]{1,0:T(8,128)(2,1)S(1)}, u32[]{:S(2)}, u32[]{:S(2)}) collective-permute-start(bf16[528,256]{1,0:T(8,128)(2,1)S(1)} %get-tuple-element.39), channel_id=1, source_target_pairs={{0,16},{1,20},{2,18},{3,22},{4,17},{5,21},{6,19},{7,23},{8,25},{9,... | collective-permute-start | bytes 811016 | tf_op jit(solution)/shard_map/ppermute | solution.py:555
  15.2 20.1 %collective-permute-start.3 = (bf16[528,256]{1,0:T(8,128)(2,1)S(1)}, bf16[528,256]{1,0:T(8,128)(2,1)S(1)}, u32[]{:S(2)}, u32[]{:S(2)}) collective-permute-start(bf16[528,256]{1,0:T(8,128)(2,1)S(1)} %get-tuple-element.40), channel_id=1, source_target_pairs={{0,24},{1,28},{2,26},{3,30},{4,25},{5,29},{6,27},{7,31},{8,17},{9,... | collective-permute-start | bytes 811016 | tf_op jit(solution)/shard_map/ppermute | solution.py:555
  15.3 20.0 %collective-permute-start.4 = (bf16[528,256]{1,0:T(8,128)(2,1)S(1)}, bf16[528,256]{1,0:T(8,128)(2,1)S(1)}, u32[]{:S(2)}, u32[]{:S(2)}) collective-permute-start(bf16[528,256]{1,0:T(8,128)(2,1)S(1)} %collective-permute-done.refs_0_), channel_id=1, source_target_pairs={{0,1},{1,0},{2,3},{3,2},{4,5},{5,4},{6,7},{7,6},{8,9},{9,8},{10,11... | collective-permute-start | bytes 811016 | tf_op jit(solution)/shard_map/ppermute | solution.py:568
  25.1 37.8 %collective-permute-start.23 = (bf16[256,1024]{1,0:T(8,128)(2,1)S(1)}, bf16[256,1024]{1,0:T(8,128)(2,1)S(1)}, u32[]{:S(2)}, u32[]{:S(2)}) collective-permute-start(bf16[256,1024]{1,0:T(8,128)(2,1)S(1)} %get-tuple-element.56), channel_id=1, source_target_pairs={{0,2},{1,3},{2,0},{3,1},{4,6},{5,7},{6,4},{7,5},{8,10},{9,11},{10,... | collective-permute-start | bytes 1572872 | tf_op jit(solution)/shard_map/ppermute | solution.py:558
  34.5 8.7 %collective-permute-start.5 = (bf16[528,256]{1,0:T(8,128)(2,1)S(1)}, bf16[528,256]{1,0:T(8,128)(2,1)S(1)}, u32[]{:S(2)}, u32[]{:S(2)}) collective-permute-start(bf16[528,256]{1,0:T(8,128)(2,1)S(1)} %collective-permute-done.1.refs_1_), channel_id=1, source_target_pairs={{0,1},{1,0},{2,3},{3,2},{4,5},{5,4},{6,7},{7,6},{8,9},{9,8},{10,11... | collective-permute-start | bytes 811016 | tf_op jit(solution)/shard_map/ppermute | solution.py:568
  35.3 9.5 %collective-permute-start.6 = (bf16[528,256]{1,0:T(8,128)(2,1)S(1)}, bf16[528,256]{1,0:T(8,128)(2,1)S(1)}, u32[]{:S(2)}, u32[]{:S(2)}) collective-permute-start(bf16[528,256]{1,0:T(8,128)(2,1)S(1)} %collective-permute-done.2.refs_2_), channel_id=1, source_target_pairs={{0,1},{1,0},{2,3},{3,2},{4,5},{5,4},{6,7},{7,6},{8,9},{9,8},{10,11... | collective-permute-start | bytes 811016 | tf_op jit(solution)/shard_map/ppermute | solution.py:568
  35.3 9.5 %collective-permute-start.7 = (bf16[528,256]{1,0:T(8,128)(2,1)S(1)}, bf16[528,256]{1,0:T(8,128)(2,1)S(1)}, u32[]{:S(2)}, u32[]{:S(2)}) collective-permute-start(bf16[528,256]{1,0:T(8,128)(2,1)S(1)} %collective-permute-done.3.refs_3_), channel_id=1, source_target_pairs={{0,1},{1,0},{2,3},{3,2},{4,5},{5,4},{6,7},{7,6},{8,9},{9,8},{10,11... | collective-permute-start | bytes 811016 | tf_op jit(solution)/shard_map/ppermute | solution.py:568
  43.2 37.6 %collective-permute-start.13 = (bf16[256,1024]{1,0:T(8,128)(2,1)S(1)}, bf16[256,1024]{1,0:T(8,128)(2,1)S(1)}, u32[]{:S(2)}, u32[]{:S(2)}) collective-permute-start(bf16[256,1024]{1,0:T(8,128)(2,1)S(1)} %get-tuple-element.49), channel_id=1, source_target_pairs={{0,2},{1,3},{2,0},{3,1},{4,6},{5,7},{6,4},{7,5},{8,10},{9,11},{10,... | collective-permute-start | bytes 1572872 | tf_op jit(solution)/shard_map/ppermute | solution.py:558
  44.8 48.8 %collective-permute-start.27 = (bf16[2,128,2048]{2,1,0:T(8,128)(2,1)S(1)}, bf16[2,128,2048]{2,1,0:T(8,128)(2,1)S(1)}, u32[]{:S(2)}, u32[]{:S(2)}) collective-permute-start(bf16[2,128,2048]{2,1,0:T(8,128)(2,1)S(1)} %get-tuple-element.58), channel_id=1, source_target_pairs={{0,1},{1,0},{2,3},{3,2},{4,5},{5,4},{6,7},{7,6},{8,9},{9,8},{10,11... | collective-permute-start | bytes 3145736 | tf_op jit(solution)/shard_map/ppermute | solution.py:566
  55.4 14.9 %collective-permute-start.8 = (bf16[544,128]{1,0:T(8,128)(2,1)S(1)}, bf16[544,128]{1,0:T(8,128)(2,1)S(1)}, u32[]{:S(2)}, u32[]{:S(2)}) collective-permute-start(bf16[544,128]{1,0:T(8,128)(2,1)S(1)} %get-tuple-element.43), channel_id=1, source_target_pairs={{16,0},{20,1},{18,2},{22,3},{17,4},{21,5},{19,6},{23,7},{25,8},{29... | collective-permute-start | bytes 417800 | tf_op jit(solution)/shard_map/ppermute | solution.py:579
  62.9 8.9 %collective-permute-start.9 = (bf16[544,128]{1,0:T(8,128)(2,1)S(1)}, bf16[544,128]{1,0:T(8,128)(2,1)S(1)}, u32[]{:S(2)}, u32[]{:S(2)}) collective-permute-start(bf16[544,128]{1,0:T(8,128)(2,1)S(1)} %get-tuple-element.44), channel_id=1, source_target_pairs={{8,0},{12,1},{10,2},{14,3},{9,4},{13,5},{11,6},{15,7},{1,8},{5,9},... | collective-permute-start | bytes 417800 | tf_op jit(solution)/shard_map/ppermute | solution.py:579
  70.3 8.2 %collective-permute-start.17 = (bf16[544,128]{1,0:T(8,128)(2,1)S(1)}, bf16[544,128]{1,0:T(8,128)(2,1)S(1)}, u32[]{:S(2)}, u32[]{:S(2)}) collective-permute-start(bf16[544,128]{1,0:T(8,128)(2,1)S(1)} %get-tuple-element.50), channel_id=1, source_target_pairs={{24,0},{28,1},{26,2},{30,3},{25,4},{29,5},{27,6},{31,7},{17,8},{21... | collective-permute-start | bytes 417800 | tf_op jit(solution)/shard_map/ppermute | solution.py:576
  78.5 15.1 %collective-permute-start.24 = (bf16[256,1024]{1,0:T(8,128)(2,1)S(1)}, bf16[256,1024]{1,0:T(8,128)(2,1)S(1)}, u32[]{:S(2)}, u32[]{:S(2)}) collective-permute-start(bf16[256,1024]{1,0:T(8,128)(2,1)S(1)} %collective-permute-done.23.refs_6_), channel_id=1, source_target_pairs={{0,4},{4,0},{8,12},{12,8},{16,20},{20,16},{24,28},{28,24},{1,5},{5... | collective-permute-start | bytes 1572872 | tf_op jit(solution)/shard_map/ppermute | solution.py:559
  82.1 21.9 %collective-permute-start.14 = (bf16[256,1024]{1,0:T(8,128)(2,1)S(1)}, bf16[256,1024]{1,0:T(8,128)(2,1)S(1)}, u32[]{:S(2)}, u32[]{:S(2)}) collective-permute-start(bf16[256,1024]{1,0:T(8,128)(2,1)S(1)} %collective-permute-done.13.refs_4_), channel_id=1, source_target_pairs={{0,4},{4,0},{8,12},{12,8},{16,20},{20,16},{24,28},{28,24},{1,5},{5... | collective-permute-start | bytes 1572872 | tf_op jit(solution)/shard_map/ppermute | solution.py:559
  85.4 18.7 %collective-permute-start.25 = (bf16[256,1024]{1,0:T(8,128)(2,1)S(1)}, bf16[256,1024]{1,0:T(8,128)(2,1)S(1)}, u32[]{:S(2)}, u32[]{:S(2)}) collective-permute-start(bf16[256,1024]{1,0:T(8,128)(2,1)S(1)} %collective-permute-done.23.refs_6_), channel_id=1, source_target_pairs={{0,1},{1,0},{2,3},{3,2},{4,5},{5,4},{6,7},{7,6},{8,9},{9,8},{10,11... | collective-permute-start | bytes 1572872 | tf_op jit(solution)/shard_map/ppermute | solution.py:560
  93.6 11.0 %collective-permute-start.26 = (bf16[256,1024]{1,0:T(8,128)(2,1)S(1)}, bf16[256,1024]{1,0:T(8,128)(2,1)S(1)}, u32[]{:S(2)}, u32[]{:S(2)}) collective-permute-start(bf16[256,1024]{1,0:T(8,128)(2,1)S(1)} %collective-permute-done.24.refs_7_), channel_id=1, source_target_pairs={{0,1},{1,0},{2,3},{3,2},{4,5},{5,4},{6,7},{7,6},{8,9},{9,8},{10,11... | collective-permute-start | bytes 1572872 | tf_op jit(solution)/shard_map/ppermute | solution.py:560
  97.3 23.5 %collective-permute-start.15 = (bf16[256,1024]{1,0:T(8,128)(2,1)S(1)}, bf16[256,1024]{1,0:T(8,128)(2,1)S(1)}, u32[]{:S(2)}, u32[]{:S(2)}) collective-permute-start(bf16[256,1024]{1,0:T(8,128)(2,1)S(1)} %collective-permute-done.13.refs_4_), channel_id=1, source_target_pairs={{0,1},{1,0},{2,3},{3,2},{4,5},{5,4},{6,7},{7,6},{8,9},{9,8},{10,11... | collective-permute-start | bytes 1572872 | tf_op jit(solution)/shard_map/ppermute | solution.py:560
  104.0 16.7 %collective-permute-start.16 = (bf16[256,1024]{1,0:T(8,128)(2,1)S(1)}, bf16[256,1024]{1,0:T(8,128)(2,1)S(1)}, u32[]{:S(2)}, u32[]{:S(2)}) collective-permute-start(bf16[256,1024]{1,0:T(8,128)(2,1)S(1)} %collective-permute-done.14.refs_5_), channel_id=1, source_target_pairs={{0,1},{1,0},{2,3},{3,2},{4,5},{5,4},{6,7},{7,6},{8,9},{9,8},{10,11... | collective-permute-start | bytes 1572872 | tf_op jit(solution)/shard_map/ppermute | solution.py:560
  104.1 16.7 %collective-permute-start.28 = (bf16[128,2048]{1,0:T(8,128)(2,1)S(1)}, bf16[128,2048]{1,0:T(8,128)(2,1)S(1)}, u32[]{:S(2)}, u32[]{:S(2)}) collective-permute-start(bf16[128,2048]{1,0:T(8,128)(2,1)S(1)} %shard_map.113), channel_id=1, source_target_pairs={{0,2},{1,3},{2,0},{3,1},{4,6},{5,7},{6,4},{7,5},{8,10},{9,11},{10,... | collective-permute-start | bytes 1572872 | tf_op jit(solution)/shard_map/ppermute | solution.py:570
  104.6 15.7 %collective-permute-start.11 = (bf16[2,128,128]{2,1,0:T(8,128)(2,1)S(1)}, bf16[2,128,128]{2,1,0:T(8,128)(2,1)S(1)}, u32[]{:S(2)}, u32[]{:S(2)}) collective-permute-start(bf16[2,128,128]{2,1,0:T(8,128)(2,1)S(1)} %get-tuple-element.47), channel_id=1, source_target_pairs={{0,2},{1,3},{2,0},{3,1},{4,6},{5,7},{6,4},{7,5},{8,10},{9,11},{10,... | collective-permute-start | bytes 196616 | tf_op jit(solution)/shard_map/ppermute | solution.py:584
  106.1 14.6 %collective-permute-start.12 = (bf16[2,128,128]{2,1,0:T(8,128)(2,1)S(1)}, bf16[2,128,128]{2,1,0:T(8,128)(2,1)S(1)}, u32[]{:S(2)}, u32[]{:S(2)}) collective-permute-start(bf16[2,128,128]{2,1,0:T(8,128)(2,1)S(1)} %get-tuple-element.48), channel_id=1, source_target_pairs={{0,3},{1,2},{2,1},{3,0},{4,7},{5,6},{6,5},{7,4},{8,11},{9,10},{10,... | collective-permute-start | bytes 196616 | tf_op jit(solution)/shard_map/ppermute | solution.py:584
  (8 other events, 86.1 us)

commit v4 on v3

--- a/solution.py
+++ b/solution.py
@@ -217,12 +217,13 @@
     )(normed, w_up)
 
 
-def down_body(hidden, w_down, mine, far, away, held, *, share):
+def down_body(hidden, w_down, *rest, share):
+    mine, far, away, held_rows = rest[-4:]
     at = lax.axis_index(TENSOR)
-    held[...] = jnp.dot(hidden[...], w_down[...], preferred_element_type=jnp.float32)
+    held_rows[...] = jnp.dot(hidden[...], w_down[...], preferred_element_type=jnp.float32)
 
     def quarter(turn):
-        return held[pl.ds(pl.multiple_of((at ^ turn) * share, share), share), :]
+        return held_rows[pl.ds(pl.multiple_of((at ^ turn) * share, share), share), :]
 
     mine[...] = quarter(0)
     far[...] = quarter(2)
@@ -230,11 +231,11 @@
     away[1] = quarter(3).astype(jnp.bfloat16)
 
 
-def down(hidden, w_down, share, blocks=2):
+def down(hidden, w_down, share, part, earlier=(), parts=2, blocks=2):
     rows, units = hidden.shape
     depth = w_down.shape[1]
-    block = depth // blocks
-    one = pl.BlockSpec((share, block), lambda i: (0, i))
+    block = depth // (parts * blocks)
+    one = pl.BlockSpec((share, block), lambda i: (0, part * blocks + i))
     return pl.pallas_call(
         functools.partial(down_body, share=share),
         grid=(blocks,),
@@ -245,13 +246,21 @@
         ),
         in_specs=[
             pl.BlockSpec((rows, units), lambda i: (0, 0)),
-            pl.BlockSpec((units, block), lambda i: (0, i)),
-        ],
-        out_specs=(one, one, pl.BlockSpec((2, share, block), lambda i: (0, 0, i))),
+            pl.BlockSpec((units, block), lambda i: (0, part * blocks + i)),
+        ]
+        + [any_spec()] * len(earlier),
+        out_specs=(
+            one,
+            one,
+            pl.BlockSpec((2, share, block), lambda i: (0, 0, part * blocks + i)),
+        ),
         scratch_shapes=[pltpu.VMEM((rows, block), jnp.float32)],
-        compiler_params=params(26),
-        cost_estimate=cost(2 * rows * depth * units, 2 * depth * units + 6 * rows * depth),
-    )(hidden, w_down)
+        input_output_aliases={2 + i: i for i in range(len(earlier))},
+        compiler_params=params(20),
+        cost_estimate=cost(
+            2 * rows * depth * units // parts, (2 * depth * units + 6 * rows * depth) // parts
+        ),
+    )(hidden, w_down, *earlier)
 
 
 def pick_body(far, got, sent):
@@ -562,7 +571,8 @@
     for k in (1, 0):
         own[k] = lax.ppermute(messages[k], BOTH, steps[k])
     hidden = up(normed, held(w_up))
-    mine, far, sent = down(hidden, held(w_down), share)
+    half_down = down(hidden, held(w_down), share, 0)
+    mine, far, sent = down(hidden, held(w_down), share, 1, half_down)
     got = lax.ppermute(sent, TENSOR, swaps[1])
     for k in range(heads):
         other[k] = lax.ppermute(own[k], TENSOR, swaps[1])

time: 123 us -> 108 us (0.88)
  the two profiles are of different devices: /device:TPU:0 before, /device:TPU:9 now
where the time goes in v4:
time: 108 us; the launch traced here: 107 us
  starting transfers between devices  37.2 us (34%)
  Pallas kernels  35.8 us (33%)
  waiting for transfers between devices  33.5 us (31%)
    ppermute x4, waiting for transfers between devices, by_heads(): own[k] = lax.ppermute(messages[k], BOTH, steps[k])  12.1 us
    pallas_call x2, Pallas kernels, attend(): pl.pallas_call(functools.partial(attend_body, heads=heads, width=width, o...  10.6 us
    ppermute x2, waiting for transfers between devices, by_heads(): there = lax.ppermute(here, SEQ, swap_y)  9.83 us
    ppermute x4, starting transfers between devices, by_heads(): lax.ppermute(w, TENSOR, swaps[1])  8.86 us
    pallas_call x2, Pallas kernels, down(): pl.pallas_call(functools.partial(down_body, share=share), grid=(blocks,),...  8.73 us
    ppermute x4, starting transfers between devices, by_heads(): back[k] = lax.ppermute(result, BOTH, turned(steps[k]))  7.27 us
    ppermute x6, waiting for transfers between devices, by_heads(): lax.ppermute(away[d - 1], TENSOR, swaps[d])  7.1 us
    pallas_call x1, Pallas kernels, up(): pl.pallas_call(up_body, grid=(blocks,), out_shape=shape((rows, units)), i...  7 us
  transfers between devices with their start and end apart: 29, of which 11 were waited for; matrix products, arithmetic and copies ran while one was open for 0% of the time, Pallas kernels for 27%

profile of v4, /device:TPU:9, one launch (start us, length us, event | category | flops | bytes accessed | tf_op | source)
XLA Modules:
  0.0 107.3 jit_solution(1830902413431447000)
XLA Ops:
  0.6 4.4 %shard_map.104 = (bf16[528,256]{1,0:T(8,128)(2,1)S(1)}, bf16[528,256]{1,0:T(8,128)(2,1)S(1)}, bf16[512,2048]{1,0:T(8,128)(2,1)S(1)}, s32[4,512]{1,0:T(4,128)S(1)...) custom-call(bf16[512,2048]{1,0:T(8,128)(2,1)} %refs_10_.1, ...), custom_call_target="tpu_custom_call" | custom-call | flops 1073741824 | bytes 5242880 | tf_op jit(solution)/shard_map/pallas_call | solution.py:152
  6.5 3.2 %collective-permute-start = (bf16[528,256]{1,0:T(8,128)(2,1)S(1)}, bf16[528,256]{1,0:T(8,128)(2,1)S(1)}, u32[]{:S(2)}, u32[]{:S(2)}) collective-permute-start(bf16[528,256]{1,0:T(8,128)(2,1)S(1)} %get-tuple-element.40), channel_id=1, source_target_pairs={{0,0},{1,4},{2,2},{3,6},{4,1},{5,5},{6,3},{7,7},{8,9},{9,13},{10,1... | collective-permute-start | bytes 811016 | tf_op jit(solution)/shard_map/ppermute | solution.py:572
  10.3 2.6 %collective-permute-start.2 = (bf16[528,256]{1,0:T(8,128)(2,1)S(1)}, bf16[528,256]{1,0:T(8,128)(2,1)S(1)}, u32[]{:S(2)}, u32[]{:S(2)}) collective-permute-start(bf16[528,256]{1,0:T(8,128)(2,1)S(1)} %get-tuple-element.42), channel_id=1, source_target_pairs={{0,16},{1,20},{2,18},{3,22},{4,17},{5,21},{6,19},{7,23},{8,25},{9,... | collective-permute-start | bytes 811016 | tf_op jit(solution)/shard_map/ppermute | solution.py:564
  13.8 2.8 %collective-permute-start.4 = (bf16[528,256]{1,0:T(8,128)(2,1)S(1)}, bf16[528,256]{1,0:T(8,128)(2,1)S(1)}, u32[]{:S(2)}, u32[]{:S(2)}) collective-permute-start(bf16[528,256]{1,0:T(8,128)(2,1)S(1)} %collective-permute-done.refs_0_), channel_id=1, source_target_pairs={{0,1},{1,0},{2,3},{3,2},{4,5},{5,4},{6,7},{7,6},{8,9},{9,8},{10,11... | collective-permute-start | bytes 811016 | tf_op jit(solution)/shard_map/ppermute | solution.py:578
  16.6 7.0 %shard_map.110.hidden = bf16[512,2048]{1,0:T(8,128)(2,1)S(1)} custom-call(bf16[512,2048]{1,0:T(8,128)(2,1)S(1)} %get-tuple-element.36.normed, bf16[2048,2048]{1,0:T(8,128)(2,1)} %w_up.1), custom_call_target="tpu_custom_call" | custom-call | flops 4294967296 | bytes 12582912 | tf_op jit(solution)/shard_map/pallas_call | solution.py:206
  24.9 5.7 %collective-permute-done.2.refs_2_ = bf16[528,256]{1,0:T(8,128)(2,1)S(1)} collective-permute-done((bf16[528,256]{1,0:T(8,128)(2,1)S(1)}, bf16[528,256]{1,0:T(8,128)(2,1)S(1)}, u32[]{:S(2)}, u32[]{:S(2)}) %collective-permute-start.2) | collective-permute-done | bytes 270368 | tf_op jit(solution)/shard_map/ppermute | solution.py:564
  31.5 5.9 %collective-permute-done.3.refs_3_ = bf16[528,256]{1,0:T(8,128)(2,1)S(1)} collective-permute-done((bf16[528,256]{1,0:T(8,128)(2,1)S(1)}, bf16[528,256]{1,0:T(8,128)(2,1)S(1)}, u32[]{:S(2)}, u32[]{:S(2)}) %collective-permute-start.3) | collective-permute-done | bytes 270368 | tf_op jit(solution)/shard_map/ppermute | solution.py:564
  38.5 4.4 %shard_map.111 = (f32[128,2048]{1,0:T(8,128)S(1)}, f32[128,2048]{1,0:T(8,128)S(1)}, bf16[2,128,2048]{2,1,0:T(8,128)(2,1)S(1)}) custom-call(bf16[512,2048]{1,0:T(8,128)(2,1)S(1)} %shard_map.110.hidden, bf16[2048,2048]{1,0:T(8,128)(2,1)} %w_down.3), custom_call_target="tpu_custom_call" | custom-call | flops 2147483648 | bytes 7340032 | tf_op jit(solution)/shard_map/pallas_call | solution.py:239
  42.8 4.4 %shard_map.112 = (f32[128,2048]{1,0:T(8,128)S(1)}, f32[128,2048]{1,0:T(8,128)S(1)}, bf16[2,128,2048]{2,1,0:T(8,128)(2,1)S(1)}) custom-call(bf16[512,2048]{1,0:T(8,128)(2,1)S(1)} %shard_map.110.hidden, bf16[2048,2048]{1,0:T(8,128)(2,1)} %w_down.3, ...), custom_call_target="tpu_custom_call", output_to_operand_aliasing={{0}: (2, {}), {1}: (3, {}), {2}: (4, {})} | custom-call | flops 2147483648 | bytes 7340032 | tf_op jit(solution)/shard_map/pallas_call | solution.py:239
  49.0 5.4 %shard_map.106 = (bf16[544,128]{1,0:T(8,128)(2,1)S(1)}, bf16[544,128]{1,0:T(8,128)(2,1)S(1)}, bf16[8,512,256]{2,1,0:T(8,128)(2,1)S(1)}, f32[8,8,512]{2,1,0:T(8,128)S(1)}) custom-call(bf16[528,256]{1,0:T(8,128)(2,1)S(1)} %collective-permute-done.refs_0_, bf16[528,256]{1,0:T(8,128)(2,1)S(1)} %collective-permute-done.1.refs_1_, ...), custom_call_target="tpu_custom_call" | custom-call | flops 2415919104 | bytes 2097152 | tf_op jit(solution)/shard_map/pallas_call | solution.py:379
  54.4 2.2 %collective-permute-start.17 = (bf16[544,128]{1,0:T(8,128)(2,1)S(1)}, bf16[544,128]{1,0:T(8,128)(2,1)S(1)}, u32[]{:S(2)}, u32[]{:S(2)}) collective-permute-start(bf16[544,128]{1,0:T(8,128)(2,1)S(1)} %get-tuple-element.53), channel_id=1, source_target_pairs={{24,0},{28,1},{26,2},{30,3},{25,4},{29,5},{27,6},{31,7},{17,8},{21... | collective-permute-start | bytes 417800 | tf_op jit(solution)/shard_map/ppermute | solution.py:586
  56.6 2.5 %collective-permute-start.18 = (bf16[544,128]{1,0:T(8,128)(2,1)S(1)}, bf16[544,128]{1,0:T(8,128)(2,1)S(1)}, u32[]{:S(2)}, u32[]{:S(2)}) collective-permute-start(bf16[544,128]{1,0:T(8,128)(2,1)S(1)} %get-tuple-element.54), channel_id=1, source_target_pairs={{0,0},{4,1},{2,2},{6,3},{1,4},{5,5},{3,6},{7,7},{9,8},{13,9},{11,1... | collective-permute-start | bytes 417800 | tf_op jit(solution)/shard_map/ppermute | solution.py:586
  59.2 5.2 %shard_map.107 = (bf16[544,128]{1,0:T(8,128)(2,1)S(1)}, bf16[544,128]{1,0:T(8,128)(2,1)S(1)}) custom-call(bf16[8,512,256]{2,1,0:T(8,128)(2,1)S(1)} %get-tuple-element.44.refs_0_, f32[8,8,512]{2,1,0:T(8,128)S(1)} %get-tuple-element.45.refs_1_), custom_call_target="tpu_custom_call" | custom-call | flops 2415919104 | bytes 2097152 | tf_op jit(solution)/shard_map/pallas_call | solution.py:379
  64.5 2.4 %collective-permute-start.9 = (bf16[544,128]{1,0:T(8,128)(2,1)S(1)}, bf16[544,128]{1,0:T(8,128)(2,1)S(1)}, u32[]{:S(2)}, u32[]{:S(2)}) collective-permute-start(bf16[544,128]{1,0:T(8,128)(2,1)S(1)} %get-tuple-element.47), channel_id=1, source_target_pairs={{8,0},{12,1},{10,2},{14,3},{9,4},{13,5},{11,6},{15,7},{1,8},{5,9},... | collective-permute-start | bytes 417800 | tf_op jit(solution)/shard_map/ppermute | solution.py:589
  67.0 4.4 %collective-permute-done.8.refs_0_ = bf16[544,128]{1,0:T(8,128)(2,1)S(1)} collective-permute-done((bf16[544,128]{1,0:T(8,128)(2,1)S(1)}, bf16[544,128]{1,0:T(8,128)(2,1)S(1)}, u32[]{:S(2)}, u32[]{:S(2)}) %collective-permute-start.8) | collective-permute-done | bytes 139296 | tf_op jit(solution)/shard_map/ppermute | solution.py:589
  72.7 2.9 %collective-permute-start.21 = (bf16[2,128,128]{2,1,0:T(8,128)(2,1)S(1)}, bf16[2,128,128]{2,1,0:T(8,128)(2,1)S(1)}, u32[]{:S(2)}, u32[]{:S(2)}) collective-permute-start(bf16[2,128,128]{2,1,0:T(8,128)(2,1)S(1)} %get-tuple-element.58), channel_id=1, source_target_pairs={{0,3},{1,2},{2,1},{3,0},{4,7},{5,6},{6,5},{7,4},{8,11},{9,10},{10,... | collective-permute-start | bytes 196616 | tf_op jit(solution)/shard_map/ppermute | solution.py:594
  75.9 3.1 %collective-permute-start.25 = (bf16[256,1024]{1,0:T(8,128)(2,1)S(1)}, bf16[256,1024]{1,0:T(8,128)(2,1)S(1)}, u32[]{:S(2)}, u32[]{:S(2)}) collective-permute-start(bf16[256,1024]{1,0:T(8,128)(2,1)S(1)} %collective-permute-done.23.refs_6_), channel_id=1, source_target_pairs={{0,1},{1,0},{2,3},{3,2},{4,5},{5,4},{6,7},{7,6},{8,9},{9,8},{10,11... | collective-permute-start | bytes 1572872 | tf_op jit(solution)/shard_map/ppermute | solution.py:569
  79.5 4.3 %collective-permute-done.24.refs_7_ = bf16[256,1024]{1,0:T(8,128)(2,1)S(1)} collective-permute-done((bf16[256,1024]{1,0:T(8,128)(2,1)S(1)}, bf16[256,1024]{1,0:T(8,128)(2,1)S(1)}, u32[]{:S(2)}, u32[]{:S(2)}) %collective-permute-start.24) | collective-permute-done | bytes 524320 | tf_op jit(solution)/shard_map/ppermute | solution.py:568
  83.8 3.5 %collective-permute-start.26 = (bf16[256,1024]{1,0:T(8,128)(2,1)S(1)}, bf16[256,1024]{1,0:T(8,128)(2,1)S(1)}, u32[]{:S(2)}, u32[]{:S(2)}) collective-permute-start(bf16[256,1024]{1,0:T(8,128)(2,1)S(1)} %collective-permute-done.24.refs_7_), channel_id=1, source_target_pairs={{0,1},{1,0},{2,3},{3,2},{4,5},{5,4},{6,7},{7,6},{8,9},{9,8},{10,11... | collective-permute-start | bytes 1572872 | tf_op jit(solution)/shard_map/ppermute | solution.py:569
  89.6 5.5 %collective-permute-done.14.refs_5_ = bf16[256,1024]{1,0:T(8,128)(2,1)S(1)} collective-permute-done((bf16[256,1024]{1,0:T(8,128)(2,1)S(1)}, bf16[256,1024]{1,0:T(8,128)(2,1)S(1)}, u32[]{:S(2)}, u32[]{:S(2)}) %collective-permute-start.14) | collective-permute-done | bytes 524320 | tf_op jit(solution)/shard_map/ppermute | solution.py:568
  95.1 1.9 %collective-permute-start.16 = (bf16[256,1024]{1,0:T(8,128)(2,1)S(1)}, bf16[256,1024]{1,0:T(8,128)(2,1)S(1)}, u32[]{:S(2)}, u32[]{:S(2)}) collective-permute-start(bf16[256,1024]{1,0:T(8,128)(2,1)S(1)} %collective-permute-done.14.refs_5_), channel_id=1, source_target_pairs={{0,1},{1,0},{2,3},{3,2},{4,5},{5,4},{6,7},{7,6},{8,9},{9,8},{10,11... | collective-permute-start | bytes 1572872 | tf_op jit(solution)/shard_map/ppermute | solution.py:569
  98.7 2.0 %shard_map.113 = (f32[128,2048]{1,0:T(8,128)S(1)}, bf16[512,2048]{1,0:T(8,128)(2,1)S(1)}) custom-call(bf16[2,128,128]{2,1,0:T(8,128)(2,1)S(1)} %get-tuple-element.55.refs_0_, bf16[2,128,128]{2,1,0:T(8,128)(2,1)S(1)} %collective-permute-done.19.refs_1_, bf16[2,128,128]{2,1,0:T(8,128)(2,1)S(1)} %collective-permute-done.20.refs_2_, ...), custom_call_target="tpu_custom_call" | custom-call | flops 536870912 | bytes 10485760 | tf_op jit(solution)/shard_map/pallas_call | solution.py:490
  100.7 3.3 %collective-permute-done.11.refs_2_ = bf16[2,128,128]{2,1,0:T(8,128)(2,1)S(1)} collective-permute-done((bf16[2,128,128]{2,1,0:T(8,128)(2,1)S(1)}, bf16[2,128,128]{2,1,0:T(8,128)(2,1)S(1)}, u32[]{:S(2)}, u32[]{:S(2)}) %collective-permute-start.11) | collective-permute-done | bytes 65568 | tf_op jit(solution)/shard_map/ppermute | solution.py:594
  104.1 1.7 %collective-permute-done.12.refs_3_ = bf16[2,128,128]{2,1,0:T(8,128)(2,1)S(1)} collective-permute-done((bf16[2,128,128]{2,1,0:T(8,128)(2,1)S(1)}, bf16[2,128,128]{2,1,0:T(8,128)(2,1)S(1)}, u32[]{:S(2)}, u32[]{:S(2)}) %collective-permute-start.12) | collective-permute-done | bytes 65568 | tf_op jit(solution)/shard_map/ppermute | solution.py:594
  (52 shorter events, 15.6 us)
Async XLA Ops:
  6.5 7.3 %collective-permute-start = (bf16[528,256]{1,0:T(8,128)(2,1)S(1)}, bf16[528,256]{1,0:T(8,128)(2,1)S(1)}, u32[]{:S(2)}, u32[]{:S(2)}) collective-permute-start(bf16[528,256]{1,0:T(8,128)(2,1)S(1)} %get-tuple-element.40), channel_id=1, source_target_pairs={{0,0},{1,4},{2,2},{3,6},{4,1},{5,5},{6,3},{7,7},{8,9},{9,13},{10,1... | collective-permute-start | bytes 811016 | tf_op jit(solution)/shard_map/ppermute | solution.py:572
  9.6 87.6 %collective-permute-start.22 = (bf16[512,2048]{1,0:T(8,128)(2,1)S(1)}, bf16[512,2048]{1,0:T(8,128)(2,1)S(1)}, u32[]{:S(2)}, u32[]{:S(2)}) collective-permute-start(bf16[512,2048]{1,0:T(8,128)(2,1)S(1)} %copy-done.2), channel_id=1, source_target_pairs={{0,1},{1,0},{2,3},{3,2},{4,5},{5,4},{6,7},{7,6},{8,9},{9,8},{10,11... | collective-permute-start | bytes 6291464 | tf_op jit(solution)/shard_map/ppermute | solution.py:555
  9.7 13.9 %collective-permute-start.1 = (bf16[528,256]{1,0:T(8,128)(2,1)S(1)}, bf16[528,256]{1,0:T(8,128)(2,1)S(1)}, u32[]{:S(2)}, u32[]{:S(2)}) collective-permute-start(bf16[528,256]{1,0:T(8,128)(2,1)S(1)} %get-tuple-element.41), channel_id=1, source_target_pairs={{0,8},{1,12},{2,10},{3,14},{4,9},{5,13},{6,11},{7,15},{8,1},{9,5},... | collective-permute-start | bytes 811016 | tf_op jit(solution)/shard_map/ppermute | solution.py:572
  10.3 20.3 %collective-permute-start.2 = (bf16[528,256]{1,0:T(8,128)(2,1)S(1)}, bf16[528,256]{1,0:T(8,128)(2,1)S(1)}, u32[]{:S(2)}, u32[]{:S(2)}) collective-permute-start(bf16[528,256]{1,0:T(8,128)(2,1)S(1)} %get-tuple-element.42), channel_id=1, source_target_pairs={{0,16},{1,20},{2,18},{3,22},{4,17},{5,21},{6,19},{7,23},{8,25},{9,... | collective-permute-start | bytes 811016 | tf_op jit(solution)/shard_map/ppermute | solution.py:564
  12.9 24.5 %collective-permute-start.3 = (bf16[528,256]{1,0:T(8,128)(2,1)S(1)}, bf16[528,256]{1,0:T(8,128)(2,1)S(1)}, u32[]{:S(2)}, u32[]{:S(2)}) collective-permute-start(bf16[528,256]{1,0:T(8,128)(2,1)S(1)} %get-tuple-element.43), channel_id=1, source_target_pairs={{0,24},{1,28},{2,26},{3,30},{4,25},{5,29},{6,27},{7,31},{8,17},{9,... | collective-permute-start | bytes 811016 | tf_op jit(solution)/shard_map/ppermute | solution.py:564
  13.8 24.7 %collective-permute-start.4 = (bf16[528,256]{1,0:T(8,128)(2,1)S(1)}, bf16[528,256]{1,0:T(8,128)(2,1)S(1)}, u32[]{:S(2)}, u32[]{:S(2)}) collective-permute-start(bf16[528,256]{1,0:T(8,128)(2,1)S(1)} %collective-permute-done.refs_0_), channel_id=1, source_target_pairs={{0,1},{1,0},{2,3},{3,2},{4,5},{5,4},{6,7},{7,6},{8,9},{9,8},{10,11... | collective-permute-start | bytes 811016 | tf_op jit(solution)/shard_map/ppermute | solution.py:578
  23.6 33.0 %collective-permute-start.23 = (bf16[256,1024]{1,0:T(8,128)(2,1)S(1)}, bf16[256,1024]{1,0:T(8,128)(2,1)S(1)}, u32[]{:S(2)}, u32[]{:S(2)}) collective-permute-start(bf16[256,1024]{1,0:T(8,128)(2,1)S(1)} %get-tuple-element.59), channel_id=1, source_target_pairs={{0,2},{1,3},{2,0},{3,1},{4,6},{5,7},{6,4},{7,5},{8,10},{9,11},{10,... | collective-permute-start | bytes 1572872 | tf_op jit(solution)/shard_map/ppermute | solution.py:567
  30.6 16.6 %collective-permute-start.5 = (bf16[528,256]{1,0:T(8,128)(2,1)S(1)}, bf16[528,256]{1,0:T(8,128)(2,1)S(1)}, u32[]{:S(2)}, u32[]{:S(2)}) collective-permute-start(bf16[528,256]{1,0:T(8,128)(2,1)S(1)} %collective-permute-done.1.refs_1_), channel_id=1, source_target_pairs={{0,1},{1,0},{2,3},{3,2},{4,5},{5,4},{6,7},{7,6},{8,9},{9,8},{10,11... | collective-permute-start | bytes 811016 | tf_op jit(solution)/shard_map/ppermute | solution.py:578
  37.4 10.4 %collective-permute-start.6 = (bf16[528,256]{1,0:T(8,128)(2,1)S(1)}, bf16[528,256]{1,0:T(8,128)(2,1)S(1)}, u32[]{:S(2)}, u32[]{:S(2)}) collective-permute-start(bf16[528,256]{1,0:T(8,128)(2,1)S(1)} %collective-permute-done.2.refs_2_), channel_id=1, source_target_pairs={{0,1},{1,0},{2,3},{3,2},{4,5},{5,4},{6,7},{7,6},{8,9},{9,8},{10,11... | collective-permute-start | bytes 811016 | tf_op jit(solution)/shard_map/ppermute | solution.py:578
  38.5 10.6 %collective-permute-start.7 = (bf16[528,256]{1,0:T(8,128)(2,1)S(1)}, bf16[528,256]{1,0:T(8,128)(2,1)S(1)}, u32[]{:S(2)}, u32[]{:S(2)}) collective-permute-start(bf16[528,256]{1,0:T(8,128)(2,1)S(1)} %collective-permute-done.3.refs_3_), channel_id=1, source_target_pairs={{0,1},{1,0},{2,3},{3,2},{4,5},{5,4},{6,7},{7,6},{8,9},{9,8},{10,11... | collective-permute-start | bytes 811016 | tf_op jit(solution)/shard_map/ppermute | solution.py:578
  47.2 40.1 %collective-permute-start.27 = (bf16[2,128,2048]{2,1,0:T(8,128)(2,1)S(1)}, bf16[2,128,2048]{2,1,0:T(8,128)(2,1)S(1)}, u32[]{:S(2)}, u32[]{:S(2)}) collective-permute-start(bf16[2,128,2048]{2,1,0:T(8,128)(2,1)S(1)} %get-tuple-element.64), channel_id=1, source_target_pairs={{0,1},{1,0},{2,3},{3,2},{4,5},{5,4},{6,7},{7,6},{8,9},{9,8},{10,11... | collective-permute-start | bytes 3145736 | tf_op jit(solution)/shard_map/ppermute | solution.py:576
  47.8 19.1 %collective-permute-start.13 = (bf16[256,1024]{1,0:T(8,128)(2,1)S(1)}, bf16[256,1024]{1,0:T(8,128)(2,1)S(1)}, u32[]{:S(2)}, u32[]{:S(2)}) collective-permute-start(bf16[256,1024]{1,0:T(8,128)(2,1)S(1)} %get-tuple-element.52), channel_id=1, source_target_pairs={{0,2},{1,3},{2,0},{3,1},{4,6},{5,7},{6,4},{7,5},{8,10},{9,11},{10,... | collective-permute-start | bytes 1572872 | tf_op jit(solution)/shard_map/ppermute | solution.py:567
  54.4 10.0 %collective-permute-start.17 = (bf16[544,128]{1,0:T(8,128)(2,1)S(1)}, bf16[544,128]{1,0:T(8,128)(2,1)S(1)}, u32[]{:S(2)}, u32[]{:S(2)}) collective-permute-start(bf16[544,128]{1,0:T(8,128)(2,1)S(1)} %get-tuple-element.53), channel_id=1, source_target_pairs={{24,0},{28,1},{26,2},{30,3},{25,4},{29,5},{27,6},{31,7},{17,8},{21... | collective-permute-start | bytes 417800 | tf_op jit(solution)/shard_map/ppermute | solution.py:586
  56.6 7.8 %collective-permute-start.18 = (bf16[544,128]{1,0:T(8,128)(2,1)S(1)}, bf16[544,128]{1,0:T(8,128)(2,1)S(1)}, u32[]{:S(2)}, u32[]{:S(2)}) collective-permute-start(bf16[544,128]{1,0:T(8,128)(2,1)S(1)} %get-tuple-element.54), channel_id=1, source_target_pairs={{0,0},{4,1},{2,2},{6,3},{1,4},{5,5},{3,6},{7,7},{9,8},{13,9},{11,1... | collective-permute-start | bytes 417800 | tf_op jit(solution)/shard_map/ppermute | solution.py:586
  64.5 8.0 %collective-permute-start.9 = (bf16[544,128]{1,0:T(8,128)(2,1)S(1)}, bf16[544,128]{1,0:T(8,128)(2,1)S(1)}, u32[]{:S(2)}, u32[]{:S(2)}) collective-permute-start(bf16[544,128]{1,0:T(8,128)(2,1)S(1)} %get-tuple-element.47), channel_id=1, source_target_pairs={{8,0},{12,1},{10,2},{14,3},{9,4},{13,5},{11,6},{15,7},{1,8},{5,9},... | collective-permute-start | bytes 417800 | tf_op jit(solution)/shard_map/ppermute | solution.py:589
  71.4 12.4 %collective-permute-start.24 = (bf16[256,1024]{1,0:T(8,128)(2,1)S(1)}, bf16[256,1024]{1,0:T(8,128)(2,1)S(1)}, u32[]{:S(2)}, u32[]{:S(2)}) collective-permute-start(bf16[256,1024]{1,0:T(8,128)(2,1)S(1)} %collective-permute-done.23.refs_6_), channel_id=1, source_target_pairs={{0,4},{4,0},{8,12},{12,8},{16,20},{20,16},{24,28},{28,24},{1,5},{5... | collective-permute-start | bytes 1572872 | tf_op jit(solution)/shard_map/ppermute | solution.py:568
  75.9 13.5 %collective-permute-start.25 = (bf16[256,1024]{1,0:T(8,128)(2,1)S(1)}, bf16[256,1024]{1,0:T(8,128)(2,1)S(1)}, u32[]{:S(2)}, u32[]{:S(2)}) collective-permute-start(bf16[256,1024]{1,0:T(8,128)(2,1)S(1)} %collective-permute-done.23.refs_6_), channel_id=1, source_target_pairs={{0,1},{1,0},{2,3},{3,2},{4,5},{5,4},{6,7},{7,6},{8,9},{9,8},{10,11... | collective-permute-start | bytes 1572872 | tf_op jit(solution)/shard_map/ppermute | solution.py:569
  79.3 15.8 %collective-permute-start.14 = (bf16[256,1024]{1,0:T(8,128)(2,1)S(1)}, bf16[256,1024]{1,0:T(8,128)(2,1)S(1)}, u32[]{:S(2)}, u32[]{:S(2)}) collective-permute-start(bf16[256,1024]{1,0:T(8,128)(2,1)S(1)} %collective-permute-done.13.refs_4_), channel_id=1, source_target_pairs={{0,4},{4,0},{8,12},{12,8},{16,20},{20,16},{24,28},{28,24},{1,5},{5... | collective-permute-start | bytes 1572872 | tf_op jit(solution)/shard_map/ppermute | solution.py:568
  83.8 13.2 %collective-permute-start.26 = (bf16[256,1024]{1,0:T(8,128)(2,1)S(1)}, bf16[256,1024]{1,0:T(8,128)(2,1)S(1)}, u32[]{:S(2)}, u32[]{:S(2)}) collective-permute-start(bf16[256,1024]{1,0:T(8,128)(2,1)S(1)} %collective-permute-done.24.refs_7_), channel_id=1, source_target_pairs={{0,1},{1,0},{2,3},{3,2},{4,5},{5,4},{6,7},{7,6},{8,9},{9,8},{10,11... | collective-permute-start | bytes 1572872 | tf_op jit(solution)/shard_map/ppermute | solution.py:569
  88.9 16.8 %collective-permute-start.15 = (bf16[256,1024]{1,0:T(8,128)(2,1)S(1)}, bf16[256,1024]{1,0:T(8,128)(2,1)S(1)}, u32[]{:S(2)}, u32[]{:S(2)}) collective-permute-start(bf16[256,1024]{1,0:T(8,128)(2,1)S(1)} %collective-permute-done.13.refs_4_), channel_id=1, source_target_pairs={{0,1},{1,0},{2,3},{3,2},{4,5},{5,4},{6,7},{7,6},{8,9},{9,8},{10,11... | collective-permute-start | bytes 1572872 | tf_op jit(solution)/shard_map/ppermute | solution.py:569
  89.3 16.5 %collective-permute-start.28 = (bf16[128,2048]{1,0:T(8,128)(2,1)S(1)}, bf16[128,2048]{1,0:T(8,128)(2,1)S(1)}, u32[]{:S(2)}, u32[]{:S(2)}) collective-permute-start(bf16[128,2048]{1,0:T(8,128)(2,1)S(1)} %shard_map.114), channel_id=1, source_target_pairs={{0,2},{1,3},{2,0},{3,1},{4,6},{5,7},{6,4},{7,5},{8,10},{9,11},{10,... | collective-permute-start | bytes 1572872 | tf_op jit(solution)/shard_map/ppermute | solution.py:580
  95.1 10.7 %collective-permute-start.16 = (bf16[256,1024]{1,0:T(8,128)(2,1)S(1)}, bf16[256,1024]{1,0:T(8,128)(2,1)S(1)}, u32[]{:S(2)}, u32[]{:S(2)}) collective-permute-start(bf16[256,1024]{1,0:T(8,128)(2,1)S(1)} %collective-permute-done.14.refs_5_), channel_id=1, source_target_pairs={{0,1},{1,0},{2,3},{3,2},{4,5},{5,4},{6,7},{7,6},{8,9},{9,8},{10,11... | collective-permute-start | bytes 1572872 | tf_op jit(solution)/shard_map/ppermute | solution.py:569
  97.0 7.1 %collective-permute-start.11 = (bf16[2,128,128]{2,1,0:T(8,128)(2,1)S(1)}, bf16[2,128,128]{2,1,0:T(8,128)(2,1)S(1)}, u32[]{:S(2)}, u32[]{:S(2)}) collective-permute-start(bf16[2,128,128]{2,1,0:T(8,128)(2,1)S(1)} %get-tuple-element.50), channel_id=1, source_target_pairs={{0,2},{1,3},{2,0},{3,1},{4,6},{5,7},{6,4},{7,5},{8,10},{9,11},{10,... | collective-permute-start | bytes 196616 | tf_op jit(solution)/shard_map/ppermute | solution.py:594
  97.3 8.5 %collective-permute-start.12 = (bf16[2,128,128]{2,1,0:T(8,128)(2,1)S(1)}, bf16[2,128,128]{2,1,0:T(8,128)(2,1)S(1)}, u32[]{:S(2)}, u32[]{:S(2)}) collective-permute-start(bf16[2,128,128]{2,1,0:T(8,128)(2,1)S(1)} %get-tuple-element.51), channel_id=1, source_target_pairs={{0,3},{1,2},{2,1},{3,0},{4,7},{5,6},{6,5},{7,4},{8,11},{9,10},{10,... | collective-permute-start | bytes 196616 | tf_op jit(solution)/shard_map/ppermute | solution.py:594
  (8 other events, 70.3 us)

commit v5 on v3

--- a/solution.py
+++ b/solution.py
@@ -93,8 +93,8 @@
 def project_far_body(
     tokens_at, gain_at, w_qk, w_value, clusters_at, w_out, *rest, width, stages, parts
 ):
-    out_low, out_high, normed, clusters, qk_next, val_next, out_early, out_late = rest[:8]
-    tokens, gain, qk_buf, val_buf, sems, token_sems, out_sems = rest[8:]
+    out_low, out_high, normed, clusters, qk_next, val_next, out_early, out_late, out_rest = rest[:9]
+    tokens, gain, qk_buf, val_buf, sems, token_sems, out_sems = rest[9:]
     z = lax.axis_index(SEQ) >> 1
     y = lax.axis_index(SEQ) & 1
     step = tokens.shape[0] // parts
@@ -110,9 +110,13 @@
 
     first, second = columns(1 ^ (z >> 1)), columns(z >> 1)
     half = out_early.shape[1]
-    out_cols = pl.ds(pl.multiple_of(y * half, half), half)
     out_copies = []
-    for part, turns in ((out_early, stages[0]), (out_late, stages[1])):
+    for part, turns, at in (
+        (out_early, stages[0], y),
+        (out_late, stages[1], y),
+        (out_rest, stages[1], 1 - y),
+    ):
+        out_cols = pl.ds(pl.multiple_of(at * half, half), half)
         for i, k in enumerate(turns):
             here = pl.ds(pl.multiple_of((z ^ k) * width, width), width)
             out_copies.append(
@@ -160,9 +164,10 @@
             shape(pair),
             shape((2 * width, w_out.shape[1] // 2)),
             shape((2 * width, w_out.shape[1] // 2)),
+            shape((2 * width, w_out.shape[1] // 2)),
         ),
         in_specs=[any_spec()] * 6,
-        out_specs=(vmem_spec(),) * 8,
+        out_specs=(vmem_spec(),) * 9,
         scratch_shapes=[
             pltpu.VMEM((rows, depth), jnp.bfloat16),
             pltpu.VMEM((1, depth), jnp.float32),
@@ -170,88 +175,113 @@
             pltpu.VMEM(pair, jnp.bfloat16),
             pltpu.SemaphoreType.DMA((6,)),
             pltpu.SemaphoreType.DMA((parts,)),
-            pltpu.SemaphoreType.DMA((4,)),
+            pltpu.SemaphoreType.DMA((6,)),
         ],
         compiler_params=params(20),
         cost_estimate=cost(8 * rows * depth * width, 2 * rows * depth + 12 * depth * width),
     )(*[held(a) for a in (tokens, gain.reshape(1, depth), w_qk, w_value, clusters, w_out)])
 
 
-def project_near_body(normed, w_qk, w_value, clusters, out_low, out_high, *, width):
+def project_near_body(
+    normed, w_qk, w_value, clusters, w_up, out_low, out_high, next_half, sem, *, width
+):
+    copy = pltpu.make_async_copy(w_up.at[:, pl.ds(0, next_half.shape[1])], next_half, sem)
+    copy.start()
     unit_heads(normed, w_qk, w_value, (out_low, out_high), clusters, (0, 1), width)
-
-
-def project_near(normed, w_qk, w_value, clusters, width):
+    copy.wait()
+
+
+def project_near(normed, w_qk, w_value, clusters, w_up, width):
     rows, depth = normed.shape
     message = shape((rows + EXTRA, 2 * width))
     return pl.pallas_call(
         functools.partial(project_near_body, width=width),
-        out_shape=(message, message),
-        in_specs=[vmem_spec()] * 4,
-        out_specs=(vmem_spec(),) * 2,
-        compiler_params=params(14),
+        out_shape=(message, message, shape((depth, w_up.shape[1] // 2))),
+        in_specs=[vmem_spec()] * 4 + [any_spec()],
+        out_specs=(vmem_spec(),) * 3,
+        scratch_shapes=[pltpu.SemaphoreType.DMA],
+        compiler_params=params(16),
         cost_estimate=cost(8 * rows * depth * width, 2 * rows * depth + 8 * depth * width),
-    )(normed, w_qk, w_value, clusters)
-
-
-def up_body(normed, w_up, hidden):
-    grown = jnp.dot(normed[...], w_up[...], preferred_element_type=jnp.float32)
-    hidden[...] = jnp.maximum(grown, 0.0).astype(jnp.bfloat16)
-
-
-def up(normed, w_up, blocks=2):
+    )(normed, w_qk, w_value, clusters, held(w_up))
+
+
+def up_body(normed, first, w_up, w_down, hidden, next_half, second, sems):
+    half = first.shape[1]
+    copies = (
+        pltpu.make_async_copy(w_up.at[:, pl.ds(half, half)], second, sems.at[0]),
+        pltpu.make_async_copy(
+            w_down.at[:, pl.ds(0, next_half.shape[1])], next_half, sems.at[1]
+        ),
+    )
+    for copy in copies:
+        copy.start()
+    for at, weights in enumerate((first, second)):
+        if at == 1:
+            copies[0].wait()
+        grown = jnp.dot(normed[...], weights[...], preferred_element_type=jnp.float32)
+        hidden[:, at * half : (at + 1) * half] = jnp.maximum(grown, 0.0).astype(jnp.bfloat16)
+    copies[1].wait()
+
+
+def up(normed, first, w_up, w_down):
     rows, depth = normed.shape
     units = w_up.shape[1]
-    block = units // blocks
     return pl.pallas_call(
         up_body,
-        grid=(blocks,),
-        out_shape=shape((rows, units)),
-        in_specs=[
-            pl.BlockSpec((rows, depth), lambda i: (0, 0)),
-            pl.BlockSpec((depth, block), lambda i: (0, i)),
+        out_shape=(shape((rows, units)), shape((units, w_down.shape[1] // 2))),
+        in_specs=[vmem_spec(), vmem_spec(), any_spec(), any_spec()],
+        out_specs=(vmem_spec(), vmem_spec()),
+        scratch_shapes=[
+            pltpu.VMEM((depth, units // 2), jnp.bfloat16),
+            pltpu.SemaphoreType.DMA((2,)),
         ],
-        out_specs=pl.BlockSpec((rows, block), lambda i: (0, i)),
         compiler_params=params(24),
         cost_estimate=cost(2 * rows * depth * units, 2 * depth * units + 4 * rows * depth),
-    )(normed, w_up)
-
-
-def down_body(hidden, w_down, mine, far, away, held, *, share):
+    )(normed, first, held(w_up), held(w_down))
+
+
+def down_body(hidden, first, w_down, mine, far, away, second, held_rows, sem, *, share):
     at = lax.axis_index(TENSOR)
-    held[...] = jnp.dot(hidden[...], w_down[...], preferred_element_type=jnp.float32)
+    half = first.shape[1]
+    copy = pltpu.make_async_copy(w_down.at[:, pl.ds(half, half)], second, sem)
+    copy.start()
 
     def quarter(turn):
-        return held[pl.ds(pl.multiple_of((at ^ turn) * share, share), share), :]
-
-    mine[...] = quarter(0)
-    far[...] = quarter(2)
-    away[0] = quarter(1).astype(jnp.bfloat16)
-    away[1] = quarter(3).astype(jnp.bfloat16)
-
-
-def down(hidden, w_down, share, blocks=2):
+        return held_rows[pl.ds(pl.multiple_of((at ^ turn) * share, share), share), :]
+
+    for part, weights in enumerate((first, second)):
+        if part == 1:
+            copy.wait()
+        cols = slice(part * half, (part + 1) * half)
+        held_rows[...] = jnp.dot(
+            hidden[...], weights[...], preferred_element_type=jnp.float32
+        )
+        mine[:, cols] = quarter(0)
+        far[:, cols] = quarter(2)
+        away[0, :, cols] = quarter(1).astype(jnp.bfloat16)
+        away[1, :, cols] = quarter(3).astype(jnp.bfloat16)
+
+
+def down(hidden, first, w_down, share):
     rows, units = hidden.shape
     depth = w_down.shape[1]
-    block = depth // blocks
-    one = pl.BlockSpec((share, block), lambda i: (0, i))
     return pl.pallas_call(
         functools.partial(down_body, share=share),
-        grid=(blocks,),
         out_shape=(
             shape((share, depth), jnp.float32),
             shape((share, depth), jnp.float32),
             shape((2, share, depth)),
         ),
-        in_specs=[
-            pl.BlockSpec((rows, units), lambda i: (0, 0)),
-            pl.BlockSpec((units, block), lambda i: (0, i)),
+        in_specs=[vmem_spec(), vmem_spec(), any_spec()],
+        out_specs=(vmem_spec(),) * 3,
+        scratch_shapes=[
+            pltpu.VMEM((units, depth // 2), jnp.bfloat16),
+            pltpu.VMEM((rows, depth // 2), jnp.float32),
+            pltpu.SemaphoreType.DMA,
         ],
-        out_specs=(one, one, pl.BlockSpec((2, share, block), lambda i: (0, 0, i))),
-        scratch_shapes=[pltpu.VMEM((rows, block), jnp.float32)],
-        compiler_params=params(26),
+        compiler_params=params(24),
         cost_estimate=cost(2 * rows * depth * units, 2 * depth * units + 6 * rows * depth),
-    )(hidden, w_down)
+    )(hidden, first, held(w_down))
 
 
 def pick_body(far, got, sent):
@@ -554,15 +584,18 @@
     for k in (3, 2):
         own[k] = lax.ppermute(messages[k], BOTH, steps[k])
     halves = {}
-    for name, part in zip("el", out_parts):
-        here = lax.ppermute(part, TENSOR, swaps[2])
-        there = lax.ppermute(here, SEQ, swap_y)
+    for name in "el":
+        here = lax.ppermute(out_parts.pop(0), TENSOR, swaps[2])
+        if name == "e":
+            there = lax.ppermute(here, SEQ, swap_y)
+        else:
+            there = lax.ppermute(out_parts.pop(0), TENSOR, swaps[2])
         halves[name] = [here, there] + [lax.ppermute(w, TENSOR, swaps[1]) for w in (here, there)]
-    messages[0], messages[1] = project_near(normed, qk_next, val_next, ids, width)
+    messages[0], messages[1], up_first = project_near(normed, qk_next, val_next, ids, w_up, width)
     for k in (1, 0):
         own[k] = lax.ppermute(messages[k], BOTH, steps[k])
-    hidden = up(normed, held(w_up))
-    mine, far, sent = down(hidden, held(w_down), share)
+    hidden, down_first = up(normed, up_first, w_up, w_down)
+    mine, far, sent = down(hidden, down_first, w_down, share)
     got = lax.ppermute(sent, TENSOR, swaps[1])
     for k in range(heads):
         other[k] = lax.ppermute(own[k], TENSOR, swaps[1])

time: 123 us -> 128 us (1.041)
  starting transfers between devices: 30.7 us -> 38.7 us
  Pallas kernels: 34.5 us -> 31.6 us
    ppermute x2 -> x3, waiting for transfers between devices: 0.01 us -> 19.9 us  [the longest x2 10.3 us: by_heads(): here = lax.ppermute(out_parts.pop(0), TENSOR, swaps[2])]
    ppermute x2 -> x1, waiting for transfers between devices: 14.1 us -> 0.01 us  [by_heads(): there = lax.ppermute(here, SEQ, swap_y)]
    ppermute x4, starting transfers between devices: 3.33 us -> 12.4 us  [by_heads(): other[k] = lax.ppermute(own[k], TENSOR, swaps[1])]
    pallas_call x2, Pallas kernels: 14.4 us -> 9.66 us  [the longest x1 4.98 us: down(): pl.pallas_call(functools.partial(down_body, share=share), out_shape=(shap...]
    ppermute x4, starting transfers between devices: 8.99 us -> 4.37 us  [by_heads(): back[k] = lax.ppermute(result, BOTH, turned(steps[k]))]
    ppermute x6, starting transfers between devices: 2.88 us -> 6.09 us  [by_heads(): lax.ppermute(away[d - 1], TENSOR, swaps[d])]
    ppermute x4, starting transfers between devices: 4.42 us -> 7.62 us  [by_heads(): own[k] = lax.ppermute(messages[k], BOTH, steps[k])]
    ppermute x1, starting transfers between devices: 4.41 us -> 1.68 us  [by_heads(): w_core = lax.ppermute(w_out, TENSOR, swaps[1])]
  transfers between devices with their start and end apart: 29 -> 29, of which waited for: 12 -> 10; matrix products, arithmetic and copies ran while one was open for 0% -> 0% of each run, Pallas kernels for 22% -> 18%
where the time goes in v5:
time: 128 us
  waiting for transfers between devices  56.6 us (44%)
  starting transfers between devices  38.7 us (30%)
  Pallas kernels  31.6 us (25%)
    ppermute x6, waiting for transfers between devices, by_heads(): lax.ppermute(away[d - 1], TENSOR, swaps[d])  17.9 us
    ppermute x4, starting transfers between devices, by_heads(): other[k] = lax.ppermute(own[k], TENSOR, swaps[1])  12.4 us
    ppermute x4, waiting for transfers between devices, by_heads(): back[k] = lax.ppermute(result, BOTH, turned(steps[k]))  11.6 us
    pallas_call x2, Pallas kernels, attend(): pl.pallas_call(functools.partial(attend_body, heads=heads, width=width, o...  10.6 us
    ppermute x2, waiting for transfers between devices, by_heads(): here = lax.ppermute(out_parts.pop(0), TENSOR, swaps[2])  10.3 us
    ppermute x1, waiting for transfers between devices, by_heads(): there = lax.ppermute(out_parts.pop(0), TENSOR, swaps[2])  9.68 us
    ppermute x4, starting transfers between devices, by_heads(): own[k] = lax.ppermute(messages[k], BOTH, steps[k])  7.62 us
    ppermute x4, waiting for transfers between devices, by_heads(): own[k] = lax.ppermute(messages[k], BOTH, steps[k])  7.1 us
  transfers between devices with their start and end apart: 29, of which 10 were waited for; matrix products, arithmetic and copies ran while one was open for 0% of the time, Pallas kernels for 18%

profile of v5, /device:TPU:0, one launch (start us, length us, event | category | flops | bytes accessed | tf_op | source)
XLA Modules:
  0.0 127.7 jit_solution(14759107539435971804)
XLA Ops:
  0.6 4.3 %shard_map.104 = (bf16[528,256]{1,0:T(8,128)(2,1)S(1)}, bf16[528,256]{1,0:T(8,128)(2,1)S(1)}, bf16[512,2048]{1,0:T(8,128)(2,1)S(1)}, s32[4,512]{1,0:T(4,128)S(1)...) custom-call(bf16[512,2048]{1,0:T(8,128)(2,1)} %refs_10_.1, ...), custom_call_target="tpu_custom_call" | custom-call | flops 1073741824 | bytes 5242880 | tf_op jit(solution)/shard_map/pallas_call | solution.py:156
  5.0 3.3 %shard_map.105 = (bf16[528,256]{1,0:T(8,128)(2,1)S(1)}, bf16[528,256]{1,0:T(8,128)(2,1)S(1)}, bf16[2048,1024]{1,0:T(8,128)(2,1)S(1)}) custom-call(bf16[512,2048]{1,0:T(8,128)(2,1)S(1)} %get-tuple-element.37.normed, bf16[2048,256]{1,0:T(8,128)(2,1)S(1)} %get-tuple-element.38.w_qk, bf16[2048,256]{1,0:T(8,128)(2,1)S(1)} %get-tuple-element.39.w_value, ...), custom_call_target="tpu_custom_call" | custom-call | flops 1073741824 | bytes 4194304 | tf_op jit(solution)/shard_map/pallas_call | solution.py:197
  9.0 4.3 %collective-permute-start.1 = (bf16[528,256]{1,0:T(8,128)(2,1)S(1)}, bf16[528,256]{1,0:T(8,128)(2,1)S(1)}, u32[]{:S(2)}, u32[]{:S(2)}) collective-permute-start(bf16[528,256]{1,0:T(8,128)(2,1)S(1)} %get-tuple-element.42), channel_id=1, source_target_pairs={{0,8},{1,12},{2,10},{3,14},{4,9},{5,13},{6,11},{7,15},{8,1},{9,5},... | collective-permute-start | bytes 811016 | tf_op jit(solution)/shard_map/ppermute | solution.py:596
  13.3 2.6 %collective-permute-start.2 = (bf16[528,256]{1,0:T(8,128)(2,1)S(1)}, bf16[528,256]{1,0:T(8,128)(2,1)S(1)}, u32[]{:S(2)}, u32[]{:S(2)}) collective-permute-start(bf16[528,256]{1,0:T(8,128)(2,1)S(1)} %get-tuple-element.43), channel_id=1, source_target_pairs={{0,16},{1,20},{2,18},{3,22},{4,17},{5,21},{6,19},{7,23},{8,25},{9,... | collective-permute-start | bytes 811016 | tf_op jit(solution)/shard_map/ppermute | solution.py:585
  15.9 1.7 %collective-permute-start.22 = (bf16[512,2048]{1,0:T(8,128)(2,1)S(1)}, bf16[512,2048]{1,0:T(8,128)(2,1)S(1)}, u32[]{:S(2)}, u32[]{:S(2)}) collective-permute-start(bf16[512,2048]{1,0:T(8,128)(2,1)S(1)} %copy-done.2), channel_id=1, source_target_pairs={{0,1},{1,0},{2,3},{3,2},{4,5},{5,4},{6,7},{7,6},{8,9},{9,8},{10,11... | collective-permute-start | bytes 6291464 | tf_op jit(solution)/shard_map/ppermute | solution.py:576
  17.6 1.6 %collective-permute-start.4 = (bf16[528,256]{1,0:T(8,128)(2,1)S(1)}, bf16[528,256]{1,0:T(8,128)(2,1)S(1)}, u32[]{:S(2)}, u32[]{:S(2)}) collective-permute-start(bf16[528,256]{1,0:T(8,128)(2,1)S(1)} %collective-permute-done.refs_0_), channel_id=1, source_target_pairs={{0,1},{1,0},{2,3},{3,2},{4,5},{5,4},{6,7},{7,6},{8,9},{9,8},{10,11... | collective-permute-start | bytes 811016 | tf_op jit(solution)/shard_map/ppermute | solution.py:601
  19.2 7.1 %collective-permute-done.1.refs_1_ = bf16[528,256]{1,0:T(8,128)(2,1)S(1)} collective-permute-done((bf16[528,256]{1,0:T(8,128)(2,1)S(1)}, bf16[528,256]{1,0:T(8,128)(2,1)S(1)}, u32[]{:S(2)}, u32[]{:S(2)}) %collective-permute-start.1) | collective-permute-done | bytes 270368 | tf_op jit(solution)/shard_map/ppermute | solution.py:596
  26.3 10.8 %collective-permute-start.6 = (bf16[528,256]{1,0:T(8,128)(2,1)S(1)}, bf16[528,256]{1,0:T(8,128)(2,1)S(1)}, u32[]{:S(2)}, u32[]{:S(2)}) collective-permute-start(bf16[528,256]{1,0:T(8,128)(2,1)S(1)} %collective-permute-done.2.refs_2_), channel_id=1, source_target_pairs={{0,1},{1,0},{2,3},{3,2},{4,5},{5,4},{6,7},{7,6},{8,9},{9,8},{10,11... | collective-permute-start | bytes 811016 | tf_op jit(solution)/shard_map/ppermute | solution.py:601
  37.1 4.7 %shard_map.110 = (bf16[512,2048]{1,0:T(8,128)(2,1)S(1)}, bf16[2048,1024]{1,0:T(8,128)(2,1)S(1)}) custom-call(bf16[512,2048]{1,0:T(8,128)(2,1)S(1)} %get-tuple-element.37.normed, bf16[2048,1024]{1,0:T(8,128)(2,1)S(1)} %get-tuple-element.62.first, bf16[2048,2048]{1,0:T(8,128)(2,1)} %w_up.3, bf16[2048,2048]{1,0:T(8,128)(2,1)} %w_down.3), custom_call_target="tpu_custom_call" | custom-call | flops 4294967296 | bytes 12582912 | tf_op jit(solution)/shard_map/pallas_call | solution.py:229
  41.8 1.6 %collective-permute-start.23 = (bf16[256,1024]{1,0:T(8,128)(2,1)S(1)}, bf16[256,1024]{1,0:T(8,128)(2,1)S(1)}, u32[]{:S(2)}, u32[]{:S(2)}) collective-permute-start(bf16[256,1024]{1,0:T(8,128)(2,1)S(1)} %get-tuple-element.61), channel_id=1, source_target_pairs={{0,2},{1,3},{2,0},{3,1},{4,6},{5,7},{6,4},{7,5},{8,10},{9,11},{10,... | collective-permute-start | bytes 1572872 | tf_op jit(solution)/shard_map/ppermute | solution.py:588
  43.9 1.5 %collective-permute-start.14 = (bf16[256,1024]{1,0:T(8,128)(2,1)S(1)}, bf16[256,1024]{1,0:T(8,128)(2,1)S(1)}, u32[]{:S(2)}, u32[]{:S(2)}) collective-permute-start(bf16[256,1024]{1,0:T(8,128)(2,1)S(1)} %get-tuple-element.54), channel_id=1, source_target_pairs={{0,2},{1,3},{2,0},{3,1},{4,6},{5,7},{6,4},{7,5},{8,10},{9,11},{10,... | collective-permute-start | bytes 1572872 | tf_op jit(solution)/shard_map/ppermute | solution.py:592
  45.4 5.0 %shard_map.111 = (f32[128,2048]{1,0:T(8,128)S(1)}, f32[128,2048]{1,0:T(8,128)S(1)}, bf16[2,128,2048]{2,1,0:T(8,128)(2,1)S(1)}) custom-call(bf16[512,2048]{1,0:T(8,128)(2,1)S(1)} %get-tuple-element.63.hidden, bf16[2048,1024]{1,0:T(8,128)(2,1)S(1)} %get-tuple-element.64.first, bf16[2048,2048]{1,0:T(8,128)(2,1)} %w_down.3), custom_call_target="tpu_custom_call" | custom-call | flops 4294967296 | bytes 14680064 | tf_op jit(solution)/shard_map/pallas_call | solution.py:268
  50.9 5.4 %shard_map.106 = (bf16[544,128]{1,0:T(8,128)(2,1)S(1)}, bf16[544,128]{1,0:T(8,128)(2,1)S(1)}, bf16[8,512,256]{2,1,0:T(8,128)(2,1)S(1)}, f32[8,8,512]{2,1,0:T(8,128)S(1)}) custom-call(bf16[528,256]{1,0:T(8,128)(2,1)S(1)} %collective-permute-done.refs_0_, bf16[528,256]{1,0:T(8,128)(2,1)S(1)} %collective-permute-done.1.refs_1_, ...), custom_call_target="tpu_custom_call" | custom-call | flops 2415919104 | bytes 2097152 | tf_op jit(solution)/shard_map/pallas_call | solution.py:400
  57.9 10.0 %collective-permute-done.13.refs_4_ = bf16[256,1024]{1,0:T(8,128)(2,1)S(1)} collective-permute-done((bf16[256,1024]{1,0:T(8,128)(2,1)S(1)}, bf16[256,1024]{1,0:T(8,128)(2,1)S(1)}, u32[]{:S(2)}, u32[]{:S(2)}) %collective-permute-start.13) | collective-permute-done | bytes 524320 | tf_op jit(solution)/shard_map/ppermute | solution.py:588
  68.5 9.7 %collective-permute-done.14.refs_5_ = bf16[256,1024]{1,0:T(8,128)(2,1)S(1)} collective-permute-done((bf16[256,1024]{1,0:T(8,128)(2,1)S(1)}, bf16[256,1024]{1,0:T(8,128)(2,1)S(1)}, u32[]{:S(2)}, u32[]{:S(2)}) %collective-permute-start.14) | collective-permute-done | bytes 524320 | tf_op jit(solution)/shard_map/ppermute | solution.py:592
  78.8 5.2 %shard_map.107 = (bf16[544,128]{1,0:T(8,128)(2,1)S(1)}, bf16[544,128]{1,0:T(8,128)(2,1)S(1)}) custom-call(bf16[8,512,256]{2,1,0:T(8,128)(2,1)S(1)} %get-tuple-element.45.refs_0_, f32[8,8,512]{2,1,0:T(8,128)S(1)} %get-tuple-element.46.refs_1_), custom_call_target="tpu_custom_call" | custom-call | flops 2415919104 | bytes 2097152 | tf_op jit(solution)/shard_map/pallas_call | solution.py:400
  85.0 8.0 %collective-permute-done.8.refs_0_ = bf16[544,128]{1,0:T(8,128)(2,1)S(1)} collective-permute-done((bf16[544,128]{1,0:T(8,128)(2,1)S(1)}, bf16[544,128]{1,0:T(8,128)(2,1)S(1)}, u32[]{:S(2)}, u32[]{:S(2)}) %collective-permute-start.8) | collective-permute-done | bytes 139296 | tf_op jit(solution)/shard_map/ppermute | solution.py:612
  94.5 3.6 %collective-permute-done.9.refs_1_ = bf16[544,128]{1,0:T(8,128)(2,1)S(1)} collective-permute-done((bf16[544,128]{1,0:T(8,128)(2,1)S(1)}, bf16[544,128]{1,0:T(8,128)(2,1)S(1)}, u32[]{:S(2)}, u32[]{:S(2)}) %collective-permute-start.9) | collective-permute-done | bytes 139296 | tf_op jit(solution)/shard_map/ppermute | solution.py:612
  98.1 1.9 %collective-permute-start.19 = (bf16[2,128,128]{2,1,0:T(8,128)(2,1)S(1)}, bf16[2,128,128]{2,1,0:T(8,128)(2,1)S(1)}, u32[]{:S(2)}, u32[]{:S(2)}) collective-permute-start(bf16[2,128,128]{2,1,0:T(8,128)(2,1)S(1)} %get-tuple-element.58), channel_id=1, source_target_pairs={{0,1},{1,0},{2,3},{3,2},{4,5},{5,4},{6,7},{7,6},{8,9},{9,8},{10,11... | collective-permute-start | bytes 196616 | tf_op jit(solution)/shard_map/ppermute | solution.py:617
  102.5 2.7 %collective-permute-done.20.refs_2_ = bf16[2,128,128]{2,1,0:T(8,128)(2,1)S(1)} collective-permute-done((bf16[2,128,128]{2,1,0:T(8,128)(2,1)S(1)}, bf16[2,128,128]{2,1,0:T(8,128)(2,1)S(1)}, u32[]{:S(2)}, u32[]{:S(2)}) %collective-permute-start.20) | collective-permute-done | bytes 65568 | tf_op jit(solution)/shard_map/ppermute | solution.py:617
  106.9 2.7 %collective-permute-done.21.refs_3_ = bf16[2,128,128]{2,1,0:T(8,128)(2,1)S(1)} collective-permute-done((bf16[2,128,128]{2,1,0:T(8,128)(2,1)S(1)}, bf16[2,128,128]{2,1,0:T(8,128)(2,1)S(1)}, u32[]{:S(2)}, u32[]{:S(2)}) %collective-permute-start.21) | collective-permute-done | bytes 65568 | tf_op jit(solution)/shard_map/ppermute | solution.py:617
  112.4 2.0 %shard_map.112 = (f32[128,2048]{1,0:T(8,128)S(1)}, bf16[512,2048]{1,0:T(8,128)(2,1)S(1)}) custom-call(bf16[2,128,128]{2,1,0:T(8,128)(2,1)S(1)} %get-tuple-element.57.refs_0_, bf16[2,128,128]{2,1,0:T(8,128)(2,1)S(1)} %collective-permute-done.19.refs_1_, bf16[2,128,128]{2,1,0:T(8,128)(2,1)S(1)} %collective-permute-done.20.refs_2_, ...), custom_call_target="tpu_custom_call" | custom-call | flops 536870912 | bytes 10485760 | tf_op jit(solution)/shard_map/pallas_call | solution.py:511
  114.5 11.6 %collective-permute-done.11.refs_2_ = bf16[2,128,128]{2,1,0:T(8,128)(2,1)S(1)} collective-permute-done((bf16[2,128,128]{2,1,0:T(8,128)(2,1)S(1)}, bf16[2,128,128]{2,1,0:T(8,128)(2,1)S(1)}, u32[]{:S(2)}, u32[]{:S(2)}) %collective-permute-start.11) | collective-permute-done | bytes 65568 | tf_op jit(solution)/shard_map/ppermute | solution.py:617
  126.2 1.5 %shard_map.114 = (bf16[128,2048]{1,0:T(8,128)(2,1)}, f32[4,32,128]{2,1,0:T(8,128)}) custom-call(bf16[2,128,128]{2,1,0:T(8,128)(2,1)S(1)} %get-tuple-element.49.refs_0_, bf16[2,128,128]{2,1,0:T(8,128)(2,1)S(1)} %collective-permute-done.10.refs_1_, bf16[2,128,128]{2,1,0:T(8,128)(2,1)S(1)} %collective-permute-done.11.refs_2_, ...), custom_call_target="tpu_custom_call" | custom-call | flops 536870912 | bytes 6291456 | tf_op jit(solution)/shard_map/pallas_call | solution.py:554
  (51 shorter events, 14.3 us)
Async XLA Ops:
  8.3 9.3 %collective-permute-start = (bf16[528,256]{1,0:T(8,128)(2,1)S(1)}, bf16[528,256]{1,0:T(8,128)(2,1)S(1)}, u32[]{:S(2)}, u32[]{:S(2)}) collective-permute-start(bf16[528,256]{1,0:T(8,128)(2,1)S(1)} %get-tuple-element.41), channel_id=1, source_target_pairs={{0,0},{1,4},{2,2},{3,6},{4,1},{5,5},{6,3},{7,7},{8,9},{9,13},{10,1... | collective-permute-start | bytes 811016 | tf_op jit(solution)/shard_map/ppermute | solution.py:596
  9.0 17.3 %collective-permute-start.1 = (bf16[528,256]{1,0:T(8,128)(2,1)S(1)}, bf16[528,256]{1,0:T(8,128)(2,1)S(1)}, u32[]{:S(2)}, u32[]{:S(2)}) collective-permute-start(bf16[528,256]{1,0:T(8,128)(2,1)S(1)} %get-tuple-element.42), channel_id=1, source_target_pairs={{0,8},{1,12},{2,10},{3,14},{4,9},{5,13},{6,11},{7,15},{8,1},{9,5},... | collective-permute-start | bytes 811016 | tf_op jit(solution)/shard_map/ppermute | solution.py:596
  13.3 13.0 %collective-permute-start.2 = (bf16[528,256]{1,0:T(8,128)(2,1)S(1)}, bf16[528,256]{1,0:T(8,128)(2,1)S(1)}, u32[]{:S(2)}, u32[]{:S(2)}) collective-permute-start(bf16[528,256]{1,0:T(8,128)(2,1)S(1)} %get-tuple-element.43), channel_id=1, source_target_pairs={{0,16},{1,20},{2,18},{3,22},{4,17},{5,21},{6,19},{7,23},{8,25},{9,... | collective-permute-start | bytes 811016 | tf_op jit(solution)/shard_map/ppermute | solution.py:585
  15.9 96.2 %collective-permute-start.22 = (bf16[512,2048]{1,0:T(8,128)(2,1)S(1)}, bf16[512,2048]{1,0:T(8,128)(2,1)S(1)}, u32[]{:S(2)}, u32[]{:S(2)}) collective-permute-start(bf16[512,2048]{1,0:T(8,128)(2,1)S(1)} %copy-done.2), channel_id=1, source_target_pairs={{0,1},{1,0},{2,3},{3,2},{4,5},{5,4},{6,7},{7,6},{8,9},{9,8},{10,11... | collective-permute-start | bytes 6291464 | tf_op jit(solution)/shard_map/ppermute | solution.py:576
  17.6 24.2 %collective-permute-start.3 = (bf16[528,256]{1,0:T(8,128)(2,1)S(1)}, bf16[528,256]{1,0:T(8,128)(2,1)S(1)}, u32[]{:S(2)}, u32[]{:S(2)}) collective-permute-start(bf16[528,256]{1,0:T(8,128)(2,1)S(1)} %get-tuple-element.44), channel_id=1, source_target_pairs={{0,24},{1,28},{2,26},{3,30},{4,25},{5,29},{6,27},{7,31},{8,17},{9,... | collective-permute-start | bytes 811016 | tf_op jit(solution)/shard_map/ppermute | solution.py:585
  17.6 25.7 %collective-permute-start.4 = (bf16[528,256]{1,0:T(8,128)(2,1)S(1)}, bf16[528,256]{1,0:T(8,128)(2,1)S(1)}, u32[]{:S(2)}, u32[]{:S(2)}) collective-permute-start(bf16[528,256]{1,0:T(8,128)(2,1)S(1)} %collective-permute-done.refs_0_), channel_id=1, source_target_pairs={{0,1},{1,0},{2,3},{3,2},{4,5},{5,4},{6,7},{7,6},{8,9},{9,8},{10,11... | collective-permute-start | bytes 811016 | tf_op jit(solution)/shard_map/ppermute | solution.py:601
  26.3 17.6 %collective-permute-start.5 = (bf16[528,256]{1,0:T(8,128)(2,1)S(1)}, bf16[528,256]{1,0:T(8,128)(2,1)S(1)}, u32[]{:S(2)}, u32[]{:S(2)}) collective-permute-start(bf16[528,256]{1,0:T(8,128)(2,1)S(1)} %collective-permute-done.1.refs_1_), channel_id=1, source_target_pairs={{0,1},{1,0},{2,3},{3,2},{4,5},{5,4},{6,7},{7,6},{8,9},{9,8},{10,11... | collective-permute-start | bytes 811016 | tf_op jit(solution)/shard_map/ppermute | solution.py:601
  26.3 19.1 %collective-permute-start.6 = (bf16[528,256]{1,0:T(8,128)(2,1)S(1)}, bf16[528,256]{1,0:T(8,128)(2,1)S(1)}, u32[]{:S(2)}, u32[]{:S(2)}) collective-permute-start(bf16[528,256]{1,0:T(8,128)(2,1)S(1)} %collective-permute-done.2.refs_2_), channel_id=1, source_target_pairs={{0,1},{1,0},{2,3},{3,2},{4,5},{5,4},{6,7},{7,6},{8,9},{9,8},{10,11... | collective-permute-start | bytes 811016 | tf_op jit(solution)/shard_map/ppermute | solution.py:601
  41.8 14.9 %collective-permute-start.23 = (bf16[256,1024]{1,0:T(8,128)(2,1)S(1)}, bf16[256,1024]{1,0:T(8,128)(2,1)S(1)}, u32[]{:S(2)}, u32[]{:S(2)}) collective-permute-start(bf16[256,1024]{1,0:T(8,128)(2,1)S(1)} %get-tuple-element.61), channel_id=1, source_target_pairs={{0,2},{1,3},{2,0},{3,1},{4,6},{5,7},{6,4},{7,5},{8,10},{9,11},{10,... | collective-permute-start | bytes 1572872 | tf_op jit(solution)/shard_map/ppermute | solution.py:588
  43.3 24.5 %collective-permute-start.13 = (bf16[256,1024]{1,0:T(8,128)(2,1)S(1)}, bf16[256,1024]{1,0:T(8,128)(2,1)S(1)}, u32[]{:S(2)}, u32[]{:S(2)}) collective-permute-start(bf16[256,1024]{1,0:T(8,128)(2,1)S(1)} %get-tuple-element.53), channel_id=1, source_target_pairs={{0,2},{1,3},{2,0},{3,1},{4,6},{5,7},{6,4},{7,5},{8,10},{9,11},{10,... | collective-permute-start | bytes 1572872 | tf_op jit(solution)/shard_map/ppermute | solution.py:588
  43.9 34.3 %collective-permute-start.14 = (bf16[256,1024]{1,0:T(8,128)(2,1)S(1)}, bf16[256,1024]{1,0:T(8,128)(2,1)S(1)}, u32[]{:S(2)}, u32[]{:S(2)}) collective-permute-start(bf16[256,1024]{1,0:T(8,128)(2,1)S(1)} %get-tuple-element.54), channel_id=1, source_target_pairs={{0,2},{1,3},{2,0},{3,1},{4,6},{5,7},{6,4},{7,5},{8,10},{9,11},{10,... | collective-permute-start | bytes 1572872 | tf_op jit(solution)/shard_map/ppermute | solution.py:592
  50.4 55.4 %collective-permute-start.27 = (bf16[2,128,2048]{2,1,0:T(8,128)(2,1)S(1)}, bf16[2,128,2048]{2,1,0:T(8,128)(2,1)S(1)}, u32[]{:S(2)}, u32[]{:S(2)}) collective-permute-start(bf16[2,128,2048]{2,1,0:T(8,128)(2,1)S(1)} %get-tuple-element.66), channel_id=1, source_target_pairs={{0,1},{1,0},{2,3},{3,2},{4,5},{5,4},{6,7},{7,6},{8,9},{9,8},{10,11... | collective-permute-start | bytes 3145736 | tf_op jit(solution)/shard_map/ppermute | solution.py:599
  56.6 21.5 %collective-permute-start.17 = (bf16[544,128]{1,0:T(8,128)(2,1)S(1)}, bf16[544,128]{1,0:T(8,128)(2,1)S(1)}, u32[]{:S(2)}, u32[]{:S(2)}) collective-permute-start(bf16[544,128]{1,0:T(8,128)(2,1)S(1)} %get-tuple-element.55), channel_id=1, source_target_pairs={{24,0},{28,1},{26,2},{30,3},{25,4},{29,5},{27,6},{31,7},{17,8},{21... | collective-permute-start | bytes 417800 | tf_op jit(solution)/shard_map/ppermute | solution.py:609
  67.9 34.5 %collective-permute-start.24 = (bf16[256,1024]{1,0:T(8,128)(2,1)S(1)}, bf16[256,1024]{1,0:T(8,128)(2,1)S(1)}, u32[]{:S(2)}, u32[]{:S(2)}) collective-permute-start(bf16[256,1024]{1,0:T(8,128)(2,1)S(1)} %collective-permute-done.23.refs_6_), channel_id=1, source_target_pairs={{0,4},{4,0},{8,12},{12,8},{16,20},{20,16},{24,28},{28,24},{1,5},{5... | collective-permute-start | bytes 1572872 | tf_op jit(solution)/shard_map/ppermute | solution.py:590
  78.1 32.0 %collective-permute-start.25 = (bf16[256,1024]{1,0:T(8,128)(2,1)S(1)}, bf16[256,1024]{1,0:T(8,128)(2,1)S(1)}, u32[]{:S(2)}, u32[]{:S(2)}) collective-permute-start(bf16[256,1024]{1,0:T(8,128)(2,1)S(1)} %collective-permute-done.23.refs_6_), channel_id=1, source_target_pairs={{0,1},{1,0},{2,3},{3,2},{4,5},{5,4},{6,7},{7,6},{8,9},{9,8},{10,11... | collective-permute-start | bytes 1572872 | tf_op jit(solution)/shard_map/ppermute | solution.py:593
  78.1 5.9 %collective-permute-start.18 = (bf16[544,128]{1,0:T(8,128)(2,1)S(1)}, bf16[544,128]{1,0:T(8,128)(2,1)S(1)}, u32[]{:S(2)}, u32[]{:S(2)}) collective-permute-start(bf16[544,128]{1,0:T(8,128)(2,1)S(1)} %get-tuple-element.56), channel_id=1, source_target_pairs={{0,0},{4,1},{2,2},{6,3},{1,4},{5,5},{3,6},{7,7},{9,8},{13,9},{11,1... | collective-permute-start | bytes 417800 | tf_op jit(solution)/shard_map/ppermute | solution.py:609
  84.0 9.0 %collective-permute-start.8 = (bf16[544,128]{1,0:T(8,128)(2,1)S(1)}, bf16[544,128]{1,0:T(8,128)(2,1)S(1)}, u32[]{:S(2)}, u32[]{:S(2)}) collective-permute-start(bf16[544,128]{1,0:T(8,128)(2,1)S(1)} %get-tuple-element.47), channel_id=1, source_target_pairs={{16,0},{20,1},{18,2},{22,3},{17,4},{21,5},{19,6},{23,7},{25,8},{29... | collective-permute-start | bytes 417800 | tf_op jit(solution)/shard_map/ppermute | solution.py:612
  93.0 5.1 %collective-permute-start.9 = (bf16[544,128]{1,0:T(8,128)(2,1)S(1)}, bf16[544,128]{1,0:T(8,128)(2,1)S(1)}, u32[]{:S(2)}, u32[]{:S(2)}) collective-permute-start(bf16[544,128]{1,0:T(8,128)(2,1)S(1)} %get-tuple-element.48), channel_id=1, source_target_pairs={{8,0},{12,1},{10,2},{14,3},{9,4},{13,5},{11,6},{15,7},{1,8},{5,9},... | collective-permute-start | bytes 417800 | tf_op jit(solution)/shard_map/ppermute | solution.py:612
  102.4 8.9 %collective-permute-start.26 = (bf16[256,1024]{1,0:T(8,128)(2,1)S(1)}, bf16[256,1024]{1,0:T(8,128)(2,1)S(1)}, u32[]{:S(2)}, u32[]{:S(2)}) collective-permute-start(bf16[256,1024]{1,0:T(8,128)(2,1)S(1)} %collective-permute-done.24.refs_7_), channel_id=1, source_target_pairs={{0,1},{1,0},{2,3},{3,2},{4,5},{5,4},{6,7},{7,6},{8,9},{9,8},{10,11... | collective-permute-start | bytes 1572872 | tf_op jit(solution)/shard_map/ppermute | solution.py:593
  109.6 16.6 %collective-permute-start.15 = (bf16[256,1024]{1,0:T(8,128)(2,1)S(1)}, bf16[256,1024]{1,0:T(8,128)(2,1)S(1)}, u32[]{:S(2)}, u32[]{:S(2)}) collective-permute-start(bf16[256,1024]{1,0:T(8,128)(2,1)S(1)} %collective-permute-done.13.refs_4_), channel_id=1, source_target_pairs={{0,1},{1,0},{2,3},{3,2},{4,5},{5,4},{6,7},{7,6},{8,9},{9,8},{10,11... | collective-permute-start | bytes 1572872 | tf_op jit(solution)/shard_map/ppermute | solution.py:593
  109.7 16.5 %collective-permute-start.16 = (bf16[256,1024]{1,0:T(8,128)(2,1)S(1)}, bf16[256,1024]{1,0:T(8,128)(2,1)S(1)}, u32[]{:S(2)}, u32[]{:S(2)}) collective-permute-start(bf16[256,1024]{1,0:T(8,128)(2,1)S(1)} %collective-permute-done.14.refs_5_), channel_id=1, source_target_pairs={{0,1},{1,0},{2,3},{3,2},{4,5},{5,4},{6,7},{7,6},{8,9},{9,8},{10,11... | collective-permute-start | bytes 1572872 | tf_op jit(solution)/shard_map/ppermute | solution.py:593
  110.1 16.1 %collective-permute-start.28 = (bf16[128,2048]{1,0:T(8,128)(2,1)S(1)}, bf16[128,2048]{1,0:T(8,128)(2,1)S(1)}, u32[]{:S(2)}, u32[]{:S(2)}) collective-permute-start(bf16[128,2048]{1,0:T(8,128)(2,1)S(1)} %shard_map.113), channel_id=1, source_target_pairs={{0,2},{1,3},{2,0},{3,1},{4,6},{5,7},{6,4},{7,5},{8,10},{9,11},{10,... | collective-permute-start | bytes 1572872 | tf_op jit(solution)/shard_map/ppermute | solution.py:603
  111.3 14.8 %collective-permute-start.11 = (bf16[2,128,128]{2,1,0:T(8,128)(2,1)S(1)}, bf16[2,128,128]{2,1,0:T(8,128)(2,1)S(1)}, u32[]{:S(2)}, u32[]{:S(2)}) collective-permute-start(bf16[2,128,128]{2,1,0:T(8,128)(2,1)S(1)} %get-tuple-element.51), channel_id=1, source_target_pairs={{0,2},{1,3},{2,0},{3,1},{4,6},{5,7},{6,4},{7,5},{8,10},{9,11},{10,... | collective-permute-start | bytes 196616 | tf_op jit(solution)/shard_map/ppermute | solution.py:617
  112.1 14.0 %collective-permute-start.12 = (bf16[2,128,128]{2,1,0:T(8,128)(2,1)S(1)}, bf16[2,128,128]{2,1,0:T(8,128)(2,1)S(1)}, u32[]{:S(2)}, u32[]{:S(2)}) collective-permute-start(bf16[2,128,128]{2,1,0:T(8,128)(2,1)S(1)} %get-tuple-element.52), channel_id=1, source_target_pairs={{0,3},{1,2},{2,1},{3,0},{4,7},{5,6},{6,5},{7,4},{8,11},{9,10},{10,... | collective-permute-start | bytes 196616 | tf_op jit(solution)/shard_map/ppermute | solution.py:617
  (8 other events, 73.5 us)

commit v6 on v5

--- a/solution.py
+++ b/solution.py
@@ -17,6 +17,7 @@
 SEQ, TENSOR = "seq", "tensor"
 BOTH = (SEQ, TENSOR)
 EXTRA = 16
+SLABS = 4
 MIB = 1024 * 1024
 
 
@@ -63,6 +64,19 @@
 
 def shape(dims, kind=jnp.bfloat16):
     return jax.ShapeDtypeStruct(dims, kind)
+
+
+def slab_copies(source, column, buf, sems):
+    step = buf.shape[0] // SLABS
+    cols = pl.ds(column, buf.shape[1])
+    return [
+        pltpu.make_async_copy(
+            source.at[pl.ds(r * step, step), cols],
+            buf.at[pl.ds(r * step, step), :],
+            sems.at[r],
+        )
+        for r in range(SLABS)
+    ]
 
 
 def unit_heads(normed, w_qk, w_value, outs, clusters, steps, width):
@@ -183,12 +197,14 @@
 
 
 def project_near_body(
-    normed, w_qk, w_value, clusters, w_up, out_low, out_high, next_half, sem, *, width
+    normed, w_qk, w_value, clusters, w_up, out_low, out_high, next_half, sems, *, width
 ):
-    copy = pltpu.make_async_copy(w_up.at[:, pl.ds(0, next_half.shape[1])], next_half, sem)
-    copy.start()
+    copies = slab_copies(w_up, 0, next_half, sems)
+    for copy in copies:
+        copy.start()
     unit_heads(normed, w_qk, w_value, (out_low, out_high), clusters, (0, 1), width)
-    copy.wait()
+    for copy in copies:
+        copy.wait()
 
 
 def project_near(normed, w_qk, w_value, clusters, w_up, width):
@@ -199,28 +215,25 @@
         out_shape=(message, message, shape((depth, w_up.shape[1] // 2))),
         in_specs=[vmem_spec()] * 4 + [any_spec()],
         out_specs=(vmem_spec(),) * 3,
-        scratch_shapes=[pltpu.SemaphoreType.DMA],
+        scratch_shapes=[pltpu.SemaphoreType.DMA((SLABS,))],
         compiler_params=params(16),
         cost_estimate=cost(8 * rows * depth * width, 2 * rows * depth + 8 * depth * width),
     )(normed, w_qk, w_value, clusters, held(w_up))
 
 
-def up_body(normed, first, w_up, w_down, hidden, next_half, second, sems):
+def up_body(normed, first, w_up, w_down, hidden, next_half, second, sems, later_sems):
     half = first.shape[1]
-    copies = (
-        pltpu.make_async_copy(w_up.at[:, pl.ds(half, half)], second, sems.at[0]),
-        pltpu.make_async_copy(
-            w_down.at[:, pl.ds(0, next_half.shape[1])], next_half, sems.at[1]
-        ),
-    )
-    for copy in copies:
+    copies = slab_copies(w_up, half, second, sems)
+    later = slab_copies(w_down, 0, next_half, later_sems)
+    for copy in copies + later:
         copy.start()
     for at, weights in enumerate((first, second)):
-        if at == 1:
-            copies[0].wait()
+        for copy in copies if at == 1 else []:
+            copy.wait()
         grown = jnp.dot(normed[...], weights[...], preferred_element_type=jnp.float32)
         hidden[:, at * half : (at + 1) * half] = jnp.maximum(grown, 0.0).astype(jnp.bfloat16)
-    copies[1].wait()
+    for copy in later:
+        copy.wait()
 
 
 def up(normed, first, w_up, w_down):
@@ -233,24 +246,26 @@
         out_specs=(vmem_spec(), vmem_spec()),
         scratch_shapes=[
             pltpu.VMEM((depth, units // 2), jnp.bfloat16),
-            pltpu.SemaphoreType.DMA((2,)),
+            pltpu.SemaphoreType.DMA((SLABS,)),
+            pltpu.SemaphoreType.DMA((SLABS,)),
         ],
         compiler_params=params(24),
         cost_estimate=cost(2 * rows * depth * units, 2 * depth * units + 4 * rows * depth),
     )(normed, first, held(w_up), held(w_down))
 
 
-def down_body(hidden, first, w_down, mine, far, away, second, held_rows, sem, *, share):
+def down_body(hidden, first, w_down, mine, far, away, second, held_rows, sems, *, share):
     at = lax.axis_index(TENSOR)
     half = first.shape[1]
-    copy = pltpu.make_async_copy(w_down.at[:, pl.ds(half, half)], second, sem)
-    copy.start()
+    copies = slab_copies(w_down, half, second, sems)
+    for copy in copies:
+        copy.start()
 
     def quarter(turn):
         return held_rows[pl.ds(pl.multiple_of((at ^ turn) * share, share), share), :]
 
     for part, weights in enumerate((first, second)):
-        if part == 1:
+        for copy in copies if part == 1 else []:
             copy.wait()
         cols = slice(part * half, (part + 1) * half)
         held_rows[...] = jnp.dot(
@@ -277,7 +292,7 @@
         scratch_shapes=[
             pltpu.VMEM((units, depth // 2), jnp.bfloat16),
             pltpu.VMEM((rows, depth // 2), jnp.float32),
-            pltpu.SemaphoreType.DMA,
+            pltpu.SemaphoreType.DMA((SLABS,)),
         ],
         compiler_params=params(24),
         cost_estimate=cost(2 * rows * depth * units, 2 * depth * units + 6 * rows * depth),

time: 128 us -> 129 us (level)
  Pallas kernels: 31.6 us -> 33.9 us
    ppermute x2, waiting for transfers between devices: 10.3 us -> 8.65 us  [by_heads(): here = lax.ppermute(out_parts.pop(0), TENSOR, swaps[2])]
    pallas_call x1, Pallas kernels: 4.98 us -> 6.37 us  [down(): pl.pallas_call(functools.partial(down_body, share=share), out_shape=(shap...]
  transfers between devices with their start and end apart: 29 -> 29, of which waited for: 10 -> 9; matrix products, arithmetic and copies ran while one was open for 0% -> 0% of each run, Pallas kernels for 18% -> 19%
where the time goes in v6:
time: 129 us; the launch traced here: 128 us
  waiting for transfers between devices  55.8 us (43%)
  starting transfers between devices  37.9 us (29%)
  Pallas kernels  33.9 us (26%)
    ppermute x6, waiting for transfers between devices, by_heads(): lax.ppermute(away[d - 1], TENSOR, swaps[d])  17.9 us
    ppermute x4, waiting for transfers between devices, by_heads(): back[k] = lax.ppermute(result, BOTH, turned(steps[k]))  12.5 us
    ppermute x4, starting transfers between devices, by_heads(): other[k] = lax.ppermute(own[k], TENSOR, swaps[1])  12.4 us
    pallas_call x2, Pallas kernels, attend(): pl.pallas_call(functools.partial(attend_body, heads=heads, width=width, o...  10.6 us
    ppermute x1, waiting for transfers between devices, by_heads(): there = lax.ppermute(out_parts.pop(0), TENSOR, swaps[2])  9.68 us
    ppermute x2, waiting for transfers between devices, by_heads(): here = lax.ppermute(out_parts.pop(0), TENSOR, swaps[2])  8.65 us
    ppermute x4, starting transfers between devices, by_heads(): own[k] = lax.ppermute(messages[k], BOTH, steps[k])  7.62 us
    ppermute x4, waiting for transfers between devices, by_heads(): own[k] = lax.ppermute(messages[k], BOTH, steps[k])  7.1 us
  transfers between devices with their start and end apart: 29, of which 9 were waited for; matrix products, arithmetic and copies ran while one was open for 0% of the time, Pallas kernels for 19%

profile of v6, /device:TPU:0, one launch (start us, length us, event | category | flops | bytes accessed | tf_op | source)
XLA Modules:
  0.0 128.4 jit_solution(7224119631451820618)
XLA Ops:
  0.6 4.3 %shard_map.104 = (bf16[528,256]{1,0:T(8,128)(2,1)S(1)}, bf16[528,256]{1,0:T(8,128)(2,1)S(1)}, bf16[512,2048]{1,0:T(8,128)(2,1)S(1)}, s32[4,512]{1,0:T(4,128)S(1)...) custom-call(bf16[512,2048]{1,0:T(8,128)(2,1)} %refs_10_.1, ...), custom_call_target="tpu_custom_call" | custom-call | flops 1073741824 | bytes 5242880 | tf_op jit(solution)/shard_map/pallas_call | solution.py:170
  5.0 3.4 %shard_map.105 = (bf16[528,256]{1,0:T(8,128)(2,1)S(1)}, bf16[528,256]{1,0:T(8,128)(2,1)S(1)}, bf16[2048,1024]{1,0:T(8,128)(2,1)S(1)}) custom-call(bf16[512,2048]{1,0:T(8,128)(2,1)S(1)} %get-tuple-element.37.normed, bf16[2048,256]{1,0:T(8,128)(2,1)S(1)} %get-tuple-element.38.w_qk, bf16[2048,256]{1,0:T(8,128)(2,1)S(1)} %get-tuple-element.39.w_value, ...), custom_call_target="tpu_custom_call" | custom-call | flops 1073741824 | bytes 4194304 | tf_op jit(solution)/shard_map/pallas_call | solution.py:213
  9.0 4.3 %collective-permute-start.1 = (bf16[528,256]{1,0:T(8,128)(2,1)S(1)}, bf16[528,256]{1,0:T(8,128)(2,1)S(1)}, u32[]{:S(2)}, u32[]{:S(2)}) collective-permute-start(bf16[528,256]{1,0:T(8,128)(2,1)S(1)} %get-tuple-element.42), channel_id=1, source_target_pairs={{0,8},{1,12},{2,10},{3,14},{4,9},{5,13},{6,11},{7,15},{8,1},{9,5},... | collective-permute-start | bytes 811016 | tf_op jit(solution)/shard_map/ppermute | solution.py:611
  13.4 2.6 %collective-permute-start.2 = (bf16[528,256]{1,0:T(8,128)(2,1)S(1)}, bf16[528,256]{1,0:T(8,128)(2,1)S(1)}, u32[]{:S(2)}, u32[]{:S(2)}) collective-permute-start(bf16[528,256]{1,0:T(8,128)(2,1)S(1)} %get-tuple-element.43), channel_id=1, source_target_pairs={{0,16},{1,20},{2,18},{3,22},{4,17},{5,21},{6,19},{7,23},{8,25},{9,... | collective-permute-start | bytes 811016 | tf_op jit(solution)/shard_map/ppermute | solution.py:600
  16.0 1.7 %collective-permute-start.22 = (bf16[512,2048]{1,0:T(8,128)(2,1)S(1)}, bf16[512,2048]{1,0:T(8,128)(2,1)S(1)}, u32[]{:S(2)}, u32[]{:S(2)}) collective-permute-start(bf16[512,2048]{1,0:T(8,128)(2,1)S(1)} %copy-done.2), channel_id=1, source_target_pairs={{0,1},{1,0},{2,3},{3,2},{4,5},{5,4},{6,7},{7,6},{8,9},{9,8},{10,11... | collective-permute-start | bytes 6291464 | tf_op jit(solution)/shard_map/ppermute | solution.py:591
  17.7 1.6 %collective-permute-start.4 = (bf16[528,256]{1,0:T(8,128)(2,1)S(1)}, bf16[528,256]{1,0:T(8,128)(2,1)S(1)}, u32[]{:S(2)}, u32[]{:S(2)}) collective-permute-start(bf16[528,256]{1,0:T(8,128)(2,1)S(1)} %collective-permute-done.refs_0_), channel_id=1, source_target_pairs={{0,1},{1,0},{2,3},{3,2},{4,5},{5,4},{6,7},{7,6},{8,9},{9,8},{10,11... | collective-permute-start | bytes 811016 | tf_op jit(solution)/shard_map/ppermute | solution.py:616
  19.2 7.1 %collective-permute-done.1.refs_1_ = bf16[528,256]{1,0:T(8,128)(2,1)S(1)} collective-permute-done((bf16[528,256]{1,0:T(8,128)(2,1)S(1)}, bf16[528,256]{1,0:T(8,128)(2,1)S(1)}, u32[]{:S(2)}, u32[]{:S(2)}) %collective-permute-start.1) | collective-permute-done | bytes 270368 | tf_op jit(solution)/shard_map/ppermute | solution.py:611
  26.4 10.8 %collective-permute-start.6 = (bf16[528,256]{1,0:T(8,128)(2,1)S(1)}, bf16[528,256]{1,0:T(8,128)(2,1)S(1)}, u32[]{:S(2)}, u32[]{:S(2)}) collective-permute-start(bf16[528,256]{1,0:T(8,128)(2,1)S(1)} %collective-permute-done.2.refs_2_), channel_id=1, source_target_pairs={{0,1},{1,0},{2,3},{3,2},{4,5},{5,4},{6,7},{7,6},{8,9},{9,8},{10,11... | collective-permute-start | bytes 811016 | tf_op jit(solution)/shard_map/ppermute | solution.py:616
  37.1 5.5 %shard_map.110 = (bf16[512,2048]{1,0:T(8,128)(2,1)S(1)}, bf16[2048,1024]{1,0:T(8,128)(2,1)S(1)}) custom-call(bf16[512,2048]{1,0:T(8,128)(2,1)S(1)} %get-tuple-element.37.normed, bf16[2048,1024]{1,0:T(8,128)(2,1)S(1)} %get-tuple-element.62.first, bf16[2048,2048]{1,0:T(8,128)(2,1)} %w_up.3, bf16[2048,2048]{1,0:T(8,128)(2,1)} %w_down.3), custom_call_target="tpu_custom_call" | custom-call | flops 4294967296 | bytes 12582912 | tf_op jit(solution)/shard_map/pallas_call | solution.py:242
  42.7 1.6 %collective-permute-start.23 = (bf16[256,1024]{1,0:T(8,128)(2,1)S(1)}, bf16[256,1024]{1,0:T(8,128)(2,1)S(1)}, u32[]{:S(2)}, u32[]{:S(2)}) collective-permute-start(bf16[256,1024]{1,0:T(8,128)(2,1)S(1)} %get-tuple-element.61), channel_id=1, source_target_pairs={{0,2},{1,3},{2,0},{3,1},{4,6},{5,7},{6,4},{7,5},{8,10},{9,11},{10,... | collective-permute-start | bytes 1572872 | tf_op jit(solution)/shard_map/ppermute | solution.py:603
  44.8 1.5 %collective-permute-start.14 = (bf16[256,1024]{1,0:T(8,128)(2,1)S(1)}, bf16[256,1024]{1,0:T(8,128)(2,1)S(1)}, u32[]{:S(2)}, u32[]{:S(2)}) collective-permute-start(bf16[256,1024]{1,0:T(8,128)(2,1)S(1)} %get-tuple-element.54), channel_id=1, source_target_pairs={{0,2},{1,3},{2,0},{3,1},{4,6},{5,7},{6,4},{7,5},{8,10},{9,11},{10,... | collective-permute-start | bytes 1572872 | tf_op jit(solution)/shard_map/ppermute | solution.py:607
  46.3 6.4 %shard_map.111 = (f32[128,2048]{1,0:T(8,128)S(1)}, f32[128,2048]{1,0:T(8,128)S(1)}, bf16[2,128,2048]{2,1,0:T(8,128)(2,1)S(1)}) custom-call(bf16[512,2048]{1,0:T(8,128)(2,1)S(1)} %get-tuple-element.63.hidden, bf16[2048,1024]{1,0:T(8,128)(2,1)S(1)} %get-tuple-element.64.first, bf16[2048,2048]{1,0:T(8,128)(2,1)} %w_down.3), custom_call_target="tpu_custom_call" | custom-call | flops 4294967296 | bytes 14680064 | tf_op jit(solution)/shard_map/pallas_call | solution.py:283
  53.2 5.4 %shard_map.106 = (bf16[544,128]{1,0:T(8,128)(2,1)S(1)}, bf16[544,128]{1,0:T(8,128)(2,1)S(1)}, bf16[8,512,256]{2,1,0:T(8,128)(2,1)S(1)}, f32[8,8,512]{2,1,0:T(8,128)S(1)}) custom-call(bf16[528,256]{1,0:T(8,128)(2,1)S(1)} %collective-permute-done.refs_0_, bf16[528,256]{1,0:T(8,128)(2,1)S(1)} %collective-permute-done.1.refs_1_, ...), custom_call_target="tpu_custom_call" | custom-call | flops 2415919104 | bytes 2097152 | tf_op jit(solution)/shard_map/pallas_call | solution.py:415
  60.1 8.7 %collective-permute-done.13.refs_4_ = bf16[256,1024]{1,0:T(8,128)(2,1)S(1)} collective-permute-done((bf16[256,1024]{1,0:T(8,128)(2,1)S(1)}, bf16[256,1024]{1,0:T(8,128)(2,1)S(1)}, u32[]{:S(2)}, u32[]{:S(2)}) %collective-permute-start.13) | collective-permute-done | bytes 524320 | tf_op jit(solution)/shard_map/ppermute | solution.py:603
  69.4 9.7 %collective-permute-done.14.refs_5_ = bf16[256,1024]{1,0:T(8,128)(2,1)S(1)} collective-permute-done((bf16[256,1024]{1,0:T(8,128)(2,1)S(1)}, bf16[256,1024]{1,0:T(8,128)(2,1)S(1)}, u32[]{:S(2)}, u32[]{:S(2)}) %collective-permute-start.14) | collective-permute-done | bytes 524320 | tf_op jit(solution)/shard_map/ppermute | solution.py:607
  79.7 5.2 %shard_map.107 = (bf16[544,128]{1,0:T(8,128)(2,1)S(1)}, bf16[544,128]{1,0:T(8,128)(2,1)S(1)}) custom-call(bf16[8,512,256]{2,1,0:T(8,128)(2,1)S(1)} %get-tuple-element.45.refs_0_, f32[8,8,512]{2,1,0:T(8,128)S(1)} %get-tuple-element.46.refs_1_), custom_call_target="tpu_custom_call" | custom-call | flops 2415919104 | bytes 2097152 | tf_op jit(solution)/shard_map/pallas_call | solution.py:415
  85.1 8.8 %collective-permute-done.8.refs_0_ = bf16[544,128]{1,0:T(8,128)(2,1)S(1)} collective-permute-done((bf16[544,128]{1,0:T(8,128)(2,1)S(1)}, bf16[544,128]{1,0:T(8,128)(2,1)S(1)}, u32[]{:S(2)}, u32[]{:S(2)}) %collective-permute-start.8) | collective-permute-done | bytes 139296 | tf_op jit(solution)/shard_map/ppermute | solution.py:627
  95.4 3.6 %collective-permute-done.9.refs_1_ = bf16[544,128]{1,0:T(8,128)(2,1)S(1)} collective-permute-done((bf16[544,128]{1,0:T(8,128)(2,1)S(1)}, bf16[544,128]{1,0:T(8,128)(2,1)S(1)}, u32[]{:S(2)}, u32[]{:S(2)}) %collective-permute-start.9) | collective-permute-done | bytes 139296 | tf_op jit(solution)/shard_map/ppermute | solution.py:627
  99.0 1.7 %collective-permute-start.19 = (bf16[2,128,128]{2,1,0:T(8,128)(2,1)S(1)}, bf16[2,128,128]{2,1,0:T(8,128)(2,1)S(1)}, u32[]{:S(2)}, u32[]{:S(2)}) collective-permute-start(bf16[2,128,128]{2,1,0:T(8,128)(2,1)S(1)} %get-tuple-element.58), channel_id=1, source_target_pairs={{0,1},{1,0},{2,3},{3,2},{4,5},{5,4},{6,7},{7,6},{8,9},{9,8},{10,11... | collective-permute-start | bytes 196616 | tf_op jit(solution)/shard_map/ppermute | solution.py:632
  103.3 2.7 %collective-permute-done.20.refs_2_ = bf16[2,128,128]{2,1,0:T(8,128)(2,1)S(1)} collective-permute-done((bf16[2,128,128]{2,1,0:T(8,128)(2,1)S(1)}, bf16[2,128,128]{2,1,0:T(8,128)(2,1)S(1)}, u32[]{:S(2)}, u32[]{:S(2)}) %collective-permute-start.20) | collective-permute-done | bytes 65568 | tf_op jit(solution)/shard_map/ppermute | solution.py:632
  107.6 2.7 %collective-permute-done.21.refs_3_ = bf16[2,128,128]{2,1,0:T(8,128)(2,1)S(1)} collective-permute-done((bf16[2,128,128]{2,1,0:T(8,128)(2,1)S(1)}, bf16[2,128,128]{2,1,0:T(8,128)(2,1)S(1)}, u32[]{:S(2)}, u32[]{:S(2)}) %collective-permute-start.21) | collective-permute-done | bytes 65568 | tf_op jit(solution)/shard_map/ppermute | solution.py:632
  113.2 2.0 %shard_map.112 = (f32[128,2048]{1,0:T(8,128)S(1)}, bf16[512,2048]{1,0:T(8,128)(2,1)S(1)}) custom-call(bf16[2,128,128]{2,1,0:T(8,128)(2,1)S(1)} %get-tuple-element.57.refs_0_, bf16[2,128,128]{2,1,0:T(8,128)(2,1)S(1)} %collective-permute-done.19.refs_1_, bf16[2,128,128]{2,1,0:T(8,128)(2,1)S(1)} %collective-permute-done.20.refs_2_, ...), custom_call_target="tpu_custom_call" | custom-call | flops 536870912 | bytes 10485760 | tf_op jit(solution)/shard_map/pallas_call | solution.py:526
  115.2 11.6 %collective-permute-done.11.refs_2_ = bf16[2,128,128]{2,1,0:T(8,128)(2,1)S(1)} collective-permute-done((bf16[2,128,128]{2,1,0:T(8,128)(2,1)S(1)}, bf16[2,128,128]{2,1,0:T(8,128)(2,1)S(1)}, u32[]{:S(2)}, u32[]{:S(2)}) %collective-permute-start.11) | collective-permute-done | bytes 65568 | tf_op jit(solution)/shard_map/ppermute | solution.py:632
  126.9 1.5 %shard_map.114 = (bf16[128,2048]{1,0:T(8,128)(2,1)}, f32[4,32,128]{2,1,0:T(8,128)}) custom-call(bf16[2,128,128]{2,1,0:T(8,128)(2,1)S(1)} %get-tuple-element.49.refs_0_, bf16[2,128,128]{2,1,0:T(8,128)(2,1)S(1)} %collective-permute-done.10.refs_1_, bf16[2,128,128]{2,1,0:T(8,128)(2,1)S(1)} %collective-permute-done.11.refs_2_, ...), custom_call_target="tpu_custom_call" | custom-call | flops 536870912 | bytes 6291456 | tf_op jit(solution)/shard_map/pallas_call | solution.py:569
  (51 shorter events, 13.3 us)
Async XLA Ops:
  8.4 9.3 %collective-permute-start = (bf16[528,256]{1,0:T(8,128)(2,1)S(1)}, bf16[528,256]{1,0:T(8,128)(2,1)S(1)}, u32[]{:S(2)}, u32[]{:S(2)}) collective-permute-start(bf16[528,256]{1,0:T(8,128)(2,1)S(1)} %get-tuple-element.41), channel_id=1, source_target_pairs={{0,0},{1,4},{2,2},{3,6},{4,1},{5,5},{6,3},{7,7},{8,9},{9,13},{10,1... | collective-permute-start | bytes 811016 | tf_op jit(solution)/shard_map/ppermute | solution.py:611
  9.0 17.3 %collective-permute-start.1 = (bf16[528,256]{1,0:T(8,128)(2,1)S(1)}, bf16[528,256]{1,0:T(8,128)(2,1)S(1)}, u32[]{:S(2)}, u32[]{:S(2)}) collective-permute-start(bf16[528,256]{1,0:T(8,128)(2,1)S(1)} %get-tuple-element.42), channel_id=1, source_target_pairs={{0,8},{1,12},{2,10},{3,14},{4,9},{5,13},{6,11},{7,15},{8,1},{9,5},... | collective-permute-start | bytes 811016 | tf_op jit(solution)/shard_map/ppermute | solution.py:611
  13.4 13.0 %collective-permute-start.2 = (bf16[528,256]{1,0:T(8,128)(2,1)S(1)}, bf16[528,256]{1,0:T(8,128)(2,1)S(1)}, u32[]{:S(2)}, u32[]{:S(2)}) collective-permute-start(bf16[528,256]{1,0:T(8,128)(2,1)S(1)} %get-tuple-element.43), channel_id=1, source_target_pairs={{0,16},{1,20},{2,18},{3,22},{4,17},{5,21},{6,19},{7,23},{8,25},{9,... | collective-permute-start | bytes 811016 | tf_op jit(solution)/shard_map/ppermute | solution.py:600
  16.0 96.9 %collective-permute-start.22 = (bf16[512,2048]{1,0:T(8,128)(2,1)S(1)}, bf16[512,2048]{1,0:T(8,128)(2,1)S(1)}, u32[]{:S(2)}, u32[]{:S(2)}) collective-permute-start(bf16[512,2048]{1,0:T(8,128)(2,1)S(1)} %copy-done.2), channel_id=1, source_target_pairs={{0,1},{1,0},{2,3},{3,2},{4,5},{5,4},{6,7},{7,6},{8,9},{9,8},{10,11... | collective-permute-start | bytes 6291464 | tf_op jit(solution)/shard_map/ppermute | solution.py:591
  17.7 25.0 %collective-permute-start.3 = (bf16[528,256]{1,0:T(8,128)(2,1)S(1)}, bf16[528,256]{1,0:T(8,128)(2,1)S(1)}, u32[]{:S(2)}, u32[]{:S(2)}) collective-permute-start(bf16[528,256]{1,0:T(8,128)(2,1)S(1)} %get-tuple-element.44), channel_id=1, source_target_pairs={{0,24},{1,28},{2,26},{3,30},{4,25},{5,29},{6,27},{7,31},{8,17},{9,... | collective-permute-start | bytes 811016 | tf_op jit(solution)/shard_map/ppermute | solution.py:600
  17.7 26.6 %collective-permute-start.4 = (bf16[528,256]{1,0:T(8,128)(2,1)S(1)}, bf16[528,256]{1,0:T(8,128)(2,1)S(1)}, u32[]{:S(2)}, u32[]{:S(2)}) collective-permute-start(bf16[528,256]{1,0:T(8,128)(2,1)S(1)} %collective-permute-done.refs_0_), channel_id=1, source_target_pairs={{0,1},{1,0},{2,3},{3,2},{4,5},{5,4},{6,7},{7,6},{8,9},{9,8},{10,11... | collective-permute-start | bytes 811016 | tf_op jit(solution)/shard_map/ppermute | solution.py:616
  26.3 18.5 %collective-permute-start.5 = (bf16[528,256]{1,0:T(8,128)(2,1)S(1)}, bf16[528,256]{1,0:T(8,128)(2,1)S(1)}, u32[]{:S(2)}, u32[]{:S(2)}) collective-permute-start(bf16[528,256]{1,0:T(8,128)(2,1)S(1)} %collective-permute-done.1.refs_1_), channel_id=1, source_target_pairs={{0,1},{1,0},{2,3},{3,2},{4,5},{5,4},{6,7},{7,6},{8,9},{9,8},{10,11... | collective-permute-start | bytes 811016 | tf_op jit(solution)/shard_map/ppermute | solution.py:616
  26.4 19.9 %collective-permute-start.6 = (bf16[528,256]{1,0:T(8,128)(2,1)S(1)}, bf16[528,256]{1,0:T(8,128)(2,1)S(1)}, u32[]{:S(2)}, u32[]{:S(2)}) collective-permute-start(bf16[528,256]{1,0:T(8,128)(2,1)S(1)} %collective-permute-done.2.refs_2_), channel_id=1, source_target_pairs={{0,1},{1,0},{2,3},{3,2},{4,5},{5,4},{6,7},{7,6},{8,9},{9,8},{10,11... | collective-permute-start | bytes 811016 | tf_op jit(solution)/shard_map/ppermute | solution.py:616
  42.7 16.0 %collective-permute-start.23 = (bf16[256,1024]{1,0:T(8,128)(2,1)S(1)}, bf16[256,1024]{1,0:T(8,128)(2,1)S(1)}, u32[]{:S(2)}, u32[]{:S(2)}) collective-permute-start(bf16[256,1024]{1,0:T(8,128)(2,1)S(1)} %get-tuple-element.61), channel_id=1, source_target_pairs={{0,2},{1,3},{2,0},{3,1},{4,6},{5,7},{6,4},{7,5},{8,10},{9,11},{10,... | collective-permute-start | bytes 1572872 | tf_op jit(solution)/shard_map/ppermute | solution.py:603
  44.2 24.5 %collective-permute-start.13 = (bf16[256,1024]{1,0:T(8,128)(2,1)S(1)}, bf16[256,1024]{1,0:T(8,128)(2,1)S(1)}, u32[]{:S(2)}, u32[]{:S(2)}) collective-permute-start(bf16[256,1024]{1,0:T(8,128)(2,1)S(1)} %get-tuple-element.53), channel_id=1, source_target_pairs={{0,2},{1,3},{2,0},{3,1},{4,6},{5,7},{6,4},{7,5},{8,10},{9,11},{10,... | collective-permute-start | bytes 1572872 | tf_op jit(solution)/shard_map/ppermute | solution.py:603
  44.8 34.3 %collective-permute-start.14 = (bf16[256,1024]{1,0:T(8,128)(2,1)S(1)}, bf16[256,1024]{1,0:T(8,128)(2,1)S(1)}, u32[]{:S(2)}, u32[]{:S(2)}) collective-permute-start(bf16[256,1024]{1,0:T(8,128)(2,1)S(1)} %get-tuple-element.54), channel_id=1, source_target_pairs={{0,2},{1,3},{2,0},{3,1},{4,6},{5,7},{6,4},{7,5},{8,10},{9,11},{10,... | collective-permute-start | bytes 1572872 | tf_op jit(solution)/shard_map/ppermute | solution.py:607
  46.3 6.4 %collective-permute-start.7 = (bf16[528,256]{1,0:T(8,128)(2,1)S(1)}, bf16[528,256]{1,0:T(8,128)(2,1)S(1)}, u32[]{:S(2)}, u32[]{:S(2)}) collective-permute-start(bf16[528,256]{1,0:T(8,128)(2,1)S(1)} %collective-permute-done.3.refs_3_), channel_id=1, source_target_pairs={{0,1},{1,0},{2,3},{3,2},{4,5},{5,4},{6,7},{7,6},{8,9},{9,8},{10,11... | collective-permute-start | bytes 811016 | tf_op jit(solution)/shard_map/ppermute | solution.py:616
  52.7 53.9 %collective-permute-start.27 = (bf16[2,128,2048]{2,1,0:T(8,128)(2,1)S(1)}, bf16[2,128,2048]{2,1,0:T(8,128)(2,1)S(1)}, u32[]{:S(2)}, u32[]{:S(2)}) collective-permute-start(bf16[2,128,2048]{2,1,0:T(8,128)(2,1)S(1)} %get-tuple-element.66), channel_id=1, source_target_pairs={{0,1},{1,0},{2,3},{3,2},{4,5},{5,4},{6,7},{7,6},{8,9},{9,8},{10,11... | collective-permute-start | bytes 3145736 | tf_op jit(solution)/shard_map/ppermute | solution.py:614
  58.7 20.4 %collective-permute-start.17 = (bf16[544,128]{1,0:T(8,128)(2,1)S(1)}, bf16[544,128]{1,0:T(8,128)(2,1)S(1)}, u32[]{:S(2)}, u32[]{:S(2)}) collective-permute-start(bf16[544,128]{1,0:T(8,128)(2,1)S(1)} %get-tuple-element.55), channel_id=1, source_target_pairs={{24,0},{28,1},{26,2},{30,3},{25,4},{29,5},{27,6},{31,7},{17,8},{21... | collective-permute-start | bytes 417800 | tf_op jit(solution)/shard_map/ppermute | solution.py:624
  68.8 34.3 %collective-permute-start.24 = (bf16[256,1024]{1,0:T(8,128)(2,1)S(1)}, bf16[256,1024]{1,0:T(8,128)(2,1)S(1)}, u32[]{:S(2)}, u32[]{:S(2)}) collective-permute-start(bf16[256,1024]{1,0:T(8,128)(2,1)S(1)} %collective-permute-done.23.refs_6_), channel_id=1, source_target_pairs={{0,4},{4,0},{8,12},{12,8},{16,20},{20,16},{24,28},{28,24},{1,5},{5... | collective-permute-start | bytes 1572872 | tf_op jit(solution)/shard_map/ppermute | solution.py:605
  79.1 31.8 %collective-permute-start.25 = (bf16[256,1024]{1,0:T(8,128)(2,1)S(1)}, bf16[256,1024]{1,0:T(8,128)(2,1)S(1)}, u32[]{:S(2)}, u32[]{:S(2)}) collective-permute-start(bf16[256,1024]{1,0:T(8,128)(2,1)S(1)} %collective-permute-done.23.refs_6_), channel_id=1, source_target_pairs={{0,1},{1,0},{2,3},{3,2},{4,5},{5,4},{6,7},{7,6},{8,9},{9,8},{10,11... | collective-permute-start | bytes 1572872 | tf_op jit(solution)/shard_map/ppermute | solution.py:608
  79.1 5.9 %collective-permute-start.18 = (bf16[544,128]{1,0:T(8,128)(2,1)S(1)}, bf16[544,128]{1,0:T(8,128)(2,1)S(1)}, u32[]{:S(2)}, u32[]{:S(2)}) collective-permute-start(bf16[544,128]{1,0:T(8,128)(2,1)S(1)} %get-tuple-element.56), channel_id=1, source_target_pairs={{0,0},{4,1},{2,2},{6,3},{1,4},{5,5},{3,6},{7,7},{9,8},{13,9},{11,1... | collective-permute-start | bytes 417800 | tf_op jit(solution)/shard_map/ppermute | solution.py:624
  84.9 9.0 %collective-permute-start.8 = (bf16[544,128]{1,0:T(8,128)(2,1)S(1)}, bf16[544,128]{1,0:T(8,128)(2,1)S(1)}, u32[]{:S(2)}, u32[]{:S(2)}) collective-permute-start(bf16[544,128]{1,0:T(8,128)(2,1)S(1)} %get-tuple-element.47), channel_id=1, source_target_pairs={{16,0},{20,1},{18,2},{22,3},{17,4},{21,5},{19,6},{23,7},{25,8},{29... | collective-permute-start | bytes 417800 | tf_op jit(solution)/shard_map/ppermute | solution.py:627
  103.1 8.9 %collective-permute-start.26 = (bf16[256,1024]{1,0:T(8,128)(2,1)S(1)}, bf16[256,1024]{1,0:T(8,128)(2,1)S(1)}, u32[]{:S(2)}, u32[]{:S(2)}) collective-permute-start(bf16[256,1024]{1,0:T(8,128)(2,1)S(1)} %collective-permute-done.24.refs_7_), channel_id=1, source_target_pairs={{0,1},{1,0},{2,3},{3,2},{4,5},{5,4},{6,7},{7,6},{8,9},{9,8},{10,11... | collective-permute-start | bytes 1572872 | tf_op jit(solution)/shard_map/ppermute | solution.py:608
  110.3 16.6 %collective-permute-start.15 = (bf16[256,1024]{1,0:T(8,128)(2,1)S(1)}, bf16[256,1024]{1,0:T(8,128)(2,1)S(1)}, u32[]{:S(2)}, u32[]{:S(2)}) collective-permute-start(bf16[256,1024]{1,0:T(8,128)(2,1)S(1)} %collective-permute-done.13.refs_4_), channel_id=1, source_target_pairs={{0,1},{1,0},{2,3},{3,2},{4,5},{5,4},{6,7},{7,6},{8,9},{9,8},{10,11... | collective-permute-start | bytes 1572872 | tf_op jit(solution)/shard_map/ppermute | solution.py:608
  110.4 16.5 %collective-permute-start.16 = (bf16[256,1024]{1,0:T(8,128)(2,1)S(1)}, bf16[256,1024]{1,0:T(8,128)(2,1)S(1)}, u32[]{:S(2)}, u32[]{:S(2)}) collective-permute-start(bf16[256,1024]{1,0:T(8,128)(2,1)S(1)} %collective-permute-done.14.refs_5_), channel_id=1, source_target_pairs={{0,1},{1,0},{2,3},{3,2},{4,5},{5,4},{6,7},{7,6},{8,9},{9,8},{10,11... | collective-permute-start | bytes 1572872 | tf_op jit(solution)/shard_map/ppermute | solution.py:608
  110.8 16.1 %collective-permute-start.28 = (bf16[128,2048]{1,0:T(8,128)(2,1)S(1)}, bf16[128,2048]{1,0:T(8,128)(2,1)S(1)}, u32[]{:S(2)}, u32[]{:S(2)}) collective-permute-start(bf16[128,2048]{1,0:T(8,128)(2,1)S(1)} %shard_map.113), channel_id=1, source_target_pairs={{0,2},{1,3},{2,0},{3,1},{4,6},{5,7},{6,4},{7,5},{8,10},{9,11},{10,... | collective-permute-start | bytes 1572872 | tf_op jit(solution)/shard_map/ppermute | solution.py:618
  112.0 14.8 %collective-permute-start.11 = (bf16[2,128,128]{2,1,0:T(8,128)(2,1)S(1)}, bf16[2,128,128]{2,1,0:T(8,128)(2,1)S(1)}, u32[]{:S(2)}, u32[]{:S(2)}) collective-permute-start(bf16[2,128,128]{2,1,0:T(8,128)(2,1)S(1)} %get-tuple-element.51), channel_id=1, source_target_pairs={{0,2},{1,3},{2,0},{3,1},{4,6},{5,7},{6,4},{7,5},{8,10},{9,11},{10,... | collective-permute-start | bytes 196616 | tf_op jit(solution)/shard_map/ppermute | solution.py:632
  112.8 14.0 %collective-permute-start.12 = (bf16[2,128,128]{2,1,0:T(8,128)(2,1)S(1)}, bf16[2,128,128]{2,1,0:T(8,128)(2,1)S(1)}, u32[]{:S(2)}, u32[]{:S(2)}) collective-permute-start(bf16[2,128,128]{2,1,0:T(8,128)(2,1)S(1)} %get-tuple-element.52), channel_id=1, source_target_pairs={{0,3},{1,2},{2,1},{3,0},{4,7},{5,6},{6,5},{7,4},{8,11},{9,10},{10,... | collective-permute-start | bytes 196616 | tf_op jit(solution)/shard_map/ppermute | solution.py:632
  (8 other events, 73.2 us)

commit v7 on v5

--- a/solution.py
+++ b/solution.py
@@ -337,33 +337,40 @@
         one_hot = jnp.where(wanted == id_rows[b, :1, :], 1.0, 0.0).astype(jnp.bfloat16)
         sums = sums + jnp.dot(one_hot, kv[b, :, :width], preferred_element_type=jnp.float32)
 
-    def pair(b, masked):
-        score = lax.dot_general(
-            query[...],
-            kv[b, :, :width],
-            (((1,), (1,)), ((), ())),
-            preferred_element_type=jnp.float32,
-        )
-        weight = jnp.exp(score)
-        same = jnp.concatenate([id_cols[...]] * (rows // width), axis=1) == id_rows[b, :1, :]
+    def pair(blocks, masked):
+        spread = jnp.concatenate([id_cols[...]] * (rows // width), axis=1)
+        shares, mixes = [], []
+        for b in blocks:
+            score = lax.dot_general(
+                query[...],
+                kv[b, :, :width],
+                (((1,), (1,)), ((), ())),
+                preferred_element_type=jnp.float32,
+            )
+            weight = jnp.exp(score)
+            same = spread == id_rows[b, :1, :]
+            if masked:
+                row_at = lax.broadcasted_iota(jnp.int32, weight.shape, 0)
+                col_at = lax.broadcasted_iota(jnp.int32, weight.shape, 1)
+                same = jnp.logical_and(same, col_at <= row_at)
+            weight = jnp.where(same, weight, 0.0)
+            shares += [
+                weight[:, part * width : (part + 1) * width] for part in range(rows // width)
+            ]
+            mixes.append(
+                jnp.dot(
+                    weight.astype(jnp.bfloat16),
+                    kv[b, :, width:],
+                    preferred_element_type=jnp.float32,
+                )
+            )
         if masked:
-            row_at = lax.broadcasted_iota(jnp.int32, weight.shape, 0)
-            col_at = lax.broadcasted_iota(jnp.int32, weight.shape, 1)
-            same = jnp.logical_and(same, col_at <= row_at)
-        weight = jnp.where(same, weight, 0.0)
-        share = weight[:, :width]
-        for part in range(1, rows // width):
-            share = share + weight[:, part * width : (part + 1) * width]
-        mixed = jnp.dot(
-            weight.astype(jnp.bfloat16), kv[b, :, width:], preferred_element_type=jnp.float32
-        )
-        if masked:
-            den[...] = share
-            acc[...] = mixed
+            den[...], acc[...] = sum(shares[1:], shares[0]), sum(mixes[1:], mixes[0])
         else:
-            den[...] += share
-            acc[...] += mixed
-
+            den[...] += sum(shares[1:], shares[0])
+            acc[...] += sum(mixes[1:], mixes[0])
+
+    z = lax.axis_index(SEQ) >> 1
     for at, k in enumerate(steps):
         query[...] = kv[k, :, :width] * jnp.bfloat16(SCORE_SCALE)
         for part in range(rows // width):
@@ -371,17 +378,22 @@
             id_cols[here, :] = jnp.transpose(
                 jnp.broadcast_to(id_rows[k, :1, part * width : (part + 1) * width], (width, width))
             )
-        pair(k, True)
-        block = block_of(k, heads)
-
-        def per_key(b, carry):
-            @pl.when(block_of(b, heads) < block)
+        pair((k,), True)
+
+        @pl.when(block_of(k + heads, heads) < block_of(k, heads))
+        def _():
+            pair((k + heads,), False)
+
+        def per_pair(turn, carry):
+            b = k ^ turn
+
+            @pl.when((z ^ b) < (z ^ k))
             def _():
-                pair(b, False)
+                pair((b, b + heads), False)
 
             return carry
 
-        lax.fori_loop(0, count, per_key, 0)
+        lax.fori_loop(1, heads, per_pair, 0)
         out = outs[at]
         whole = jnp.sum(den[...], axis=-1, keepdims=True)
         out[:rows, :] = (acc[...] / whole).astype(jnp.bfloat16)

time: 128 us -> 128 us (level)
  transfers between devices with their start and end apart: 29 -> 29, of which waited for: 10 -> 10; matrix products, arithmetic and copies ran while one was open for 0% -> 0% of each run, Pallas kernels for 18% -> 17%
where the time goes in v7:
time: 128 us; the launch traced here: 127 us
  waiting for transfers between devices  56.7 us (44%)
  starting transfers between devices  38.7 us (30%)
  Pallas kernels  31.1 us (24%)
    ppermute x6, waiting for transfers between devices, by_heads(): lax.ppermute(away[d - 1], TENSOR, swaps[d])  17.9 us
    ppermute x4, starting transfers between devices, by_heads(): other[k] = lax.ppermute(own[k], TENSOR, swaps[1])  12.4 us
    ppermute x4, waiting for transfers between devices, by_heads(): back[k] = lax.ppermute(result, BOTH, turned(steps[k]))  11.6 us
    ppermute x2, waiting for transfers between devices, by_heads(): here = lax.ppermute(out_parts.pop(0), TENSOR, swaps[2])  10.4 us
    pallas_call x2, Pallas kernels, attend(): pl.pallas_call(functools.partial(attend_body, heads=heads, width=width, o...  10.1 us
    ppermute x1, waiting for transfers between devices, by_heads(): there = lax.ppermute(out_parts.pop(0), TENSOR, swaps[2])  9.68 us
    ppermute x4, starting transfers between devices, by_heads(): own[k] = lax.ppermute(messages[k], BOTH, steps[k])  7.62 us
    ppermute x4, waiting for transfers between devices, by_heads(): own[k] = lax.ppermute(messages[k], BOTH, steps[k])  7.1 us
  transfers between devices with their start and end apart: 29, of which 10 were waited for; matrix products, arithmetic and copies ran while one was open for 0% of the time, Pallas kernels for 17%

profile of v7, /device:TPU:0, one launch (start us, length us, event | category | flops | bytes accessed | tf_op | source)
XLA Modules:
  0.0 127.4 jit_solution(12378366284752742732)
XLA Ops:
  0.6 4.3 %shard_map.104 = (bf16[528,256]{1,0:T(8,128)(2,1)S(1)}, bf16[528,256]{1,0:T(8,128)(2,1)S(1)}, bf16[512,2048]{1,0:T(8,128)(2,1)S(1)}, s32[4,512]{1,0:T(4,128)S(1)...) custom-call(bf16[512,2048]{1,0:T(8,128)(2,1)} %refs_10_.1, ...), custom_call_target="tpu_custom_call" | custom-call | flops 1073741824 | bytes 5242880 | tf_op jit(solution)/shard_map/pallas_call | solution.py:156
  5.0 3.3 %shard_map.105 = (bf16[528,256]{1,0:T(8,128)(2,1)S(1)}, bf16[528,256]{1,0:T(8,128)(2,1)S(1)}, bf16[2048,1024]{1,0:T(8,128)(2,1)S(1)}) custom-call(bf16[512,2048]{1,0:T(8,128)(2,1)S(1)} %get-tuple-element.37.normed, bf16[2048,256]{1,0:T(8,128)(2,1)S(1)} %get-tuple-element.38.w_qk, bf16[2048,256]{1,0:T(8,128)(2,1)S(1)} %get-tuple-element.39.w_value, ...), custom_call_target="tpu_custom_call" | custom-call | flops 1073741824 | bytes 4194304 | tf_op jit(solution)/shard_map/pallas_call | solution.py:197
  9.0 4.3 %collective-permute-start.1 = (bf16[528,256]{1,0:T(8,128)(2,1)S(1)}, bf16[528,256]{1,0:T(8,128)(2,1)S(1)}, u32[]{:S(2)}, u32[]{:S(2)}) collective-permute-start(bf16[528,256]{1,0:T(8,128)(2,1)S(1)} %get-tuple-element.42), channel_id=1, source_target_pairs={{0,8},{1,12},{2,10},{3,14},{4,9},{5,13},{6,11},{7,15},{8,1},{9,5},... | collective-permute-start | bytes 811016 | tf_op jit(solution)/shard_map/ppermute | solution.py:608
  13.3 2.6 %collective-permute-start.2 = (bf16[528,256]{1,0:T(8,128)(2,1)S(1)}, bf16[528,256]{1,0:T(8,128)(2,1)S(1)}, u32[]{:S(2)}, u32[]{:S(2)}) collective-permute-start(bf16[528,256]{1,0:T(8,128)(2,1)S(1)} %get-tuple-element.43), channel_id=1, source_target_pairs={{0,16},{1,20},{2,18},{3,22},{4,17},{5,21},{6,19},{7,23},{8,25},{9,... | collective-permute-start | bytes 811016 | tf_op jit(solution)/shard_map/ppermute | solution.py:597
  15.9 1.7 %collective-permute-start.22 = (bf16[512,2048]{1,0:T(8,128)(2,1)S(1)}, bf16[512,2048]{1,0:T(8,128)(2,1)S(1)}, u32[]{:S(2)}, u32[]{:S(2)}) collective-permute-start(bf16[512,2048]{1,0:T(8,128)(2,1)S(1)} %copy-done.2), channel_id=1, source_target_pairs={{0,1},{1,0},{2,3},{3,2},{4,5},{5,4},{6,7},{7,6},{8,9},{9,8},{10,11... | collective-permute-start | bytes 6291464 | tf_op jit(solution)/shard_map/ppermute | solution.py:588
  17.6 1.6 %collective-permute-start.4 = (bf16[528,256]{1,0:T(8,128)(2,1)S(1)}, bf16[528,256]{1,0:T(8,128)(2,1)S(1)}, u32[]{:S(2)}, u32[]{:S(2)}) collective-permute-start(bf16[528,256]{1,0:T(8,128)(2,1)S(1)} %collective-permute-done.refs_0_), channel_id=1, source_target_pairs={{0,1},{1,0},{2,3},{3,2},{4,5},{5,4},{6,7},{7,6},{8,9},{9,8},{10,11... | collective-permute-start | bytes 811016 | tf_op jit(solution)/shard_map/ppermute | solution.py:613
  19.2 7.1 %collective-permute-done.1.refs_1_ = bf16[528,256]{1,0:T(8,128)(2,1)S(1)} collective-permute-done((bf16[528,256]{1,0:T(8,128)(2,1)S(1)}, bf16[528,256]{1,0:T(8,128)(2,1)S(1)}, u32[]{:S(2)}, u32[]{:S(2)}) %collective-permute-start.1) | collective-permute-done | bytes 270368 | tf_op jit(solution)/shard_map/ppermute | solution.py:608
  26.3 10.8 %collective-permute-start.6 = (bf16[528,256]{1,0:T(8,128)(2,1)S(1)}, bf16[528,256]{1,0:T(8,128)(2,1)S(1)}, u32[]{:S(2)}, u32[]{:S(2)}) collective-permute-start(bf16[528,256]{1,0:T(8,128)(2,1)S(1)} %collective-permute-done.2.refs_2_), channel_id=1, source_target_pairs={{0,1},{1,0},{2,3},{3,2},{4,5},{5,4},{6,7},{7,6},{8,9},{9,8},{10,11... | collective-permute-start | bytes 811016 | tf_op jit(solution)/shard_map/ppermute | solution.py:613
  37.1 4.7 %shard_map.110 = (bf16[512,2048]{1,0:T(8,128)(2,1)S(1)}, bf16[2048,1024]{1,0:T(8,128)(2,1)S(1)}) custom-call(bf16[512,2048]{1,0:T(8,128)(2,1)S(1)} %get-tuple-element.37.normed, bf16[2048,1024]{1,0:T(8,128)(2,1)S(1)} %get-tuple-element.62.first, bf16[2048,2048]{1,0:T(8,128)(2,1)} %w_up.3, bf16[2048,2048]{1,0:T(8,128)(2,1)} %w_down.3), custom_call_target="tpu_custom_call" | custom-call | flops 4294967296 | bytes 12582912 | tf_op jit(solution)/shard_map/pallas_call | solution.py:229
  41.8 1.6 %collective-permute-start.23 = (bf16[256,1024]{1,0:T(8,128)(2,1)S(1)}, bf16[256,1024]{1,0:T(8,128)(2,1)S(1)}, u32[]{:S(2)}, u32[]{:S(2)}) collective-permute-start(bf16[256,1024]{1,0:T(8,128)(2,1)S(1)} %get-tuple-element.61), channel_id=1, source_target_pairs={{0,2},{1,3},{2,0},{3,1},{4,6},{5,7},{6,4},{7,5},{8,10},{9,11},{10,... | collective-permute-start | bytes 1572872 | tf_op jit(solution)/shard_map/ppermute | solution.py:600
  43.9 1.5 %collective-permute-start.14 = (bf16[256,1024]{1,0:T(8,128)(2,1)S(1)}, bf16[256,1024]{1,0:T(8,128)(2,1)S(1)}, u32[]{:S(2)}, u32[]{:S(2)}) collective-permute-start(bf16[256,1024]{1,0:T(8,128)(2,1)S(1)} %get-tuple-element.54), channel_id=1, source_target_pairs={{0,2},{1,3},{2,0},{3,1},{4,6},{5,7},{6,4},{7,5},{8,10},{9,11},{10,... | collective-permute-start | bytes 1572872 | tf_op jit(solution)/shard_map/ppermute | solution.py:604
  45.4 5.0 %shard_map.111 = (f32[128,2048]{1,0:T(8,128)S(1)}, f32[128,2048]{1,0:T(8,128)S(1)}, bf16[2,128,2048]{2,1,0:T(8,128)(2,1)S(1)}) custom-call(bf16[512,2048]{1,0:T(8,128)(2,1)S(1)} %get-tuple-element.63.hidden, bf16[2048,1024]{1,0:T(8,128)(2,1)S(1)} %get-tuple-element.64.first, bf16[2048,2048]{1,0:T(8,128)(2,1)} %w_down.3), custom_call_target="tpu_custom_call" | custom-call | flops 4294967296 | bytes 14680064 | tf_op jit(solution)/shard_map/pallas_call | solution.py:268
  50.9 5.2 %shard_map.106 = (bf16[544,128]{1,0:T(8,128)(2,1)S(1)}, bf16[544,128]{1,0:T(8,128)(2,1)S(1)}, bf16[8,512,256]{2,1,0:T(8,128)(2,1)S(1)}, f32[8,8,512]{2,1,0:T(8,128)S(1)}) custom-call(bf16[528,256]{1,0:T(8,128)(2,1)S(1)} %collective-permute-done.refs_0_, bf16[528,256]{1,0:T(8,128)(2,1)S(1)} %collective-permute-done.1.refs_1_, ...), custom_call_target="tpu_custom_call" | custom-call | flops 2415919104 | bytes 2097152 | tf_op jit(solution)/shard_map/pallas_call | solution.py:412
  57.9 10.0 %collective-permute-done.13.refs_4_ = bf16[256,1024]{1,0:T(8,128)(2,1)S(1)} collective-permute-done((bf16[256,1024]{1,0:T(8,128)(2,1)S(1)}, bf16[256,1024]{1,0:T(8,128)(2,1)S(1)}, u32[]{:S(2)}, u32[]{:S(2)}) %collective-permute-start.13) | collective-permute-done | bytes 524320 | tf_op jit(solution)/shard_map/ppermute | solution.py:600
  68.5 9.7 %collective-permute-done.14.refs_5_ = bf16[256,1024]{1,0:T(8,128)(2,1)S(1)} collective-permute-done((bf16[256,1024]{1,0:T(8,128)(2,1)S(1)}, bf16[256,1024]{1,0:T(8,128)(2,1)S(1)}, u32[]{:S(2)}, u32[]{:S(2)}) %collective-permute-start.14) | collective-permute-done | bytes 524320 | tf_op jit(solution)/shard_map/ppermute | solution.py:604
  78.8 4.8 %shard_map.107 = (bf16[544,128]{1,0:T(8,128)(2,1)S(1)}, bf16[544,128]{1,0:T(8,128)(2,1)S(1)}) custom-call(bf16[8,512,256]{2,1,0:T(8,128)(2,1)S(1)} %get-tuple-element.45.refs_0_, f32[8,8,512]{2,1,0:T(8,128)S(1)} %get-tuple-element.46.refs_1_), custom_call_target="tpu_custom_call" | custom-call | flops 2415919104 | bytes 2097152 | tf_op jit(solution)/shard_map/pallas_call | solution.py:412
  84.7 8.0 %collective-permute-done.8.refs_0_ = bf16[544,128]{1,0:T(8,128)(2,1)S(1)} collective-permute-done((bf16[544,128]{1,0:T(8,128)(2,1)S(1)}, bf16[544,128]{1,0:T(8,128)(2,1)S(1)}, u32[]{:S(2)}, u32[]{:S(2)}) %collective-permute-start.8) | collective-permute-done | bytes 139296 | tf_op jit(solution)/shard_map/ppermute | solution.py:624
  94.1 3.6 %collective-permute-done.9.refs_1_ = bf16[544,128]{1,0:T(8,128)(2,1)S(1)} collective-permute-done((bf16[544,128]{1,0:T(8,128)(2,1)S(1)}, bf16[544,128]{1,0:T(8,128)(2,1)S(1)}, u32[]{:S(2)}, u32[]{:S(2)}) %collective-permute-start.9) | collective-permute-done | bytes 139296 | tf_op jit(solution)/shard_map/ppermute | solution.py:624
  97.7 1.9 %collective-permute-start.19 = (bf16[2,128,128]{2,1,0:T(8,128)(2,1)S(1)}, bf16[2,128,128]{2,1,0:T(8,128)(2,1)S(1)}, u32[]{:S(2)}, u32[]{:S(2)}) collective-permute-start(bf16[2,128,128]{2,1,0:T(8,128)(2,1)S(1)} %get-tuple-element.58), channel_id=1, source_target_pairs={{0,1},{1,0},{2,3},{3,2},{4,5},{5,4},{6,7},{7,6},{8,9},{9,8},{10,11... | collective-permute-start | bytes 196616 | tf_op jit(solution)/shard_map/ppermute | solution.py:629
  102.2 2.7 %collective-permute-done.20.refs_2_ = bf16[2,128,128]{2,1,0:T(8,128)(2,1)S(1)} collective-permute-done((bf16[2,128,128]{2,1,0:T(8,128)(2,1)S(1)}, bf16[2,128,128]{2,1,0:T(8,128)(2,1)S(1)}, u32[]{:S(2)}, u32[]{:S(2)}) %collective-permute-start.20) | collective-permute-done | bytes 65568 | tf_op jit(solution)/shard_map/ppermute | solution.py:629
  106.6 2.7 %collective-permute-done.21.refs_3_ = bf16[2,128,128]{2,1,0:T(8,128)(2,1)S(1)} collective-permute-done((bf16[2,128,128]{2,1,0:T(8,128)(2,1)S(1)}, bf16[2,128,128]{2,1,0:T(8,128)(2,1)S(1)}, u32[]{:S(2)}, u32[]{:S(2)}) %collective-permute-start.21) | collective-permute-done | bytes 65568 | tf_op jit(solution)/shard_map/ppermute | solution.py:629
  112.1 2.1 %shard_map.112 = (f32[128,2048]{1,0:T(8,128)S(1)}, bf16[512,2048]{1,0:T(8,128)(2,1)S(1)}) custom-call(bf16[2,128,128]{2,1,0:T(8,128)(2,1)S(1)} %get-tuple-element.57.refs_0_, bf16[2,128,128]{2,1,0:T(8,128)(2,1)S(1)} %collective-permute-done.19.refs_1_, bf16[2,128,128]{2,1,0:T(8,128)(2,1)S(1)} %collective-permute-done.20.refs_2_, ...), custom_call_target="tpu_custom_call" | custom-call | flops 536870912 | bytes 10485760 | tf_op jit(solution)/shard_map/pallas_call | solution.py:523
  114.2 11.6 %collective-permute-done.11.refs_2_ = bf16[2,128,128]{2,1,0:T(8,128)(2,1)S(1)} collective-permute-done((bf16[2,128,128]{2,1,0:T(8,128)(2,1)S(1)}, bf16[2,128,128]{2,1,0:T(8,128)(2,1)S(1)}, u32[]{:S(2)}, u32[]{:S(2)}) %collective-permute-start.11) | collective-permute-done | bytes 65568 | tf_op jit(solution)/shard_map/ppermute | solution.py:629
  125.8 1.5 %shard_map.114 = (bf16[128,2048]{1,0:T(8,128)(2,1)}, f32[4,32,128]{2,1,0:T(8,128)}) custom-call(bf16[2,128,128]{2,1,0:T(8,128)(2,1)S(1)} %get-tuple-element.49.refs_0_, bf16[2,128,128]{2,1,0:T(8,128)(2,1)S(1)} %collective-permute-done.10.refs_1_, bf16[2,128,128]{2,1,0:T(8,128)(2,1)S(1)} %collective-permute-done.11.refs_2_, ...), custom_call_target="tpu_custom_call" | custom-call | flops 536870912 | bytes 6291456 | tf_op jit(solution)/shard_map/pallas_call | solution.py:566
  (51 shorter events, 14.4 us)
Async XLA Ops:
  8.3 9.3 %collective-permute-start = (bf16[528,256]{1,0:T(8,128)(2,1)S(1)}, bf16[528,256]{1,0:T(8,128)(2,1)S(1)}, u32[]{:S(2)}, u32[]{:S(2)}) collective-permute-start(bf16[528,256]{1,0:T(8,128)(2,1)S(1)} %get-tuple-element.41), channel_id=1, source_target_pairs={{0,0},{1,4},{2,2},{3,6},{4,1},{5,5},{6,3},{7,7},{8,9},{9,13},{10,1... | collective-permute-start | bytes 811016 | tf_op jit(solution)/shard_map/ppermute | solution.py:608
  9.0 17.3 %collective-permute-start.1 = (bf16[528,256]{1,0:T(8,128)(2,1)S(1)}, bf16[528,256]{1,0:T(8,128)(2,1)S(1)}, u32[]{:S(2)}, u32[]{:S(2)}) collective-permute-start(bf16[528,256]{1,0:T(8,128)(2,1)S(1)} %get-tuple-element.42), channel_id=1, source_target_pairs={{0,8},{1,12},{2,10},{3,14},{4,9},{5,13},{6,11},{7,15},{8,1},{9,5},... | collective-permute-start | bytes 811016 | tf_op jit(solution)/shard_map/ppermute | solution.py:608
  13.3 13.0 %collective-permute-start.2 = (bf16[528,256]{1,0:T(8,128)(2,1)S(1)}, bf16[528,256]{1,0:T(8,128)(2,1)S(1)}, u32[]{:S(2)}, u32[]{:S(2)}) collective-permute-start(bf16[528,256]{1,0:T(8,128)(2,1)S(1)} %get-tuple-element.43), channel_id=1, source_target_pairs={{0,16},{1,20},{2,18},{3,22},{4,17},{5,21},{6,19},{7,23},{8,25},{9,... | collective-permute-start | bytes 811016 | tf_op jit(solution)/shard_map/ppermute | solution.py:597
  15.9 95.9 %collective-permute-start.22 = (bf16[512,2048]{1,0:T(8,128)(2,1)S(1)}, bf16[512,2048]{1,0:T(8,128)(2,1)S(1)}, u32[]{:S(2)}, u32[]{:S(2)}) collective-permute-start(bf16[512,2048]{1,0:T(8,128)(2,1)S(1)} %copy-done.2), channel_id=1, source_target_pairs={{0,1},{1,0},{2,3},{3,2},{4,5},{5,4},{6,7},{7,6},{8,9},{9,8},{10,11... | collective-permute-start | bytes 6291464 | tf_op jit(solution)/shard_map/ppermute | solution.py:588
  17.6 24.2 %collective-permute-start.3 = (bf16[528,256]{1,0:T(8,128)(2,1)S(1)}, bf16[528,256]{1,0:T(8,128)(2,1)S(1)}, u32[]{:S(2)}, u32[]{:S(2)}) collective-permute-start(bf16[528,256]{1,0:T(8,128)(2,1)S(1)} %get-tuple-element.44), channel_id=1, source_target_pairs={{0,24},{1,28},{2,26},{3,30},{4,25},{5,29},{6,27},{7,31},{8,17},{9,... | collective-permute-start | bytes 811016 | tf_op jit(solution)/shard_map/ppermute | solution.py:597
  17.6 25.7 %collective-permute-start.4 = (bf16[528,256]{1,0:T(8,128)(2,1)S(1)}, bf16[528,256]{1,0:T(8,128)(2,1)S(1)}, u32[]{:S(2)}, u32[]{:S(2)}) collective-permute-start(bf16[528,256]{1,0:T(8,128)(2,1)S(1)} %collective-permute-done.refs_0_), channel_id=1, source_target_pairs={{0,1},{1,0},{2,3},{3,2},{4,5},{5,4},{6,7},{7,6},{8,9},{9,8},{10,11... | collective-permute-start | bytes 811016 | tf_op jit(solution)/shard_map/ppermute | solution.py:613
  26.3 17.6 %collective-permute-start.5 = (bf16[528,256]{1,0:T(8,128)(2,1)S(1)}, bf16[528,256]{1,0:T(8,128)(2,1)S(1)}, u32[]{:S(2)}, u32[]{:S(2)}) collective-permute-start(bf16[528,256]{1,0:T(8,128)(2,1)S(1)} %collective-permute-done.1.refs_1_), channel_id=1, source_target_pairs={{0,1},{1,0},{2,3},{3,2},{4,5},{5,4},{6,7},{7,6},{8,9},{9,8},{10,11... | collective-permute-start | bytes 811016 | tf_op jit(solution)/shard_map/ppermute | solution.py:613
  26.3 19.1 %collective-permute-start.6 = (bf16[528,256]{1,0:T(8,128)(2,1)S(1)}, bf16[528,256]{1,0:T(8,128)(2,1)S(1)}, u32[]{:S(2)}, u32[]{:S(2)}) collective-permute-start(bf16[528,256]{1,0:T(8,128)(2,1)S(1)} %collective-permute-done.2.refs_2_), channel_id=1, source_target_pairs={{0,1},{1,0},{2,3},{3,2},{4,5},{5,4},{6,7},{7,6},{8,9},{9,8},{10,11... | collective-permute-start | bytes 811016 | tf_op jit(solution)/shard_map/ppermute | solution.py:613
  41.8 14.9 %collective-permute-start.23 = (bf16[256,1024]{1,0:T(8,128)(2,1)S(1)}, bf16[256,1024]{1,0:T(8,128)(2,1)S(1)}, u32[]{:S(2)}, u32[]{:S(2)}) collective-permute-start(bf16[256,1024]{1,0:T(8,128)(2,1)S(1)} %get-tuple-element.61), channel_id=1, source_target_pairs={{0,2},{1,3},{2,0},{3,1},{4,6},{5,7},{6,4},{7,5},{8,10},{9,11},{10,... | collective-permute-start | bytes 1572872 | tf_op jit(solution)/shard_map/ppermute | solution.py:600
  43.3 24.5 %collective-permute-start.13 = (bf16[256,1024]{1,0:T(8,128)(2,1)S(1)}, bf16[256,1024]{1,0:T(8,128)(2,1)S(1)}, u32[]{:S(2)}, u32[]{:S(2)}) collective-permute-start(bf16[256,1024]{1,0:T(8,128)(2,1)S(1)} %get-tuple-element.53), channel_id=1, source_target_pairs={{0,2},{1,3},{2,0},{3,1},{4,6},{5,7},{6,4},{7,5},{8,10},{9,11},{10,... | collective-permute-start | bytes 1572872 | tf_op jit(solution)/shard_map/ppermute | solution.py:600
  43.9 34.3 %collective-permute-start.14 = (bf16[256,1024]{1,0:T(8,128)(2,1)S(1)}, bf16[256,1024]{1,0:T(8,128)(2,1)S(1)}, u32[]{:S(2)}, u32[]{:S(2)}) collective-permute-start(bf16[256,1024]{1,0:T(8,128)(2,1)S(1)} %get-tuple-element.54), channel_id=1, source_target_pairs={{0,2},{1,3},{2,0},{3,1},{4,6},{5,7},{6,4},{7,5},{8,10},{9,11},{10,... | collective-permute-start | bytes 1572872 | tf_op jit(solution)/shard_map/ppermute | solution.py:604
  50.4 55.1 %collective-permute-start.27 = (bf16[2,128,2048]{2,1,0:T(8,128)(2,1)S(1)}, bf16[2,128,2048]{2,1,0:T(8,128)(2,1)S(1)}, u32[]{:S(2)}, u32[]{:S(2)}) collective-permute-start(bf16[2,128,2048]{2,1,0:T(8,128)(2,1)S(1)} %get-tuple-element.66), channel_id=1, source_target_pairs={{0,1},{1,0},{2,3},{3,2},{4,5},{5,4},{6,7},{7,6},{8,9},{9,8},{10,11... | collective-permute-start | bytes 3145736 | tf_op jit(solution)/shard_map/ppermute | solution.py:611
  56.6 21.5 %collective-permute-start.17 = (bf16[544,128]{1,0:T(8,128)(2,1)S(1)}, bf16[544,128]{1,0:T(8,128)(2,1)S(1)}, u32[]{:S(2)}, u32[]{:S(2)}) collective-permute-start(bf16[544,128]{1,0:T(8,128)(2,1)S(1)} %get-tuple-element.55), channel_id=1, source_target_pairs={{24,0},{28,1},{26,2},{30,3},{25,4},{29,5},{27,6},{31,7},{17,8},{21... | collective-permute-start | bytes 417800 | tf_op jit(solution)/shard_map/ppermute | solution.py:621
  67.9 34.2 %collective-permute-start.24 = (bf16[256,1024]{1,0:T(8,128)(2,1)S(1)}, bf16[256,1024]{1,0:T(8,128)(2,1)S(1)}, u32[]{:S(2)}, u32[]{:S(2)}) collective-permute-start(bf16[256,1024]{1,0:T(8,128)(2,1)S(1)} %collective-permute-done.23.refs_6_), channel_id=1, source_target_pairs={{0,4},{4,0},{8,12},{12,8},{16,20},{20,16},{24,28},{28,24},{1,5},{5... | collective-permute-start | bytes 1572872 | tf_op jit(solution)/shard_map/ppermute | solution.py:602
  78.1 31.6 %collective-permute-start.25 = (bf16[256,1024]{1,0:T(8,128)(2,1)S(1)}, bf16[256,1024]{1,0:T(8,128)(2,1)S(1)}, u32[]{:S(2)}, u32[]{:S(2)}) collective-permute-start(bf16[256,1024]{1,0:T(8,128)(2,1)S(1)} %collective-permute-done.23.refs_6_), channel_id=1, source_target_pairs={{0,1},{1,0},{2,3},{3,2},{4,5},{5,4},{6,7},{7,6},{8,9},{9,8},{10,11... | collective-permute-start | bytes 1572872 | tf_op jit(solution)/shard_map/ppermute | solution.py:605
  78.1 5.5 %collective-permute-start.18 = (bf16[544,128]{1,0:T(8,128)(2,1)S(1)}, bf16[544,128]{1,0:T(8,128)(2,1)S(1)}, u32[]{:S(2)}, u32[]{:S(2)}) collective-permute-start(bf16[544,128]{1,0:T(8,128)(2,1)S(1)} %get-tuple-element.56), channel_id=1, source_target_pairs={{0,0},{4,1},{2,2},{6,3},{1,4},{5,5},{3,6},{7,7},{9,8},{13,9},{11,1... | collective-permute-start | bytes 417800 | tf_op jit(solution)/shard_map/ppermute | solution.py:621
  83.7 9.0 %collective-permute-start.8 = (bf16[544,128]{1,0:T(8,128)(2,1)S(1)}, bf16[544,128]{1,0:T(8,128)(2,1)S(1)}, u32[]{:S(2)}, u32[]{:S(2)}) collective-permute-start(bf16[544,128]{1,0:T(8,128)(2,1)S(1)} %get-tuple-element.47), channel_id=1, source_target_pairs={{16,0},{20,1},{18,2},{22,3},{17,4},{21,5},{19,6},{23,7},{25,8},{29... | collective-permute-start | bytes 417800 | tf_op jit(solution)/shard_map/ppermute | solution.py:624
  92.7 5.1 %collective-permute-start.9 = (bf16[544,128]{1,0:T(8,128)(2,1)S(1)}, bf16[544,128]{1,0:T(8,128)(2,1)S(1)}, u32[]{:S(2)}, u32[]{:S(2)}) collective-permute-start(bf16[544,128]{1,0:T(8,128)(2,1)S(1)} %get-tuple-element.48), channel_id=1, source_target_pairs={{8,0},{12,1},{10,2},{14,3},{9,4},{13,5},{11,6},{15,7},{1,8},{5,9},... | collective-permute-start | bytes 417800 | tf_op jit(solution)/shard_map/ppermute | solution.py:624
  102.0 8.9 %collective-permute-start.26 = (bf16[256,1024]{1,0:T(8,128)(2,1)S(1)}, bf16[256,1024]{1,0:T(8,128)(2,1)S(1)}, u32[]{:S(2)}, u32[]{:S(2)}) collective-permute-start(bf16[256,1024]{1,0:T(8,128)(2,1)S(1)} %collective-permute-done.24.refs_7_), channel_id=1, source_target_pairs={{0,1},{1,0},{2,3},{3,2},{4,5},{5,4},{6,7},{7,6},{8,9},{9,8},{10,11... | collective-permute-start | bytes 1572872 | tf_op jit(solution)/shard_map/ppermute | solution.py:605
  109.2 16.6 %collective-permute-start.15 = (bf16[256,1024]{1,0:T(8,128)(2,1)S(1)}, bf16[256,1024]{1,0:T(8,128)(2,1)S(1)}, u32[]{:S(2)}, u32[]{:S(2)}) collective-permute-start(bf16[256,1024]{1,0:T(8,128)(2,1)S(1)} %collective-permute-done.13.refs_4_), channel_id=1, source_target_pairs={{0,1},{1,0},{2,3},{3,2},{4,5},{5,4},{6,7},{7,6},{8,9},{9,8},{10,11... | collective-permute-start | bytes 1572872 | tf_op jit(solution)/shard_map/ppermute | solution.py:605
  109.4 16.5 %collective-permute-start.16 = (bf16[256,1024]{1,0:T(8,128)(2,1)S(1)}, bf16[256,1024]{1,0:T(8,128)(2,1)S(1)}, u32[]{:S(2)}, u32[]{:S(2)}) collective-permute-start(bf16[256,1024]{1,0:T(8,128)(2,1)S(1)} %collective-permute-done.14.refs_5_), channel_id=1, source_target_pairs={{0,1},{1,0},{2,3},{3,2},{4,5},{5,4},{6,7},{7,6},{8,9},{9,8},{10,11... | collective-permute-start | bytes 1572872 | tf_op jit(solution)/shard_map/ppermute | solution.py:605
  109.8 16.1 %collective-permute-start.28 = (bf16[128,2048]{1,0:T(8,128)(2,1)S(1)}, bf16[128,2048]{1,0:T(8,128)(2,1)S(1)}, u32[]{:S(2)}, u32[]{:S(2)}) collective-permute-start(bf16[128,2048]{1,0:T(8,128)(2,1)S(1)} %shard_map.113), channel_id=1, source_target_pairs={{0,2},{1,3},{2,0},{3,1},{4,6},{5,7},{6,4},{7,5},{8,10},{9,11},{10,... | collective-permute-start | bytes 1572872 | tf_op jit(solution)/shard_map/ppermute | solution.py:615
  111.0 14.9 %collective-permute-start.11 = (bf16[2,128,128]{2,1,0:T(8,128)(2,1)S(1)}, bf16[2,128,128]{2,1,0:T(8,128)(2,1)S(1)}, u32[]{:S(2)}, u32[]{:S(2)}) collective-permute-start(bf16[2,128,128]{2,1,0:T(8,128)(2,1)S(1)} %get-tuple-element.51), channel_id=1, source_target_pairs={{0,2},{1,3},{2,0},{3,1},{4,6},{5,7},{6,4},{7,5},{8,10},{9,11},{10,... | collective-permute-start | bytes 196616 | tf_op jit(solution)/shard_map/ppermute | solution.py:629
  111.8 14.0 %collective-permute-start.12 = (bf16[2,128,128]{2,1,0:T(8,128)(2,1)S(1)}, bf16[2,128,128]{2,1,0:T(8,128)(2,1)S(1)}, u32[]{:S(2)}, u32[]{:S(2)}) collective-permute-start(bf16[2,128,128]{2,1,0:T(8,128)(2,1)S(1)} %get-tuple-element.52), channel_id=1, source_target_pairs={{0,3},{1,2},{2,1},{3,0},{4,7},{5,6},{6,5},{7,4},{8,11},{9,10},{10,... | collective-permute-start | bytes 196616 | tf_op jit(solution)/shard_map/ppermute | solution.py:629
  (8 other events, 73.5 us)

commit v8 on v7

--- a/solution.py
+++ b/solution.py
@@ -16,7 +16,8 @@
 NORM_EPS = 1e-06
 SEQ, TENSOR = "seq", "tensor"
 BOTH = (SEQ, TENSOR)
-EXTRA = 16
+EXTRA = 8
+CHUNKS = 4
 MIB = 1024 * 1024
 
 
@@ -63,6 +64,21 @@
 
 def shape(dims, kind=jnp.bfloat16):
     return jax.ShapeDtypeStruct(dims, kind)
+
+
+def out_rows(w_out, wanted, sems, width):
+    z = lax.axis_index(SEQ) >> 1
+    copies = []
+    for part, turns, at in wanted:
+        half = part.shape[1]
+        cols = pl.ds(pl.multiple_of(at * half, half), half)
+        for i, k in enumerate(turns):
+            here = pl.ds(pl.multiple_of((z ^ k) * width, width), width)
+            to = part.at[pl.ds(i * width, width), :]
+            copies.append(
+                pltpu.make_async_copy(w_out.at[here, cols], to, sems.at[len(copies)])
+            )
+    return copies
 
 
 def unit_heads(normed, w_qk, w_value, outs, clusters, steps, width):
@@ -93,8 +109,8 @@
 def project_far_body(
     tokens_at, gain_at, w_qk, w_value, clusters_at, w_out, *rest, width, stages, parts
 ):
-    out_low, out_high, normed, clusters, qk_next, val_next, out_early, out_late, out_rest = rest[:9]
-    tokens, gain, qk_buf, val_buf, sems, token_sems, out_sems = rest[9:]
+    out_low, out_high, normed, clusters, qk_next, val_next, out_early = rest[:7]
+    tokens, gain, qk_buf, val_buf, sems, token_sems, out_sems = rest[7:]
     z = lax.axis_index(SEQ) >> 1
     y = lax.axis_index(SEQ) & 1
     step = tokens.shape[0] // parts
@@ -109,23 +125,7 @@
         return pl.ds(pl.multiple_of(block * span, span), span)
 
     first, second = columns(1 ^ (z >> 1)), columns(z >> 1)
-    half = out_early.shape[1]
-    out_copies = []
-    for part, turns, at in (
-        (out_early, stages[0], y),
-        (out_late, stages[1], y),
-        (out_rest, stages[1], 1 - y),
-    ):
-        out_cols = pl.ds(pl.multiple_of(at * half, half), half)
-        for i, k in enumerate(turns):
-            here = pl.ds(pl.multiple_of((z ^ k) * width, width), width)
-            out_copies.append(
-                pltpu.make_async_copy(
-                    w_out.at[here, out_cols],
-                    part.at[pl.ds(i * width, width), :],
-                    out_sems.at[len(out_copies)],
-                )
-            )
+    out_copies = out_rows(w_out, ((out_early, stages[0], y),), out_sems, width)
     copies = [
         pltpu.make_async_copy(gain_at, gain, sems.at[0]),
         pltpu.make_async_copy(w_qk.at[:, first], qk_buf, sems.at[1]),
@@ -163,11 +163,9 @@
             shape(pair),
             shape(pair),
             shape((2 * width, w_out.shape[1] // 2)),
-            shape((2 * width, w_out.shape[1] // 2)),
-            shape((2 * width, w_out.shape[1] // 2)),
         ),
         in_specs=[any_spec()] * 6,
-        out_specs=(vmem_spec(),) * 9,
+        out_specs=(vmem_spec(),) * 7,
         scratch_shapes=[
             pltpu.VMEM((rows, depth), jnp.bfloat16),
             pltpu.VMEM((1, depth), jnp.float32),
@@ -175,7 +173,7 @@
             pltpu.VMEM(pair, jnp.bfloat16),
             pltpu.SemaphoreType.DMA((6,)),
             pltpu.SemaphoreType.DMA((parts,)),
-            pltpu.SemaphoreType.DMA((6,)),
+            pltpu.SemaphoreType.DMA((2,)),
         ],
         compiler_params=params(20),
         cost_estimate=cost(8 * rows * depth * width, 2 * rows * depth + 12 * depth * width),
@@ -183,44 +181,60 @@
 
 
 def project_near_body(
-    normed, w_qk, w_value, clusters, w_up, out_low, out_high, next_half, sem, *, width
+    normed, w_qk, w_value, clusters, w_up, w_out, *rest, width, late
 ):
-    copy = pltpu.make_async_copy(w_up.at[:, pl.ds(0, next_half.shape[1])], next_half, sem)
-    copy.start()
+    out_low, out_high, first, out_late, out_rest, sem, out_sems = rest
+    y = lax.axis_index(SEQ) & 1
+    wanted = ((out_late, late, y), (out_rest, late, 1 - y))
+    copies = [
+        pltpu.make_async_copy(w_up.at[:, pl.ds(0, first.shape[1])], first, sem),
+        *out_rows(w_out, wanted, out_sems, width),
+    ]
+    for copy in copies:
+        copy.start()
     unit_heads(normed, w_qk, w_value, (out_low, out_high), clusters, (0, 1), width)
-    copy.wait()
-
-
-def project_near(normed, w_qk, w_value, clusters, w_up, width):
+    for copy in copies:
+        copy.wait()
+
+
+def project_near(normed, w_qk, w_value, clusters, w_up, w_out, width, late):
     rows, depth = normed.shape
     message = shape((rows + EXTRA, 2 * width))
-    return pl.pallas_call(
-        functools.partial(project_near_body, width=width),
-        out_shape=(message, message, shape((depth, w_up.shape[1] // 2))),
-        in_specs=[vmem_spec()] * 4 + [any_spec()],
-        out_specs=(vmem_spec(),) * 3,
-        scratch_shapes=[pltpu.SemaphoreType.DMA],
+    part = shape((2 * width, w_out.shape[1] // 2))
+    return pl.pallas_call(
+        functools.partial(project_near_body, width=width, late=late),
+        out_shape=(message, message, shape((depth, w_up.shape[1] // CHUNKS)), part, part),
+        in_specs=[vmem_spec()] * 4 + [any_spec()] * 2,
+        out_specs=(vmem_spec(),) * 5,
+        scratch_shapes=[pltpu.SemaphoreType.DMA, pltpu.SemaphoreType.DMA((4,))],
         compiler_params=params(16),
         cost_estimate=cost(8 * rows * depth * width, 2 * rows * depth + 8 * depth * width),
-    )(normed, w_qk, w_value, clusters, held(w_up))
-
-
-def up_body(normed, first, w_up, w_down, hidden, next_half, second, sems):
-    half = first.shape[1]
-    copies = (
-        pltpu.make_async_copy(w_up.at[:, pl.ds(half, half)], second, sems.at[0]),
-        pltpu.make_async_copy(
-            w_down.at[:, pl.ds(0, next_half.shape[1])], next_half, sems.at[1]
-        ),
-    )
-    for copy in copies:
+    )(normed, w_qk, w_value, clusters, held(w_up), held(w_out))
+
+
+def chunk_copies(source, buf, sems):
+    step = buf.shape[2]
+    return [
+        pltpu.make_async_copy(source.at[:, pl.ds((c + 1) * step, step)], buf.at[c], sems.at[c])
+        for c in range(CHUNKS - 1)
+    ]
+
+
+def up_body(normed, first, w_up, w_down, hidden, next_first, others, sems, next_sem):
+    step = first.shape[1]
+    copies = chunk_copies(w_up, others, sems)
+    later = pltpu.make_async_copy(
+        w_down.at[:, pl.ds(0, next_first.shape[1])], next_first, next_sem
+    )
+    for copy in (*copies, later):
         copy.start()
-    for at, weights in enumerate((first, second)):
-        if at == 1:
-            copies[0].wait()
-        grown = jnp.dot(normed[...], weights[...], preferred_element_type=jnp.float32)
-        hidden[:, at * half : (at + 1) * half] = jnp.maximum(grown, 0.0).astype(jnp.bfloat16)
-    copies[1].wait()
+    for c in range(CHUNKS):
+        if c:
+            copies[c - 1].wait()
+        weights = others[c - 1] if c else first[...]
+        grown = jnp.dot(normed[...], weights, preferred_element_type=jnp.float32)
+        hidden[:, c * step : (c + 1) * step] = jnp.maximum(grown, 0.0).astype(jnp.bfloat16)
+    later.wait()
 
 
 def up(normed, first, w_up, w_down):
@@ -228,34 +242,35 @@
     units = w_up.shape[1]
     return pl.pallas_call(
         up_body,
-        out_shape=(shape((rows, units)), shape((units, w_down.shape[1] // 2))),
+        out_shape=(shape((rows, units)), shape((units, w_down.shape[1] // CHUNKS))),
         in_specs=[vmem_spec(), vmem_spec(), any_spec(), any_spec()],
         out_specs=(vmem_spec(), vmem_spec()),
         scratch_shapes=[
-            pltpu.VMEM((depth, units // 2), jnp.bfloat16),
-            pltpu.SemaphoreType.DMA((2,)),
+            pltpu.VMEM((CHUNKS - 1, depth, units // CHUNKS), jnp.bfloat16),
+            pltpu.SemaphoreType.DMA((CHUNKS - 1,)),
+            pltpu.SemaphoreType.DMA,
         ],
         compiler_params=params(24),
         cost_estimate=cost(2 * rows * depth * units, 2 * depth * units + 4 * rows * depth),
     )(normed, first, held(w_up), held(w_down))
 
 
-def down_body(hidden, first, w_down, mine, far, away, second, held_rows, sem, *, share):
+def down_body(hidden, first, w_down, mine, far, away, others, held_rows, sems, *, share):
     at = lax.axis_index(TENSOR)
-    half = first.shape[1]
-    copy = pltpu.make_async_copy(w_down.at[:, pl.ds(half, half)], second, sem)
-    copy.start()
+    step = first.shape[1]
+    copies = chunk_copies(w_down, others, sems)
+    for copy in copies:
+        copy.start()
 
     def quarter(turn):
         return held_rows[pl.ds(pl.multiple_of((at ^ turn) * share, share), share), :]
 
-    for part, weights in enumerate((first, second)):
-        if part == 1:
-            copy.wait()
-        cols = slice(part * half, (part + 1) * half)
-        held_rows[...] = jnp.dot(
-            hidden[...], weights[...], preferred_element_type=jnp.float32
-        )
+    for c in range(CHUNKS):
+        if c:
+            copies[c - 1].wait()
+        weights = others[c - 1] if c else first[...]
+        cols = slice(c * step, (c + 1) * step)
+        held_rows[...] = jnp.dot(hidden[...], weights, preferred_element_type=jnp.float32)
         mine[:, cols] = quarter(0)
         far[:, cols] = quarter(2)
         away[0, :, cols] = quarter(1).astype(jnp.bfloat16)
@@ -275,9 +290,9 @@
         in_specs=[vmem_spec(), vmem_spec(), any_spec()],
         out_specs=(vmem_spec(),) * 3,
         scratch_shapes=[
-            pltpu.VMEM((units, depth // 2), jnp.bfloat16),
-            pltpu.VMEM((rows, depth // 2), jnp.float32),
-            pltpu.SemaphoreType.DMA,
+            pltpu.VMEM((CHUNKS - 1, units, depth // CHUNKS), jnp.bfloat16),
+            pltpu.VMEM((rows, depth // CHUNKS), jnp.float32),
+            pltpu.SemaphoreType.DMA((CHUNKS - 1,)),
         ],
         compiler_params=params(24),
         cost_estimate=cost(2 * rows * depth * units, 2 * depth * units + 6 * rows * depth),
@@ -590,20 +605,21 @@
     swap_y = [(s, s ^ 1) for s in range(seq_count)]
     messages, own, other = [None] * heads, [None] * heads, [None] * heads
     early, late = (heads - 1, 0), (heads - 2, 1)
-    messages[2], messages[3], normed, ids, qk_next, val_next, *out_parts = project_far(
+    messages[2], messages[3], normed, ids, qk_next, val_next, out_early = project_far(
         tokens, norm_gain, w_qk, w_value, clusters, w_out, width, (early, late)
     )
     for k in (3, 2):
         own[k] = lax.ppermute(messages[k], BOTH, steps[k])
-    halves = {}
-    for name in "el":
-        here = lax.ppermute(out_parts.pop(0), TENSOR, swaps[2])
-        if name == "e":
-            there = lax.ppermute(here, SEQ, swap_y)
-        else:
-            there = lax.ppermute(out_parts.pop(0), TENSOR, swaps[2])
-        halves[name] = [here, there] + [lax.ppermute(w, TENSOR, swaps[1]) for w in (here, there)]
-    messages[0], messages[1], up_first = project_near(normed, qk_next, val_next, ids, w_up, width)
+    fx_early = lax.ppermute(out_early, TENSOR, swaps[2])
+    messages[0], messages[1], up_first, out_late, out_rest = project_near(
+        normed, qk_next, val_next, ids, w_up, w_out, width, late
+    )
+    halves = {
+        "e": [fx_early, lax.ppermute(fx_early, SEQ, swap_y)],
+        "l": [lax.ppermute(out_late, TENSOR, swaps[2]), lax.ppermute(out_rest, TENSOR, swaps[2])],
+    }
+    for pair in halves.values():
+        pair += [lax.ppermute(w, TENSOR, swaps[1]) for w in (pair[0], pair[1])]
     for k in (1, 0):
         own[k] = lax.ppermute(messages[k], BOTH, steps[k])
     hidden, down_first = up(normed, up_first, w_up, w_down)

time: 128 us -> 128 us (level)
  transfers between devices with their start and end apart: 29 -> 29, of which waited for: 10 -> 9; matrix products, arithmetic and copies ran while one was open for 0% -> 0% of each run, Pallas kernels for 17% -> 18%
where the time goes in v8:
time: 128 us; the launch traced here: 127 us
  waiting for transfers between devices  56.8 us (44%)
  starting transfers between devices  37.6 us (29%)
  Pallas kernels  32.2 us (25%)
    ppermute x6, waiting for transfers between devices, by_heads(): lax.ppermute(away[d - 1], TENSOR, swaps[d])  17.9 us
    ppermute x4, waiting for transfers between devices, by_heads(): back[k] = lax.ppermute(result, BOTH, turned(steps[k]))  12.4 us
    ppermute x4, starting transfers between devices, by_heads(): other[k] = lax.ppermute(own[k], TENSOR, swaps[1])  12.2 us
    pallas_call x2, Pallas kernels, attend(): pl.pallas_call(functools.partial(attend_body, heads=heads, width=width, o...  10 us
    ppermute x1, waiting for transfers between devices, by_heads(): lax.ppermute(out_late, TENSOR, swaps[2])  9.78 us
    ppermute x1, waiting for transfers between devices, by_heads(): lax.ppermute(out_rest, TENSOR, swaps[2])  9.69 us
    ppermute x4, starting transfers between devices, by_heads(): own[k] = lax.ppermute(messages[k], BOTH, steps[k])  7.62 us
    ppermute x4, waiting for transfers between devices, by_heads(): own[k] = lax.ppermute(messages[k], BOTH, steps[k])  7.02 us
  transfers between devices with their start and end apart: 29, of which 9 were waited for; matrix products, arithmetic and copies ran while one was open for 0% of the time, Pallas kernels for 18%

profile of v8, /device:TPU:0, one launch (start us, length us, event | category | flops | bytes accessed | tf_op | source)
XLA Modules:
  0.0 127.4 jit_solution(12078844599480839320)
XLA Ops:
  0.6 4.3 %shard_map.104 = (bf16[520,256]{1,0:T(8,128)(2,1)S(1)}, bf16[520,256]{1,0:T(8,128)(2,1)S(1)}, bf16[512,2048]{1,0:T(8,128)(2,1)S(1)}, s32[4,512]{1,0:T(4,128)S(1)...) custom-call(bf16[512,2048]{1,0:T(8,128)(2,1)} %refs_10_.1, ...), custom_call_target="tpu_custom_call" | custom-call | flops 1073741824 | bytes 5242880 | tf_op jit(solution)/shard_map/pallas_call | solution.py:156
  4.9 3.2 %shard_map.105 = (bf16[520,256]{1,0:T(8,128)(2,1)S(1)}, bf16[520,256]{1,0:T(8,128)(2,1)S(1)}, bf16[2048,512]{1,0:T(8,128)(2,1)S(1)}, bf16[256,1024]{1,0:T(8,128)(2,1)S(1)}, bf16[256,1024]{1,0:T(8,128)(2,1)S(1)}) custom-call(bf16[512,2048]{1,0:T(8,128)(2,1)S(1)} %get-tuple-element.37.normed, bf16[2048,256]{1,0:T(8,128)(2,1)S(1)} %get-tuple-element.38.w_qk, ...), custom_call_target="tpu_custom_call" | custom-call | flops 1073741824 | bytes 4194304 | tf_op jit(solution)/shard_map/pallas_call | solution.py:204
  8.8 4.3 %collective-permute-start.1 = (bf16[520,256]{1,0:T(8,128)(2,1)S(1)}, bf16[520,256]{1,0:T(8,128)(2,1)S(1)}, u32[]{:S(2)}, u32[]{:S(2)}) collective-permute-start(bf16[520,256]{1,0:T(8,128)(2,1)S(1)} %get-tuple-element.42), channel_id=1, source_target_pairs={{0,8},{1,12},{2,10},{3,14},{4,9},{5,13},{6,11},{7,15},{8,1},{9,5},... | collective-permute-start | bytes 798728 | tf_op jit(solution)/shard_map/ppermute | solution.py:624
  13.1 2.6 %collective-permute-start.2 = (bf16[520,256]{1,0:T(8,128)(2,1)S(1)}, bf16[520,256]{1,0:T(8,128)(2,1)S(1)}, u32[]{:S(2)}, u32[]{:S(2)}) collective-permute-start(bf16[520,256]{1,0:T(8,128)(2,1)S(1)} %get-tuple-element.43), channel_id=1, source_target_pairs={{0,16},{1,20},{2,18},{3,22},{4,17},{5,21},{6,19},{7,23},{8,25},{9,... | collective-permute-start | bytes 798728 | tf_op jit(solution)/shard_map/ppermute | solution.py:612
  15.7 1.7 %collective-permute-start.22 = (bf16[512,2048]{1,0:T(8,128)(2,1)S(1)}, bf16[512,2048]{1,0:T(8,128)(2,1)S(1)}, u32[]{:S(2)}, u32[]{:S(2)}) collective-permute-start(bf16[512,2048]{1,0:T(8,128)(2,1)S(1)} %copy-done.2), channel_id=1, source_target_pairs={{0,1},{1,0},{2,3},{3,2},{4,5},{5,4},{6,7},{7,6},{8,9},{9,8},{10,11... | collective-permute-start | bytes 6291464 | tf_op jit(solution)/shard_map/ppermute | solution.py:603
  18.9 7.0 %collective-permute-done.1.refs_1_ = bf16[520,256]{1,0:T(8,128)(2,1)S(1)} collective-permute-done((bf16[520,256]{1,0:T(8,128)(2,1)S(1)}, bf16[520,256]{1,0:T(8,128)(2,1)S(1)}, u32[]{:S(2)}, u32[]{:S(2)}) %collective-permute-start.1) | collective-permute-done | bytes 266272 | tf_op jit(solution)/shard_map/ppermute | solution.py:624
  25.9 10.7 %collective-permute-start.6 = (bf16[520,256]{1,0:T(8,128)(2,1)S(1)}, bf16[520,256]{1,0:T(8,128)(2,1)S(1)}, u32[]{:S(2)}, u32[]{:S(2)}) collective-permute-start(bf16[520,256]{1,0:T(8,128)(2,1)S(1)} %collective-permute-done.2.refs_2_), channel_id=1, source_target_pairs={{0,1},{1,0},{2,3},{3,2},{4,5},{5,4},{6,7},{7,6},{8,9},{9,8},{10,11... | collective-permute-start | bytes 798728 | tf_op jit(solution)/shard_map/ppermute | solution.py:629
  36.6 5.4 %shard_map.110 = (bf16[512,2048]{1,0:T(8,128)(2,1)S(1)}, bf16[2048,512]{1,0:T(8,128)(2,1)S(1)}) custom-call(bf16[512,2048]{1,0:T(8,128)(2,1)S(1)} %get-tuple-element.37.normed, bf16[2048,512]{1,0:T(8,128)(2,1)S(1)} %get-tuple-element.62.first, bf16[2048,2048]{1,0:T(8,128)(2,1)} %w_up.3, bf16[2048,2048]{1,0:T(8,128)(2,1)} %w_down.3), custom_call_target="tpu_custom_call" | custom-call | flops 4294967296 | bytes 12582912 | tf_op jit(solution)/shard_map/pallas_call | solution.py:243
  42.0 1.6 %collective-permute-start.23 = (bf16[256,1024]{1,0:T(8,128)(2,1)S(1)}, bf16[256,1024]{1,0:T(8,128)(2,1)S(1)}, u32[]{:S(2)}, u32[]{:S(2)}) collective-permute-start(bf16[256,1024]{1,0:T(8,128)(2,1)S(1)} %get-tuple-element.61), channel_id=1, source_target_pairs={{0,2},{1,3},{2,0},{3,1},{4,6},{5,7},{6,4},{7,5},{8,10},{9,11},{10,... | collective-permute-start | bytes 1572872 | tf_op jit(solution)/shard_map/ppermute | solution.py:613
  44.1 1.5 %collective-permute-start.14 = (bf16[256,1024]{1,0:T(8,128)(2,1)S(1)}, bf16[256,1024]{1,0:T(8,128)(2,1)S(1)}, u32[]{:S(2)}, u32[]{:S(2)}) collective-permute-start(bf16[256,1024]{1,0:T(8,128)(2,1)S(1)} %get-tuple-element.54), channel_id=1, source_target_pairs={{0,2},{1,3},{2,0},{3,1},{4,6},{5,7},{6,4},{7,5},{8,10},{9,11},{10,... | collective-permute-start | bytes 1572872 | tf_op jit(solution)/shard_map/ppermute | solution.py:619
  45.6 5.6 %shard_map.111 = (f32[128,2048]{1,0:T(8,128)S(1)}, f32[128,2048]{1,0:T(8,128)S(1)}, bf16[2,128,2048]{2,1,0:T(8,128)(2,1)S(1)}) custom-call(bf16[512,2048]{1,0:T(8,128)(2,1)S(1)} %get-tuple-element.63.hidden, bf16[2048,512]{1,0:T(8,128)(2,1)S(1)} %get-tuple-element.64.first, bf16[2048,2048]{1,0:T(8,128)(2,1)} %w_down.3), custom_call_target="tpu_custom_call" | custom-call | flops 4294967296 | bytes 14680064 | tf_op jit(solution)/shard_map/pallas_call | solution.py:283
  51.8 5.2 %shard_map.106 = (bf16[544,128]{1,0:T(8,128)(2,1)S(1)}, bf16[544,128]{1,0:T(8,128)(2,1)S(1)}, bf16[8,512,256]{2,1,0:T(8,128)(2,1)S(1)}, f32[8,8,512]{2,1,0:T(8,128)S(1)}) custom-call(bf16[520,256]{1,0:T(8,128)(2,1)S(1)} %collective-permute-done.refs_0_, bf16[520,256]{1,0:T(8,128)(2,1)S(1)} %collective-permute-done.1.refs_1_, ...), custom_call_target="tpu_custom_call" | custom-call | flops 2415919104 | bytes 2097152 | tf_op jit(solution)/shard_map/pallas_call | solution.py:427
  58.3 9.8 %collective-permute-done.13.refs_4_ = bf16[256,1024]{1,0:T(8,128)(2,1)S(1)} collective-permute-done((bf16[256,1024]{1,0:T(8,128)(2,1)S(1)}, bf16[256,1024]{1,0:T(8,128)(2,1)S(1)}, u32[]{:S(2)}, u32[]{:S(2)}) %collective-permute-start.13) | collective-permute-done | bytes 524320 | tf_op jit(solution)/shard_map/ppermute | solution.py:619
  68.7 9.7 %collective-permute-done.14.refs_5_ = bf16[256,1024]{1,0:T(8,128)(2,1)S(1)} collective-permute-done((bf16[256,1024]{1,0:T(8,128)(2,1)S(1)}, bf16[256,1024]{1,0:T(8,128)(2,1)S(1)}, u32[]{:S(2)}, u32[]{:S(2)}) %collective-permute-start.14) | collective-permute-done | bytes 524320 | tf_op jit(solution)/shard_map/ppermute | solution.py:619
  79.0 4.8 %shard_map.107 = (bf16[544,128]{1,0:T(8,128)(2,1)S(1)}, bf16[544,128]{1,0:T(8,128)(2,1)S(1)}) custom-call(bf16[8,512,256]{2,1,0:T(8,128)(2,1)S(1)} %get-tuple-element.45.refs_0_, f32[8,8,512]{2,1,0:T(8,128)S(1)} %get-tuple-element.46.refs_1_), custom_call_target="tpu_custom_call" | custom-call | flops 2415919104 | bytes 2097152 | tf_op jit(solution)/shard_map/pallas_call | solution.py:427
  84.1 8.8 %collective-permute-done.8.refs_0_ = bf16[544,128]{1,0:T(8,128)(2,1)S(1)} collective-permute-done((bf16[544,128]{1,0:T(8,128)(2,1)S(1)}, bf16[544,128]{1,0:T(8,128)(2,1)S(1)}, u32[]{:S(2)}, u32[]{:S(2)}) %collective-permute-start.8) | collective-permute-done | bytes 139296 | tf_op jit(solution)/shard_map/ppermute | solution.py:640
  94.3 3.6 %collective-permute-done.9.refs_1_ = bf16[544,128]{1,0:T(8,128)(2,1)S(1)} collective-permute-done((bf16[544,128]{1,0:T(8,128)(2,1)S(1)}, bf16[544,128]{1,0:T(8,128)(2,1)S(1)}, u32[]{:S(2)}, u32[]{:S(2)}) %collective-permute-start.9) | collective-permute-done | bytes 139296 | tf_op jit(solution)/shard_map/ppermute | solution.py:640
  98.0 1.7 %collective-permute-start.19 = (bf16[2,128,128]{2,1,0:T(8,128)(2,1)S(1)}, bf16[2,128,128]{2,1,0:T(8,128)(2,1)S(1)}, u32[]{:S(2)}, u32[]{:S(2)}) collective-permute-start(bf16[2,128,128]{2,1,0:T(8,128)(2,1)S(1)} %get-tuple-element.58), channel_id=1, source_target_pairs={{0,1},{1,0},{2,3},{3,2},{4,5},{5,4},{6,7},{7,6},{8,9},{9,8},{10,11... | collective-permute-start | bytes 196616 | tf_op jit(solution)/shard_map/ppermute | solution.py:645
  100.5 1.5 %collective-permute-start.20 = (bf16[2,128,128]{2,1,0:T(8,128)(2,1)S(1)}, bf16[2,128,128]{2,1,0:T(8,128)(2,1)S(1)}, u32[]{:S(2)}, u32[]{:S(2)}) collective-permute-start(bf16[2,128,128]{2,1,0:T(8,128)(2,1)S(1)} %get-tuple-element.59), channel_id=1, source_target_pairs={{0,2},{1,3},{2,0},{3,1},{4,6},{5,7},{6,4},{7,5},{8,10},{9,11},{10,... | collective-permute-start | bytes 196616 | tf_op jit(solution)/shard_map/ppermute | solution.py:645
  102.2 2.7 %collective-permute-done.20.refs_2_ = bf16[2,128,128]{2,1,0:T(8,128)(2,1)S(1)} collective-permute-done((bf16[2,128,128]{2,1,0:T(8,128)(2,1)S(1)}, bf16[2,128,128]{2,1,0:T(8,128)(2,1)S(1)}, u32[]{:S(2)}, u32[]{:S(2)}) %collective-permute-start.20) | collective-permute-done | bytes 65568 | tf_op jit(solution)/shard_map/ppermute | solution.py:645
  106.6 2.6 %collective-permute-done.21.refs_3_ = bf16[2,128,128]{2,1,0:T(8,128)(2,1)S(1)} collective-permute-done((bf16[2,128,128]{2,1,0:T(8,128)(2,1)S(1)}, bf16[2,128,128]{2,1,0:T(8,128)(2,1)S(1)}, u32[]{:S(2)}, u32[]{:S(2)}) %collective-permute-start.21) | collective-permute-done | bytes 65568 | tf_op jit(solution)/shard_map/ppermute | solution.py:645
  112.1 2.1 %shard_map.112 = (f32[128,2048]{1,0:T(8,128)S(1)}, bf16[512,2048]{1,0:T(8,128)(2,1)S(1)}) custom-call(bf16[2,128,128]{2,1,0:T(8,128)(2,1)S(1)} %get-tuple-element.57.refs_0_, bf16[2,128,128]{2,1,0:T(8,128)(2,1)S(1)} %collective-permute-done.19.refs_1_, bf16[2,128,128]{2,1,0:T(8,128)(2,1)S(1)} %collective-permute-done.20.refs_2_, ...), custom_call_target="tpu_custom_call" | custom-call | flops 536870912 | bytes 10485760 | tf_op jit(solution)/shard_map/pallas_call | solution.py:538
  114.2 11.6 %collective-permute-done.11.refs_2_ = bf16[2,128,128]{2,1,0:T(8,128)(2,1)S(1)} collective-permute-done((bf16[2,128,128]{2,1,0:T(8,128)(2,1)S(1)}, bf16[2,128,128]{2,1,0:T(8,128)(2,1)S(1)}, u32[]{:S(2)}, u32[]{:S(2)}) %collective-permute-start.11) | collective-permute-done | bytes 65568 | tf_op jit(solution)/shard_map/ppermute | solution.py:645
  125.8 1.5 %shard_map.114 = (bf16[128,2048]{1,0:T(8,128)(2,1)}, f32[4,32,128]{2,1,0:T(8,128)}) custom-call(bf16[2,128,128]{2,1,0:T(8,128)(2,1)S(1)} %get-tuple-element.49.refs_0_, bf16[2,128,128]{2,1,0:T(8,128)(2,1)S(1)} %collective-permute-done.10.refs_1_, bf16[2,128,128]{2,1,0:T(8,128)(2,1)S(1)} %collective-permute-done.11.refs_2_, ...), custom_call_target="tpu_custom_call" | custom-call | flops 536870912 | bytes 6291456 | tf_op jit(solution)/shard_map/pallas_call | solution.py:581
  (51 shorter events, 13.2 us)
Async XLA Ops:
  8.1 9.3 %collective-permute-start = (bf16[520,256]{1,0:T(8,128)(2,1)S(1)}, bf16[520,256]{1,0:T(8,128)(2,1)S(1)}, u32[]{:S(2)}, u32[]{:S(2)}) collective-permute-start(bf16[520,256]{1,0:T(8,128)(2,1)S(1)} %get-tuple-element.41), channel_id=1, source_target_pairs={{0,0},{1,4},{2,2},{3,6},{4,1},{5,5},{6,3},{7,7},{8,9},{9,13},{10,1... | collective-permute-start | bytes 798728 | tf_op jit(solution)/shard_map/ppermute | solution.py:624
  8.8 17.1 %collective-permute-start.1 = (bf16[520,256]{1,0:T(8,128)(2,1)S(1)}, bf16[520,256]{1,0:T(8,128)(2,1)S(1)}, u32[]{:S(2)}, u32[]{:S(2)}) collective-permute-start(bf16[520,256]{1,0:T(8,128)(2,1)S(1)} %get-tuple-element.42), channel_id=1, source_target_pairs={{0,8},{1,12},{2,10},{3,14},{4,9},{5,13},{6,11},{7,15},{8,1},{9,5},... | collective-permute-start | bytes 798728 | tf_op jit(solution)/shard_map/ppermute | solution.py:624
  13.1 12.8 %collective-permute-start.2 = (bf16[520,256]{1,0:T(8,128)(2,1)S(1)}, bf16[520,256]{1,0:T(8,128)(2,1)S(1)}, u32[]{:S(2)}, u32[]{:S(2)}) collective-permute-start(bf16[520,256]{1,0:T(8,128)(2,1)S(1)} %get-tuple-element.43), channel_id=1, source_target_pairs={{0,16},{1,20},{2,18},{3,22},{4,17},{5,21},{6,19},{7,23},{8,25},{9,... | collective-permute-start | bytes 798728 | tf_op jit(solution)/shard_map/ppermute | solution.py:612
  15.7 96.1 %collective-permute-start.22 = (bf16[512,2048]{1,0:T(8,128)(2,1)S(1)}, bf16[512,2048]{1,0:T(8,128)(2,1)S(1)}, u32[]{:S(2)}, u32[]{:S(2)}) collective-permute-start(bf16[512,2048]{1,0:T(8,128)(2,1)S(1)} %copy-done.2), channel_id=1, source_target_pairs={{0,1},{1,0},{2,3},{3,2},{4,5},{5,4},{6,7},{7,6},{8,9},{9,8},{10,11... | collective-permute-start | bytes 6291464 | tf_op jit(solution)/shard_map/ppermute | solution.py:603
  17.4 24.6 %collective-permute-start.3 = (bf16[520,256]{1,0:T(8,128)(2,1)S(1)}, bf16[520,256]{1,0:T(8,128)(2,1)S(1)}, u32[]{:S(2)}, u32[]{:S(2)}) collective-permute-start(bf16[520,256]{1,0:T(8,128)(2,1)S(1)} %get-tuple-element.44), channel_id=1, source_target_pairs={{0,24},{1,28},{2,26},{3,30},{4,25},{5,29},{6,27},{7,31},{8,17},{9,... | collective-permute-start | bytes 798728 | tf_op jit(solution)/shard_map/ppermute | solution.py:612
  17.4 26.2 %collective-permute-start.4 = (bf16[520,256]{1,0:T(8,128)(2,1)S(1)}, bf16[520,256]{1,0:T(8,128)(2,1)S(1)}, u32[]{:S(2)}, u32[]{:S(2)}) collective-permute-start(bf16[520,256]{1,0:T(8,128)(2,1)S(1)} %collective-permute-done.refs_0_), channel_id=1, source_target_pairs={{0,1},{1,0},{2,3},{3,2},{4,5},{5,4},{6,7},{7,6},{8,9},{9,8},{10,11... | collective-permute-start | bytes 798728 | tf_op jit(solution)/shard_map/ppermute | solution.py:629
  25.9 18.2 %collective-permute-start.5 = (bf16[520,256]{1,0:T(8,128)(2,1)S(1)}, bf16[520,256]{1,0:T(8,128)(2,1)S(1)}, u32[]{:S(2)}, u32[]{:S(2)}) collective-permute-start(bf16[520,256]{1,0:T(8,128)(2,1)S(1)} %collective-permute-done.1.refs_1_), channel_id=1, source_target_pairs={{0,1},{1,0},{2,3},{3,2},{4,5},{5,4},{6,7},{7,6},{8,9},{9,8},{10,11... | collective-permute-start | bytes 798728 | tf_op jit(solution)/shard_map/ppermute | solution.py:629
  25.9 19.7 %collective-permute-start.6 = (bf16[520,256]{1,0:T(8,128)(2,1)S(1)}, bf16[520,256]{1,0:T(8,128)(2,1)S(1)}, u32[]{:S(2)}, u32[]{:S(2)}) collective-permute-start(bf16[520,256]{1,0:T(8,128)(2,1)S(1)} %collective-permute-done.2.refs_2_), channel_id=1, source_target_pairs={{0,1},{1,0},{2,3},{3,2},{4,5},{5,4},{6,7},{7,6},{8,9},{9,8},{10,11... | collective-permute-start | bytes 798728 | tf_op jit(solution)/shard_map/ppermute | solution.py:629
  42.0 15.0 %collective-permute-start.23 = (bf16[256,1024]{1,0:T(8,128)(2,1)S(1)}, bf16[256,1024]{1,0:T(8,128)(2,1)S(1)}, u32[]{:S(2)}, u32[]{:S(2)}) collective-permute-start(bf16[256,1024]{1,0:T(8,128)(2,1)S(1)} %get-tuple-element.61), channel_id=1, source_target_pairs={{0,2},{1,3},{2,0},{3,1},{4,6},{5,7},{6,4},{7,5},{8,10},{9,11},{10,... | collective-permute-start | bytes 1572872 | tf_op jit(solution)/shard_map/ppermute | solution.py:613
  43.6 24.5 %collective-permute-start.13 = (bf16[256,1024]{1,0:T(8,128)(2,1)S(1)}, bf16[256,1024]{1,0:T(8,128)(2,1)S(1)}, u32[]{:S(2)}, u32[]{:S(2)}) collective-permute-start(bf16[256,1024]{1,0:T(8,128)(2,1)S(1)} %get-tuple-element.53), channel_id=1, source_target_pairs={{0,2},{1,3},{2,0},{3,1},{4,6},{5,7},{6,4},{7,5},{8,10},{9,11},{10,... | collective-permute-start | bytes 1572872 | tf_op jit(solution)/shard_map/ppermute | solution.py:619
  44.1 34.3 %collective-permute-start.14 = (bf16[256,1024]{1,0:T(8,128)(2,1)S(1)}, bf16[256,1024]{1,0:T(8,128)(2,1)S(1)}, u32[]{:S(2)}, u32[]{:S(2)}) collective-permute-start(bf16[256,1024]{1,0:T(8,128)(2,1)S(1)} %get-tuple-element.54), channel_id=1, source_target_pairs={{0,2},{1,3},{2,0},{3,1},{4,6},{5,7},{6,4},{7,5},{8,10},{9,11},{10,... | collective-permute-start | bytes 1572872 | tf_op jit(solution)/shard_map/ppermute | solution.py:619
  45.6 5.6 %collective-permute-start.7 = (bf16[520,256]{1,0:T(8,128)(2,1)S(1)}, bf16[520,256]{1,0:T(8,128)(2,1)S(1)}, u32[]{:S(2)}, u32[]{:S(2)}) collective-permute-start(bf16[520,256]{1,0:T(8,128)(2,1)S(1)} %collective-permute-done.3.refs_3_), channel_id=1, source_target_pairs={{0,1},{1,0},{2,3},{3,2},{4,5},{5,4},{6,7},{7,6},{8,9},{9,8},{10,11... | collective-permute-start | bytes 798728 | tf_op jit(solution)/shard_map/ppermute | solution.py:629
  51.2 54.3 %collective-permute-start.27 = (bf16[2,128,2048]{2,1,0:T(8,128)(2,1)S(1)}, bf16[2,128,2048]{2,1,0:T(8,128)(2,1)S(1)}, u32[]{:S(2)}, u32[]{:S(2)}) collective-permute-start(bf16[2,128,2048]{2,1,0:T(8,128)(2,1)S(1)} %get-tuple-element.66), channel_id=1, source_target_pairs={{0,1},{1,0},{2,3},{3,2},{4,5},{5,4},{6,7},{7,6},{8,9},{9,8},{10,11... | collective-permute-start | bytes 3145736 | tf_op jit(solution)/shard_map/ppermute | solution.py:627
  57.0 21.4 %collective-permute-start.17 = (bf16[544,128]{1,0:T(8,128)(2,1)S(1)}, bf16[544,128]{1,0:T(8,128)(2,1)S(1)}, u32[]{:S(2)}, u32[]{:S(2)}) collective-permute-start(bf16[544,128]{1,0:T(8,128)(2,1)S(1)} %get-tuple-element.55), channel_id=1, source_target_pairs={{24,0},{28,1},{26,2},{30,3},{25,4},{29,5},{27,6},{31,7},{17,8},{21... | collective-permute-start | bytes 417800 | tf_op jit(solution)/shard_map/ppermute | solution.py:637
  68.1 34.0 %collective-permute-start.24 = (bf16[256,1024]{1,0:T(8,128)(2,1)S(1)}, bf16[256,1024]{1,0:T(8,128)(2,1)S(1)}, u32[]{:S(2)}, u32[]{:S(2)}) collective-permute-start(bf16[256,1024]{1,0:T(8,128)(2,1)S(1)} %collective-permute-done.23.refs_6_), channel_id=1, source_target_pairs={{0,4},{4,0},{8,12},{12,8},{16,20},{20,16},{24,28},{28,24},{1,5},{5... | collective-permute-start | bytes 1572872 | tf_op jit(solution)/shard_map/ppermute | solution.py:618
  78.4 31.4 %collective-permute-start.25 = (bf16[256,1024]{1,0:T(8,128)(2,1)S(1)}, bf16[256,1024]{1,0:T(8,128)(2,1)S(1)}, u32[]{:S(2)}, u32[]{:S(2)}) collective-permute-start(bf16[256,1024]{1,0:T(8,128)(2,1)S(1)} %collective-permute-done.23.refs_6_), channel_id=1, source_target_pairs={{0,1},{1,0},{2,3},{3,2},{4,5},{5,4},{6,7},{7,6},{8,9},{9,8},{10,11... | collective-permute-start | bytes 1572872 | tf_op jit(solution)/shard_map/ppermute | solution.py:622
  78.4 5.5 %collective-permute-start.18 = (bf16[544,128]{1,0:T(8,128)(2,1)S(1)}, bf16[544,128]{1,0:T(8,128)(2,1)S(1)}, u32[]{:S(2)}, u32[]{:S(2)}) collective-permute-start(bf16[544,128]{1,0:T(8,128)(2,1)S(1)} %get-tuple-element.56), channel_id=1, source_target_pairs={{0,0},{4,1},{2,2},{6,3},{1,4},{5,5},{3,6},{7,7},{9,8},{13,9},{11,1... | collective-permute-start | bytes 417800 | tf_op jit(solution)/shard_map/ppermute | solution.py:637
  83.9 9.0 %collective-permute-start.8 = (bf16[544,128]{1,0:T(8,128)(2,1)S(1)}, bf16[544,128]{1,0:T(8,128)(2,1)S(1)}, u32[]{:S(2)}, u32[]{:S(2)}) collective-permute-start(bf16[544,128]{1,0:T(8,128)(2,1)S(1)} %get-tuple-element.47), channel_id=1, source_target_pairs={{16,0},{20,1},{18,2},{22,3},{17,4},{21,5},{19,6},{23,7},{25,8},{29... | collective-permute-start | bytes 417800 | tf_op jit(solution)/shard_map/ppermute | solution.py:640
  102.1 8.9 %collective-permute-start.26 = (bf16[256,1024]{1,0:T(8,128)(2,1)S(1)}, bf16[256,1024]{1,0:T(8,128)(2,1)S(1)}, u32[]{:S(2)}, u32[]{:S(2)}) collective-permute-start(bf16[256,1024]{1,0:T(8,128)(2,1)S(1)} %collective-permute-done.24.refs_7_), channel_id=1, source_target_pairs={{0,1},{1,0},{2,3},{3,2},{4,5},{5,4},{6,7},{7,6},{8,9},{9,8},{10,11... | collective-permute-start | bytes 1572872 | tf_op jit(solution)/shard_map/ppermute | solution.py:622
  109.2 16.6 %collective-permute-start.15 = (bf16[256,1024]{1,0:T(8,128)(2,1)S(1)}, bf16[256,1024]{1,0:T(8,128)(2,1)S(1)}, u32[]{:S(2)}, u32[]{:S(2)}) collective-permute-start(bf16[256,1024]{1,0:T(8,128)(2,1)S(1)} %collective-permute-done.13.refs_4_), channel_id=1, source_target_pairs={{0,1},{1,0},{2,3},{3,2},{4,5},{5,4},{6,7},{7,6},{8,9},{9,8},{10,11... | collective-permute-start | bytes 1572872 | tf_op jit(solution)/shard_map/ppermute | solution.py:622
  109.4 16.5 %collective-permute-start.16 = (bf16[256,1024]{1,0:T(8,128)(2,1)S(1)}, bf16[256,1024]{1,0:T(8,128)(2,1)S(1)}, u32[]{:S(2)}, u32[]{:S(2)}) collective-permute-start(bf16[256,1024]{1,0:T(8,128)(2,1)S(1)} %collective-permute-done.14.refs_5_), channel_id=1, source_target_pairs={{0,1},{1,0},{2,3},{3,2},{4,5},{5,4},{6,7},{7,6},{8,9},{9,8},{10,11... | collective-permute-start | bytes 1572872 | tf_op jit(solution)/shard_map/ppermute | solution.py:622
  109.8 16.1 %collective-permute-start.28 = (bf16[128,2048]{1,0:T(8,128)(2,1)S(1)}, bf16[128,2048]{1,0:T(8,128)(2,1)S(1)}, u32[]{:S(2)}, u32[]{:S(2)}) collective-permute-start(bf16[128,2048]{1,0:T(8,128)(2,1)S(1)} %shard_map.113), channel_id=1, source_target_pairs={{0,2},{1,3},{2,0},{3,1},{4,6},{5,7},{6,4},{7,5},{8,10},{9,11},{10,... | collective-permute-start | bytes 1572872 | tf_op jit(solution)/shard_map/ppermute | solution.py:631
  111.0 14.8 %collective-permute-start.11 = (bf16[2,128,128]{2,1,0:T(8,128)(2,1)S(1)}, bf16[2,128,128]{2,1,0:T(8,128)(2,1)S(1)}, u32[]{:S(2)}, u32[]{:S(2)}) collective-permute-start(bf16[2,128,128]{2,1,0:T(8,128)(2,1)S(1)} %get-tuple-element.51), channel_id=1, source_target_pairs={{0,2},{1,3},{2,0},{3,1},{4,6},{5,7},{6,4},{7,5},{8,10},{9,11},{10,... | collective-permute-start | bytes 196616 | tf_op jit(solution)/shard_map/ppermute | solution.py:645
  111.8 14.0 %collective-permute-start.12 = (bf16[2,128,128]{2,1,0:T(8,128)(2,1)S(1)}, bf16[2,128,128]{2,1,0:T(8,128)(2,1)S(1)}, u32[]{:S(2)}, u32[]{:S(2)}) collective-permute-start(bf16[2,128,128]{2,1,0:T(8,128)(2,1)S(1)} %get-tuple-element.52), channel_id=1, source_target_pairs={{0,3},{1,2},{2,1},{3,0},{4,7},{5,6},{6,5},{7,4},{8,11},{9,10},{10,... | collective-permute-start | bytes 196616 | tf_op jit(solution)/shard_map/ppermute | solution.py:645
  (8 other events, 73.0 us)

commit v9 on v7

--- a/solution.py
+++ b/solution.py
@@ -65,23 +65,26 @@
     return jax.ShapeDtypeStruct(dims, kind)
 
 
-def unit_heads(normed, w_qk, w_value, outs, clusters, steps, width):
-    z = lax.axis_index(SEQ) >> 1
-    rows = normed.shape[0]
-    span = 2 * width
-    odd = (z & 1) == 1
-    row_at = lax.broadcasted_iota(jnp.int32, (EXTRA, span), 0)
-    key_proj = jnp.dot(normed[...], w_qk[...], preferred_element_type=jnp.float32)
+def unit_rows(normed, w_qk, w_value, outs, width, here):
+    odd = ((lax.axis_index(SEQ) >> 1) & 1) == 1
+    key_proj = jnp.dot(normed[here, :], w_qk[...], preferred_element_type=jnp.float32)
     units = []
     for q in range(2):
         k = key_proj[:, q * width : (q + 1) * width]
         total = jnp.sum(k * k, axis=-1, keepdims=True)
         units.append((k * lax.rsqrt(total + NORM_EPS)).astype(jnp.bfloat16))
-    val_proj = jnp.dot(normed[...], w_value[...], preferred_element_type=jnp.float32)
+    val_proj = jnp.dot(normed[here, :], w_value[...], preferred_element_type=jnp.float32)
     values = [val_proj[:, q * width : (q + 1) * width].astype(jnp.bfloat16) for q in range(2)]
     for q, out in enumerate(outs):
-        out[:rows, :width] = jnp.where(odd, units[1 - q], units[q])
-        out[:rows, width:] = jnp.where(odd, values[1 - q], values[q])
+        out[here, :width] = jnp.where(odd, units[1 - q], units[q])
+        out[here, width:] = jnp.where(odd, values[1 - q], values[q])
+
+
+def id_tails(outs, clusters, steps, rows, width):
+    z = lax.axis_index(SEQ) >> 1
+    span = 2 * width
+    row_at = lax.broadcasted_iota(jnp.int32, (EXTRA, span), 0)
+    for q, out in enumerate(outs):
         id_row = clusters[pl.ds(steps[q] ^ z, 1), :].astype(jnp.float32)
         tail = jnp.zeros((EXTRA, span), jnp.float32)
         for part in range(rows // span):
@@ -91,10 +94,10 @@
 
 
 def project_far_body(
-    tokens_at, gain_at, w_qk, w_value, clusters_at, w_out, *rest, width, stages, parts
+    tokens_at, gain_at, w_qk, w_value, clusters_at, w_out, w_up, *rest, width, stages, parts
 ):
-    out_low, out_high, normed, clusters, qk_next, val_next, out_early, out_late, out_rest = rest[:9]
-    tokens, gain, qk_buf, val_buf, sems, token_sems, out_sems = rest[9:]
+    out_low, out_high, normed, clusters, qk_next, val_next, out_early, out_late, out_rest, up_part = rest[:10]
+    tokens, gain, qk_buf, val_buf, sems, token_sems, out_sems = rest[10:]
     z = lax.axis_index(SEQ) >> 1
     y = lax.axis_index(SEQ) & 1
     step = tokens.shape[0] // parts
@@ -133,23 +136,35 @@
         pltpu.make_async_copy(clusters_at, clusters, sems.at[3]),
         pltpu.make_async_copy(w_qk.at[:, second], qk_next, sems.at[4]),
         pltpu.make_async_copy(w_value.at[:, second], val_next, sems.at[5]),
+        pltpu.make_async_copy(w_up.at[:, pl.ds(0, up_part.shape[1])], up_part, sems.at[6]),
     ]
     for copy in (copies[0], *slab_copies, *copies[1:4], *out_copies, *copies[4:]):
         copy.start()
     copies[0].wait()
-    for copy, here in zip(slab_copies, slabs):
-        copy.wait()
+    half_rows = tokens.shape[0] // 2
+    row_halves = [pl.ds(h * half_rows, half_rows) for h in range(2)]
+
+    def normalize(h):
+        here = row_halves[h]
         wide = tokens[here, :].astype(jnp.float32)
         mean = jnp.mean(wide * wide, axis=-1, keepdims=True)
         normed[here, :] = (wide * lax.rsqrt(mean + NORM_EPS) * gain[...]).astype(jnp.bfloat16)
-    for copy in copies[1:4]:
+
+    for copy in slab_copies[: parts // 2]:
         copy.wait()
-    unit_heads(normed, qk_buf, val_buf, (out_low, out_high), clusters, (2, 3), width)
+    normalize(0)
+    for copy in slab_copies[parts // 2 :] + copies[1:4]:
+        copy.wait()
+    outs = (out_low, out_high)
+    unit_rows(normed, qk_buf, val_buf, outs, width, row_halves[0])
+    normalize(1)
+    unit_rows(normed, qk_buf, val_buf, outs, width, row_halves[1])
+    id_tails(outs, clusters, (2, 3), tokens.shape[0], width)
     for copy in copies[4:] + out_copies:
         copy.wait()
 
 
-def project_far(tokens, gain, w_qk, w_value, clusters, w_out, width, stages, parts=4):
+def project_far(tokens, gain, w_qk, w_value, clusters, w_out, w_up, width, stages, parts=4):
     rows, depth = tokens.shape
     message = shape((rows + EXTRA, 2 * width))
     pair = (depth, 2 * width)
@@ -165,29 +180,34 @@
             shape((2 * width, w_out.shape[1] // 2)),
             shape((2 * width, w_out.shape[1] // 2)),
             shape((2 * width, w_out.shape[1] // 2)),
+            shape((depth, w_up.shape[1] // 4)),
         ),
-        in_specs=[any_spec()] * 6,
-        out_specs=(vmem_spec(),) * 9,
+        in_specs=[any_spec()] * 7,
+        out_specs=(vmem_spec(),) * 10,
         scratch_shapes=[
             pltpu.VMEM((rows, depth), jnp.bfloat16),
             pltpu.VMEM((1, depth), jnp.float32),
             pltpu.VMEM(pair, jnp.bfloat16),
             pltpu.VMEM(pair, jnp.bfloat16),
-            pltpu.SemaphoreType.DMA((6,)),
+            pltpu.SemaphoreType.DMA((7,)),
             pltpu.SemaphoreType.DMA((parts,)),
             pltpu.SemaphoreType.DMA((6,)),
         ],
         compiler_params=params(20),
         cost_estimate=cost(8 * rows * depth * width, 2 * rows * depth + 12 * depth * width),
-    )(*[held(a) for a in (tokens, gain.reshape(1, depth), w_qk, w_value, clusters, w_out)])
+    )(*[held(a) for a in (tokens, gain.reshape(1, depth), w_qk, w_value, clusters, w_out, w_up)])
 
 
 def project_near_body(
-    normed, w_qk, w_value, clusters, w_up, out_low, out_high, next_half, sem, *, width
+    normed, w_qk, w_value, clusters, w_up, out_low, out_high, next_part, sem, *, width
 ):
-    copy = pltpu.make_async_copy(w_up.at[:, pl.ds(0, next_half.shape[1])], next_half, sem)
+    step = next_part.shape[1]
+    copy = pltpu.make_async_copy(w_up.at[:, pl.ds(step, step)], next_part, sem)
     copy.start()
-    unit_heads(normed, w_qk, w_value, (out_low, out_high), clusters, (0, 1), width)
+    rows = normed.shape[0]
+    outs = (out_low, out_high)
+    unit_rows(normed, w_qk, w_value, outs, width, pl.ds(0, rows))
+    id_tails(outs, clusters, (0, 1), rows, width)
     copy.wait()
 
 
@@ -196,7 +216,7 @@
     message = shape((rows + EXTRA, 2 * width))
     return pl.pallas_call(
         functools.partial(project_near_body, width=width),
-        out_shape=(message, message, shape((depth, w_up.shape[1] // 2))),
+        out_shape=(message, message, shape((depth, w_up.shape[1] // 4))),
         in_specs=[vmem_spec()] * 4 + [any_spec()],
         out_specs=(vmem_spec(),) * 3,
         scratch_shapes=[pltpu.SemaphoreType.DMA],
@@ -205,8 +225,8 @@
     )(normed, w_qk, w_value, clusters, held(w_up))
 
 
-def up_body(normed, first, w_up, w_down, hidden, next_half, second, sems):
-    half = first.shape[1]
+def up_body(normed, first, next_to, w_up, w_down, hidden, next_half, second, sems):
+    step, half = first.shape[1], 2 * first.shape[1]
     copies = (
         pltpu.make_async_copy(w_up.at[:, pl.ds(half, half)], second, sems.at[0]),
         pltpu.make_async_copy(
@@ -215,21 +235,22 @@
     )
     for copy in copies:
         copy.start()
-    for at, weights in enumerate((first, second)):
-        if at == 1:
+    for at, weights in ((0, first), (step, next_to), (half, second)):
+        if at == half:
             copies[0].wait()
         grown = jnp.dot(normed[...], weights[...], preferred_element_type=jnp.float32)
-        hidden[:, at * half : (at + 1) * half] = jnp.maximum(grown, 0.0).astype(jnp.bfloat16)
+        cols = slice(at, at + weights.shape[1])
+        hidden[:, cols] = jnp.maximum(grown, 0.0).astype(jnp.bfloat16)
     copies[1].wait()
 
 
-def up(normed, first, w_up, w_down):
+def up(normed, first, next_to, w_up, w_down):
     rows, depth = normed.shape
     units = w_up.shape[1]
     return pl.pallas_call(
         up_body,
         out_shape=(shape((rows, units)), shape((units, w_down.shape[1] // 2))),
-        in_specs=[vmem_spec(), vmem_spec(), any_spec(), any_spec()],
+        in_specs=[vmem_spec()] * 3 + [any_spec()] * 2,
         out_specs=(vmem_spec(), vmem_spec()),
         scratch_shapes=[
             pltpu.VMEM((depth, units // 2), jnp.bfloat16),
@@ -237,7 +258,7 @@
         ],
         compiler_params=params(24),
         cost_estimate=cost(2 * rows * depth * units, 2 * depth * units + 4 * rows * depth),
-    )(normed, first, held(w_up), held(w_down))
+    )(normed, first, next_to, held(w_up), held(w_down))
 
 
 def down_body(hidden, first, w_down, mine, far, away, second, held_rows, sem, *, share):
@@ -590,8 +611,8 @@
     swap_y = [(s, s ^ 1) for s in range(seq_count)]
     messages, own, other = [None] * heads, [None] * heads, [None] * heads
     early, late = (heads - 1, 0), (heads - 2, 1)
-    messages[2], messages[3], normed, ids, qk_next, val_next, *out_parts = project_far(
-        tokens, norm_gain, w_qk, w_value, clusters, w_out, width, (early, late)
+    messages[2], messages[3], normed, ids, qk_next, val_next, *out_parts, up_part = project_far(
+        tokens, norm_gain, w_qk, w_value, clusters, w_out, w_up, width, (early, late)
     )
     for k in (3, 2):
         own[k] = lax.ppermute(messages[k], BOTH, steps[k])
@@ -606,7 +627,7 @@
     messages[0], messages[1], up_first = project_near(normed, qk_next, val_next, ids, w_up, width)
     for k in (1, 0):
         own[k] = lax.ppermute(messages[k], BOTH, steps[k])
-    hidden, down_first = up(normed, up_first, w_up, w_down)
+    hidden, down_first = up(normed, up_part, up_first, w_up, w_down)
     mine, far, sent = down(hidden, down_first, w_down, share)
     got = lax.ppermute(sent, TENSOR, swaps[1])
     for k in range(heads):

time: 128 us -> 128 us (level)
  waiting for transfers between devices: 56.7 us -> 54 us
  starting transfers between devices: 38.7 us -> 41.3 us
    ppermute x4, waiting for transfers between devices: 11.6 us -> 8.9 us  [by_heads(): back[k] = lax.ppermute(result, BOTH, turned(steps[k]))]
    ppermute x4, starting transfers between devices: 4.39 us -> 6.9 us  [by_heads(): back[k] = lax.ppermute(result, BOTH, turned(steps[k]))]
  transfers between devices with their start and end apart: 29 -> 29, of which waited for: 10 -> 10; matrix products, arithmetic and copies ran while one was open for 0% -> 0% of each run, Pallas kernels for 17% -> 18%
where the time goes in v9:
time: 128 us
  waiting for transfers between devices  54 us (42%)
  starting transfers between devices  41.3 us (32%)
  Pallas kernels  31.8 us (25%)
    ppermute x6, waiting for transfers between devices, by_heads(): lax.ppermute(away[d - 1], TENSOR, swaps[d])  17.9 us
    ppermute x4, starting transfers between devices, by_heads(): other[k] = lax.ppermute(own[k], TENSOR, swaps[1])  12.3 us
    ppermute x2, waiting for transfers between devices, by_heads(): here = lax.ppermute(out_parts.pop(0), TENSOR, swaps[2])  10.3 us
    pallas_call x2, Pallas kernels, attend(): pl.pallas_call(functools.partial(attend_body, heads=heads, width=width, o...  10.1 us
    ppermute x1, waiting for transfers between devices, by_heads(): there = lax.ppermute(out_parts.pop(0), TENSOR, swaps[2])  9.67 us
    ppermute x4, waiting for transfers between devices, by_heads(): back[k] = lax.ppermute(result, BOTH, turned(steps[k]))  8.9 us
    ppermute x4, starting transfers between devices, by_heads(): own[k] = lax.ppermute(messages[k], BOTH, steps[k])  7.62 us
    ppermute x4, waiting for transfers between devices, by_heads(): own[k] = lax.ppermute(messages[k], BOTH, steps[k])  7.18 us
  transfers between devices with their start and end apart: 29, of which 10 were waited for; matrix products, arithmetic and copies ran while one was open for 0% of the time, Pallas kernels for 18%

profile of v9, /device:TPU:0, one launch (start us, length us, event | category | flops | bytes accessed | tf_op | source)
XLA Modules:
  0.0 127.9 jit_solution(8401028605178420848)
XLA Ops:
  0.6 4.8 %shard_map.104 = (bf16[528,256]{1,0:T(8,128)(2,1)S(1)}, bf16[528,256]{1,0:T(8,128)(2,1)S(1)}, bf16[512,2048]{1,0:T(8,128)(2,1)S(1)}, s32[4,512]{1,0:T(4,128)S(1)...) custom-call(bf16[512,2048]{1,0:T(8,128)(2,1)} %refs_10_.1, ...), custom_call_target="tpu_custom_call" | custom-call | flops 1073741824 | bytes 5242880 | tf_op jit(solution)/shard_map/pallas_call | solution.py:171
  5.5 2.7 %shard_map.105 = (bf16[528,256]{1,0:T(8,128)(2,1)S(1)}, bf16[528,256]{1,0:T(8,128)(2,1)S(1)}, bf16[2048,512]{1,0:T(8,128)(2,1)S(1)}) custom-call(bf16[512,2048]{1,0:T(8,128)(2,1)S(1)} %get-tuple-element.38.normed, bf16[2048,256]{1,0:T(8,128)(2,1)S(1)} %get-tuple-element.39.w_qk, bf16[2048,256]{1,0:T(8,128)(2,1)S(1)} %get-tuple-element.40.w_value, ...), custom_call_target="tpu_custom_call" | custom-call | flops 1073741824 | bytes 4194304 | tf_op jit(solution)/shard_map/pallas_call | solution.py:217
  8.9 4.3 %collective-permute-start.1 = (bf16[528,256]{1,0:T(8,128)(2,1)S(1)}, bf16[528,256]{1,0:T(8,128)(2,1)S(1)}, u32[]{:S(2)}, u32[]{:S(2)}) collective-permute-start(bf16[528,256]{1,0:T(8,128)(2,1)S(1)} %get-tuple-element.43), channel_id=1, source_target_pairs={{0,8},{1,12},{2,10},{3,14},{4,9},{5,13},{6,11},{7,15},{8,1},{9,5},... | collective-permute-start | bytes 811016 | tf_op jit(solution)/shard_map/ppermute | solution.py:629
  13.3 2.6 %collective-permute-start.2 = (bf16[528,256]{1,0:T(8,128)(2,1)S(1)}, bf16[528,256]{1,0:T(8,128)(2,1)S(1)}, u32[]{:S(2)}, u32[]{:S(2)}) collective-permute-start(bf16[528,256]{1,0:T(8,128)(2,1)S(1)} %get-tuple-element.44), channel_id=1, source_target_pairs={{0,16},{1,20},{2,18},{3,22},{4,17},{5,21},{6,19},{7,23},{8,25},{9,... | collective-permute-start | bytes 811016 | tf_op jit(solution)/shard_map/ppermute | solution.py:618
  15.8 1.7 %collective-permute-start.22 = (bf16[512,2048]{1,0:T(8,128)(2,1)S(1)}, bf16[512,2048]{1,0:T(8,128)(2,1)S(1)}, u32[]{:S(2)}, u32[]{:S(2)}) collective-permute-start(bf16[512,2048]{1,0:T(8,128)(2,1)S(1)} %copy-done.2), channel_id=1, source_target_pairs={{0,1},{1,0},{2,3},{3,2},{4,5},{5,4},{6,7},{7,6},{8,9},{9,8},{10,11... | collective-permute-start | bytes 6291464 | tf_op jit(solution)/shard_map/ppermute | solution.py:609
  17.5 1.5 %collective-permute-start.4 = (bf16[528,256]{1,0:T(8,128)(2,1)S(1)}, bf16[528,256]{1,0:T(8,128)(2,1)S(1)}, u32[]{:S(2)}, u32[]{:S(2)}) collective-permute-start(bf16[528,256]{1,0:T(8,128)(2,1)S(1)} %collective-permute-done.refs_0_), channel_id=1, source_target_pairs={{0,1},{1,0},{2,3},{3,2},{4,5},{5,4},{6,7},{7,6},{8,9},{9,8},{10,11... | collective-permute-start | bytes 811016 | tf_op jit(solution)/shard_map/ppermute | solution.py:634
  19.1 7.2 %collective-permute-done.1.refs_1_ = bf16[528,256]{1,0:T(8,128)(2,1)S(1)} collective-permute-done((bf16[528,256]{1,0:T(8,128)(2,1)S(1)}, bf16[528,256]{1,0:T(8,128)(2,1)S(1)}, u32[]{:S(2)}, u32[]{:S(2)}) %collective-permute-start.1) | collective-permute-done | bytes 270368 | tf_op jit(solution)/shard_map/ppermute | solution.py:629
  26.3 10.7 %collective-permute-start.6 = (bf16[528,256]{1,0:T(8,128)(2,1)S(1)}, bf16[528,256]{1,0:T(8,128)(2,1)S(1)}, u32[]{:S(2)}, u32[]{:S(2)}) collective-permute-start(bf16[528,256]{1,0:T(8,128)(2,1)S(1)} %collective-permute-done.2.refs_2_), channel_id=1, source_target_pairs={{0,1},{1,0},{2,3},{3,2},{4,5},{5,4},{6,7},{7,6},{8,9},{9,8},{10,11... | collective-permute-start | bytes 811016 | tf_op jit(solution)/shard_map/ppermute | solution.py:634
  37.0 5.4 %shard_map.110 = (bf16[512,2048]{1,0:T(8,128)(2,1)S(1)}, bf16[2048,1024]{1,0:T(8,128)(2,1)S(1)}) custom-call(bf16[512,2048]{1,0:T(8,128)(2,1)S(1)} %get-tuple-element.38.normed, bf16[2048,512]{1,0:T(8,128)(2,1)S(1)} %get-tuple-element.63.first, bf16[2048,512]{1,0:T(8,128)(2,1)S(1)} %get-tuple-element.64.next_to, bf16[2048,2048]{1,0:T(8,128)(2,1)} %w_up.5, ...), custom_call_target="tpu_custom_call" | custom-call | flops 4294967296 | bytes 12582912 | tf_op jit(solution)/shard_map/pallas_call | solution.py:250
  42.4 1.6 %collective-permute-start.23 = (bf16[256,1024]{1,0:T(8,128)(2,1)S(1)}, bf16[256,1024]{1,0:T(8,128)(2,1)S(1)}, u32[]{:S(2)}, u32[]{:S(2)}) collective-permute-start(bf16[256,1024]{1,0:T(8,128)(2,1)S(1)} %get-tuple-element.62), channel_id=1, source_target_pairs={{0,2},{1,3},{2,0},{3,1},{4,6},{5,7},{6,4},{7,5},{8,10},{9,11},{10,... | collective-permute-start | bytes 1572872 | tf_op jit(solution)/shard_map/ppermute | solution.py:621
  46.0 5.0 %shard_map.111 = (f32[128,2048]{1,0:T(8,128)S(1)}, f32[128,2048]{1,0:T(8,128)S(1)}, bf16[2,128,2048]{2,1,0:T(8,128)(2,1)S(1)}) custom-call(bf16[512,2048]{1,0:T(8,128)(2,1)S(1)} %get-tuple-element.65.hidden, bf16[2048,1024]{1,0:T(8,128)(2,1)S(1)} %get-tuple-element.66.first, bf16[2048,2048]{1,0:T(8,128)(2,1)} %w_down.3), custom_call_target="tpu_custom_call" | custom-call | flops 4294967296 | bytes 14680064 | tf_op jit(solution)/shard_map/pallas_call | solution.py:289
  51.6 5.2 %shard_map.106 = (bf16[544,128]{1,0:T(8,128)(2,1)S(1)}, bf16[544,128]{1,0:T(8,128)(2,1)S(1)}, bf16[8,512,256]{2,1,0:T(8,128)(2,1)S(1)}, f32[8,8,512]{2,1,0:T(8,128)S(1)}) custom-call(bf16[528,256]{1,0:T(8,128)(2,1)S(1)} %collective-permute-done.refs_0_, bf16[528,256]{1,0:T(8,128)(2,1)S(1)} %collective-permute-done.1.refs_1_, ...), custom_call_target="tpu_custom_call" | custom-call | flops 2415919104 | bytes 2097152 | tf_op jit(solution)/shard_map/pallas_call | solution.py:433
  58.7 9.8 %collective-permute-done.13.refs_4_ = bf16[256,1024]{1,0:T(8,128)(2,1)S(1)} collective-permute-done((bf16[256,1024]{1,0:T(8,128)(2,1)S(1)}, bf16[256,1024]{1,0:T(8,128)(2,1)S(1)}, u32[]{:S(2)}, u32[]{:S(2)}) %collective-permute-start.13) | collective-permute-done | bytes 524320 | tf_op jit(solution)/shard_map/ppermute | solution.py:621
  69.1 9.7 %collective-permute-done.14.refs_5_ = bf16[256,1024]{1,0:T(8,128)(2,1)S(1)} collective-permute-done((bf16[256,1024]{1,0:T(8,128)(2,1)S(1)}, bf16[256,1024]{1,0:T(8,128)(2,1)S(1)}, u32[]{:S(2)}, u32[]{:S(2)}) %collective-permute-start.14) | collective-permute-done | bytes 524320 | tf_op jit(solution)/shard_map/ppermute | solution.py:625
  79.5 4.8 %shard_map.107 = (bf16[544,128]{1,0:T(8,128)(2,1)S(1)}, bf16[544,128]{1,0:T(8,128)(2,1)S(1)}) custom-call(bf16[8,512,256]{2,1,0:T(8,128)(2,1)S(1)} %get-tuple-element.46.refs_0_, f32[8,8,512]{2,1,0:T(8,128)S(1)} %get-tuple-element.47.refs_1_), custom_call_target="tpu_custom_call" | custom-call | flops 2415919104 | bytes 2097152 | tf_op jit(solution)/shard_map/pallas_call | solution.py:433
  84.7 5.7 %collective-permute-done.8.refs_0_ = bf16[544,128]{1,0:T(8,128)(2,1)S(1)} collective-permute-done((bf16[544,128]{1,0:T(8,128)(2,1)S(1)}, bf16[544,128]{1,0:T(8,128)(2,1)S(1)}, u32[]{:S(2)}, u32[]{:S(2)}) %collective-permute-start.8) | collective-permute-done | bytes 139296 | tf_op jit(solution)/shard_map/ppermute | solution.py:645
  90.4 4.5 %collective-permute-start.9 = (bf16[544,128]{1,0:T(8,128)(2,1)S(1)}, bf16[544,128]{1,0:T(8,128)(2,1)S(1)}, u32[]{:S(2)}, u32[]{:S(2)}) collective-permute-start(bf16[544,128]{1,0:T(8,128)(2,1)S(1)} %get-tuple-element.49), channel_id=1, source_target_pairs={{8,0},{12,1},{10,2},{14,3},{9,4},{13,5},{11,6},{15,7},{1,8},{5,9},... | collective-permute-start | bytes 417800 | tf_op jit(solution)/shard_map/ppermute | solution.py:645
  94.9 3.2 %collective-permute-done.9.refs_1_ = bf16[544,128]{1,0:T(8,128)(2,1)S(1)} collective-permute-done((bf16[544,128]{1,0:T(8,128)(2,1)S(1)}, bf16[544,128]{1,0:T(8,128)(2,1)S(1)}, u32[]{:S(2)}, u32[]{:S(2)}) %collective-permute-start.9) | collective-permute-done | bytes 139296 | tf_op jit(solution)/shard_map/ppermute | solution.py:645
  98.1 2.0 %collective-permute-start.19 = (bf16[2,128,128]{2,1,0:T(8,128)(2,1)S(1)}, bf16[2,128,128]{2,1,0:T(8,128)(2,1)S(1)}, u32[]{:S(2)}, u32[]{:S(2)}) collective-permute-start(bf16[2,128,128]{2,1,0:T(8,128)(2,1)S(1)} %get-tuple-element.59), channel_id=1, source_target_pairs={{0,1},{1,0},{2,3},{3,2},{4,5},{5,4},{6,7},{7,6},{8,9},{9,8},{10,11... | collective-permute-start | bytes 196616 | tf_op jit(solution)/shard_map/ppermute | solution.py:650
  102.7 2.7 %collective-permute-done.20.refs_2_ = bf16[2,128,128]{2,1,0:T(8,128)(2,1)S(1)} collective-permute-done((bf16[2,128,128]{2,1,0:T(8,128)(2,1)S(1)}, bf16[2,128,128]{2,1,0:T(8,128)(2,1)S(1)}, u32[]{:S(2)}, u32[]{:S(2)}) %collective-permute-start.20) | collective-permute-done | bytes 65568 | tf_op jit(solution)/shard_map/ppermute | solution.py:650
  107.1 2.6 %collective-permute-done.21.refs_3_ = bf16[2,128,128]{2,1,0:T(8,128)(2,1)S(1)} collective-permute-done((bf16[2,128,128]{2,1,0:T(8,128)(2,1)S(1)}, bf16[2,128,128]{2,1,0:T(8,128)(2,1)S(1)}, u32[]{:S(2)}, u32[]{:S(2)}) %collective-permute-start.21) | collective-permute-done | bytes 65568 | tf_op jit(solution)/shard_map/ppermute | solution.py:650
  112.6 2.1 %shard_map.112 = (f32[128,2048]{1,0:T(8,128)S(1)}, bf16[512,2048]{1,0:T(8,128)(2,1)S(1)}) custom-call(bf16[2,128,128]{2,1,0:T(8,128)(2,1)S(1)} %get-tuple-element.58.refs_0_, bf16[2,128,128]{2,1,0:T(8,128)(2,1)S(1)} %collective-permute-done.19.refs_1_, bf16[2,128,128]{2,1,0:T(8,128)(2,1)S(1)} %collective-permute-done.20.refs_2_, ...), custom_call_target="tpu_custom_call" | custom-call | flops 536870912 | bytes 10485760 | tf_op jit(solution)/shard_map/pallas_call | solution.py:544
  114.6 11.6 %collective-permute-done.11.refs_2_ = bf16[2,128,128]{2,1,0:T(8,128)(2,1)S(1)} collective-permute-done((bf16[2,128,128]{2,1,0:T(8,128)(2,1)S(1)}, bf16[2,128,128]{2,1,0:T(8,128)(2,1)S(1)}, u32[]{:S(2)}, u32[]{:S(2)}) %collective-permute-start.11) | collective-permute-done | bytes 65568 | tf_op jit(solution)/shard_map/ppermute | solution.py:650
  126.3 1.5 %shard_map.114 = (bf16[128,2048]{1,0:T(8,128)(2,1)}, f32[4,32,128]{2,1,0:T(8,128)}) custom-call(bf16[2,128,128]{2,1,0:T(8,128)(2,1)S(1)} %get-tuple-element.50.refs_0_, bf16[2,128,128]{2,1,0:T(8,128)(2,1)S(1)} %collective-permute-done.10.refs_1_, bf16[2,128,128]{2,1,0:T(8,128)(2,1)S(1)} %collective-permute-done.11.refs_2_, ...), custom_call_target="tpu_custom_call" | custom-call | flops 536870912 | bytes 6291456 | tf_op jit(solution)/shard_map/pallas_call | solution.py:587
  (51 shorter events, 14.0 us)
Async XLA Ops:
  8.2 9.3 %collective-permute-start = (bf16[528,256]{1,0:T(8,128)(2,1)S(1)}, bf16[528,256]{1,0:T(8,128)(2,1)S(1)}, u32[]{:S(2)}, u32[]{:S(2)}) collective-permute-start(bf16[528,256]{1,0:T(8,128)(2,1)S(1)} %get-tuple-element.42), channel_id=1, source_target_pairs={{0,0},{1,4},{2,2},{3,6},{4,1},{5,5},{6,3},{7,7},{8,9},{9,13},{10,1... | collective-permute-start | bytes 811016 | tf_op jit(solution)/shard_map/ppermute | solution.py:629
  8.9 17.3 %collective-permute-start.1 = (bf16[528,256]{1,0:T(8,128)(2,1)S(1)}, bf16[528,256]{1,0:T(8,128)(2,1)S(1)}, u32[]{:S(2)}, u32[]{:S(2)}) collective-permute-start(bf16[528,256]{1,0:T(8,128)(2,1)S(1)} %get-tuple-element.43), channel_id=1, source_target_pairs={{0,8},{1,12},{2,10},{3,14},{4,9},{5,13},{6,11},{7,15},{8,1},{9,5},... | collective-permute-start | bytes 811016 | tf_op jit(solution)/shard_map/ppermute | solution.py:629
  13.3 13.0 %collective-permute-start.2 = (bf16[528,256]{1,0:T(8,128)(2,1)S(1)}, bf16[528,256]{1,0:T(8,128)(2,1)S(1)}, u32[]{:S(2)}, u32[]{:S(2)}) collective-permute-start(bf16[528,256]{1,0:T(8,128)(2,1)S(1)} %get-tuple-element.44), channel_id=1, source_target_pairs={{0,16},{1,20},{2,18},{3,22},{4,17},{5,21},{6,19},{7,23},{8,25},{9,... | collective-permute-start | bytes 811016 | tf_op jit(solution)/shard_map/ppermute | solution.py:618
  15.8 96.4 %collective-permute-start.22 = (bf16[512,2048]{1,0:T(8,128)(2,1)S(1)}, bf16[512,2048]{1,0:T(8,128)(2,1)S(1)}, u32[]{:S(2)}, u32[]{:S(2)}) collective-permute-start(bf16[512,2048]{1,0:T(8,128)(2,1)S(1)} %copy-done.2), channel_id=1, source_target_pairs={{0,1},{1,0},{2,3},{3,2},{4,5},{5,4},{6,7},{7,6},{8,9},{9,8},{10,11... | collective-permute-start | bytes 6291464 | tf_op jit(solution)/shard_map/ppermute | solution.py:609
  17.5 24.9 %collective-permute-start.3 = (bf16[528,256]{1,0:T(8,128)(2,1)S(1)}, bf16[528,256]{1,0:T(8,128)(2,1)S(1)}, u32[]{:S(2)}, u32[]{:S(2)}) collective-permute-start(bf16[528,256]{1,0:T(8,128)(2,1)S(1)} %get-tuple-element.45), channel_id=1, source_target_pairs={{0,24},{1,28},{2,26},{3,30},{4,25},{5,29},{6,27},{7,31},{8,17},{9,... | collective-permute-start | bytes 811016 | tf_op jit(solution)/shard_map/ppermute | solution.py:618
  17.5 26.5 %collective-permute-start.4 = (bf16[528,256]{1,0:T(8,128)(2,1)S(1)}, bf16[528,256]{1,0:T(8,128)(2,1)S(1)}, u32[]{:S(2)}, u32[]{:S(2)}) collective-permute-start(bf16[528,256]{1,0:T(8,128)(2,1)S(1)} %collective-permute-done.refs_0_), channel_id=1, source_target_pairs={{0,1},{1,0},{2,3},{3,2},{4,5},{5,4},{6,7},{7,6},{8,9},{9,8},{10,11... | collective-permute-start | bytes 811016 | tf_op jit(solution)/shard_map/ppermute | solution.py:634
  26.2 18.3 %collective-permute-start.5 = (bf16[528,256]{1,0:T(8,128)(2,1)S(1)}, bf16[528,256]{1,0:T(8,128)(2,1)S(1)}, u32[]{:S(2)}, u32[]{:S(2)}) collective-permute-start(bf16[528,256]{1,0:T(8,128)(2,1)S(1)} %collective-permute-done.1.refs_1_), channel_id=1, source_target_pairs={{0,1},{1,0},{2,3},{3,2},{4,5},{5,4},{6,7},{7,6},{8,9},{9,8},{10,11... | collective-permute-start | bytes 811016 | tf_op jit(solution)/shard_map/ppermute | solution.py:634
  26.3 19.8 %collective-permute-start.6 = (bf16[528,256]{1,0:T(8,128)(2,1)S(1)}, bf16[528,256]{1,0:T(8,128)(2,1)S(1)}, u32[]{:S(2)}, u32[]{:S(2)}) collective-permute-start(bf16[528,256]{1,0:T(8,128)(2,1)S(1)} %collective-permute-done.2.refs_2_), channel_id=1, source_target_pairs={{0,1},{1,0},{2,3},{3,2},{4,5},{5,4},{6,7},{7,6},{8,9},{9,8},{10,11... | collective-permute-start | bytes 811016 | tf_op jit(solution)/shard_map/ppermute | solution.py:634
  42.4 14.9 %collective-permute-start.23 = (bf16[256,1024]{1,0:T(8,128)(2,1)S(1)}, bf16[256,1024]{1,0:T(8,128)(2,1)S(1)}, u32[]{:S(2)}, u32[]{:S(2)}) collective-permute-start(bf16[256,1024]{1,0:T(8,128)(2,1)S(1)} %get-tuple-element.62), channel_id=1, source_target_pairs={{0,2},{1,3},{2,0},{3,1},{4,6},{5,7},{6,4},{7,5},{8,10},{9,11},{10,... | collective-permute-start | bytes 1572872 | tf_op jit(solution)/shard_map/ppermute | solution.py:621
  44.0 24.5 %collective-permute-start.13 = (bf16[256,1024]{1,0:T(8,128)(2,1)S(1)}, bf16[256,1024]{1,0:T(8,128)(2,1)S(1)}, u32[]{:S(2)}, u32[]{:S(2)}) collective-permute-start(bf16[256,1024]{1,0:T(8,128)(2,1)S(1)} %get-tuple-element.54), channel_id=1, source_target_pairs={{0,2},{1,3},{2,0},{3,1},{4,6},{5,7},{6,4},{7,5},{8,10},{9,11},{10,... | collective-permute-start | bytes 1572872 | tf_op jit(solution)/shard_map/ppermute | solution.py:621
  44.5 34.3 %collective-permute-start.14 = (bf16[256,1024]{1,0:T(8,128)(2,1)S(1)}, bf16[256,1024]{1,0:T(8,128)(2,1)S(1)}, u32[]{:S(2)}, u32[]{:S(2)}) collective-permute-start(bf16[256,1024]{1,0:T(8,128)(2,1)S(1)} %get-tuple-element.55), channel_id=1, source_target_pairs={{0,2},{1,3},{2,0},{3,1},{4,6},{5,7},{6,4},{7,5},{8,10},{9,11},{10,... | collective-permute-start | bytes 1572872 | tf_op jit(solution)/shard_map/ppermute | solution.py:625
  51.0 54.9 %collective-permute-start.27 = (bf16[2,128,2048]{2,1,0:T(8,128)(2,1)S(1)}, bf16[2,128,2048]{2,1,0:T(8,128)(2,1)S(1)}, u32[]{:S(2)}, u32[]{:S(2)}) collective-permute-start(bf16[2,128,2048]{2,1,0:T(8,128)(2,1)S(1)} %get-tuple-element.68), channel_id=1, source_target_pairs={{0,1},{1,0},{2,3},{3,2},{4,5},{5,4},{6,7},{7,6},{8,9},{9,8},{10,11... | collective-permute-start | bytes 3145736 | tf_op jit(solution)/shard_map/ppermute | solution.py:632
  57.3 21.5 %collective-permute-start.17 = (bf16[544,128]{1,0:T(8,128)(2,1)S(1)}, bf16[544,128]{1,0:T(8,128)(2,1)S(1)}, u32[]{:S(2)}, u32[]{:S(2)}) collective-permute-start(bf16[544,128]{1,0:T(8,128)(2,1)S(1)} %get-tuple-element.56), channel_id=1, source_target_pairs={{24,0},{28,1},{26,2},{30,3},{25,4},{29,5},{27,6},{31,7},{17,8},{21... | collective-permute-start | bytes 417800 | tf_op jit(solution)/shard_map/ppermute | solution.py:642
  68.5 34.0 %collective-permute-start.24 = (bf16[256,1024]{1,0:T(8,128)(2,1)S(1)}, bf16[256,1024]{1,0:T(8,128)(2,1)S(1)}, u32[]{:S(2)}, u32[]{:S(2)}) collective-permute-start(bf16[256,1024]{1,0:T(8,128)(2,1)S(1)} %collective-permute-done.23.refs_6_), channel_id=1, source_target_pairs={{0,4},{4,0},{8,12},{12,8},{16,20},{20,16},{24,28},{28,24},{1,5},{5... | collective-permute-start | bytes 1572872 | tf_op jit(solution)/shard_map/ppermute | solution.py:623
  78.8 31.4 %collective-permute-start.25 = (bf16[256,1024]{1,0:T(8,128)(2,1)S(1)}, bf16[256,1024]{1,0:T(8,128)(2,1)S(1)}, u32[]{:S(2)}, u32[]{:S(2)}) collective-permute-start(bf16[256,1024]{1,0:T(8,128)(2,1)S(1)} %collective-permute-done.23.refs_6_), channel_id=1, source_target_pairs={{0,1},{1,0},{2,3},{3,2},{4,5},{5,4},{6,7},{7,6},{8,9},{9,8},{10,11... | collective-permute-start | bytes 1572872 | tf_op jit(solution)/shard_map/ppermute | solution.py:626
  78.8 5.5 %collective-permute-start.18 = (bf16[544,128]{1,0:T(8,128)(2,1)S(1)}, bf16[544,128]{1,0:T(8,128)(2,1)S(1)}, u32[]{:S(2)}, u32[]{:S(2)}) collective-permute-start(bf16[544,128]{1,0:T(8,128)(2,1)S(1)} %get-tuple-element.57), channel_id=1, source_target_pairs={{0,0},{4,1},{2,2},{6,3},{1,4},{5,5},{3,6},{7,7},{9,8},{13,9},{11,1... | collective-permute-start | bytes 417800 | tf_op jit(solution)/shard_map/ppermute | solution.py:642
  84.3 6.0 %collective-permute-start.8 = (bf16[544,128]{1,0:T(8,128)(2,1)S(1)}, bf16[544,128]{1,0:T(8,128)(2,1)S(1)}, u32[]{:S(2)}, u32[]{:S(2)}) collective-permute-start(bf16[544,128]{1,0:T(8,128)(2,1)S(1)} %get-tuple-element.48), channel_id=1, source_target_pairs={{16,0},{20,1},{18,2},{22,3},{17,4},{21,5},{19,6},{23,7},{25,8},{29... | collective-permute-start | bytes 417800 | tf_op jit(solution)/shard_map/ppermute | solution.py:645
  90.4 7.7 %collective-permute-start.9 = (bf16[544,128]{1,0:T(8,128)(2,1)S(1)}, bf16[544,128]{1,0:T(8,128)(2,1)S(1)}, u32[]{:S(2)}, u32[]{:S(2)}) collective-permute-start(bf16[544,128]{1,0:T(8,128)(2,1)S(1)} %get-tuple-element.49), channel_id=1, source_target_pairs={{8,0},{12,1},{10,2},{14,3},{9,4},{13,5},{11,6},{15,7},{1,8},{5,9},... | collective-permute-start | bytes 417800 | tf_op jit(solution)/shard_map/ppermute | solution.py:645
  102.5 8.9 %collective-permute-start.26 = (bf16[256,1024]{1,0:T(8,128)(2,1)S(1)}, bf16[256,1024]{1,0:T(8,128)(2,1)S(1)}, u32[]{:S(2)}, u32[]{:S(2)}) collective-permute-start(bf16[256,1024]{1,0:T(8,128)(2,1)S(1)} %collective-permute-done.24.refs_7_), channel_id=1, source_target_pairs={{0,1},{1,0},{2,3},{3,2},{4,5},{5,4},{6,7},{7,6},{8,9},{9,8},{10,11... | collective-permute-start | bytes 1572872 | tf_op jit(solution)/shard_map/ppermute | solution.py:626
  109.7 16.6 %collective-permute-start.15 = (bf16[256,1024]{1,0:T(8,128)(2,1)S(1)}, bf16[256,1024]{1,0:T(8,128)(2,1)S(1)}, u32[]{:S(2)}, u32[]{:S(2)}) collective-permute-start(bf16[256,1024]{1,0:T(8,128)(2,1)S(1)} %collective-permute-done.13.refs_4_), channel_id=1, source_target_pairs={{0,1},{1,0},{2,3},{3,2},{4,5},{5,4},{6,7},{7,6},{8,9},{9,8},{10,11... | collective-permute-start | bytes 1572872 | tf_op jit(solution)/shard_map/ppermute | solution.py:626
  109.8 16.5 %collective-permute-start.16 = (bf16[256,1024]{1,0:T(8,128)(2,1)S(1)}, bf16[256,1024]{1,0:T(8,128)(2,1)S(1)}, u32[]{:S(2)}, u32[]{:S(2)}) collective-permute-start(bf16[256,1024]{1,0:T(8,128)(2,1)S(1)} %collective-permute-done.14.refs_5_), channel_id=1, source_target_pairs={{0,1},{1,0},{2,3},{3,2},{4,5},{5,4},{6,7},{7,6},{8,9},{9,8},{10,11... | collective-permute-start | bytes 1572872 | tf_op jit(solution)/shard_map/ppermute | solution.py:626
  110.2 16.1 %collective-permute-start.28 = (bf16[128,2048]{1,0:T(8,128)(2,1)S(1)}, bf16[128,2048]{1,0:T(8,128)(2,1)S(1)}, u32[]{:S(2)}, u32[]{:S(2)}) collective-permute-start(bf16[128,2048]{1,0:T(8,128)(2,1)S(1)} %shard_map.113), channel_id=1, source_target_pairs={{0,2},{1,3},{2,0},{3,1},{4,6},{5,7},{6,4},{7,5},{8,10},{9,11},{10,... | collective-permute-start | bytes 1572872 | tf_op jit(solution)/shard_map/ppermute | solution.py:636
  111.4 14.8 %collective-permute-start.11 = (bf16[2,128,128]{2,1,0:T(8,128)(2,1)S(1)}, bf16[2,128,128]{2,1,0:T(8,128)(2,1)S(1)}, u32[]{:S(2)}, u32[]{:S(2)}) collective-permute-start(bf16[2,128,128]{2,1,0:T(8,128)(2,1)S(1)} %get-tuple-element.52), channel_id=1, source_target_pairs={{0,2},{1,3},{2,0},{3,1},{4,6},{5,7},{6,4},{7,5},{8,10},{9,11},{10,... | collective-permute-start | bytes 196616 | tf_op jit(solution)/shard_map/ppermute | solution.py:650
  112.3 14.0 %collective-permute-start.12 = (bf16[2,128,128]{2,1,0:T(8,128)(2,1)S(1)}, bf16[2,128,128]{2,1,0:T(8,128)(2,1)S(1)}, u32[]{:S(2)}, u32[]{:S(2)}) collective-permute-start(bf16[2,128,128]{2,1,0:T(8,128)(2,1)S(1)} %get-tuple-element.53), channel_id=1, source_target_pairs={{0,3},{1,2},{2,1},{3,0},{4,7},{5,6},{6,5},{7,4},{8,11},{9,10},{10,... | collective-permute-start | bytes 196616 | tf_op jit(solution)/shard_map/ppermute | solution.py:650
  (8 other events, 72.8 us)

commit v10 on v7

--- a/solution.py
+++ b/solution.py
@@ -311,8 +311,8 @@
         own, other = refs[:heads], refs[heads : 2 * heads]
         refs = refs[2 * heads :]
         outs = refs[: len(steps)]
-        kv, id_rows = refs[len(steps) : len(steps) + 2]
-        query, id_cols, acc, den = refs[len(steps) + 2 :]
+        kv, id_rows, later_sums = refs[len(steps) : len(steps) + 3]
+        query, id_cols, acc, den = refs[len(steps) + 3 :]
         rows = kv.shape[1]
         for b, source in enumerate(list(own) + list(other)):
             kv[b] = source[:rows, :]
@@ -322,20 +322,24 @@
             )
             id_rows[b] = jnp.broadcast_to(id_row, (8, rows))
     else:
-        kv, id_rows = refs[:2]
-        outs = refs[2 : 2 + len(steps)]
-        query, id_cols, acc, den = refs[2 + len(steps) :]
+        kv, id_rows, sums = refs[:3]
+        outs = refs[3 : 3 + len(steps)]
+        query, id_cols, acc, den = refs[3 + len(steps) :]
         rows = kv.shape[1]
 
-    count = 2 * heads
-    cluster_col = lax.broadcasted_iota(jnp.int32, (owned, rows), 0)
-    wanted = jnp.concatenate(
-        [cluster_col + owned * block_of(k, heads) for k in steps], axis=0
-    ).astype(jnp.float32)
-    sums = jnp.zeros((len(steps) * owned, width), jnp.float32)
-    for b in range(count):
-        one_hot = jnp.where(wanted == id_rows[b, :1, :], 1.0, 0.0).astype(jnp.bfloat16)
-        sums = sums + jnp.dot(one_hot, kv[b, :, :width], preferred_element_type=jnp.float32)
+    if first:
+        cluster_col = lax.broadcasted_iota(jnp.int32, (owned, rows), 0)
+        order = [*steps, *(k for k in range(heads - 1, -1, -1) if k not in steps)]
+        wanted = jnp.concatenate(
+            [cluster_col + owned * block_of(k, heads) for k in order], axis=0
+        ).astype(jnp.float32)
+        sums = jnp.zeros((heads * owned, width), jnp.float32)
+        for b in range(2 * heads):
+            one_hot = jnp.where(wanted == id_rows[b, :1, :], 1.0, 0.0).astype(jnp.bfloat16)
+            sums = sums + jnp.dot(
+                one_hot, kv[b, :, :width], preferred_element_type=jnp.float32
+            )
+        later_sums[...] = sums[len(steps) * owned :]
 
     def pair(blocks, masked):
         spread = jnp.concatenate([id_cols[...]] * (rows // width), axis=1)
@@ -407,6 +411,7 @@
         out_shape += (
             shape((2 * heads, rows, 2 * width)),
             shape((2 * heads, 8, rows), jnp.float32),
+            shape(((heads - len(steps)) * owned, width), jnp.float32),
         )
     units = (heads * heads + heads // 2) * len(steps) // heads
     return pl.pallas_call(
@@ -614,12 +619,12 @@
     picked = pick(far, got)
     came = lax.ppermute(picked, TENSOR, swaps[2])
     back, pieces, sums = [None] * heads, {}, {}
-    *results, kv, id_rows = attend(
+    *results, kv, id_rows, late_sums = attend(
         own + other, heads, tok_rows, width, owned, early, True
     )
     for k, result in zip(early, results):
         back[k] = lax.ppermute(result, BOTH, turned(steps[k]))
-    results = attend([kv, id_rows], heads, tok_rows, width, owned, late, False)
+    results = attend([kv, id_rows, late_sums], heads, tok_rows, width, owned, late, False)
     for k, result in zip(late, results):
         back[k] = lax.ppermute(result, BOTH, turned(steps[k]))
 

time: 128 us -> 127 us (level)
  no operation moved by 1% of the time
where the time goes in v10:
time: 127 us
  waiting for transfers between devices  56.7 us (45%)
  starting transfers between devices  38.7 us (30%)
  Pallas kernels  30.9 us (24%)
    ppermute x6, waiting for transfers between devices, by_heads(): lax.ppermute(away[d - 1], TENSOR, swaps[d])  17.8 us
    ppermute x4, starting transfers between devices, by_heads(): other[k] = lax.ppermute(own[k], TENSOR, swaps[1])  12.4 us
    ppermute x4, waiting for transfers between devices, by_heads(): back[k] = lax.ppermute(result, BOTH, turned(steps[k]))  11.6 us
    ppermute x2, waiting for transfers between devices, by_heads(): here = lax.ppermute(out_parts.pop(0), TENSOR, swaps[2])  10.4 us
    pallas_call x2, Pallas kernels, attend(): pl.pallas_call(functools.partial(attend_body, heads=heads, width=width, o...  9.87 us
    ppermute x1, waiting for transfers between devices, by_heads(): there = lax.ppermute(out_parts.pop(0), TENSOR, swaps[2])  9.68 us
    ppermute x4, starting transfers between devices, by_heads(): own[k] = lax.ppermute(messages[k], BOTH, steps[k])  7.62 us
    ppermute x4, waiting for transfers between devices, by_heads(): own[k] = lax.ppermute(messages[k], BOTH, steps[k])  7.1 us
  transfers between devices with their start and end apart: 29, of which 10 were waited for; matrix products, arithmetic and copies ran while one was open for 0% of the time, Pallas kernels for 17%

profile of v10, /device:TPU:0, one launch (start us, length us, event | category | flops | bytes accessed | tf_op | source)
XLA Modules:
  0.0 127.2 jit_solution(4802324191900474292)
XLA Ops:
  0.6 4.3 %shard_map.104 = (bf16[528,256]{1,0:T(8,128)(2,1)S(1)}, bf16[528,256]{1,0:T(8,128)(2,1)S(1)}, bf16[512,2048]{1,0:T(8,128)(2,1)S(1)}, s32[4,512]{1,0:T(4,128)S(1)...) custom-call(bf16[512,2048]{1,0:T(8,128)(2,1)} %refs_10_.1, ...), custom_call_target="tpu_custom_call" | custom-call | flops 1073741824 | bytes 5242880 | tf_op jit(solution)/shard_map/pallas_call | solution.py:156
  5.0 3.3 %shard_map.105 = (bf16[528,256]{1,0:T(8,128)(2,1)S(1)}, bf16[528,256]{1,0:T(8,128)(2,1)S(1)}, bf16[2048,1024]{1,0:T(8,128)(2,1)S(1)}) custom-call(bf16[512,2048]{1,0:T(8,128)(2,1)S(1)} %get-tuple-element.38.normed, bf16[2048,256]{1,0:T(8,128)(2,1)S(1)} %get-tuple-element.39.w_qk, bf16[2048,256]{1,0:T(8,128)(2,1)S(1)} %get-tuple-element.40.w_value, ...), custom_call_target="tpu_custom_call" | custom-call | flops 1073741824 | bytes 4194304 | tf_op jit(solution)/shard_map/pallas_call | solution.py:197
  9.0 4.3 %collective-permute-start.1 = (bf16[528,256]{1,0:T(8,128)(2,1)S(1)}, bf16[528,256]{1,0:T(8,128)(2,1)S(1)}, u32[]{:S(2)}, u32[]{:S(2)}) collective-permute-start(bf16[528,256]{1,0:T(8,128)(2,1)S(1)} %get-tuple-element.43), channel_id=1, source_target_pairs={{0,8},{1,12},{2,10},{3,14},{4,9},{5,13},{6,11},{7,15},{8,1},{9,5},... | collective-permute-start | bytes 811016 | tf_op jit(solution)/shard_map/ppermute | solution.py:613
  13.3 2.6 %collective-permute-start.2 = (bf16[528,256]{1,0:T(8,128)(2,1)S(1)}, bf16[528,256]{1,0:T(8,128)(2,1)S(1)}, u32[]{:S(2)}, u32[]{:S(2)}) collective-permute-start(bf16[528,256]{1,0:T(8,128)(2,1)S(1)} %get-tuple-element.44), channel_id=1, source_target_pairs={{0,16},{1,20},{2,18},{3,22},{4,17},{5,21},{6,19},{7,23},{8,25},{9,... | collective-permute-start | bytes 811016 | tf_op jit(solution)/shard_map/ppermute | solution.py:602
  15.9 1.7 %collective-permute-start.22 = (bf16[512,2048]{1,0:T(8,128)(2,1)S(1)}, bf16[512,2048]{1,0:T(8,128)(2,1)S(1)}, u32[]{:S(2)}, u32[]{:S(2)}) collective-permute-start(bf16[512,2048]{1,0:T(8,128)(2,1)S(1)} %copy-done.2), channel_id=1, source_target_pairs={{0,1},{1,0},{2,3},{3,2},{4,5},{5,4},{6,7},{7,6},{8,9},{9,8},{10,11... | collective-permute-start | bytes 6291464 | tf_op jit(solution)/shard_map/ppermute | solution.py:593
  17.6 1.6 %collective-permute-start.4 = (bf16[528,256]{1,0:T(8,128)(2,1)S(1)}, bf16[528,256]{1,0:T(8,128)(2,1)S(1)}, u32[]{:S(2)}, u32[]{:S(2)}) collective-permute-start(bf16[528,256]{1,0:T(8,128)(2,1)S(1)} %collective-permute-done.refs_0_), channel_id=1, source_target_pairs={{0,1},{1,0},{2,3},{3,2},{4,5},{5,4},{6,7},{7,6},{8,9},{9,8},{10,11... | collective-permute-start | bytes 811016 | tf_op jit(solution)/shard_map/ppermute | solution.py:618
  19.2 7.1 %collective-permute-done.1.refs_1_ = bf16[528,256]{1,0:T(8,128)(2,1)S(1)} collective-permute-done((bf16[528,256]{1,0:T(8,128)(2,1)S(1)}, bf16[528,256]{1,0:T(8,128)(2,1)S(1)}, u32[]{:S(2)}, u32[]{:S(2)}) %collective-permute-start.1) | collective-permute-done | bytes 270368 | tf_op jit(solution)/shard_map/ppermute | solution.py:613
  26.3 10.8 %collective-permute-start.6 = (bf16[528,256]{1,0:T(8,128)(2,1)S(1)}, bf16[528,256]{1,0:T(8,128)(2,1)S(1)}, u32[]{:S(2)}, u32[]{:S(2)}) collective-permute-start(bf16[528,256]{1,0:T(8,128)(2,1)S(1)} %collective-permute-done.2.refs_2_), channel_id=1, source_target_pairs={{0,1},{1,0},{2,3},{3,2},{4,5},{5,4},{6,7},{7,6},{8,9},{9,8},{10,11... | collective-permute-start | bytes 811016 | tf_op jit(solution)/shard_map/ppermute | solution.py:618
  37.1 4.7 %shard_map.110 = (bf16[512,2048]{1,0:T(8,128)(2,1)S(1)}, bf16[2048,1024]{1,0:T(8,128)(2,1)S(1)}) custom-call(bf16[512,2048]{1,0:T(8,128)(2,1)S(1)} %get-tuple-element.38.normed, bf16[2048,1024]{1,0:T(8,128)(2,1)S(1)} %get-tuple-element.64.first, bf16[2048,2048]{1,0:T(8,128)(2,1)} %w_up.3, bf16[2048,2048]{1,0:T(8,128)(2,1)} %w_down.3), custom_call_target="tpu_custom_call" | custom-call | flops 4294967296 | bytes 12582912 | tf_op jit(solution)/shard_map/pallas_call | solution.py:229
  41.8 1.6 %collective-permute-start.23 = (bf16[256,1024]{1,0:T(8,128)(2,1)S(1)}, bf16[256,1024]{1,0:T(8,128)(2,1)S(1)}, u32[]{:S(2)}, u32[]{:S(2)}) collective-permute-start(bf16[256,1024]{1,0:T(8,128)(2,1)S(1)} %get-tuple-element.63), channel_id=1, source_target_pairs={{0,2},{1,3},{2,0},{3,1},{4,6},{5,7},{6,4},{7,5},{8,10},{9,11},{10,... | collective-permute-start | bytes 1572872 | tf_op jit(solution)/shard_map/ppermute | solution.py:605
  45.4 5.0 %shard_map.111 = (f32[128,2048]{1,0:T(8,128)S(1)}, f32[128,2048]{1,0:T(8,128)S(1)}, bf16[2,128,2048]{2,1,0:T(8,128)(2,1)S(1)}) custom-call(bf16[512,2048]{1,0:T(8,128)(2,1)S(1)} %get-tuple-element.65.hidden, bf16[2048,1024]{1,0:T(8,128)(2,1)S(1)} %get-tuple-element.66.first, bf16[2048,2048]{1,0:T(8,128)(2,1)} %w_down.3), custom_call_target="tpu_custom_call" | custom-call | flops 4294967296 | bytes 14680064 | tf_op jit(solution)/shard_map/pallas_call | solution.py:268
  50.9 5.2 %shard_map.106 = (bf16[544,128]{1,0:T(8,128)(2,1)S(1)}, bf16[544,128]{1,0:T(8,128)(2,1)S(1)}, bf16[8,512,256]{2,1,0:T(8,128)(2,1)S(1)}, f32[8,8,512]{2,1,0:T(8,128)S(1)}, f32[64,128]{1,0:T(8,128)S(1)}) custom-call(bf16[528,256]{1,0:T(8,128)(2,1)S(1)} %collective-permute-done.refs_0_, bf16[528,256]{1,0:T(8,128)(2,1)S(1)} %collective-permute-done.1.refs_1_, ...), custom_call_target="tpu_custom_call" | custom-call | flops 2415919104 | bytes 2097152 | tf_op jit(solution)/shard_map/pallas_call | solution.py:417
  57.9 10.0 %collective-permute-done.13.refs_4_ = bf16[256,1024]{1,0:T(8,128)(2,1)S(1)} collective-permute-done((bf16[256,1024]{1,0:T(8,128)(2,1)S(1)}, bf16[256,1024]{1,0:T(8,128)(2,1)S(1)}, u32[]{:S(2)}, u32[]{:S(2)}) %collective-permute-start.13) | collective-permute-done | bytes 524320 | tf_op jit(solution)/shard_map/ppermute | solution.py:605
  68.5 9.7 %collective-permute-done.14.refs_5_ = bf16[256,1024]{1,0:T(8,128)(2,1)S(1)} collective-permute-done((bf16[256,1024]{1,0:T(8,128)(2,1)S(1)}, bf16[256,1024]{1,0:T(8,128)(2,1)S(1)}, u32[]{:S(2)}, u32[]{:S(2)}) %collective-permute-start.14) | collective-permute-done | bytes 524320 | tf_op jit(solution)/shard_map/ppermute | solution.py:609
  78.8 4.6 %shard_map.107 = (bf16[544,128]{1,0:T(8,128)(2,1)S(1)}, bf16[544,128]{1,0:T(8,128)(2,1)S(1)}) custom-call(bf16[8,512,256]{2,1,0:T(8,128)(2,1)S(1)} %get-tuple-element.46.refs_0_, f32[8,8,512]{2,1,0:T(8,128)S(1)} %get-tuple-element.47.refs_1_, f32[64,128]{1,0:T(8,128)S(1)} %get-tuple-element.48.refs_2_), custom_call_target="tpu_custom_call" | custom-call | flops 2415919104 | bytes 2097152 | tf_op jit(solution)/shard_map/pallas_call | solution.py:417
  84.5 8.0 %collective-permute-done.8.refs_0_ = bf16[544,128]{1,0:T(8,128)(2,1)S(1)} collective-permute-done((bf16[544,128]{1,0:T(8,128)(2,1)S(1)}, bf16[544,128]{1,0:T(8,128)(2,1)S(1)}, u32[]{:S(2)}, u32[]{:S(2)}) %collective-permute-start.8) | collective-permute-done | bytes 139296 | tf_op jit(solution)/shard_map/ppermute | solution.py:629
  93.9 3.6 %collective-permute-done.9.refs_1_ = bf16[544,128]{1,0:T(8,128)(2,1)S(1)} collective-permute-done((bf16[544,128]{1,0:T(8,128)(2,1)S(1)}, bf16[544,128]{1,0:T(8,128)(2,1)S(1)}, u32[]{:S(2)}, u32[]{:S(2)}) %collective-permute-start.9) | collective-permute-done | bytes 139296 | tf_op jit(solution)/shard_map/ppermute | solution.py:629
  97.6 1.9 %collective-permute-start.19 = (bf16[2,128,128]{2,1,0:T(8,128)(2,1)S(1)}, bf16[2,128,128]{2,1,0:T(8,128)(2,1)S(1)}, u32[]{:S(2)}, u32[]{:S(2)}) collective-permute-start(bf16[2,128,128]{2,1,0:T(8,128)(2,1)S(1)} %get-tuple-element.60), channel_id=1, source_target_pairs={{0,1},{1,0},{2,3},{3,2},{4,5},{5,4},{6,7},{7,6},{8,9},{9,8},{10,11... | collective-permute-start | bytes 196616 | tf_op jit(solution)/shard_map/ppermute | solution.py:634
  100.3 1.5 %collective-permute-start.20 = (bf16[2,128,128]{2,1,0:T(8,128)(2,1)S(1)}, bf16[2,128,128]{2,1,0:T(8,128)(2,1)S(1)}, u32[]{:S(2)}, u32[]{:S(2)}) collective-permute-start(bf16[2,128,128]{2,1,0:T(8,128)(2,1)S(1)} %get-tuple-element.61), channel_id=1, source_target_pairs={{0,2},{1,3},{2,0},{3,1},{4,6},{5,7},{6,4},{7,5},{8,10},{9,11},{10,... | collective-permute-start | bytes 196616 | tf_op jit(solution)/shard_map/ppermute | solution.py:634
  102.0 2.7 %collective-permute-done.20.refs_2_ = bf16[2,128,128]{2,1,0:T(8,128)(2,1)S(1)} collective-permute-done((bf16[2,128,128]{2,1,0:T(8,128)(2,1)S(1)}, bf16[2,128,128]{2,1,0:T(8,128)(2,1)S(1)}, u32[]{:S(2)}, u32[]{:S(2)}) %collective-permute-start.20) | collective-permute-done | bytes 65568 | tf_op jit(solution)/shard_map/ppermute | solution.py:634
  106.4 2.6 %collective-permute-done.21.refs_3_ = bf16[2,128,128]{2,1,0:T(8,128)(2,1)S(1)} collective-permute-done((bf16[2,128,128]{2,1,0:T(8,128)(2,1)S(1)}, bf16[2,128,128]{2,1,0:T(8,128)(2,1)S(1)}, u32[]{:S(2)}, u32[]{:S(2)}) %collective-permute-start.21) | collective-permute-done | bytes 65568 | tf_op jit(solution)/shard_map/ppermute | solution.py:634
  111.9 2.0 %shard_map.112 = (f32[128,2048]{1,0:T(8,128)S(1)}, bf16[512,2048]{1,0:T(8,128)(2,1)S(1)}) custom-call(bf16[2,128,128]{2,1,0:T(8,128)(2,1)S(1)} %get-tuple-element.59.refs_0_, bf16[2,128,128]{2,1,0:T(8,128)(2,1)S(1)} %collective-permute-done.19.refs_1_, bf16[2,128,128]{2,1,0:T(8,128)(2,1)S(1)} %collective-permute-done.20.refs_2_, ...), custom_call_target="tpu_custom_call" | custom-call | flops 536870912 | bytes 10485760 | tf_op jit(solution)/shard_map/pallas_call | solution.py:528
  114.0 11.6 %collective-permute-done.11.refs_2_ = bf16[2,128,128]{2,1,0:T(8,128)(2,1)S(1)} collective-permute-done((bf16[2,128,128]{2,1,0:T(8,128)(2,1)S(1)}, bf16[2,128,128]{2,1,0:T(8,128)(2,1)S(1)}, u32[]{:S(2)}, u32[]{:S(2)}) %collective-permute-start.11) | collective-permute-done | bytes 65568 | tf_op jit(solution)/shard_map/ppermute | solution.py:634
  125.6 1.5 %shard_map.114 = (bf16[128,2048]{1,0:T(8,128)(2,1)}, f32[4,32,128]{2,1,0:T(8,128)}) custom-call(bf16[2,128,128]{2,1,0:T(8,128)(2,1)S(1)} %get-tuple-element.51.refs_0_, bf16[2,128,128]{2,1,0:T(8,128)(2,1)S(1)} %collective-permute-done.10.refs_1_, bf16[2,128,128]{2,1,0:T(8,128)(2,1)S(1)} %collective-permute-done.11.refs_2_, ...), custom_call_target="tpu_custom_call" | custom-call | flops 536870912 | bytes 6291456 | tf_op jit(solution)/shard_map/pallas_call | solution.py:571
  (51 shorter events, 14.5 us)
Async XLA Ops:
  8.3 9.3 %collective-permute-start = (bf16[528,256]{1,0:T(8,128)(2,1)S(1)}, bf16[528,256]{1,0:T(8,128)(2,1)S(1)}, u32[]{:S(2)}, u32[]{:S(2)}) collective-permute-start(bf16[528,256]{1,0:T(8,128)(2,1)S(1)} %get-tuple-element.42), channel_id=1, source_target_pairs={{0,0},{1,4},{2,2},{3,6},{4,1},{5,5},{6,3},{7,7},{8,9},{9,13},{10,1... | collective-permute-start | bytes 811016 | tf_op jit(solution)/shard_map/ppermute | solution.py:613
  9.0 17.3 %collective-permute-start.1 = (bf16[528,256]{1,0:T(8,128)(2,1)S(1)}, bf16[528,256]{1,0:T(8,128)(2,1)S(1)}, u32[]{:S(2)}, u32[]{:S(2)}) collective-permute-start(bf16[528,256]{1,0:T(8,128)(2,1)S(1)} %get-tuple-element.43), channel_id=1, source_target_pairs={{0,8},{1,12},{2,10},{3,14},{4,9},{5,13},{6,11},{7,15},{8,1},{9,5},... | collective-permute-start | bytes 811016 | tf_op jit(solution)/shard_map/ppermute | solution.py:613
  13.3 13.0 %collective-permute-start.2 = (bf16[528,256]{1,0:T(8,128)(2,1)S(1)}, bf16[528,256]{1,0:T(8,128)(2,1)S(1)}, u32[]{:S(2)}, u32[]{:S(2)}) collective-permute-start(bf16[528,256]{1,0:T(8,128)(2,1)S(1)} %get-tuple-element.44), channel_id=1, source_target_pairs={{0,16},{1,20},{2,18},{3,22},{4,17},{5,21},{6,19},{7,23},{8,25},{9,... | collective-permute-start | bytes 811016 | tf_op jit(solution)/shard_map/ppermute | solution.py:602
  15.9 95.6 %collective-permute-start.22 = (bf16[512,2048]{1,0:T(8,128)(2,1)S(1)}, bf16[512,2048]{1,0:T(8,128)(2,1)S(1)}, u32[]{:S(2)}, u32[]{:S(2)}) collective-permute-start(bf16[512,2048]{1,0:T(8,128)(2,1)S(1)} %copy-done.2), channel_id=1, source_target_pairs={{0,1},{1,0},{2,3},{3,2},{4,5},{5,4},{6,7},{7,6},{8,9},{9,8},{10,11... | collective-permute-start | bytes 6291464 | tf_op jit(solution)/shard_map/ppermute | solution.py:593
  17.6 24.2 %collective-permute-start.3 = (bf16[528,256]{1,0:T(8,128)(2,1)S(1)}, bf16[528,256]{1,0:T(8,128)(2,1)S(1)}, u32[]{:S(2)}, u32[]{:S(2)}) collective-permute-start(bf16[528,256]{1,0:T(8,128)(2,1)S(1)} %get-tuple-element.45), channel_id=1, source_target_pairs={{0,24},{1,28},{2,26},{3,30},{4,25},{5,29},{6,27},{7,31},{8,17},{9,... | collective-permute-start | bytes 811016 | tf_op jit(solution)/shard_map/ppermute | solution.py:602
  17.6 25.7 %collective-permute-start.4 = (bf16[528,256]{1,0:T(8,128)(2,1)S(1)}, bf16[528,256]{1,0:T(8,128)(2,1)S(1)}, u32[]{:S(2)}, u32[]{:S(2)}) collective-permute-start(bf16[528,256]{1,0:T(8,128)(2,1)S(1)} %collective-permute-done.refs_0_), channel_id=1, source_target_pairs={{0,1},{1,0},{2,3},{3,2},{4,5},{5,4},{6,7},{7,6},{8,9},{9,8},{10,11... | collective-permute-start | bytes 811016 | tf_op jit(solution)/shard_map/ppermute | solution.py:618
  26.3 17.6 %collective-permute-start.5 = (bf16[528,256]{1,0:T(8,128)(2,1)S(1)}, bf16[528,256]{1,0:T(8,128)(2,1)S(1)}, u32[]{:S(2)}, u32[]{:S(2)}) collective-permute-start(bf16[528,256]{1,0:T(8,128)(2,1)S(1)} %collective-permute-done.1.refs_1_), channel_id=1, source_target_pairs={{0,1},{1,0},{2,3},{3,2},{4,5},{5,4},{6,7},{7,6},{8,9},{9,8},{10,11... | collective-permute-start | bytes 811016 | tf_op jit(solution)/shard_map/ppermute | solution.py:618
  26.3 19.1 %collective-permute-start.6 = (bf16[528,256]{1,0:T(8,128)(2,1)S(1)}, bf16[528,256]{1,0:T(8,128)(2,1)S(1)}, u32[]{:S(2)}, u32[]{:S(2)}) collective-permute-start(bf16[528,256]{1,0:T(8,128)(2,1)S(1)} %collective-permute-done.2.refs_2_), channel_id=1, source_target_pairs={{0,1},{1,0},{2,3},{3,2},{4,5},{5,4},{6,7},{7,6},{8,9},{9,8},{10,11... | collective-permute-start | bytes 811016 | tf_op jit(solution)/shard_map/ppermute | solution.py:618
  41.8 14.9 %collective-permute-start.23 = (bf16[256,1024]{1,0:T(8,128)(2,1)S(1)}, bf16[256,1024]{1,0:T(8,128)(2,1)S(1)}, u32[]{:S(2)}, u32[]{:S(2)}) collective-permute-start(bf16[256,1024]{1,0:T(8,128)(2,1)S(1)} %get-tuple-element.63), channel_id=1, source_target_pairs={{0,2},{1,3},{2,0},{3,1},{4,6},{5,7},{6,4},{7,5},{8,10},{9,11},{10,... | collective-permute-start | bytes 1572872 | tf_op jit(solution)/shard_map/ppermute | solution.py:605
  43.3 24.5 %collective-permute-start.13 = (bf16[256,1024]{1,0:T(8,128)(2,1)S(1)}, bf16[256,1024]{1,0:T(8,128)(2,1)S(1)}, u32[]{:S(2)}, u32[]{:S(2)}) collective-permute-start(bf16[256,1024]{1,0:T(8,128)(2,1)S(1)} %get-tuple-element.55), channel_id=1, source_target_pairs={{0,2},{1,3},{2,0},{3,1},{4,6},{5,7},{6,4},{7,5},{8,10},{9,11},{10,... | collective-permute-start | bytes 1572872 | tf_op jit(solution)/shard_map/ppermute | solution.py:605
  43.9 34.3 %collective-permute-start.14 = (bf16[256,1024]{1,0:T(8,128)(2,1)S(1)}, bf16[256,1024]{1,0:T(8,128)(2,1)S(1)}, u32[]{:S(2)}, u32[]{:S(2)}) collective-permute-start(bf16[256,1024]{1,0:T(8,128)(2,1)S(1)} %get-tuple-element.56), channel_id=1, source_target_pairs={{0,2},{1,3},{2,0},{3,1},{4,6},{5,7},{6,4},{7,5},{8,10},{9,11},{10,... | collective-permute-start | bytes 1572872 | tf_op jit(solution)/shard_map/ppermute | solution.py:609
  50.4 54.9 %collective-permute-start.27 = (bf16[2,128,2048]{2,1,0:T(8,128)(2,1)S(1)}, bf16[2,128,2048]{2,1,0:T(8,128)(2,1)S(1)}, u32[]{:S(2)}, u32[]{:S(2)}) collective-permute-start(bf16[2,128,2048]{2,1,0:T(8,128)(2,1)S(1)} %get-tuple-element.68), channel_id=1, source_target_pairs={{0,1},{1,0},{2,3},{3,2},{4,5},{5,4},{6,7},{7,6},{8,9},{9,8},{10,11... | collective-permute-start | bytes 3145736 | tf_op jit(solution)/shard_map/ppermute | solution.py:616
  56.6 21.5 %collective-permute-start.17 = (bf16[544,128]{1,0:T(8,128)(2,1)S(1)}, bf16[544,128]{1,0:T(8,128)(2,1)S(1)}, u32[]{:S(2)}, u32[]{:S(2)}) collective-permute-start(bf16[544,128]{1,0:T(8,128)(2,1)S(1)} %get-tuple-element.57), channel_id=1, source_target_pairs={{24,0},{28,1},{26,2},{30,3},{25,4},{29,5},{27,6},{31,7},{17,8},{21... | collective-permute-start | bytes 417800 | tf_op jit(solution)/shard_map/ppermute | solution.py:626
  67.9 34.0 %collective-permute-start.24 = (bf16[256,1024]{1,0:T(8,128)(2,1)S(1)}, bf16[256,1024]{1,0:T(8,128)(2,1)S(1)}, u32[]{:S(2)}, u32[]{:S(2)}) collective-permute-start(bf16[256,1024]{1,0:T(8,128)(2,1)S(1)} %collective-permute-done.23.refs_6_), channel_id=1, source_target_pairs={{0,4},{4,0},{8,12},{12,8},{16,20},{20,16},{24,28},{28,24},{1,5},{5... | collective-permute-start | bytes 1572872 | tf_op jit(solution)/shard_map/ppermute | solution.py:607
  78.1 31.4 %collective-permute-start.25 = (bf16[256,1024]{1,0:T(8,128)(2,1)S(1)}, bf16[256,1024]{1,0:T(8,128)(2,1)S(1)}, u32[]{:S(2)}, u32[]{:S(2)}) collective-permute-start(bf16[256,1024]{1,0:T(8,128)(2,1)S(1)} %collective-permute-done.23.refs_6_), channel_id=1, source_target_pairs={{0,1},{1,0},{2,3},{3,2},{4,5},{5,4},{6,7},{7,6},{8,9},{9,8},{10,11... | collective-permute-start | bytes 1572872 | tf_op jit(solution)/shard_map/ppermute | solution.py:610
  78.1 5.3 %collective-permute-start.18 = (bf16[544,128]{1,0:T(8,128)(2,1)S(1)}, bf16[544,128]{1,0:T(8,128)(2,1)S(1)}, u32[]{:S(2)}, u32[]{:S(2)}) collective-permute-start(bf16[544,128]{1,0:T(8,128)(2,1)S(1)} %get-tuple-element.58), channel_id=1, source_target_pairs={{0,0},{4,1},{2,2},{6,3},{1,4},{5,5},{3,6},{7,7},{9,8},{13,9},{11,1... | collective-permute-start | bytes 417800 | tf_op jit(solution)/shard_map/ppermute | solution.py:626
  83.5 9.0 %collective-permute-start.8 = (bf16[544,128]{1,0:T(8,128)(2,1)S(1)}, bf16[544,128]{1,0:T(8,128)(2,1)S(1)}, u32[]{:S(2)}, u32[]{:S(2)}) collective-permute-start(bf16[544,128]{1,0:T(8,128)(2,1)S(1)} %get-tuple-element.49), channel_id=1, source_target_pairs={{16,0},{20,1},{18,2},{22,3},{17,4},{21,5},{19,6},{23,7},{25,8},{29... | collective-permute-start | bytes 417800 | tf_op jit(solution)/shard_map/ppermute | solution.py:629
  92.5 5.1 %collective-permute-start.9 = (bf16[544,128]{1,0:T(8,128)(2,1)S(1)}, bf16[544,128]{1,0:T(8,128)(2,1)S(1)}, u32[]{:S(2)}, u32[]{:S(2)}) collective-permute-start(bf16[544,128]{1,0:T(8,128)(2,1)S(1)} %get-tuple-element.50), channel_id=1, source_target_pairs={{8,0},{12,1},{10,2},{14,3},{9,4},{13,5},{11,6},{15,7},{1,8},{5,9},... | collective-permute-start | bytes 417800 | tf_op jit(solution)/shard_map/ppermute | solution.py:629
  101.9 8.9 %collective-permute-start.26 = (bf16[256,1024]{1,0:T(8,128)(2,1)S(1)}, bf16[256,1024]{1,0:T(8,128)(2,1)S(1)}, u32[]{:S(2)}, u32[]{:S(2)}) collective-permute-start(bf16[256,1024]{1,0:T(8,128)(2,1)S(1)} %collective-permute-done.24.refs_7_), channel_id=1, source_target_pairs={{0,1},{1,0},{2,3},{3,2},{4,5},{5,4},{6,7},{7,6},{8,9},{9,8},{10,11... | collective-permute-start | bytes 1572872 | tf_op jit(solution)/shard_map/ppermute | solution.py:610
  109.0 16.6 %collective-permute-start.15 = (bf16[256,1024]{1,0:T(8,128)(2,1)S(1)}, bf16[256,1024]{1,0:T(8,128)(2,1)S(1)}, u32[]{:S(2)}, u32[]{:S(2)}) collective-permute-start(bf16[256,1024]{1,0:T(8,128)(2,1)S(1)} %collective-permute-done.13.refs_4_), channel_id=1, source_target_pairs={{0,1},{1,0},{2,3},{3,2},{4,5},{5,4},{6,7},{7,6},{8,9},{9,8},{10,11... | collective-permute-start | bytes 1572872 | tf_op jit(solution)/shard_map/ppermute | solution.py:610
  109.1 16.5 %collective-permute-start.16 = (bf16[256,1024]{1,0:T(8,128)(2,1)S(1)}, bf16[256,1024]{1,0:T(8,128)(2,1)S(1)}, u32[]{:S(2)}, u32[]{:S(2)}) collective-permute-start(bf16[256,1024]{1,0:T(8,128)(2,1)S(1)} %collective-permute-done.14.refs_5_), channel_id=1, source_target_pairs={{0,1},{1,0},{2,3},{3,2},{4,5},{5,4},{6,7},{7,6},{8,9},{9,8},{10,11... | collective-permute-start | bytes 1572872 | tf_op jit(solution)/shard_map/ppermute | solution.py:610
  109.5 16.1 %collective-permute-start.28 = (bf16[128,2048]{1,0:T(8,128)(2,1)S(1)}, bf16[128,2048]{1,0:T(8,128)(2,1)S(1)}, u32[]{:S(2)}, u32[]{:S(2)}) collective-permute-start(bf16[128,2048]{1,0:T(8,128)(2,1)S(1)} %shard_map.113), channel_id=1, source_target_pairs={{0,2},{1,3},{2,0},{3,1},{4,6},{5,7},{6,4},{7,5},{8,10},{9,11},{10,... | collective-permute-start | bytes 1572872 | tf_op jit(solution)/shard_map/ppermute | solution.py:620
  110.8 14.8 %collective-permute-start.11 = (bf16[2,128,128]{2,1,0:T(8,128)(2,1)S(1)}, bf16[2,128,128]{2,1,0:T(8,128)(2,1)S(1)}, u32[]{:S(2)}, u32[]{:S(2)}) collective-permute-start(bf16[2,128,128]{2,1,0:T(8,128)(2,1)S(1)} %get-tuple-element.53), channel_id=1, source_target_pairs={{0,2},{1,3},{2,0},{3,1},{4,6},{5,7},{6,4},{7,5},{8,10},{9,11},{10,... | collective-permute-start | bytes 196616 | tf_op jit(solution)/shard_map/ppermute | solution.py:634
  111.6 14.0 %collective-permute-start.12 = (bf16[2,128,128]{2,1,0:T(8,128)(2,1)S(1)}, bf16[2,128,128]{2,1,0:T(8,128)(2,1)S(1)}, u32[]{:S(2)}, u32[]{:S(2)}) collective-permute-start(bf16[2,128,128]{2,1,0:T(8,128)(2,1)S(1)} %get-tuple-element.54), channel_id=1, source_target_pairs={{0,3},{1,2},{2,1},{3,0},{4,7},{5,6},{6,5},{7,4},{8,11},{9,10},{10,... | collective-permute-start | bytes 196616 | tf_op jit(solution)/shard_map/ppermute | solution.py:634
  (8 other events, 73.4 us)
